TPU v7x, 32 devices: a whole 2x2x4 slice. The times are simulated.
32 devices in a mesh: clips: 2 (over y), frames: 4 (over z), heads: 4 (over x, core).
Axes of the slice: x: 2, y: 2, z: 4, core: 2. Of those that a mesh axis runs over, the one named last changes fastest.
Arguments:
- queries: bfloat16 [3072, 3072], P(('clips', 'frames'), 'heads'), parts along dimension 0, may hold values from -25 to 25
- keys: bfloat16 [3072, 3072], P(('clips', 'frames'), 'heads'), parts along dimension 0, may hold values from -6 to 6
- values: bfloat16 [3072, 3072], P(('clips', 'frames'), 'heads'), parts along dimension 0, may hold values from -6 to 6
- grad_out: bfloat16 [3072, 3072], P(('clips', 'frames'), 'heads'), parts along dimension 0, may hold values from -6 to 6
- offsets: int32 [16, 3], P('clips'), parts along dimension 0, may hold values from -2 to 2, as said below
- spatial: int32 [16, 3, 4, 4], P('clips'), parts along dimension 0, may hold values from 0 to 1, as said below
Outputs:
- grad_queries: bfloat16 [3072, 3072], P(('clips', 'frames'), 'heads'), parts along dimension 0
- grad_keys: bfloat16 [3072, 3072], P(('clips', 'frames'), 'heads'), parts along dimension 0
- grad_values: bfloat16 [3072, 3072], P(('clips', 'frames'), 'heads'), parts along dimension 0
There are 2 independent parts, one for each index of `clips`. A program takes and returns all parts, laid end to end along the dimension named above; each array names one. Nothing has to cross between parts.
Inputs may be any that keep to these rules, and one draw needn't show every extreme that they name: Slot 0 of every frame is offset 0; the other slots hold two different nonzero offsets. Slots whose key frame lies outside the clip see nothing. `spatial`: slot 0's diagonal blocks are always 1.
All inputs are finite; a program needn't handle non-finite values.
Results may differ from a plain program's by a relative error of at most 0.0099.
Values may be sent and summed in bfloat16 or wider, within the bound.
No kernel may reach another device: no remote copies, remote signals or barrier semaphores. Data moves between devices by JAX's collectives and lax.ppermute only.
A program may use at most 64 MiB of HBM per device.

v0:
```python
import jax
import jax.numpy as jnp
from jax import lax
from jax.sharding import PartitionSpec as P

HD = 128
TOK_FRAME = 192
FR_DEV = 2
R = 2
NSEL = 3
SB = 4


def padded(cells, sides, width):
    for axis, dim in sides:
        count = lax.axis_size(axis)
        ends = count - 1
        head = lax.slice_in_dim(cells, 0, width, axis=dim)
        tail = lax.slice_in_dim(cells, cells.shape[dim] - width, cells.shape[dim], axis=dim)
        cells = jnp.concatenate(
            [
                lax.ppermute(tail, axis, [(i, (i + 1) % count) for i in range(ends)]),
                cells,
                lax.ppermute(head, axis, [((i + 1) % count, i) for i in range(ends)]),
            ],
            axis=dim,
        )
    return cells


def from_behind(block, axis, distance):
    devices = range(lax.axis_size(axis))
    route = [(i - distance, i) for i in devices if i - distance in devices]
    return lax.ppermute(block, axis, route)


def span_mask(block_mask, inside, block_rows):
    masked = block_mask * inside[:, None, None]
    tokens = jnp.repeat(jnp.repeat(masked, block_rows, axis=1), block_rows, axis=2)
    return jnp.transpose(tokens, (1, 0, 2)).reshape(tokens.shape[1], -1) > 0


def add_frame(accum, piece, where_at):
    current = lax.dynamic_index_in_dim(accum, where_at, 1, False)
    return lax.dynamic_update_index_in_dim(accum, current + piece, where_at, 1)


def local(queries, keys, values, grad_out, offsets, spatial):
    scaling = HD ** (-0.5)
    block_rows = TOK_FRAME // SB
    heads_local = queries.shape[1] // HD
    width_local = heads_local * HD
    frames_total = offsets.shape[0]
    first_frame = lax.axis_index("frames") * FR_DEV
    shape_four = (FR_DEV, TOK_FRAME, heads_local, HD)
    query_own = queries.reshape(shape_four)
    grad_own = grad_out.reshape(shape_four)
    stacked = jnp.stack([keys, values]).reshape(2, FR_DEV, TOK_FRAME, width_local)
    window = padded(stacked, (("frames", 1),), R)
    window = window.reshape(2, FR_DEV + 2 * R, TOK_FRAME, heads_local, HD)
    grad_queries_list = []
    log_list = []
    delta_list = []
    grad_window = jnp.zeros((2, FR_DEV + 2 * R, TOK_FRAME, heads_local, HD), jnp.float32)
    for local_frame in range(FR_DEV):
        frame = first_frame + local_frame
        shifts = lax.dynamic_index_in_dim(offsets, frame, 0, False)
        spots = local_frame + R + shifts
        picked = jnp.stack(
            [lax.dynamic_index_in_dim(window, spots[slot], 1, False) for slot in range(NSEL)], 1
        )
        key_rows = picked[0].reshape(NSEL * TOK_FRAME, heads_local, HD)
        value_rows = picked[1].reshape(NSEL * TOK_FRAME, heads_local, HD)
        inside = ((frame + shifts >= 0) & (frame + shifts < frames_total)).astype(jnp.int32)
        allowed = span_mask(lax.dynamic_index_in_dim(spatial, frame, 0, False), inside, block_rows)
        query_rows = query_own[local_frame]
        grad_rows = grad_own[local_frame]
        scores = (
            jnp.einsum("qhd,khd->hqk", query_rows, key_rows, preferred_element_type=jnp.float32)
            * scaling
        )
        masked = jnp.where(allowed[None], scores, -1e30)
        highest = jnp.max(masked, -1, keepdims=True)
        log_total = highest + jnp.log(jnp.sum(jnp.exp(masked - highest), -1, keepdims=True))
        attn_prob = jnp.exp(masked - log_total)
        prob_low = attn_prob.astype(jnp.bfloat16)
        attended = jnp.einsum(
            "hqk,khd->qhd", prob_low, value_rows, preferred_element_type=jnp.float32
        )
        row_delta = jnp.transpose(jnp.sum(grad_rows.astype(jnp.float32) * attended, -1))
        grad_prob = jnp.einsum(
            "qhd,khd->hqk", grad_rows, value_rows, preferred_element_type=jnp.float32
        )
        grad_score = attn_prob * (grad_prob - row_delta[..., None])
        score_low = grad_score.astype(jnp.bfloat16)
        grad_query = (
            jnp.einsum("hqk,khd->qhd", score_low, key_rows, preferred_element_type=jnp.float32)
            * scaling
        )
        grad_queries_list.append(grad_query)
        log_list.append(log_total[..., 0])
        delta_list.append(row_delta)
        key_part = (
            jnp.einsum("hqk,qhd->khd", score_low, query_rows, preferred_element_type=jnp.float32)
            * scaling
        ).reshape(NSEL, TOK_FRAME, heads_local, HD)
        value_part = jnp.einsum(
            "hqk,qhd->khd", prob_low, grad_rows, preferred_element_type=jnp.float32
        ).reshape(NSEL, TOK_FRAME, heads_local, HD)
        for slot in range(NSEL):
            grad_window = add_frame(
                grad_window, jnp.stack([key_part[slot], value_part[slot]]), spots[slot]
            )
    owned = grad_window[:, R : R + FR_DEV]
    for rim_part, step_by in ((grad_window[:, :R], -1), (grad_window[:, R + FR_DEV :], 1)):
        arrived = from_behind(rim_part.reshape(2, R, TOK_FRAME, width_local), "frames", step_by)
        arrived = arrived.reshape(rim_part.shape)
        if step_by < 0:
            owned = owned.at[:, FR_DEV - R :].add(arrived)
        else:
            owned = owned.at[:, :R].add(arrived)
    grad_key_own = owned[0]
    grad_value_own = owned[1]
    rows_local = FR_DEV * TOK_FRAME
    grad_queries = (
        jnp.stack(grad_queries_list).reshape(rows_local, width_local).astype(jnp.bfloat16)
    )
    grad_keys = grad_key_own.reshape(rows_local, width_local).astype(jnp.bfloat16)
    grad_values = grad_value_own.reshape(rows_local, width_local).astype(jnp.bfloat16)
    return (grad_queries, grad_keys, grad_values)


def solution(mesh):
    return jax.shard_map(
        local,
        mesh=mesh,
        in_specs=(
            P(("clips", "frames"), "heads"),
            P(("clips", "frames"), "heads"),
            P(("clips", "frames"), "heads"),
            P(("clips", "frames"), "heads"),
            P("clips", None),
            P("clips", None, None, None),
        ),
        out_specs=(
            P(("clips", "frames"), "heads"),
            P(("clips", "frames"), "heads"),
            P(("clips", "frames"), "heads"),
        ),
        check_vma=False,
    )
```

profile of v0, /device:TPU:0, one launch (start us, length us, event | category | flops | bytes accessed | tf_op | source)
XLA Modules:
  0.0 126.8 jit_solution(11924624327860563475)
XLA Ops:
  0.7 1.4 %pad_maximum_fusion.3 = bf16[2,2,192,768]{3,2,1,0:T(8,128)(2,1)S(1)} fusion(bf16[1,2,192,768]{3,2,1,0:T(8,128)(2,1)} %bitcast.212, bf16[1,2,192,768]{3,2,1,0:T(8,128)(2,1)} %bitcast.214), kind=kLoop, calls=%fused_computation.38 | loop fusion | flops 589824 | bytes 2359296 | tf_op jit(solution)/shard_map/stack | solution.py:58
  2.1 1.3 %collective-permute-start.1 = (bf16[2,2,192,768]{3,2,1,0:T(8,128)(2,1)S(1)}, bf16[2,2,192,768]{3,2,1,0:T(8,128)(2,1)S(1)}, u32[]{:S(2)}, u32[]{:S(2)}) collective-permute-start(bf16[2,2,192,768]{3,2,1,0:T(8,128)(2,1)S(1)} %pad_maximum_fusion.3), channel_id=1, source_target_pairs={{4,0},{8,4},{12,8},{5,1},{9,5},{13,9},{6,2},{10,6},{14,10},{7,3},{... | collective-permute-start | bytes 3538952 | tf_op jit(solution)/shard_map/ppermute | solution.py:24
  3.4 6.6 %collective-permute-start = (bf16[2,2,192,768]{3,2,1,0:T(8,128)(2,1)S(1)}, bf16[2,2,192,768]{3,2,1,0:T(8,128)(2,1)}, u32[]{:S(2)}, u32[]{:S(2)}) collective-permute-start(bf16[2,2,192,768]{3,2,1,0:T(8,128)(2,1)S(1)} %pad_maximum_fusion.3), channel_id=1, source_target_pairs={{0,4},{4,8},{8,12},{1,5},{5,9},{9,13},{2,6},{6,10},{10,14},{3,7},{... | collective-permute-start | bytes 3538952 | tf_op jit(solution)/shard_map/ppermute | solution.py:22
  10.0 0.2 convert_reduce_fusion.1
  10.2 0.6 fusion.48
  18.4 1.4 %dynamic-slice_reduce_fusion.1 = (s32[3,4,4]{2,1,0:T(4,128)S(1)}, s32[3,4,4]{2,1,0:T(4,128)S(1)}) fusion(s32[8,3,4,4]{0,3,2,1:T(4,128)} %param.19, s32[]{:T(128)S(6)} %select_n.50, s32[]{:T(128)S(6)} %select_n.55), kind=kLoop, calls=%fused_computation.92 | loop fusion | bytes 776 | tf_op jit(solution)/shard_map/jit(dynamic_index_in_dim)/dynamic_slice | solution.py:75
  20.5 0.7 broadcast_in_dim.57
  21.2 1.8 %copy.21 = pred[192,576]{1,0:T(8,128)(4,1)} copy(pred[192,576]{0,1:T(8,128)(4,1)} %bitcast.222) | data formatting | bytes 221184 | tf_op jit(solution)/shard_map/gt | solution.py:40
  22.9 0.7 broadcast_in_dim.53
  23.6 1.8 %copy.14 = pred[192,576]{1,0:T(8,128)(4,1)} copy(pred[192,576]{0,1:T(8,128)(4,1)} %bitcast.223) | data formatting | bytes 221184 | tf_op jit(solution)/shard_map/gt | solution.py:40
  29.2 0.9 slice_bitcast_fusion.17
  30.1 0.9 slice_bitcast_fusion.16
  30.9 2.1 %collective-permute-done.1 = bf16[2,2,192,768]{3,2,1,0:T(8,128)(2,1)S(1)} collective-permute-done((bf16[2,2,192,768]{3,2,1,0:T(8,128)(2,1)S(1)}, bf16[2,2,192,768]{3,2,1,0:T(8,128)(2,1)S(1)}, u32[]{:S(2)}, u32[]{:S(2)}) %collective-permute-start.1) | collective-permute-done | bytes 1179680 | tf_op jit(solution)/shard_map/ppermute | solution.py:24
  33.0 1.1 copy-done.4
  34.2 2.2 %pad_maximum_fusion = bf16[2,6,192,768]{3,2,1,0:T(8,128)(2,1)S(1)} fusion(bf16[2,2,192,768]{3,2,1,0:T(8,128)(2,1)} %copy-done.4, bf16[1,2,192,768]{3,2,1,0:T(8,128)(2,1)} %bitcast.213, bf16[1,2,192,768]{3,2,1,0:T(8,128)(2,1)} %bitcast.215, bf16[2,2,192,768]{3,2,1,0:T(8,128)(2,1)} %collective-permute-done), kind=kLoop, calls=%fused_computation | loop fusion | flops 5308416 | bytes 7077888 | tf_op jit(solution)/shard_map/concatenate | solution.py:20
  36.4 5.4 %reshape.262 = bf16[2,6,192,6,128]{4,3,2,1,0:T(8,128)(2,1)} reshape(bf16[2,6,192,768]{3,2,1,0:T(8,128)(2,1)S(1)} %pad_maximum_fusion) | data formatting | bytes 7077888 | tf_op jit(solution)/shard_map/reshape | solution.py:60
  41.7 3.2 %constant_dynamic-slice_fusion.6 = (bf16[2,1,192,6,128]{4,3,2,1,0:T(8,128)(2,1)S(1)}, bf16[2,1,192,6,128]{4,3,2,1,0:T(8,128)(2,1)S(1)}, bf16[2,1,192,6,128]{4,3,...) fusion(bf16[2,6,192,6,128]{4,3,2,1,0:T(8,128)(2,1)} %reshape.26, ...), kind=kLoop, calls=%fused_computation.103 | loop fusion | bytes 7077912 | tf_op jit(solution)/shard_map/jit(dynamic_index_in_dim)/dynamic_slice | solution.py:70
  45.0 0.6 pad_maximum_fusion.1
  45.5 0.4 fusion.45
  45.9 0.2 copy.16
  46.1 0.2 copy.12
  46.3 0.6 pad_maximum_fusion.2
  46.9 0.4 fusion.46
  47.3 0.2 copy.23
  47.5 0.2 copy.19
  47.7 0.6 copy-done.1
  48.3 0.8 fusion.6
  49.1 0.9 exponential_reduce_fusion
  50.1 1.3 %convolution_bitcast_fusion = f32[576,6,128]{2,0,1:T(8,128)S(1)} fusion(bf16[24,6,8,128]{3,2,1,0:T(8,128)(2,1)S(1)} %copy-done.6, f32[6,576,192]{1,2,0:T(8,128)S(1)} %get-tuple-element.86, f32[6,192]{1,0:T(8,128)S(1)} %log_add_fusion, pred[192,576]{1,0:T(8,128)(4,1)S(1)} %copy-done.3), kind=kOutput, calls=%fused_computation.26 | convolution fusion | flops 172523520 | bytes 4833792 | tf_op jit(solution)/shard_map/hqk,qhd->khd/dot_general | solution.py:107
  51.4 1.2 fusion.12
  52.6 1.1 fusion
  53.7 0.8 multiply_bitcast_fusion
  54.5 0.2 slice_bitcast_fusion.3
  54.8 0.8 copy-done
  55.7 0.8 fusion.5
  56.5 0.9 exponential_reduce_fusion.1
  57.5 1.5 %convolution_bitcast_fusion.1 = f32[576,6,128]{2,0,1:T(8,128)S(1)} fusion(bf16[24,6,8,128]{3,2,1,0:T(8,128)(2,1)S(1)} %copy-done.5, f32[6,576,192]{1,2,0:T(8,128)S(1)} %get-tuple-element.88, f32[6,192]{1,0:T(8,128)S(1)} %log_add_fusion.1, pred[192,576]{1,0:T(8,128)(4,1)S(1)} %copy-done.2), kind=kOutput, calls=%fused_computation.27 | convolution fusion | flops 172523520 | bytes 4833792 | tf_op jit(solution)/shard_map/hqk,qhd->khd/dot_general | solution.py:107
  58.9 1.1 fusion.11
  60.1 1.1 fusion.1
  61.2 0.8 multiply_bitcast_fusion.1
  61.9 0.1 slice_bitcast_fusion.9
  62.1 0.1 slice_bitcast_fusion.8
  62.2 0.8 broadcast_in_dim.59
  63.2 0.2 fusion.14
  63.4 0.2 fusion.15
  63.6 0.2 fusion.16
  63.9 0.2 fusion.17
  64.1 0.2 fusion.18
  64.3 0.5 slice_bitcast_fusion.1
  64.9 0.2 copy.95
  65.1 0.2 copy.94
  65.3 4.7 %collective-permute-start.3 = (f32[2,2,192,768]{3,2,1,0:T(8,128)S(1)}, f32[2,2,192,768]{3,2,1,0:T(8,128)S(1)}, u32[]{:S(2)}, u32[]{:S(2)}) collective-permute-start(f32[2,2,192,768]{3,2,1,0:T(8,128)S(1)} %bitcast.217), channel_id=1, source_target_pairs={{0,4},{4,8},{8,12},{1,5},{5,9},{9,13},{2,6},{6,10},{10,14},{3,7},{... | collective-permute-start | bytes 7077896 | tf_op jit(solution)/shard_map/ppermute | solution.py:34
  69.9 1.3 %collective-permute-start.2 = (f32[2,2,192,768]{3,2,1,0:T(8,128)S(1)}, f32[2,2,192,768]{3,2,1,0:T(8,128)S(1)}, u32[]{:S(2)}, u32[]{:S(2)}) collective-permute-start(f32[2,2,192,768]{3,2,1,0:T(8,128)S(1)} %bitcast.216), channel_id=1, source_target_pairs={{4,0},{8,4},{12,8},{5,1},{9,5},{13,9},{6,2},{10,6},{14,10},{7,3},{... | collective-permute-start | bytes 7077896 | tf_op jit(solution)/shard_map/ppermute | solution.py:34
  71.2 0.5 fusion.19
  71.8 0.5 fusion.20
  72.4 0.4 copy.26
  72.8 0.9 copy.98
  73.7 45.7 %collective-permute-done.3 = f32[2,2,192,768]{3,2,1,0:T(8,128)S(1)} collective-permute-done((f32[2,2,192,768]{3,2,1,0:T(8,128)S(1)}, f32[2,2,192,768]{3,2,1,0:T(8,128)S(1)}, u32[]{:S(2)}, u32[]{:S(2)}) %collective-permute-start.3) | collective-permute-done | bytes 2359328 | tf_op jit(solution)/shard_map/ppermute | solution.py:34
  119.4 4.3 %collective-permute-done.2 = f32[2,2,192,768]{3,2,1,0:T(8,128)S(1)} collective-permute-done((f32[2,2,192,768]{3,2,1,0:T(8,128)S(1)}, f32[2,2,192,768]{3,2,1,0:T(8,128)S(1)}, u32[]{:S(2)}, u32[]{:S(2)}) %collective-permute-start.2) | collective-permute-done | bytes 2359328 | tf_op jit(solution)/shard_map/ppermute | solution.py:34
  123.7 0.4 fusion.4
  124.1 0.4 copy.37
  124.6 0.9 copy.96
  125.5 0.4 copy.36
  125.9 0.9 copy.97
  (31 shorter events, 1.4 us)
Async XLA Ops:
  0.6 9.4 %copy-start.9 = (s32[8,3]{0,1:T(4,128)S(1)}, s32[8,3]{0,1:T(4,128)}, u32[]{:S(2)}) copy-start(s32[8,3]{0,1:T(4,128)} %param.18) | copy-start | bytes 292
  0.6 28.6 %copy-start.7 = (bf16[384,768]{1,0:T(8,128)(2,1)S(1)}, bf16[384,768]{1,0:T(8,128)(2,1)}, u32[]{:S(2)}) copy-start(bf16[384,768]{1,0:T(8,128)(2,1)} %param.14) | copy-start | bytes 1769476
  0.7 29.4 %copy-start.8 = (bf16[384,768]{1,0:T(8,128)(2,1)S(1)}, bf16[384,768]{1,0:T(8,128)(2,1)}, u32[]{:S(2)}) copy-start(bf16[384,768]{1,0:T(8,128)(2,1)} %param.17) | copy-start | bytes 1769476
  2.1 30.9 %collective-permute-start.1 = (bf16[2,2,192,768]{3,2,1,0:T(8,128)(2,1)S(1)}, bf16[2,2,192,768]{3,2,1,0:T(8,128)(2,1)S(1)}, u32[]{:S(2)}, u32[]{:S(2)}) collective-permute-start(bf16[2,2,192,768]{3,2,1,0:T(8,128)(2,1)S(1)} %pad_maximum_fusion.3), channel_id=1, source_target_pairs={{4,0},{8,4},{12,8},{5,1},{9,5},{13,9},{6,2},{10,6},{14,10},{7,3},{... | collective-permute-start | bytes 3538952 | tf_op jit(solution)/shard_map/ppermute | solution.py:24
  3.4 30.8 %collective-permute-start = (bf16[2,2,192,768]{3,2,1,0:T(8,128)(2,1)S(1)}, bf16[2,2,192,768]{3,2,1,0:T(8,128)(2,1)}, u32[]{:S(2)}, u32[]{:S(2)}) collective-permute-start(bf16[2,2,192,768]{3,2,1,0:T(8,128)(2,1)S(1)} %pad_maximum_fusion.3), channel_id=1, source_target_pairs={{0,4},{4,8},{8,12},{1,5},{5,9},{9,13},{2,6},{6,10},{10,14},{3,7},{... | collective-permute-start | bytes 3538952 | tf_op jit(solution)/shard_map/ppermute | solution.py:22
  33.0 1.1 copy-start.4
  47.3 1.0 copy-start.1
  47.3 1.0 copy-start.3
  49.1 1.0 copy-start.6
  54.7 1.0 copy-start
  54.7 1.0 copy-start.2
  56.5 1.0 copy-start.5
  65.3 54.1 %collective-permute-start.3 = (f32[2,2,192,768]{3,2,1,0:T(8,128)S(1)}, f32[2,2,192,768]{3,2,1,0:T(8,128)S(1)}, u32[]{:S(2)}, u32[]{:S(2)}) collective-permute-start(f32[2,2,192,768]{3,2,1,0:T(8,128)S(1)} %bitcast.217), channel_id=1, source_target_pairs={{0,4},{4,8},{8,12},{1,5},{5,9},{9,13},{2,6},{6,10},{10,14},{3,7},{... | collective-permute-start | bytes 7077896 | tf_op jit(solution)/shard_map/ppermute | solution.py:34
  69.9 53.7 %collective-permute-start.2 = (f32[2,2,192,768]{3,2,1,0:T(8,128)S(1)}, f32[2,2,192,768]{3,2,1,0:T(8,128)S(1)}, u32[]{:S(2)}, u32[]{:S(2)}) collective-permute-start(f32[2,2,192,768]{3,2,1,0:T(8,128)S(1)} %bitcast.216), channel_id=1, source_target_pairs={{4,0},{8,4},{12,8},{5,1},{9,5},{13,9},{6,2},{10,6},{14,10},{7,3},{... | collective-permute-start | bytes 7077896 | tf_op jit(solution)/shard_map/ppermute | solution.py:34
where the time goes:
time: 127 us
  waiting for transfers between devices  52.2 us (41%)
  local copies, waits for them, and re-layouts  28.3 us (22%)
  starting transfers between devices  13.8 us (11%)
  between operations  12.4 us (10%)
  matrix products  11.6 us (9%)
  other arithmetic  8.52 us (7%)
    ppermute x2, waiting for transfers between devices, from_behind(): return lax.ppermute(block, axis, route)  50 us
    unnamed x26, local copies, waits for them, and re-layouts  7.57 us
    ppermute x1, starting transfers between devices, padded(): lax.ppermute(tail, axis, [(i, (i + 1) % count) for i in range(ends)])  6.57 us
    ppermute x2, starting transfers between devices, from_behind(): return lax.ppermute(block, axis, route)  5.95 us
    reshape x1, local copies, waits for them, and re-layouts, local(): window = window.reshape(2, FR_DEV + 2 * R, TOK_FRAME, heads_local, HD)  5.35 us
    gt x6, local copies, waits for them, and re-layouts, span_mask(): return jnp.transpose(tokens, (1, 0, 2)).reshape(tokens.shape[1], -1) > 0  3.97 us
    dynamic_slice x1, local copies, waits for them, and re-layouts, local(): lax.dynamic_index_in_dim(window, spots[slot], 1, False)  3.22 us
    dot_general x2, matrix products, local(): jnp.einsum('hqk,qhd->khd', prob_low, grad_rows, preferred_element_type=jn...  2.75 us
  transfers between devices with their start and end apart: 4, of which 4 were waited for; matrix products, arithmetic and copies ran while one was open for 9% of the time, Pallas kernels for 0%

commit v1 on v0

v1 whole, which is shorter than its diff:
```python
import functools
import math

import jax
import jax.numpy as jnp
from jax import lax
from jax.experimental import pallas as pl
from jax.experimental.pallas import tpu as pltpu
from jax.sharding import PartitionSpec as P

HD = 128
TOK_FRAME = 192
FR_DEV = 2
NSEL = 3
SB = 4
ROWS = FR_DEV * TOK_FRAME
BLOCK = TOK_FRAME // SB
SCALE = HD ** (-0.5)
SCALE2 = SCALE * math.log2(math.e)
NEG = -1e30
NT = (((1,), (1,)), ((), ()))
NN = (((1,), (0,)), ((), ()))
TN = (((0,), (0,)), ((), ()))


def dot(lhs, rhs, dims):
    return lax.dot_general(lhs, rhs, dims, preferred_element_type=jnp.float32)


def fill_bias(table, bias):
    q_block = lax.broadcasted_iota(jnp.int32, (BLOCK, TOK_FRAME), 1) // BLOCK
    for frame in range(FR_DEV):
        for slot in range(NSEL):
            for k_block in range(SB):
                value = jnp.zeros((BLOCK, TOK_FRAME), jnp.float32)
                for block in range(SB):
                    at = FR_DEV * NSEL + ((frame * NSEL + slot) * SB + block) * SB + k_block
                    drop = jnp.where(table[at] > 0, 0.0, NEG)
                    value = jnp.where(q_block == block, drop, value)
                bias[frame, pl.ds(slot * TOK_FRAME + k_block * BLOCK, BLOCK), :] = value


def fill_window(window, one, own, two):
    window[0:ROWS] = one[...]
    window[ROWS : 2 * ROWS] = own[...]
    window[2 * ROWS : 3 * ROWS] = two[...]


def span(table, frame, slot):
    return pl.ds(pl.multiple_of(table[frame * NSEL + slot] * TOK_FRAME, TOK_FRAME), TOK_FRAME)


def values_kernel(
    table, queries, grad_out, k_one, k_own, k_two, log_out, own_out, one_out, two_out,
    bias, window, accum,
):
    @pl.when(pl.program_id(0) == 0)
    def _():
        fill_bias(table, bias)

    fill_window(window, k_one, k_own, k_two)
    accum[...] = jnp.zeros_like(accum)
    for frame in range(FR_DEV):
        rows = pl.ds(frame * TOK_FRAME, TOK_FRAME)
        query = queries[rows, :]
        grad = grad_out[rows, :]
        masked = []
        for slot in range(NSEL):
            scores = dot(window[span(table, frame, slot), :], query, NT)
            masked.append(
                scores * SCALE2 + bias[frame, pl.ds(slot * TOK_FRAME, TOK_FRAME), :]
            )
        highest = functools.reduce(
            jnp.maximum, [jnp.max(each, 0, keepdims=True) for each in masked]
        )
        raised = [jnp.exp2(each - highest) for each in masked]
        total = functools.reduce(jnp.add, [jnp.sum(each, 0, keepdims=True) for each in raised])
        log_out[0, frame : frame + 1, :] = highest + jnp.log2(total)
        inverse = 1.0 / total
        for slot in range(NSEL):
            prob_low = (raised[slot] * inverse).astype(jnp.bfloat16)
            accum[span(table, frame, slot), :] += dot(prob_low, grad, NN)
    one_out[...] = accum[0:ROWS].astype(one_out.dtype)
    own_out[...] = accum[ROWS : 2 * ROWS].astype(own_out.dtype)
    two_out[...] = accum[2 * ROWS : 3 * ROWS].astype(two_out.dtype)


def keys_kernel(
    table, queries, grad_out, k_one, k_own, k_two, v_one, v_own, v_two, log_in,
    query_out, own_out, one_out, two_out,
    bias, window, v_window, accum,
):
    @pl.when(pl.program_id(0) == 0)
    def _():
        fill_bias(table, bias)

    fill_window(window, k_one, k_own, k_two)
    fill_window(v_window, v_one, v_own, v_two)
    accum[...] = jnp.zeros_like(accum)
    for frame in range(FR_DEV):
        rows = pl.ds(frame * TOK_FRAME, TOK_FRAME)
        query = queries[rows, :]
        grad = grad_out[rows, :]
        log_total = log_in[0, frame : frame + 1, :]
        probs = []
        grads = []
        delta = jnp.zeros((1, TOK_FRAME), jnp.float32)
        for slot in range(NSEL):
            where_at = span(table, frame, slot)
            scores = dot(window[where_at, :], query, NT)
            prob = jnp.exp2(
                scores * SCALE2
                + bias[frame, pl.ds(slot * TOK_FRAME, TOK_FRAME), :]
                - log_total
            )
            grad_prob = dot(v_window[where_at, :], grad, NT)
            low = prob.astype(jnp.bfloat16).astype(jnp.float32)
            delta += jnp.sum(low * grad_prob, 0, keepdims=True)
            probs.append(prob)
            grads.append(grad_prob)
        grad_query = jnp.zeros((TOK_FRAME, HD), jnp.float32)
        for slot in range(NSEL):
            where_at = span(table, frame, slot)
            score_low = (probs[slot] * (grads[slot] - delta)).astype(jnp.bfloat16)
            accum[where_at, :] += dot(score_low, query, NN)
            grad_query += dot(score_low, window[where_at, :], TN)
        query_out[rows, :] = (grad_query * SCALE).astype(query_out.dtype)
    one_out[...] = (accum[0:ROWS] * SCALE).astype(one_out.dtype)
    own_out[...] = (accum[ROWS : 2 * ROWS] * SCALE).astype(own_out.dtype)
    two_out[...] = (accum[2 * ROWS : 3 * ROWS] * SCALE).astype(two_out.dtype)


def exchanges(count):
    first = [(i, i + 1) for i in range(0, count - 1, 2)]
    second = [(i, i + 1) for i in range(1, count - 1, 2)]
    return tuple([pair for i, j in part for pair in ((i, j), (j, i))] for part in (first, second))


def swap(one, two):
    first, second = exchanges(lax.axis_size("frames"))
    return lax.ppermute(one, "frames", first), lax.ppermute(two, "frames", second)


def lookup(offsets, spatial):
    me = lax.axis_index("frames")
    first_frame = me * FR_DEV
    shifts = lax.dynamic_slice_in_dim(offsets, first_frame, FR_DEV, 0)
    blocks = lax.dynamic_slice_in_dim(spatial, first_frame, FR_DEV, 0)
    place = jnp.arange(FR_DEV, dtype=jnp.int32)[:, None] + shifts
    target = first_frame + place
    inside = ((target >= 0) & (target < offsets.shape[0])).astype(jnp.int32)
    side = (place >= 0).astype(jnp.int32) + (place >= FR_DEV).astype(jnp.int32)
    side = jnp.where(me % 2 == 1, side, 2 - side)
    spot = side * FR_DEV + (place % FR_DEV)
    blocks = blocks * inside[:, :, None, None]
    return jnp.concatenate([spot.reshape(-1), blocks.reshape(-1)]).astype(jnp.int32)


def local(queries, keys, values, grad_out, offsets, spatial):
    heads = queries.shape[1] // HD
    k_one, k_two = swap(keys, keys)
    v_one, v_two = swap(values, values)
    table = lookup(offsets, spatial)
    column = pl.BlockSpec((ROWS, HD), lambda head, _: (0, head))
    stat = pl.BlockSpec((1, FR_DEV, TOK_FRAME), lambda head, _: (head, 0, 0))
    low = jax.ShapeDtypeStruct(queries.shape, jnp.bfloat16)
    full = jax.ShapeDtypeStruct(queries.shape, jnp.float32)
    logs = jax.ShapeDtypeStruct((heads, FR_DEV, TOK_FRAME), jnp.float32)
    bias = pltpu.VMEM((FR_DEV, NSEL * TOK_FRAME, TOK_FRAME), jnp.float32)
    window = pltpu.VMEM((3 * ROWS, HD), jnp.bfloat16)
    accum = pltpu.VMEM((3 * ROWS, HD), jnp.float32)
    flops = 2 * heads * FR_DEV * NSEL * TOK_FRAME * TOK_FRAME * HD
    size = queries.size * 2
    log_total, gv_own, gv_one, gv_two = pl.pallas_call(
        values_kernel,
        out_shape=(logs, full, low, low),
        grid_spec=pltpu.PrefetchScalarGridSpec(
            num_scalar_prefetch=1,
            grid=(heads,),
            in_specs=[column] * 5,
            out_specs=(stat, column, column, column),
            scratch_shapes=[bias, window, accum],
        ),
        compiler_params=pltpu.CompilerParams(vmem_limit_bytes=24 << 20),
        cost_estimate=pl.CostEstimate(
            flops=2 * flops, bytes_accessed=9 * size, transcendentals=0
        ),
        name="values_part",
    )(table, queries, grad_out, k_one, keys, k_two)
    rv_one, rv_two = swap(gv_one, gv_two)
    grad_queries, gk_own, gk_one, gk_two = pl.pallas_call(
        keys_kernel,
        out_shape=(low, full, low, low),
        grid_spec=pltpu.PrefetchScalarGridSpec(
            num_scalar_prefetch=1,
            grid=(heads,),
            in_specs=[column] * 8 + [stat],
            out_specs=(column, column, column, column),
            scratch_shapes=[bias, window, window, accum],
        ),
        compiler_params=pltpu.CompilerParams(vmem_limit_bytes=24 << 20),
        cost_estimate=pl.CostEstimate(
            flops=4 * flops, bytes_accessed=13 * size, transcendentals=0
        ),
        name="keys_part",
    )(table, queries, grad_out, k_one, keys, k_two, v_one, values, v_two, log_total)
    rk_one, rk_two = swap(gk_one, gk_two)

    def joined(own, one, two):
        return (own + one.astype(jnp.float32) + two.astype(jnp.float32)).astype(jnp.bfloat16)

    return (grad_queries, joined(gk_own, rk_one, rk_two), joined(gv_own, rv_one, rv_two))


def solution(mesh):
    rows = P(("clips", "frames"), "heads")
    return jax.shard_map(
        local,
        mesh=mesh,
        in_specs=(rows, rows, rows, rows, P("clips", None), P("clips", None, None, None)),
        out_specs=(rows, rows, rows),
        check_vma=False,
    )
```

time: 127 us -> 61.7 us (0.49)
  waiting for transfers between devices: 52.2 us -> 14.4 us
  local copies, waits for them, and re-layouts: 28.3 us -> 3.64 us
  Pallas kernels: 0 us -> 18.8 us
  between operations: 12.4 us -> 0.74 us
  matrix products: 11.6 us -> 0 us
  starting transfers between devices: 13.8 us -> 18.7 us
  other arithmetic: 8.52 us -> 4.42 us
    ppermute x4 -> x8, waiting for transfers between devices: 52.2 us -> 14.4 us  [the longest x4 14.4 us: swap(): lax.ppermute(one, 'frames', first)]
    pallas_call x0 -> x2, Pallas kernels: none -> 18.8 us  [the longest x1 10.6 us: local(): pl.pallas_call(keys_kernel, out_shape=(low, full, low, low), grid_spec=pl...]
    dot_general x12 -> x0, matrix products: 11.6 us -> none  [the longest x2 2.75 us: local(): jnp.einsum('hqk,qhd->khd', prob_low, grad_rows, preferred_element_type=jn...]
    reshape x3 -> x2, local copies, waits for them, and re-layouts: 5.74 us -> 0.19 us  [the longest x1 0.1 us: lookup(): blocks.reshape(-1)]
    ppermute x4 -> x8, starting transfers between devices: 13.8 us -> 18.7 us  [the longest x4 15.9 us: swap(): lax.ppermute(one, 'frames', first)]
    dynamic_slice x2 -> x0, local copies, waits for them, and re-layouts: 4.6 us -> none  [the longest x1 3.22 us: local(): lax.dynamic_index_in_dim(window, spots[slot], 1, False)]
    unnamed x26 -> x8, local copies, waits for them, and re-layouts: 7.57 us -> 3.2 us
    gt x6 -> x0, local copies, waits for them, and re-layouts: 3.97 us -> none  [span_mask(): return jnp.transpose(tokens, (1, 0, 2)).reshape(tokens.shape[1], -1) > 0]
  transfers between devices with their start and end apart: 4 -> 8, of which waited for: 4 -> 2; matrix products, arithmetic and copies ran while one was open for 9% -> 6% of each run, Pallas kernels for 0% -> 31%
where the time goes in v1:
time: 61.7 us; the launch traced here: 60.7 us
  Pallas kernels  18.8 us (30%)
  starting transfers between devices  18.7 us (30%)
  waiting for transfers between devices  14.4 us (23%)
  other arithmetic  4.42 us (7%)
  local copies, waits for them, and re-layouts  3.64 us (6%)
  between operations  0.74 us (1%)
    ppermute x4, starting transfers between devices, swap(): lax.ppermute(one, 'frames', first)  15.9 us
    ppermute x4, waiting for transfers between devices, swap(): lax.ppermute(one, 'frames', first)  14.4 us
    pallas_call x1, Pallas kernels, local(): pl.pallas_call(keys_kernel, out_shape=(low, full, low, low), grid_spec=pl...  10.6 us
    pallas_call x1, Pallas kernels, local(): pl.pallas_call(values_kernel, out_shape=(logs, full, low, low), grid_spec...  8.26 us
    unnamed x8, local copies, waits for them, and re-layouts  3.2 us
    ppermute x4, starting transfers between devices, swap(): lax.ppermute(two, 'frames', second)  2.75 us
    convert_element_type x2, other arithmetic, joined(): (own + one.astype(jnp.float32) + two.astype(jnp.float32)).astype(jnp.bflo...  2.01 us
  transfers between devices with their start and end apart: 8, of which 2 were waited for; matrix products, arithmetic and copies ran while one was open for 6% of the time, Pallas kernels for 31%

profile of v1, /device:TPU:0, one launch (start us, length us, event | category | flops | bytes accessed | tf_op | source)
XLA Modules:
  0.0 60.7 jit_solution(16126891745932540672)
XLA Ops:
  0.6 3.1 %collective-permute-start = (bf16[384,768]{1,0:T(8,128)(2,1)}, bf16[384,768]{1,0:T(8,128)(2,1)S(1)}, u32[]{:S(2)}, u32[]{:S(2)}) collective-permute-start(bf16[384,768]{1,0:T(8,128)(2,1)} %k_own.3), channel_id=1, source_target_pairs={{0,4},{4,0},{8,12},{12,8},{1,5},{5,1},{9,13},{13,9},{2,6},{6,2},{1... | collective-permute-start | bytes 1769480 | tf_op jit(solution)/shard_map/ppermute | solution.py:141
  3.7 0.7 %collective-permute-start.1 = (bf16[384,768]{1,0:T(8,128)(2,1)}, bf16[384,768]{1,0:T(8,128)(2,1)S(1)}, u32[]{:S(2)}, u32[]{:S(2)}) collective-permute-start(bf16[384,768]{1,0:T(8,128)(2,1)} %k_own.3), channel_id=1, source_target_pairs={{4,8},{8,4},{5,9},{9,5},{6,10},{10,6},{7,11},{11,7},{20,24},{24,20... | collective-permute-start | bytes 1769480 | tf_op jit(solution)/shard_map/ppermute | solution.py:141
  4.4 4.4 %collective-permute-start.2 = (bf16[384,768]{1,0:T(8,128)(2,1)}, bf16[384,768]{1,0:T(8,128)(2,1)S(1)}, u32[]{:S(2)}, u32[]{:S(2)}) collective-permute-start(bf16[384,768]{1,0:T(8,128)(2,1)} %v_own.1), channel_id=1, source_target_pairs={{0,4},{4,0},{8,12},{12,8},{1,5},{5,1},{9,13},{13,9},{2,6},{6,2},{1... | collective-permute-start | bytes 1769480 | tf_op jit(solution)/shard_map/ppermute | solution.py:141
  8.8 0.7 %collective-permute-start.3 = (bf16[384,768]{1,0:T(8,128)(2,1)}, bf16[384,768]{1,0:T(8,128)(2,1)S(1)}, u32[]{:S(2)}, u32[]{:S(2)}) collective-permute-start(bf16[384,768]{1,0:T(8,128)(2,1)} %v_own.1), channel_id=1, source_target_pairs={{4,8},{8,4},{5,9},{9,5},{6,10},{10,6},{7,11},{11,7},{20,24},{24,20... | collective-permute-start | bytes 1769480 | tf_op jit(solution)/shard_map/ppermute | solution.py:141
  9.6 0.8 %and_convert_fusion = s32[2,3]{0,1:T(4,128)S(1)} fusion(s32[8,3]{0,1:T(4,128)} %param.10, s32[]{:T(128)S(6)} %select_n.27, s32[]{:T(128)S(6)} %mul.14), kind=kLoop, calls=%fused_computation.11 | loop fusion | flops 36 | bytes 56 | tf_op jit(solution)/shard_map/convert_element_type | solution.py:151
  10.3 0.8 %fusion.1 = s32[2,3]{0,1:T(4,128)S(1)} fusion(s32[8,3]{0,1:T(4,128)} %param.10, s32[]{:T(128)S(6)} %select_n.27, pred[]{:T(512)S(6)} %eq.7), kind=kLoop, calls=%fused_computation.8 | loop fusion | flops 126 | bytes 53 | tf_op jit(solution)/shard_map/add | solution.py:154
  11.1 0.1 copy.9
  11.2 0.1 reshape.13
  11.3 0.8 %dynamic-slice_multiply_fusion = s32[2,3,4,4]{0,3,2,1:T(4,128)S(1)} fusion(s32[8,3,4,4]{0,3,2,1:T(4,128)} %param.11, s32[]{:T(128)S(6)} %select_n.27, s32[2,3]{0,1:T(4,128)S(1)} %and_convert_fusion), kind=kLoop, calls=%fused_computation.2 | loop fusion | flops 96 | bytes 796 | tf_op jit(solution)/shard_map/mul | solution.py:155
  12.1 0.2 copy.10
  12.2 0.1 reshape.14
  12.3 0.1 pad_add_fusion.table
  12.4 5.7 %collective-permute-done.k_one = bf16[384,768]{1,0:T(8,128)(2,1)S(1)} collective-permute-done((bf16[384,768]{1,0:T(8,128)(2,1)}, bf16[384,768]{1,0:T(8,128)(2,1)S(1)}, u32[]{:S(2)}, u32[]{:S(2)}) %collective-permute-start) | collective-permute-done | bytes 589856 | tf_op jit(solution)/shard_map/ppermute | solution.py:141
  18.1 0.0 collective-permute-done.1.k_two
  18.1 0.0 copy-start
  18.1 1.1 %copy-done = bf16[384,768]{1,0:T(8,128)(2,1)S(1)} copy-done((bf16[384,768]{1,0:T(8,128)(2,1)S(1)}, bf16[384,768]{1,0:T(8,128)(2,1)}, u32[]{:S(2)}) %copy-start) | copy-done | bytes 589848
  19.2 0.0 copy-start.1
  19.2 1.1 %copy-done.1 = bf16[384,768]{1,0:T(8,128)(2,1)S(1)} copy-done((bf16[384,768]{1,0:T(8,128)(2,1)S(1)}, bf16[384,768]{1,0:T(8,128)(2,1)}, u32[]{:S(2)}) %copy-start.1) | copy-done | bytes 589848
  20.2 0.0 copy-start.2
  20.2 1.1 %copy-done.2 = bf16[384,768]{1,0:T(8,128)(2,1)S(1)} copy-done((bf16[384,768]{1,0:T(8,128)(2,1)S(1)}, bf16[384,768]{1,0:T(8,128)(2,1)}, u32[]{:S(2)}) %copy-start.2) | copy-done | bytes 589848
  21.3 0.0 copy-start.3
  21.3 8.3 %values_part.1 = (f32[6,2,192]{2,1,0:T(2,128)S(1)}, f32[384,768]{1,0:T(8,128)S(1)}, bf16[384,768]{1,0:T(8,128)(2,1)S(1)}, bf16[384,768]{1,0:T(8,128)(2,1)S(1)}) custom-call(s32[102]{0:T(128)S(1)} %pad_add_fusion.table, bf16[384,768]{1,0:T(8,128)(2,1)S(1)} %copy-done, bf16[384,768]{1,0:T(8,128)(2,1)S(1)} %copy-done.1, ...), custom_call_target="tpu_custom_call" | custom-call | flops 679477248 | bytes 5308416 | tf_op jit(solution)/shard_map/values_part/pallas_call | solution.py:174
  29.6 5.1 %collective-permute-start.6 = (bf16[384,768]{1,0:T(8,128)(2,1)S(1)}, bf16[384,768]{1,0:T(8,128)(2,1)S(1)}, u32[]{:S(2)}, u32[]{:S(2)}) collective-permute-start(bf16[384,768]{1,0:T(8,128)(2,1)S(1)} %get-tuple-element.17), channel_id=1, source_target_pairs={{0,4},{4,0},{8,12},{12,8},{1,5},{5,1},{9,13},{13,9},{2,6},{6,2},{1... | collective-permute-start | bytes 1769480 | tf_op jit(solution)/shard_map/ppermute | solution.py:141
  34.7 0.7 %collective-permute-start.7 = (bf16[384,768]{1,0:T(8,128)(2,1)S(1)}, bf16[384,768]{1,0:T(8,128)(2,1)S(1)}, u32[]{:S(2)}, u32[]{:S(2)}) collective-permute-start(bf16[384,768]{1,0:T(8,128)(2,1)S(1)} %get-tuple-element.18), channel_id=1, source_target_pairs={{4,8},{8,4},{5,9},{9,5},{6,10},{10,6},{7,11},{11,7},{20,24},{24,20... | collective-permute-start | bytes 1769480 | tf_op jit(solution)/shard_map/ppermute | solution.py:141
  35.4 0.0 collective-permute-done.2.v_one
  35.4 0.0 collective-permute-done.3.v_two
  35.4 0.0 copy-done.3
  35.4 10.6 %keys_part.1 = (bf16[384,768]{1,0:T(8,128)(2,1)}, f32[384,768]{1,0:T(8,128)S(1)}, bf16[384,768]{1,0:T(8,128)(2,1)S(1)}, bf16[384,768]{1,0:T(8,128)(2,1)S(1)}) custom-call(s32[102]{0:T(128)S(1)} %pad_add_fusion.table, bf16[384,768]{1,0:T(8,128)(2,1)S(1)} %copy-done, bf16[384,768]{1,0:T(8,128)(2,1)S(1)} %copy-done.1, ...), custom_call_target="tpu_custom_call" | custom-call | flops 1358954496 | bytes 7667712 | tf_op jit(solution)/shard_map/keys_part/pallas_call | solution.py:191
  46.0 3.3 %collective-permute-start.4 = (bf16[384,768]{1,0:T(8,128)(2,1)S(1)}, bf16[384,768]{1,0:T(8,128)(2,1)S(1)}, u32[]{:S(2)}, u32[]{:S(2)}) collective-permute-start(bf16[384,768]{1,0:T(8,128)(2,1)S(1)} %get-tuple-element.14), channel_id=1, source_target_pairs={{0,4},{4,0},{8,12},{12,8},{1,5},{5,1},{9,13},{13,9},{2,6},{6,2},{1... | collective-permute-start | bytes 1769480 | tf_op jit(solution)/shard_map/ppermute | solution.py:141
  49.3 0.7 %collective-permute-start.5 = (bf16[384,768]{1,0:T(8,128)(2,1)S(1)}, bf16[384,768]{1,0:T(8,128)(2,1)S(1)}, u32[]{:S(2)}, u32[]{:S(2)}) collective-permute-start(bf16[384,768]{1,0:T(8,128)(2,1)S(1)} %get-tuple-element.15), channel_id=1, source_target_pairs={{4,8},{8,4},{5,9},{9,5},{6,10},{10,6},{7,11},{11,7},{20,24},{24,20... | collective-permute-start | bytes 1769480 | tf_op jit(solution)/shard_map/ppermute | solution.py:141
  50.0 0.0 collective-permute-done.6
  50.0 0.0 collective-permute-done.7
  50.0 1.0 %add_convert_fusion = bf16[384,768]{1,0:T(8,128)(2,1)} fusion(bf16[384,768]{1,0:T(8,128)(2,1)S(1)} %collective-permute-done.7, f32[384,768]{1,0:T(8,128)S(1)} %get-tuple-element.16, bf16[384,768]{1,0:T(8,128)(2,1)S(1)} %collective-permute-done.6), kind=kLoop, calls=%fused_computation | loop fusion | flops 1474560 | bytes 2949120 | tf_op jit(solution)/shard_map/convert_element_type | solution.py:210
  51.0 8.7 %collective-permute-done.4 = bf16[384,768]{1,0:T(8,128)(2,1)S(1)} collective-permute-done((bf16[384,768]{1,0:T(8,128)(2,1)S(1)}, bf16[384,768]{1,0:T(8,128)(2,1)S(1)}, u32[]{:S(2)}, u32[]{:S(2)}) %collective-permute-start.4) | collective-permute-done | bytes 589856 | tf_op jit(solution)/shard_map/ppermute | solution.py:141
  59.7 0.0 collective-permute-done.5
  59.7 1.0 %add_convert_fusion.1 = bf16[384,768]{1,0:T(8,128)(2,1)} fusion(bf16[384,768]{1,0:T(8,128)(2,1)S(1)} %collective-permute-done.5, f32[384,768]{1,0:T(8,128)S(1)} %get-tuple-element.13, bf16[384,768]{1,0:T(8,128)(2,1)S(1)} %collective-permute-done.4), kind=kLoop, calls=%fused_computation.1 | loop fusion | flops 1474560 | bytes 2949120 | tf_op jit(solution)/shard_map/convert_element_type | solution.py:210
Async XLA Ops:
  0.6 17.5 %collective-permute-start = (bf16[384,768]{1,0:T(8,128)(2,1)}, bf16[384,768]{1,0:T(8,128)(2,1)S(1)}, u32[]{:S(2)}, u32[]{:S(2)}) collective-permute-start(bf16[384,768]{1,0:T(8,128)(2,1)} %k_own.3), channel_id=1, source_target_pairs={{0,4},{4,0},{8,12},{12,8},{1,5},{5,1},{9,13},{13,9},{2,6},{6,2},{1... | collective-permute-start | bytes 1769480 | tf_op jit(solution)/shard_map/ppermute | solution.py:141
  3.7 14.4 %collective-permute-start.1 = (bf16[384,768]{1,0:T(8,128)(2,1)}, bf16[384,768]{1,0:T(8,128)(2,1)S(1)}, u32[]{:S(2)}, u32[]{:S(2)}) collective-permute-start(bf16[384,768]{1,0:T(8,128)(2,1)} %k_own.3), channel_id=1, source_target_pairs={{4,8},{8,4},{5,9},{9,5},{6,10},{10,6},{7,11},{11,7},{20,24},{24,20... | collective-permute-start | bytes 1769480 | tf_op jit(solution)/shard_map/ppermute | solution.py:141
  4.4 31.0 %collective-permute-start.2 = (bf16[384,768]{1,0:T(8,128)(2,1)}, bf16[384,768]{1,0:T(8,128)(2,1)S(1)}, u32[]{:S(2)}, u32[]{:S(2)}) collective-permute-start(bf16[384,768]{1,0:T(8,128)(2,1)} %v_own.1), channel_id=1, source_target_pairs={{0,4},{4,0},{8,12},{12,8},{1,5},{5,1},{9,13},{13,9},{2,6},{6,2},{1... | collective-permute-start | bytes 1769480 | tf_op jit(solution)/shard_map/ppermute | solution.py:141
  8.8 26.5 %collective-permute-start.3 = (bf16[384,768]{1,0:T(8,128)(2,1)}, bf16[384,768]{1,0:T(8,128)(2,1)S(1)}, u32[]{:S(2)}, u32[]{:S(2)}) collective-permute-start(bf16[384,768]{1,0:T(8,128)(2,1)} %v_own.1), channel_id=1, source_target_pairs={{4,8},{8,4},{5,9},{9,5},{6,10},{10,6},{7,11},{11,7},{20,24},{24,20... | collective-permute-start | bytes 1769480 | tf_op jit(solution)/shard_map/ppermute | solution.py:141
  18.1 1.1 %copy-start = (bf16[384,768]{1,0:T(8,128)(2,1)S(1)}, bf16[384,768]{1,0:T(8,128)(2,1)}, u32[]{:S(2)}) copy-start(bf16[384,768]{1,0:T(8,128)(2,1)} %queries.3) | copy-start | bytes 1769476
  19.2 1.1 %copy-start.1 = (bf16[384,768]{1,0:T(8,128)(2,1)S(1)}, bf16[384,768]{1,0:T(8,128)(2,1)}, u32[]{:S(2)}) copy-start(bf16[384,768]{1,0:T(8,128)(2,1)} %grad_out.3) | copy-start | bytes 1769476
  20.2 1.1 %copy-start.2 = (bf16[384,768]{1,0:T(8,128)(2,1)S(1)}, bf16[384,768]{1,0:T(8,128)(2,1)}, u32[]{:S(2)}) copy-start(bf16[384,768]{1,0:T(8,128)(2,1)} %k_own.3) | copy-start | bytes 1769476
  21.3 14.1 %copy-start.3 = (bf16[384,768]{1,0:T(8,128)(2,1)S(1)}, bf16[384,768]{1,0:T(8,128)(2,1)}, u32[]{:S(2)}) copy-start(bf16[384,768]{1,0:T(8,128)(2,1)} %v_own.1) | copy-start | bytes 1769476
  29.6 20.4 %collective-permute-start.6 = (bf16[384,768]{1,0:T(8,128)(2,1)S(1)}, bf16[384,768]{1,0:T(8,128)(2,1)S(1)}, u32[]{:S(2)}, u32[]{:S(2)}) collective-permute-start(bf16[384,768]{1,0:T(8,128)(2,1)S(1)} %get-tuple-element.17), channel_id=1, source_target_pairs={{0,4},{4,0},{8,12},{12,8},{1,5},{5,1},{9,13},{13,9},{2,6},{6,2},{1... | collective-permute-start | bytes 1769480 | tf_op jit(solution)/shard_map/ppermute | solution.py:141
  34.7 15.3 %collective-permute-start.7 = (bf16[384,768]{1,0:T(8,128)(2,1)S(1)}, bf16[384,768]{1,0:T(8,128)(2,1)S(1)}, u32[]{:S(2)}, u32[]{:S(2)}) collective-permute-start(bf16[384,768]{1,0:T(8,128)(2,1)S(1)} %get-tuple-element.18), channel_id=1, source_target_pairs={{4,8},{8,4},{5,9},{9,5},{6,10},{10,6},{7,11},{11,7},{20,24},{24,20... | collective-permute-start | bytes 1769480 | tf_op jit(solution)/shard_map/ppermute | solution.py:141
  46.0 13.7 %collective-permute-start.4 = (bf16[384,768]{1,0:T(8,128)(2,1)S(1)}, bf16[384,768]{1,0:T(8,128)(2,1)S(1)}, u32[]{:S(2)}, u32[]{:S(2)}) collective-permute-start(bf16[384,768]{1,0:T(8,128)(2,1)S(1)} %get-tuple-element.14), channel_id=1, source_target_pairs={{0,4},{4,0},{8,12},{12,8},{1,5},{5,1},{9,13},{13,9},{2,6},{6,2},{1... | collective-permute-start | bytes 1769480 | tf_op jit(solution)/shard_map/ppermute | solution.py:141
  49.3 10.4 %collective-permute-start.5 = (bf16[384,768]{1,0:T(8,128)(2,1)S(1)}, bf16[384,768]{1,0:T(8,128)(2,1)S(1)}, u32[]{:S(2)}, u32[]{:S(2)}) collective-permute-start(bf16[384,768]{1,0:T(8,128)(2,1)S(1)} %get-tuple-element.15), channel_id=1, source_target_pairs={{4,8},{8,4},{5,9},{9,5},{6,10},{10,6},{7,11},{11,7},{20,24},{24,20... | collective-permute-start | bytes 1769480 | tf_op jit(solution)/shard_map/ppermute | solution.py:141

commit v2 on v1

v2 whole, which is shorter than its diff:
```python
import math

import jax
import jax.numpy as jnp
from jax import lax
from jax.experimental import pallas as pl
from jax.experimental.pallas import tpu as pltpu
from jax.sharding import PartitionSpec as P

HD = 128
TOK_FRAME = 192
FR_DEV = 2
NSEL = 3
SB = 4
GROUP = 3
ROWS = FR_DEV * TOK_FRAME
BLOCK = TOK_FRAME // SB
SCALE = HD ** (-0.5)
SCALE2 = SCALE * math.log2(math.e)
NEG = -1e30
NT = (((1,), (1,)), ((), ()))
NN = (((1,), (0,)), ((), ()))
TN = (((0,), (0,)), ((), ()))


def dot(lhs, rhs, dims):
    return lax.dot_general(lhs, rhs, dims, preferred_element_type=jnp.float32)


def fill_bias(table, bias):
    q_block = lax.broadcasted_iota(jnp.int32, (BLOCK, TOK_FRAME), 1) // BLOCK
    for frame in range(FR_DEV):
        for slot in range(NSEL):
            for k_block in range(SB):
                value = jnp.zeros((BLOCK, TOK_FRAME), jnp.float32)
                for block in range(SB):
                    at = FR_DEV * NSEL + ((frame * NSEL + slot) * SB + block) * SB + k_block
                    drop = jnp.where(table[at] > 0, 0.0, NEG)
                    value = jnp.where(q_block == block, drop, value)
                bias[frame, pl.ds(slot * TOK_FRAME + k_block * BLOCK, BLOCK), :] = value


def fill_window(window, one, own, two, column):
    window[0:ROWS] = one[:, column]
    window[ROWS : 2 * ROWS] = own[:, column]
    window[2 * ROWS : 3 * ROWS] = two[:, column]


def span(table, frame, slot):
    return pl.ds(pl.multiple_of(table[frame * NSEL + slot] * TOK_FRAME, TOK_FRAME), TOK_FRAME)


def pick(table, frame, window, chosen):
    for slot in range(NSEL):
        chosen[slot * TOK_FRAME : (slot + 1) * TOK_FRAME] = window[span(table, frame, slot), :]


def spread(table, frame, accum, parts):
    for slot in range(NSEL):
        accum[span(table, frame, slot), :] += parts[slot * TOK_FRAME : (slot + 1) * TOK_FRAME]


def values_kernel(
    table, queries, grad_out, k_one, k_own, k_two, prob_out, own_out, one_out, two_out,
    bias, windows, choices, accums,
):
    @pl.when(pl.program_id(0) == 0)
    def _():
        fill_bias(table, bias)

    for head in range(GROUP):
        column = slice(head * HD, (head + 1) * HD)
        window = windows.at[head]
        accum = accums.at[head]
        fill_window(window, k_one, k_own, k_two, column)
        accum[...] = jnp.zeros_like(accum)
        for frame in range(FR_DEV):
            rows = slice(frame * TOK_FRAME, (frame + 1) * TOK_FRAME)
            chosen = choices.at[head, frame]
            pick(table, frame, window, chosen)
            scores = dot(chosen[...], queries[rows, column], NT)
            masked = scores * SCALE2 + bias[frame]
            raised = jnp.exp2(masked - jnp.max(masked, 0, keepdims=True))
            inverse = 1.0 / jnp.sum(raised, 0, keepdims=True)
            prob_low = (raised * inverse).astype(jnp.bfloat16)
            prob_out[head, frame] = prob_low
            spread(table, frame, accum, dot(prob_low, grad_out[rows, column], NN))
        one_out[:, column] = accum[0:ROWS].astype(one_out.dtype)
        own_out[:, column] = accum[ROWS : 2 * ROWS].astype(own_out.dtype)
        two_out[:, column] = accum[2 * ROWS : 3 * ROWS].astype(two_out.dtype)


def keys_kernel(
    table, queries, grad_out, k_one, k_own, k_two, v_one, v_own, v_two, prob_in,
    query_out, own_out, one_out, two_out,
    windows, v_windows, choices, v_choices, accums,
):
    for head in range(GROUP):
        column = slice(head * HD, (head + 1) * HD)
        window = windows.at[head]
        v_window = v_windows.at[head]
        accum = accums.at[head]
        fill_window(window, k_one, k_own, k_two, column)
        fill_window(v_window, v_one, v_own, v_two, column)
        accum[...] = jnp.zeros_like(accum)
        for frame in range(FR_DEV):
            rows = slice(frame * TOK_FRAME, (frame + 1) * TOK_FRAME)
            chosen = choices.at[head, frame]
            v_chosen = v_choices.at[head, frame]
            pick(table, frame, window, chosen)
            pick(table, frame, v_window, v_chosen)
            grad_prob = dot(v_chosen[...], grad_out[rows, column], NT)
            prob = prob_in[head, frame].astype(jnp.float32)
            delta = jnp.sum(prob * grad_prob, 0, keepdims=True)
            score_low = (prob * (grad_prob - delta)).astype(jnp.bfloat16)
            spread(table, frame, accum, dot(score_low, queries[rows, column], NN))
            grad_query = dot(score_low, chosen[...], TN)
            query_out[rows, column] = (grad_query * SCALE).astype(query_out.dtype)
        one_out[:, column] = (accum[0:ROWS] * SCALE).astype(one_out.dtype)
        own_out[:, column] = (accum[ROWS : 2 * ROWS] * SCALE).astype(own_out.dtype)
        two_out[:, column] = (accum[2 * ROWS : 3 * ROWS] * SCALE).astype(two_out.dtype)


def exchanges(count):
    first = [(i, i + 1) for i in range(0, count - 1, 2)]
    second = [(i, i + 1) for i in range(1, count - 1, 2)]
    return tuple([pair for i, j in part for pair in ((i, j), (j, i))] for part in (first, second))


def swap(one, two):
    first, second = exchanges(lax.axis_size("frames"))
    return lax.ppermute(one, "frames", first), lax.ppermute(two, "frames", second)


def lookup(offsets, spatial):
    me = lax.axis_index("frames")
    first_frame = me * FR_DEV
    shifts = lax.dynamic_slice_in_dim(offsets, first_frame, FR_DEV, 0)
    blocks = lax.dynamic_slice_in_dim(spatial, first_frame, FR_DEV, 0)
    place = jnp.arange(FR_DEV, dtype=jnp.int32)[:, None] + shifts
    target = first_frame + place
    inside = ((target >= 0) & (target < offsets.shape[0])).astype(jnp.int32)
    side = (place >= 0).astype(jnp.int32) + (place >= FR_DEV).astype(jnp.int32)
    side = jnp.where(me % 2 == 1, side, 2 - side)
    spot = side * FR_DEV + (place % FR_DEV)
    blocks = blocks * inside[:, :, None, None]
    return jnp.concatenate([spot.reshape(-1), blocks.reshape(-1)]).astype(jnp.int32)


def local(queries, keys, values, grad_out, offsets, spatial):
    heads = queries.shape[1] // HD
    k_one, k_two = swap(keys, keys)
    v_one, v_two = swap(values, values)
    table = lookup(offsets, spatial)
    column = pl.BlockSpec((ROWS, GROUP * HD), lambda step, _: (0, step))
    slots = NSEL * TOK_FRAME
    chance = pl.BlockSpec(
        (GROUP, FR_DEV, slots, TOK_FRAME), lambda step, _: (step, 0, 0, 0)
    )
    low = jax.ShapeDtypeStruct(queries.shape, jnp.bfloat16)
    full = jax.ShapeDtypeStruct(queries.shape, jnp.float32)
    chances = jax.ShapeDtypeStruct((heads, FR_DEV, slots, TOK_FRAME), jnp.bfloat16)
    bias = pltpu.VMEM((FR_DEV, slots, TOK_FRAME), jnp.float32)
    window = pltpu.VMEM((GROUP, 3 * ROWS, HD), jnp.bfloat16)
    choice = pltpu.VMEM((GROUP, FR_DEV, slots, HD), jnp.bfloat16)
    accum = pltpu.VMEM((GROUP, 3 * ROWS, HD), jnp.float32)
    params = pltpu.CompilerParams(vmem_limit_bytes=56 << 20)
    flops = 2 * heads * FR_DEV * NSEL * TOK_FRAME * TOK_FRAME * HD
    size = queries.size * 2
    prob_low, gv_own, gv_one, gv_two = pl.pallas_call(
        values_kernel,
        out_shape=(chances, full, low, low),
        grid_spec=pltpu.PrefetchScalarGridSpec(
            num_scalar_prefetch=1,
            grid=(heads // GROUP,),
            in_specs=[column] * 5,
            out_specs=(chance, column, column, column),
            scratch_shapes=[bias, window, choice, accum],
        ),
        compiler_params=params,
        cost_estimate=pl.CostEstimate(
            flops=2 * flops, bytes_accessed=14 * size, transcendentals=0
        ),
        name="values_part",
    )(table, queries, grad_out, k_one, keys, k_two)
    rv_one, rv_two = swap(gv_one, gv_two)
    grad_queries, gk_own, gk_one, gk_two = pl.pallas_call(
        keys_kernel,
        out_shape=(low, full, low, low),
        grid_spec=pltpu.PrefetchScalarGridSpec(
            num_scalar_prefetch=1,
            grid=(heads // GROUP,),
            in_specs=[column] * 8 + [chance],
            out_specs=(column, column, column, column),
            scratch_shapes=[window, window, choice, choice, accum],
        ),
        compiler_params=params,
        cost_estimate=pl.CostEstimate(
            flops=3 * flops, bytes_accessed=18 * size, transcendentals=0
        ),
        name="keys_part",
    )(table, queries, grad_out, k_one, keys, k_two, v_one, values, v_two, prob_low)
    rk_one, rk_two = swap(gk_one, gk_two)

    def joined(own, one, two):
        return (own + one.astype(jnp.float32) + two.astype(jnp.float32)).astype(jnp.bfloat16)

    return (grad_queries, joined(gk_own, rk_one, rk_two), joined(gv_own, rv_one, rv_two))


def solution(mesh):
    rows = P(("clips", "frames"), "heads")
    return jax.shard_map(
        local,
        mesh=mesh,
        in_specs=(rows, rows, rows, rows, P("clips", None), P("clips", None, None, None)),
        out_specs=(rows, rows, rows),
        check_vma=False,
    )
```

time: 61.7 us -> 61.3 us (level)
  Pallas kernels: 18.8 us -> 19.6 us
  starting transfers between devices: 18.7 us -> 17.9 us
    ppermute x4, starting transfers between devices: 15.9 us -> 15.1 us  [swap(): lax.ppermute(one, 'frames', first)]
    unnamed x8 -> x12, local copies, waits for them, and re-layouts: 3.2 us -> 2.71 us
  transfers between devices with their start and end apart: 8 -> 8, of which waited for: 2 -> 2; matrix products, arithmetic and copies ran while one was open for 6% -> 7% of each run, Pallas kernels for 31% -> 32%
where the time goes in v2:
time: 61.3 us; the launch traced here: 60.3 us
  Pallas kernels  19.6 us (32%)
  starting transfers between devices  17.9 us (29%)
  waiting for transfers between devices  14 us (23%)
  other arithmetic  4.99 us (8%)
  local copies, waits for them, and re-layouts  3.15 us (5%)
  between operations  0.76 us (1%)
    ppermute x4, starting transfers between devices, swap(): lax.ppermute(one, 'frames', first)  15.1 us
    ppermute x4, waiting for transfers between devices, swap(): lax.ppermute(one, 'frames', first)  14 us
    pallas_call x1, Pallas kernels, local(): pl.pallas_call(keys_kernel, out_shape=(low, full, low, low), grid_spec=pl...  11.1 us
    pallas_call x1, Pallas kernels, local(): pl.pallas_call(values_kernel, out_shape=(chances, full, low, low), grid_s...  8.53 us
    ppermute x4, starting transfers between devices, swap(): lax.ppermute(two, 'frames', second)  2.75 us
    unnamed x12, local copies, waits for them, and re-layouts  2.71 us
    convert_element_type x2, other arithmetic, joined(): (own + one.astype(jnp.float32) + two.astype(jnp.float32)).astype(jnp.bflo...  1.98 us
  transfers between devices with their start and end apart: 8, of which 2 were waited for; matrix products, arithmetic and copies ran while one was open for 7% of the time, Pallas kernels for 32%

profile of v2, /device:TPU:0, one launch (start us, length us, event | category | flops | bytes accessed | tf_op | source)
XLA Modules:
  0.0 60.3 jit_solution(1453039917525678473)
XLA Ops:
  0.6 3.1 %collective-permute-start = (bf16[384,768]{1,0:T(8,128)(2,1)}, bf16[384,768]{1,0:T(8,128)(2,1)S(1)}, u32[]{:S(2)}, u32[]{:S(2)}) collective-permute-start(bf16[384,768]{1,0:T(8,128)(2,1)} %k_own.3), channel_id=1, source_target_pairs={{0,4},{4,0},{8,12},{12,8},{1,5},{5,1},{9,13},{13,9},{2,6},{6,2},{1... | collective-permute-start | bytes 1769480 | tf_op jit(solution)/shard_map/ppermute | solution.py:132
  3.7 0.7 %collective-permute-start.1 = (bf16[384,768]{1,0:T(8,128)(2,1)}, bf16[384,768]{1,0:T(8,128)(2,1)S(1)}, u32[]{:S(2)}, u32[]{:S(2)}) collective-permute-start(bf16[384,768]{1,0:T(8,128)(2,1)} %k_own.3), channel_id=1, source_target_pairs={{4,8},{8,4},{5,9},{9,5},{6,10},{10,6},{7,11},{11,7},{20,24},{24,20... | collective-permute-start | bytes 1769480 | tf_op jit(solution)/shard_map/ppermute | solution.py:132
  4.4 4.4 %collective-permute-start.2 = (bf16[384,768]{1,0:T(8,128)(2,1)}, bf16[384,768]{1,0:T(8,128)(2,1)S(1)}, u32[]{:S(2)}, u32[]{:S(2)}) collective-permute-start(bf16[384,768]{1,0:T(8,128)(2,1)} %v_own.1), channel_id=1, source_target_pairs={{0,4},{4,0},{8,12},{12,8},{1,5},{5,1},{9,13},{13,9},{2,6},{6,2},{1... | collective-permute-start | bytes 1769480 | tf_op jit(solution)/shard_map/ppermute | solution.py:132
  8.8 0.7 %collective-permute-start.3 = (bf16[384,768]{1,0:T(8,128)(2,1)}, bf16[384,768]{1,0:T(8,128)(2,1)S(1)}, u32[]{:S(2)}, u32[]{:S(2)}) collective-permute-start(bf16[384,768]{1,0:T(8,128)(2,1)} %v_own.1), channel_id=1, source_target_pairs={{4,8},{8,4},{5,9},{9,5},{6,10},{10,6},{7,11},{11,7},{20,24},{24,20... | collective-permute-start | bytes 1769480 | tf_op jit(solution)/shard_map/ppermute | solution.py:132
  9.6 0.8 %fusion.1 = s32[2,3]{0,1:T(4,128)S(1)} fusion(s32[8,3]{0,1:T(4,128)} %param.10, s32[]{:T(128)S(6)} %select_n.27, pred[]{:T(512)S(6)} %eq.7), kind=kLoop, calls=%fused_computation.8 | loop fusion | flops 126 | bytes 53 | tf_op jit(solution)/shard_map/add | solution.py:145
  10.3 0.1 copy.9
  10.4 0.1 reshape.13
  10.5 0.8 %and_convert_fusion = s32[2,3]{0,1:T(4,128)S(1)} fusion(s32[8,3]{0,1:T(4,128)} %param.10, s32[]{:T(128)S(6)} %select_n.27, s32[]{:T(128)S(6)} %mul.14), kind=kLoop, calls=%fused_computation.11 | loop fusion | flops 36 | bytes 56 | tf_op jit(solution)/shard_map/convert_element_type | solution.py:142
  11.3 0.8 %dynamic-slice_multiply_fusion = s32[2,3,4,4]{0,3,2,1:T(4,128)S(1)} fusion(s32[8,3,4,4]{0,3,2,1:T(4,128)} %param.11, s32[]{:T(128)S(6)} %select_n.27, s32[2,3]{0,1:T(4,128)S(1)} %and_convert_fusion), kind=kLoop, calls=%fused_computation.2 | loop fusion | flops 96 | bytes 796 | tf_op jit(solution)/shard_map/mul | solution.py:146
  12.1 0.2 copy.10
  12.2 0.1 reshape.14
  12.3 0.7 %pad_add_fusion.table = s32[102]{0:T(128)} fusion(s32[96]{0:T(128)S(1)} %reshape.14, s32[6]{0:T(128)S(1)} %reshape.13), kind=kLoop, calls=%fused_computation.12 | loop fusion | flops 102 | bytes 816 | tf_op jit(solution)/shard_map/concatenate | solution.py:147
  13.0 5.1 %collective-permute-done.k_one = bf16[384,768]{1,0:T(8,128)(2,1)S(1)} collective-permute-done((bf16[384,768]{1,0:T(8,128)(2,1)}, bf16[384,768]{1,0:T(8,128)(2,1)S(1)}, u32[]{:S(2)}, u32[]{:S(2)}) %collective-permute-start) | collective-permute-done | bytes 589856 | tf_op jit(solution)/shard_map/ppermute | solution.py:132
  18.1 0.0 copy-start
  18.1 0.0 collective-permute-done.1.k_two
  18.1 0.8 %copy-done = bf16[384,768]{1,0:T(8,128)(2,1)} copy-done((bf16[384,768]{1,0:T(8,128)(2,1)}, bf16[384,768]{1,0:T(8,128)(2,1)S(1)}, u32[]{:S(2)}) %copy-start) | copy-done | bytes 589848
  18.9 0.0 copy-start.1
  18.9 0.8 %copy-done.1 = bf16[384,768]{1,0:T(8,128)(2,1)} copy-done((bf16[384,768]{1,0:T(8,128)(2,1)}, bf16[384,768]{1,0:T(8,128)(2,1)S(1)}, u32[]{:S(2)}) %copy-start.1) | copy-done | bytes 589848
  19.7 8.5 %values_part.1 = (bf16[6,2,576,192]{3,2,1,0:T(8,128)(2,1)}, f32[384,768]{1,0:T(8,128)}, bf16[384,768]{1,0:T(8,128)(2,1)}, bf16[384,768]{1,0:T(8,128)(2,1)}) custom-call(s32[102]{0:T(128)} %pad_add_fusion.table, bf16[384,768]{1,0:T(8,128)(2,1)} %queries.3, bf16[384,768]{1,0:T(8,128)(2,1)} %grad_out.3, bf16[384,768]{1,0:T(8,128)(2,1)} %copy-done, ...), custom_call_target="tpu_custom_call" | custom-call | flops 679477248 | bytes 8257536 | tf_op jit(solution)/shard_map/values_part/pallas_call | solution.py:170
  28.3 4.3 %collective-permute-start.6 = (bf16[384,768]{1,0:T(8,128)(2,1)}, bf16[384,768]{1,0:T(8,128)(2,1)S(1)}, u32[]{:S(2)}, u32[]{:S(2)}) collective-permute-start(bf16[384,768]{1,0:T(8,128)(2,1)} %get-tuple-element.17), channel_id=1, source_target_pairs={{0,4},{4,0},{8,12},{12,8},{1,5},{5,1},{9,13},{13,9},{2,6},{6,2},{1... | collective-permute-start | bytes 1769480 | tf_op jit(solution)/shard_map/ppermute | solution.py:132
  32.5 0.7 %collective-permute-start.7 = (bf16[384,768]{1,0:T(8,128)(2,1)}, bf16[384,768]{1,0:T(8,128)(2,1)S(1)}, u32[]{:S(2)}, u32[]{:S(2)}) collective-permute-start(bf16[384,768]{1,0:T(8,128)(2,1)} %get-tuple-element.18), channel_id=1, source_target_pairs={{4,8},{8,4},{5,9},{9,5},{6,10},{10,6},{7,11},{11,7},{20,24},{24,20... | collective-permute-start | bytes 1769480 | tf_op jit(solution)/shard_map/ppermute | solution.py:132
  33.2 0.0 collective-permute-done.2.v_one
  33.2 0.0 copy-start.4
  33.2 0.0 collective-permute-done.3.v_two
  33.2 0.0 copy-start.5
  33.2 0.8 %copy-done.4 = bf16[384,768]{1,0:T(8,128)(2,1)} copy-done((bf16[384,768]{1,0:T(8,128)(2,1)}, bf16[384,768]{1,0:T(8,128)(2,1)S(1)}, u32[]{:S(2)}) %copy-start.4) | copy-done | bytes 589848
  34.1 0.2 copy-done.5
  34.3 0.0 copy-start.2
  34.3 11.1 %keys_part.1 = (bf16[384,768]{1,0:T(8,128)(2,1)}, f32[384,768]{1,0:T(8,128)}, bf16[384,768]{1,0:T(8,128)(2,1)}, bf16[384,768]{1,0:T(8,128)(2,1)}) custom-call(s32[102]{0:T(128)} %pad_add_fusion.table, bf16[384,768]{1,0:T(8,128)(2,1)} %queries.3, bf16[384,768]{1,0:T(8,128)(2,1)} %grad_out.3, bf16[384,768]{1,0:T(8,128)(2,1)} %copy-done, ...), custom_call_target="tpu_custom_call" | custom-call | flops 1019215872 | bytes 10616832 | tf_op jit(solution)/shard_map/keys_part/pallas_call | solution.py:187
  45.4 3.3 %collective-permute-start.4 = (bf16[384,768]{1,0:T(8,128)(2,1)}, bf16[384,768]{1,0:T(8,128)(2,1)S(1)}, u32[]{:S(2)}, u32[]{:S(2)}) collective-permute-start(bf16[384,768]{1,0:T(8,128)(2,1)} %get-tuple-element.14), channel_id=1, source_target_pairs={{0,4},{4,0},{8,12},{12,8},{1,5},{5,1},{9,13},{13,9},{2,6},{6,2},{1... | collective-permute-start | bytes 1769480 | tf_op jit(solution)/shard_map/ppermute | solution.py:132
  48.7 0.7 %collective-permute-start.5 = (bf16[384,768]{1,0:T(8,128)(2,1)}, bf16[384,768]{1,0:T(8,128)(2,1)S(1)}, u32[]{:S(2)}, u32[]{:S(2)}) collective-permute-start(bf16[384,768]{1,0:T(8,128)(2,1)} %get-tuple-element.15), channel_id=1, source_target_pairs={{4,8},{8,4},{5,9},{9,5},{6,10},{10,6},{7,11},{11,7},{20,24},{24,20... | collective-permute-start | bytes 1769480 | tf_op jit(solution)/shard_map/ppermute | solution.py:132
  49.4 0.0 collective-permute-done.6
  49.4 0.0 collective-permute-done.7
  49.4 0.0 copy-done.2
  49.5 0.0 copy-start.3
  49.5 1.0 %add_convert_fusion = bf16[384,768]{1,0:T(8,128)(2,1)} fusion(bf16[384,768]{1,0:T(8,128)(2,1)S(1)} %collective-permute-done.7, f32[384,768]{1,0:T(8,128)S(1)} %copy-done.2, bf16[384,768]{1,0:T(8,128)(2,1)S(1)} %collective-permute-done.6), kind=kLoop, calls=%fused_computation | loop fusion | flops 1474560 | bytes 2949120 | tf_op jit(solution)/shard_map/convert_element_type | solution.py:206
  50.5 8.9 %collective-permute-done.4 = bf16[384,768]{1,0:T(8,128)(2,1)S(1)} collective-permute-done((bf16[384,768]{1,0:T(8,128)(2,1)}, bf16[384,768]{1,0:T(8,128)(2,1)S(1)}, u32[]{:S(2)}, u32[]{:S(2)}) %collective-permute-start.4) | collective-permute-done | bytes 589856 | tf_op jit(solution)/shard_map/ppermute | solution.py:132
  59.3 0.0 collective-permute-done.5
  59.3 0.0 copy-done.3
  59.3 1.0 %add_convert_fusion.1 = bf16[384,768]{1,0:T(8,128)(2,1)} fusion(bf16[384,768]{1,0:T(8,128)(2,1)S(1)} %collective-permute-done.5, f32[384,768]{1,0:T(8,128)S(1)} %copy-done.3, bf16[384,768]{1,0:T(8,128)(2,1)S(1)} %collective-permute-done.4), kind=kLoop, calls=%fused_computation.1 | loop fusion | flops 1474560 | bytes 2949120 | tf_op jit(solution)/shard_map/convert_element_type | solution.py:206
Async XLA Ops:
  0.6 17.5 %collective-permute-start = (bf16[384,768]{1,0:T(8,128)(2,1)}, bf16[384,768]{1,0:T(8,128)(2,1)S(1)}, u32[]{:S(2)}, u32[]{:S(2)}) collective-permute-start(bf16[384,768]{1,0:T(8,128)(2,1)} %k_own.3), channel_id=1, source_target_pairs={{0,4},{4,0},{8,12},{12,8},{1,5},{5,1},{9,13},{13,9},{2,6},{6,2},{1... | collective-permute-start | bytes 1769480 | tf_op jit(solution)/shard_map/ppermute | solution.py:132
  3.7 14.4 %collective-permute-start.1 = (bf16[384,768]{1,0:T(8,128)(2,1)}, bf16[384,768]{1,0:T(8,128)(2,1)S(1)}, u32[]{:S(2)}, u32[]{:S(2)}) collective-permute-start(bf16[384,768]{1,0:T(8,128)(2,1)} %k_own.3), channel_id=1, source_target_pairs={{4,8},{8,4},{5,9},{9,5},{6,10},{10,6},{7,11},{11,7},{20,24},{24,20... | collective-permute-start | bytes 1769480 | tf_op jit(solution)/shard_map/ppermute | solution.py:132
  4.4 28.8 %collective-permute-start.2 = (bf16[384,768]{1,0:T(8,128)(2,1)}, bf16[384,768]{1,0:T(8,128)(2,1)S(1)}, u32[]{:S(2)}, u32[]{:S(2)}) collective-permute-start(bf16[384,768]{1,0:T(8,128)(2,1)} %v_own.1), channel_id=1, source_target_pairs={{0,4},{4,0},{8,12},{12,8},{1,5},{5,1},{9,13},{13,9},{2,6},{6,2},{1... | collective-permute-start | bytes 1769480 | tf_op jit(solution)/shard_map/ppermute | solution.py:132
  8.8 24.4 %collective-permute-start.3 = (bf16[384,768]{1,0:T(8,128)(2,1)}, bf16[384,768]{1,0:T(8,128)(2,1)S(1)}, u32[]{:S(2)}, u32[]{:S(2)}) collective-permute-start(bf16[384,768]{1,0:T(8,128)(2,1)} %v_own.1), channel_id=1, source_target_pairs={{4,8},{8,4},{5,9},{9,5},{6,10},{10,6},{7,11},{11,7},{20,24},{24,20... | collective-permute-start | bytes 1769480 | tf_op jit(solution)/shard_map/ppermute | solution.py:132
  18.1 0.8 %copy-start = (bf16[384,768]{1,0:T(8,128)(2,1)}, bf16[384,768]{1,0:T(8,128)(2,1)S(1)}, u32[]{:S(2)}) copy-start(bf16[384,768]{1,0:T(8,128)(2,1)S(1)} %collective-permute-done.k_one) | copy-start | bytes 1769476
  18.9 0.8 %copy-start.1 = (bf16[384,768]{1,0:T(8,128)(2,1)}, bf16[384,768]{1,0:T(8,128)(2,1)S(1)}, u32[]{:S(2)}) copy-start(bf16[384,768]{1,0:T(8,128)(2,1)S(1)} %collective-permute-done.1.k_two) | copy-start | bytes 1769476
  28.3 21.2 %collective-permute-start.6 = (bf16[384,768]{1,0:T(8,128)(2,1)}, bf16[384,768]{1,0:T(8,128)(2,1)S(1)}, u32[]{:S(2)}, u32[]{:S(2)}) collective-permute-start(bf16[384,768]{1,0:T(8,128)(2,1)} %get-tuple-element.17), channel_id=1, source_target_pairs={{0,4},{4,0},{8,12},{12,8},{1,5},{5,1},{9,13},{13,9},{2,6},{6,2},{1... | collective-permute-start | bytes 1769480 | tf_op jit(solution)/shard_map/ppermute | solution.py:132
  32.5 16.9 %collective-permute-start.7 = (bf16[384,768]{1,0:T(8,128)(2,1)}, bf16[384,768]{1,0:T(8,128)(2,1)S(1)}, u32[]{:S(2)}, u32[]{:S(2)}) collective-permute-start(bf16[384,768]{1,0:T(8,128)(2,1)} %get-tuple-element.18), channel_id=1, source_target_pairs={{4,8},{8,4},{5,9},{9,5},{6,10},{10,6},{7,11},{11,7},{20,24},{24,20... | collective-permute-start | bytes 1769480 | tf_op jit(solution)/shard_map/ppermute | solution.py:132
  33.2 0.9 %copy-start.4 = (bf16[384,768]{1,0:T(8,128)(2,1)}, bf16[384,768]{1,0:T(8,128)(2,1)S(1)}, u32[]{:S(2)}) copy-start(bf16[384,768]{1,0:T(8,128)(2,1)S(1)} %collective-permute-done.2.v_one) | copy-start | bytes 1769476
  33.2 1.1 %copy-start.5 = (bf16[384,768]{1,0:T(8,128)(2,1)}, bf16[384,768]{1,0:T(8,128)(2,1)S(1)}, u32[]{:S(2)}) copy-start(bf16[384,768]{1,0:T(8,128)(2,1)S(1)} %collective-permute-done.3.v_two) | copy-start | bytes 1769476
  34.3 15.1 %copy-start.2 = (f32[384,768]{1,0:T(8,128)S(1)}, f32[384,768]{1,0:T(8,128)}, u32[]{:S(2)}) copy-start(f32[384,768]{1,0:T(8,128)} %get-tuple-element.16) | copy-start | bytes 3538948
  45.4 14.0 %collective-permute-start.4 = (bf16[384,768]{1,0:T(8,128)(2,1)}, bf16[384,768]{1,0:T(8,128)(2,1)S(1)}, u32[]{:S(2)}, u32[]{:S(2)}) collective-permute-start(bf16[384,768]{1,0:T(8,128)(2,1)} %get-tuple-element.14), channel_id=1, source_target_pairs={{0,4},{4,0},{8,12},{12,8},{1,5},{5,1},{9,13},{13,9},{2,6},{6,2},{1... | collective-permute-start | bytes 1769480 | tf_op jit(solution)/shard_map/ppermute | solution.py:132
  48.7 10.6 %collective-permute-start.5 = (bf16[384,768]{1,0:T(8,128)(2,1)}, bf16[384,768]{1,0:T(8,128)(2,1)S(1)}, u32[]{:S(2)}, u32[]{:S(2)}) collective-permute-start(bf16[384,768]{1,0:T(8,128)(2,1)} %get-tuple-element.15), channel_id=1, source_target_pairs={{4,8},{8,4},{5,9},{9,5},{6,10},{10,6},{7,11},{11,7},{20,24},{24,20... | collective-permute-start | bytes 1769480 | tf_op jit(solution)/shard_map/ppermute | solution.py:132
  49.5 9.9 %copy-start.3 = (f32[384,768]{1,0:T(8,128)S(1)}, f32[384,768]{1,0:T(8,128)}, u32[]{:S(2)}) copy-start(f32[384,768]{1,0:T(8,128)} %get-tuple-element.13) | copy-start | bytes 3538948

commit v3 on v2

v3 whole, which is shorter than its diff:
```python
import math

import jax
import jax.numpy as jnp
from jax import lax
from jax.experimental import pallas as pl
from jax.experimental.pallas import tpu as pltpu
from jax.sharding import PartitionSpec as P

HD = 128
TOK_FRAME = 192
FR_DEV = 2
NSEL = 3
SB = 4
DEPTH = 3
ROWS = FR_DEV * TOK_FRAME
BLOCK = TOK_FRAME // SB
SCALE = HD ** (-0.5)
SCALE2 = SCALE * math.log2(math.e)
NEG = -1e30
NT = (((1,), (1,)), ((), ()))
NN = (((1,), (0,)), ((), ()))
TN = (((0,), (0,)), ((), ()))


def dot(lhs, rhs, dims):
    return lax.dot_general(lhs, rhs, dims, preferred_element_type=jnp.float32)


def column_of(head):
    return slice(head * HD, (head + 1) * HD)


def rows_of(frame):
    return slice(frame * TOK_FRAME, (frame + 1) * TOK_FRAME)


def span(table, frame, slot):
    return pl.ds(pl.multiple_of(table[frame * NSEL + slot] * TOK_FRAME, TOK_FRAME), TOK_FRAME)


def fill_bias(table, bias):
    q_block = lax.broadcasted_iota(jnp.int32, (8, TOK_FRAME), 1) // BLOCK
    for frame in range(FR_DEV):
        for slot in range(NSEL):
            for k_block in range(SB):
                value = jnp.zeros((8, TOK_FRAME), jnp.float32)
                for block in range(SB):
                    at = FR_DEV * NSEL + ((frame * NSEL + slot) * SB + block) * SB + k_block
                    drop = jnp.where(table[at] > 0, 0.0, NEG)
                    value = jnp.where(q_block == block, drop, value)
                for step in range(0, BLOCK, 8):
                    bias[frame, pl.ds(slot * TOK_FRAME + k_block * BLOCK + step, 8), :] = value


def fill_window(window, one, own, two, column):
    window[0:ROWS] = one[:, column]
    window[ROWS : 2 * ROWS] = own[:, column]
    window[2 * ROWS : 3 * ROWS] = two[:, column]


def pick(table, frame, window, chosen):
    for slot in range(NSEL):
        chosen[rows_of(slot)] = window[span(table, frame, slot), :]


def spread(table, frame, accum, parts):
    for slot in range(1, NSEL):
        accum[span(table, frame, slot), :] += parts[rows_of(slot - 1)]


def stage_kernel(table, *refs):
    arrays, copies, bias, sems = refs[:4], refs[4:8], refs[8], refs[9]
    moves = [
        pltpu.make_async_copy(array, copy, sems.at[i])
        for i, (array, copy) in enumerate(zip(arrays, copies))
    ]
    for move in moves:
        move.start()
    fill_bias(table, bias)
    for move in moves:
        move.wait()


def values_kernel(
    table, queries, grad_out, k_own, bias, k_one, k_two,
    chosen_out, prob_out, own_out, one_out, two_out,
    windows, accums,
):
    for head in range(queries.shape[1] // HD):
        column = column_of(head)
        window = windows.at[head % DEPTH]
        accum = accums.at[head % DEPTH]
        fill_window(window, k_one, k_own, k_two, column)
        accum[...] = jnp.zeros_like(accum)
        for frame in range(FR_DEV):
            chosen = chosen_out.at[head, frame]
            pick(table, frame, window, chosen)
            scores = dot(chosen[...], queries[rows_of(frame), column], NT)
            masked = scores * SCALE2 + bias[frame]
            raised = jnp.exp2(masked - jnp.max(masked, 0, keepdims=True))
            inverse = 1.0 / jnp.sum(raised, 0, keepdims=True)
            prob_low = (raised * inverse).astype(jnp.bfloat16)
            prob_out[head, frame] = prob_low
            far = dot(prob_low[TOK_FRAME:], grad_out[rows_of(frame), column], NN)
            spread(table, frame, accum, far)
        one_out[:, column] = accum[0:ROWS].astype(one_out.dtype)
        own_out[:, column] = accum[ROWS : 2 * ROWS]
        two_out[:, column] = accum[2 * ROWS : 3 * ROWS].astype(two_out.dtype)


def keys_kernel(
    table, queries, grad_out, v_own, prob_in, v_one, v_two,
    score_out, own_out, one_out, two_out,
    windows, choices, accums,
):
    for head in range(queries.shape[1] // HD):
        column = column_of(head)
        window = windows.at[head % DEPTH]
        accum = accums.at[head % DEPTH]
        fill_window(window, v_one, v_own, v_two, column)
        accum[...] = jnp.zeros_like(accum)
        for frame in range(FR_DEV):
            chosen = choices.at[head % DEPTH, frame]
            pick(table, frame, window, chosen)
            grad_prob = dot(chosen[...], grad_out[rows_of(frame), column], NT)
            prob = prob_in[head, frame].astype(jnp.float32)
            delta = jnp.sum(prob * grad_prob, 0, keepdims=True)
            score_low = (prob * (grad_prob - delta)).astype(jnp.bfloat16)
            score_out[head, frame] = score_low
            far = dot(score_low[TOK_FRAME:], queries[rows_of(frame), column], NN)
            spread(table, frame, accum, far)
        one_out[:, column] = (accum[0:ROWS] * SCALE).astype(one_out.dtype)
        own_out[:, column] = accum[ROWS : 2 * ROWS]
        two_out[:, column] = (accum[2 * ROWS : 3 * ROWS] * SCALE).astype(two_out.dtype)


def rest_kernel(
    queries, grad_out, chosen_in, prob_in, score_in, gv_own, gk_own, rv_one, rv_two,
    query_out, value_out, key_out,
):
    for head in range(queries.shape[1] // HD):
        column = column_of(head)
        for frame in range(FR_DEV):
            rows = rows_of(frame)
            score_low = score_in[head, frame]
            grad_query = dot(score_low, chosen_in[head, frame], TN)
            query_out[rows, column] = (grad_query * SCALE).astype(query_out.dtype)
            near = dot(score_low[:TOK_FRAME], queries[rows, column], NN)
            key_out[rows, column] = (gk_own[rows, column] + near) * SCALE
            near = dot(prob_in[head, frame, :TOK_FRAME], grad_out[rows, column], NN)
            total = gv_own[rows, column] + near
            total += rv_one[rows, column].astype(jnp.float32)
            total += rv_two[rows, column].astype(jnp.float32)
            value_out[rows, column] = total.astype(value_out.dtype)


def exchanges(count):
    first = [(i, i + 1) for i in range(0, count - 1, 2)]
    second = [(i, i + 1) for i in range(1, count - 1, 2)]
    return tuple([pair for i, j in part for pair in ((i, j), (j, i))] for part in (first, second))


def swap(one, two):
    first, second = exchanges(lax.axis_size("frames"))
    return lax.ppermute(one, "frames", first), lax.ppermute(two, "frames", second)


def lookup(offsets, spatial):
    me = lax.axis_index("frames")
    first_frame = me * FR_DEV
    shifts = lax.dynamic_slice_in_dim(offsets, first_frame, FR_DEV, 0)
    blocks = lax.dynamic_slice_in_dim(spatial, first_frame, FR_DEV, 0)
    place = jnp.arange(FR_DEV, dtype=jnp.int32)[:, None] + shifts
    target = first_frame + place
    inside = ((target >= 0) & (target < offsets.shape[0])).astype(jnp.int32)
    side = (place >= 0).astype(jnp.int32) + (place >= FR_DEV).astype(jnp.int32)
    side = jnp.where(me % 2 == 1, side, 2 - side)
    spot = side * FR_DEV + (place % FR_DEV)
    blocks = blocks * inside[:, :, None, None]
    return jnp.concatenate([spot.reshape(-1), blocks.reshape(-1)]).astype(jnp.int32)


def call(kernel, name, scalars, arrays, outs, scratch, flops, space=pltpu.VMEM):
    if space is pltpu.VMEM:
        arrays = [pltpu.with_memory_space_constraint(array, space) for array in arrays]
    return pl.pallas_call(
        kernel,
        out_shape=outs,
        in_specs=[pl.BlockSpec(memory_space=pltpu.SMEM)] * len(scalars)
        + [pl.BlockSpec(memory_space=space)] * len(arrays),
        out_specs=tuple(pl.BlockSpec(memory_space=pltpu.VMEM) for _ in outs),
        scratch_shapes=scratch,
        compiler_params=pltpu.CompilerParams(vmem_limit_bytes=16 << 20),
        cost_estimate=pl.CostEstimate(flops=flops, bytes_accessed=0, transcendentals=0),
        name=name,
    )(*scalars, *arrays)


def local(queries, keys, values, grad_out, offsets, spatial):
    heads = queries.shape[1] // HD
    k_one, k_two = swap(keys, keys)
    v_one, v_two = swap(values, values)
    table = lookup(offsets, spatial)
    shape = queries.shape
    slots = NSEL * TOK_FRAME
    low = pltpu.VMEM(shape, jnp.bfloat16)
    full = pltpu.VMEM(shape, jnp.float32)
    pairs = pltpu.VMEM((heads, FR_DEV, slots, TOK_FRAME), jnp.bfloat16)
    choices = pltpu.VMEM((heads, FR_DEV, slots, HD), jnp.bfloat16)
    biases = pltpu.VMEM((FR_DEV, slots, TOK_FRAME), jnp.float32)
    windows = pltpu.VMEM((DEPTH, 3 * ROWS, HD), jnp.bfloat16)
    accums = pltpu.VMEM((DEPTH, 3 * ROWS, HD), jnp.float32)
    flops = 2 * heads * FR_DEV * NSEL * TOK_FRAME * TOK_FRAME * HD
    staged = call(
        stage_kernel, "stage", (table,), (queries, grad_out, keys, values),
        (low, low, low, low, biases), [pltpu.SemaphoreType.DMA((4,))], flops // 2, pl.ANY,
    )
    query, grad, key, value, bias = staged
    chosen, prob_low, gv_own, gv_one, gv_two = call(
        values_kernel, "values_part", (table,), (query, grad, key, bias, k_one, k_two),
        (choices, pairs, full, low, low), [windows, accums], 2 * flops,
    )
    rv_one, rv_two = swap(gv_one, gv_two)
    score_low, gk_own, gk_one, gk_two = call(
        keys_kernel, "keys_part", (table,), (query, grad, value, prob_low, v_one, v_two),
        (pairs, full, low, low),
        [windows, pltpu.VMEM((DEPTH, FR_DEV, slots, HD), jnp.bfloat16), accums], 2 * flops,
    )
    rk_one, rk_two = swap(gk_one, gk_two)
    grad_queries, grad_values, gk_own = call(
        rest_kernel, "rest", (),
        (query, grad, chosen, prob_low, score_low, gv_own, gk_own, rv_one, rv_two),
        (low, low, full), [], 2 * flops,
    )
    grad_keys = gk_own + rk_one.astype(jnp.float32) + rk_two.astype(jnp.float32)
    return (grad_queries, grad_keys.astype(jnp.bfloat16), grad_values)


def solution(mesh):
    rows = P(("clips", "frames"), "heads")
    return jax.shard_map(
        local,
        mesh=mesh,
        in_specs=(rows, rows, rows, rows, P("clips", None), P("clips", None, None, None)),
        out_specs=(rows, rows, rows),
        check_vma=False,
    )
```

time: 61.3 us -> 59.9 us (0.977)
  waiting for transfers between devices: 14 us -> 17.8 us
  Pallas kernels: 19.6 us -> 16.3 us
  local copies, waits for them, and re-layouts: 3.15 us -> 6.33 us
  starting transfers between devices: 17.9 us -> 14.8 us
  other arithmetic: 4.99 us -> 3.44 us
    ppermute x4, waiting for transfers between devices: 14 us -> 17.8 us  [swap(): lax.ppermute(one, 'frames', first)]
    pallas_call x2 -> x4, Pallas kernels: 19.6 us -> 16.3 us  [call(): pl.pallas_call(kernel, out_shape=outs, in_specs=[pl.BlockSpec(memory_spac...]
    ppermute x4, starting transfers between devices: 15.1 us -> 11.9 us  [swap(): lax.ppermute(one, 'frames', first)]
    unnamed x12 -> x10, local copies, waits for them, and re-layouts: 2.71 us -> 5.89 us
    convert_element_type x2 -> x1, other arithmetic: 1.98 us -> 1.03 us  [local(): return (grad_queries, grad_keys.astype(jnp.bfloat16), grad_values)]
  transfers between devices with their start and end apart: 8 -> 8, of which waited for: 2 -> 4; matrix products, arithmetic and copies ran while one was open for 7% -> 8% of each run, Pallas kernels for 32% -> 28%
where the time goes in v3:
time: 59.9 us; the launch traced here: 59.4 us
  waiting for transfers between devices  17.8 us (30%)
  Pallas kernels  16.3 us (27%)
  starting transfers between devices  14.8 us (25%)
  local copies, waits for them, and re-layouts  6.33 us (11%)
  other arithmetic  3.44 us (6%)
  between operations  0.73 us (1%)
    ppermute x4, waiting for transfers between devices, swap(): lax.ppermute(one, 'frames', first)  17.8 us
    pallas_call x4, Pallas kernels, call(): pl.pallas_call(kernel, out_shape=outs, in_specs=[pl.BlockSpec(memory_spac...  16.3 us
    ppermute x4, starting transfers between devices, swap(): lax.ppermute(one, 'frames', first)  11.9 us
    unnamed x10, local copies, waits for them, and re-layouts  5.89 us
    ppermute x4, starting transfers between devices, swap(): lax.ppermute(two, 'frames', second)  2.94 us
  transfers between devices with their start and end apart: 8, of which 4 were waited for; matrix products, arithmetic and copies ran while one was open for 8% of the time, Pallas kernels for 28%

profile of v3, /device:TPU:0, one launch (start us, length us, event | category | flops | bytes accessed | tf_op | source)
XLA Modules:
  0.0 59.4 jit_solution(9323256243684902580)
XLA Ops:
  0.6 0.7 %collective-permute-start.1 = (bf16[384,768]{1,0:T(8,128)(2,1)}, bf16[384,768]{1,0:T(8,128)(2,1)S(1)}, u32[]{:S(2)}, u32[]{:S(2)}) collective-permute-start(bf16[384,768]{1,0:T(8,128)(2,1)} %refs_2_.1), channel_id=1, source_target_pairs={{4,8},{8,4},{5,9},{9,5},{6,10},{10,6},{7,11},{11,7},{20,24},{24,20... | collective-permute-start | bytes 1769480 | tf_op jit(solution)/shard_map/ppermute | solution.py:166
  1.3 5.9 %collective-permute-start = (bf16[384,768]{1,0:T(8,128)(2,1)}, bf16[384,768]{1,0:T(8,128)(2,1)S(1)}, u32[]{:S(2)}, u32[]{:S(2)}) collective-permute-start(bf16[384,768]{1,0:T(8,128)(2,1)} %refs_2_.1), channel_id=1, source_target_pairs={{0,4},{4,0},{8,12},{12,8},{1,5},{5,1},{9,13},{13,9},{2,6},{6,2},{1... | collective-permute-start | bytes 1769480 | tf_op jit(solution)/shard_map/ppermute | solution.py:166
  7.2 0.7 %collective-permute-start.3 = (bf16[384,768]{1,0:T(8,128)(2,1)}, bf16[384,768]{1,0:T(8,128)(2,1)S(1)}, u32[]{:S(2)}, u32[]{:S(2)}) collective-permute-start(bf16[384,768]{1,0:T(8,128)(2,1)} %refs_3_.1), channel_id=1, source_target_pairs={{4,8},{8,4},{5,9},{9,5},{6,10},{10,6},{7,11},{11,7},{20,24},{24,20... | collective-permute-start | bytes 1769480 | tf_op jit(solution)/shard_map/ppermute | solution.py:166
  7.9 1.8 %collective-permute-start.2 = (bf16[384,768]{1,0:T(8,128)(2,1)}, bf16[384,768]{1,0:T(8,128)(2,1)S(1)}, u32[]{:S(2)}, u32[]{:S(2)}) collective-permute-start(bf16[384,768]{1,0:T(8,128)(2,1)} %refs_3_.1), channel_id=1, source_target_pairs={{0,4},{4,0},{8,12},{12,8},{1,5},{5,1},{9,13},{13,9},{2,6},{6,2},{1... | collective-permute-start | bytes 1769480 | tf_op jit(solution)/shard_map/ppermute | solution.py:166
  9.7 0.8 %fusion.1 = s32[2,3]{0,1:T(4,128)S(1)} fusion(s32[8,3]{0,1:T(4,128)} %param.10, s32[]{:T(128)S(6)} %select_n.27, pred[]{:T(512)S(6)} %eq.7), kind=kLoop, calls=%fused_computation.7 | loop fusion | flops 126 | bytes 53 | tf_op jit(solution)/shard_map/add | solution.py:179
  10.4 0.1 copy.9
  10.5 0.1 reshape.13
  10.6 0.8 %and_convert_fusion = s32[2,3]{0,1:T(4,128)S(1)} fusion(s32[8,3]{0,1:T(4,128)} %param.10, s32[]{:T(128)S(6)} %select_n.27, s32[]{:T(128)S(6)} %mul.14), kind=kLoop, calls=%fused_computation.10 | loop fusion | flops 36 | bytes 56 | tf_op jit(solution)/shard_map/convert_element_type | solution.py:176
  11.4 0.8 %dynamic-slice_multiply_fusion = s32[2,3,4,4]{0,3,2,1:T(4,128)S(1)} fusion(s32[8,3,4,4]{0,3,2,1:T(4,128)} %param.11, s32[]{:T(128)S(6)} %select_n.27, s32[2,3]{0,1:T(4,128)S(1)} %and_convert_fusion), kind=kLoop, calls=%fused_computation.1 | loop fusion | flops 96 | bytes 796 | tf_op jit(solution)/shard_map/mul | solution.py:180
  12.2 0.2 copy.10
  12.3 0.1 reshape.14
  12.4 0.1 pad_add_fusion.table
  12.5 0.0 copy-start
  12.5 1.1 %copy-done = bf16[384,768]{1,0:T(8,128)(2,1)S(1)} copy-done((bf16[384,768]{1,0:T(8,128)(2,1)S(1)}, bf16[384,768]{1,0:T(8,128)(2,1)}, u32[]{:S(2)}) %copy-start) | copy-done | bytes 589848
  13.6 0.0 copy-start.1
  13.6 1.1 %copy-done.1 = bf16[384,768]{1,0:T(8,128)(2,1)S(1)} copy-done((bf16[384,768]{1,0:T(8,128)(2,1)S(1)}, bf16[384,768]{1,0:T(8,128)(2,1)}, u32[]{:S(2)}) %copy-start.1) | copy-done | bytes 589848
  14.7 0.0 copy-start.2
  14.7 1.1 %copy-done.2 = bf16[384,768]{1,0:T(8,128)(2,1)S(1)} copy-done((bf16[384,768]{1,0:T(8,128)(2,1)S(1)}, bf16[384,768]{1,0:T(8,128)(2,1)}, u32[]{:S(2)}) %copy-start.2) | copy-done | bytes 589848
  15.7 0.0 copy-start.3
  15.7 1.1 %copy-done.3 = bf16[384,768]{1,0:T(8,128)(2,1)S(1)} copy-done((bf16[384,768]{1,0:T(8,128)(2,1)S(1)}, bf16[384,768]{1,0:T(8,128)(2,1)}, u32[]{:S(2)}) %copy-start.3) | copy-done | bytes 589848
  16.8 1.2 %stage.1 = (bf16[384,768]{1,0:T(8,128)(2,1)S(1)}, bf16[384,768]{1,0:T(8,128)(2,1)S(1)}, bf16[384,768]{1,0:T(8,128)(2,1)S(1)}, bf16[384,768]{1,0:T(8,128)(2,1)S(1)}, f32[2,576,192]{2,1,0:T(8,128)S(1)}) custom-call(s32[102]{0:T(128)S(1)} %pad_add_fusion.table, bf16[384,768]{1,0:T(8,128)(2,1)S(1)} %copy-done, bf16[384,768]{1,0:T(8,128)(2,1)S(1)} %copy-done.1, ...), custom_call_target="tpu_custom_call" | custom-call | flops 169869312 | tf_op jit(solution)/shard_map/stage/pallas_call | solution.py:187
  18.0 0.0 collective-permute-done.1.k_two
  18.0 3.6 %collective-permute-done.k_one = bf16[384,768]{1,0:T(8,128)(2,1)S(1)} collective-permute-done((bf16[384,768]{1,0:T(8,128)(2,1)}, bf16[384,768]{1,0:T(8,128)(2,1)S(1)}, u32[]{:S(2)}, u32[]{:S(2)}) %collective-permute-start) | collective-permute-done | bytes 589856 | tf_op jit(solution)/shard_map/ppermute | solution.py:166
  21.6 7.0 %values_part.1 = (bf16[6,2,576,128]{3,2,1,0:T(8,128)(2,1)S(1)}, bf16[6,2,576,192]{3,2,1,0:T(8,128)(2,1)S(1)}, f32[384,768]{1,0:T(8,128)S(1)}, bf16[384,768]{1,0:T(8,128)(2,1)S(1)}, bf16[384,768]{1,0:T(8,128)(2,1)S(1)}) custom-call(s32[102]{0:T(128)S(1)} %pad_add_fusion.table, bf16[384,768]{1,0:T(8,128)(2,1)S(1)} %get-tuple-element.20.queries, ...), custom_call_target="tpu_custom_call" | custom-call | flops 679477248 | tf_op jit(solution)/shard_map/values_part/pallas_call | solution.py:187
  28.6 2.1 %collective-permute-start.4 = (bf16[384,768]{1,0:T(8,128)(2,1)S(1)}, bf16[384,768]{1,0:T(8,128)(2,1)S(1)}, u32[]{:S(2)}, u32[]{:S(2)}) collective-permute-start(bf16[384,768]{1,0:T(8,128)(2,1)S(1)} %get-tuple-element.30), channel_id=1, source_target_pairs={{0,4},{4,0},{8,12},{12,8},{1,5},{5,1},{9,13},{13,9},{2,6},{6,2},{1... | collective-permute-start | bytes 1769480 | tf_op jit(solution)/shard_map/ppermute | solution.py:166
  30.7 0.9 %collective-permute-start.5 = (bf16[384,768]{1,0:T(8,128)(2,1)S(1)}, bf16[384,768]{1,0:T(8,128)(2,1)S(1)}, u32[]{:S(2)}, u32[]{:S(2)}) collective-permute-start(bf16[384,768]{1,0:T(8,128)(2,1)S(1)} %get-tuple-element.31), channel_id=1, source_target_pairs={{4,8},{8,4},{5,9},{9,5},{6,10},{10,6},{7,11},{11,7},{20,24},{24,20... | collective-permute-start | bytes 1769480 | tf_op jit(solution)/shard_map/ppermute | solution.py:166
  31.6 0.0 collective-permute-done.3.v_two
  31.6 2.6 %collective-permute-done.2.v_one = bf16[384,768]{1,0:T(8,128)(2,1)S(1)} collective-permute-done((bf16[384,768]{1,0:T(8,128)(2,1)}, bf16[384,768]{1,0:T(8,128)(2,1)S(1)}, u32[]{:S(2)}, u32[]{:S(2)}) %collective-permute-start.2) | collective-permute-done | bytes 589856 | tf_op jit(solution)/shard_map/ppermute | solution.py:166
  34.3 6.5 %keys_part.1 = (bf16[6,2,576,192]{3,2,1,0:T(8,128)(2,1)S(1)}, f32[384,768]{1,0:T(8,128)S(1)}, bf16[384,768]{1,0:T(8,128)(2,1)S(1)}, bf16[384,768]{1,0:T(8,128)(2,1)S(1)}) custom-call(s32[102]{0:T(128)S(1)} %pad_add_fusion.table, bf16[384,768]{1,0:T(8,128)(2,1)S(1)} %get-tuple-element.20.queries, bf16[384,768]{1,0:T(8,128)(2,1)S(1)} %get-tuple-element.21.grad_out, ...), custom_call_target="tpu_custom_call" | custom-call | flops 679477248 | tf_op jit(solution)/shard_map/keys_part/pallas_call | solution.py:187
  40.8 2.1 %collective-permute-start.6 = (bf16[384,768]{1,0:T(8,128)(2,1)S(1)}, bf16[384,768]{1,0:T(8,128)(2,1)S(1)}, u32[]{:S(2)}, u32[]{:S(2)}) collective-permute-start(bf16[384,768]{1,0:T(8,128)(2,1)S(1)} %get-tuple-element.34), channel_id=1, source_target_pairs={{0,4},{4,0},{8,12},{12,8},{1,5},{5,1},{9,13},{13,9},{2,6},{6,2},{1... | collective-permute-start | bytes 1769480 | tf_op jit(solution)/shard_map/ppermute | solution.py:166
  42.9 0.7 %collective-permute-start.7 = (bf16[384,768]{1,0:T(8,128)(2,1)S(1)}, bf16[384,768]{1,0:T(8,128)(2,1)S(1)}, u32[]{:S(2)}, u32[]{:S(2)}) collective-permute-start(bf16[384,768]{1,0:T(8,128)(2,1)S(1)} %get-tuple-element.35), channel_id=1, source_target_pairs={{4,8},{8,4},{5,9},{9,5},{6,10},{10,6},{7,11},{11,7},{20,24},{24,20... | collective-permute-start | bytes 1769480 | tf_op jit(solution)/shard_map/ppermute | solution.py:166
  43.6 3.3 %collective-permute-done.4.rv_one = bf16[384,768]{1,0:T(8,128)(2,1)S(1)} collective-permute-done((bf16[384,768]{1,0:T(8,128)(2,1)S(1)}, bf16[384,768]{1,0:T(8,128)(2,1)S(1)}, u32[]{:S(2)}, u32[]{:S(2)}) %collective-permute-start.4) | collective-permute-done | bytes 589856 | tf_op jit(solution)/shard_map/ppermute | solution.py:166
  46.9 0.0 collective-permute-done.5.rv_two
  46.9 1.6 %rest.1 = (bf16[384,768]{1,0:T(8,128)(2,1)S(1)}, bf16[384,768]{1,0:T(8,128)(2,1)S(1)}, f32[384,768]{1,0:T(8,128)S(1)}) custom-call(bf16[384,768]{1,0:T(8,128)(2,1)S(1)} %get-tuple-element.20.queries, bf16[384,768]{1,0:T(8,128)(2,1)S(1)} %get-tuple-element.21.grad_out, bf16[6,2,576,128]{3,2,1,0:T(8,128)(2,1)S(1)} %get-tuple-element.24.chosen_in, ...), custom_call_target="tpu_custom_call" | custom-call | flops 679477248 | tf_op jit(solution)/shard_map/rest/pallas_call | solution.py:187
  48.5 0.8 %copy.11 = bf16[384,768]{1,0:T(8,128)(2,1)} copy(bf16[384,768]{1,0:T(8,128)(2,1)S(1)} %get-tuple-element.37) | data formatting | bytes 1179648
  49.4 0.8 %copy.12 = bf16[384,768]{1,0:T(8,128)(2,1)} copy(bf16[384,768]{1,0:T(8,128)(2,1)S(1)} %get-tuple-element.39) | data formatting | bytes 1179648
  50.2 8.2 %collective-permute-done.6 = bf16[384,768]{1,0:T(8,128)(2,1)S(1)} collective-permute-done((bf16[384,768]{1,0:T(8,128)(2,1)S(1)}, bf16[384,768]{1,0:T(8,128)(2,1)S(1)}, u32[]{:S(2)}, u32[]{:S(2)}) %collective-permute-start.6) | collective-permute-done | bytes 589856 | tf_op jit(solution)/shard_map/ppermute | solution.py:166
  58.4 0.0 collective-permute-done.7
  58.4 1.0 %add_convert_fusion = bf16[384,768]{1,0:T(8,128)(2,1)} fusion(bf16[384,768]{1,0:T(8,128)(2,1)S(1)} %collective-permute-done.7, f32[384,768]{1,0:T(8,128)S(1)} %get-tuple-element.33, bf16[384,768]{1,0:T(8,128)(2,1)S(1)} %collective-permute-done.6), kind=kLoop, calls=%fused_computation | loop fusion | flops 1474560 | bytes 2949120 | tf_op jit(solution)/shard_map/convert_element_type | solution.py:237
Async XLA Ops:
  0.6 17.3 %collective-permute-start.1 = (bf16[384,768]{1,0:T(8,128)(2,1)}, bf16[384,768]{1,0:T(8,128)(2,1)S(1)}, u32[]{:S(2)}, u32[]{:S(2)}) collective-permute-start(bf16[384,768]{1,0:T(8,128)(2,1)} %refs_2_.1), channel_id=1, source_target_pairs={{4,8},{8,4},{5,9},{9,5},{6,10},{10,6},{7,11},{11,7},{20,24},{24,20... | collective-permute-start | bytes 1769480 | tf_op jit(solution)/shard_map/ppermute | solution.py:166
  1.3 20.3 %collective-permute-start = (bf16[384,768]{1,0:T(8,128)(2,1)}, bf16[384,768]{1,0:T(8,128)(2,1)S(1)}, u32[]{:S(2)}, u32[]{:S(2)}) collective-permute-start(bf16[384,768]{1,0:T(8,128)(2,1)} %refs_2_.1), channel_id=1, source_target_pairs={{0,4},{4,0},{8,12},{12,8},{1,5},{5,1},{9,13},{13,9},{2,6},{6,2},{1... | collective-permute-start | bytes 1769480 | tf_op jit(solution)/shard_map/ppermute | solution.py:166
  7.2 24.4 %collective-permute-start.3 = (bf16[384,768]{1,0:T(8,128)(2,1)}, bf16[384,768]{1,0:T(8,128)(2,1)S(1)}, u32[]{:S(2)}, u32[]{:S(2)}) collective-permute-start(bf16[384,768]{1,0:T(8,128)(2,1)} %refs_3_.1), channel_id=1, source_target_pairs={{4,8},{8,4},{5,9},{9,5},{6,10},{10,6},{7,11},{11,7},{20,24},{24,20... | collective-permute-start | bytes 1769480 | tf_op jit(solution)/shard_map/ppermute | solution.py:166
  7.9 26.4 %collective-permute-start.2 = (bf16[384,768]{1,0:T(8,128)(2,1)}, bf16[384,768]{1,0:T(8,128)(2,1)S(1)}, u32[]{:S(2)}, u32[]{:S(2)}) collective-permute-start(bf16[384,768]{1,0:T(8,128)(2,1)} %refs_3_.1), channel_id=1, source_target_pairs={{0,4},{4,0},{8,12},{12,8},{1,5},{5,1},{9,13},{13,9},{2,6},{6,2},{1... | collective-permute-start | bytes 1769480 | tf_op jit(solution)/shard_map/ppermute | solution.py:166
  12.5 1.1 %copy-start = (bf16[384,768]{1,0:T(8,128)(2,1)S(1)}, bf16[384,768]{1,0:T(8,128)(2,1)}, u32[]{:S(2)}) copy-start(bf16[384,768]{1,0:T(8,128)(2,1)} %refs_0_.1) | copy-start | bytes 1769476
  13.6 1.1 %copy-start.1 = (bf16[384,768]{1,0:T(8,128)(2,1)S(1)}, bf16[384,768]{1,0:T(8,128)(2,1)}, u32[]{:S(2)}) copy-start(bf16[384,768]{1,0:T(8,128)(2,1)} %refs_1_.1) | copy-start | bytes 1769476
  14.7 1.1 %copy-start.2 = (bf16[384,768]{1,0:T(8,128)(2,1)S(1)}, bf16[384,768]{1,0:T(8,128)(2,1)}, u32[]{:S(2)}) copy-start(bf16[384,768]{1,0:T(8,128)(2,1)} %refs_2_.1) | copy-start | bytes 1769476
  15.7 1.1 %copy-start.3 = (bf16[384,768]{1,0:T(8,128)(2,1)S(1)}, bf16[384,768]{1,0:T(8,128)(2,1)}, u32[]{:S(2)}) copy-start(bf16[384,768]{1,0:T(8,128)(2,1)} %refs_3_.1) | copy-start | bytes 1769476
  28.6 18.3 %collective-permute-start.4 = (bf16[384,768]{1,0:T(8,128)(2,1)S(1)}, bf16[384,768]{1,0:T(8,128)(2,1)S(1)}, u32[]{:S(2)}, u32[]{:S(2)}) collective-permute-start(bf16[384,768]{1,0:T(8,128)(2,1)S(1)} %get-tuple-element.30), channel_id=1, source_target_pairs={{0,4},{4,0},{8,12},{12,8},{1,5},{5,1},{9,13},{13,9},{2,6},{6,2},{1... | collective-permute-start | bytes 1769480 | tf_op jit(solution)/shard_map/ppermute | solution.py:166
  30.7 16.2 %collective-permute-start.5 = (bf16[384,768]{1,0:T(8,128)(2,1)S(1)}, bf16[384,768]{1,0:T(8,128)(2,1)S(1)}, u32[]{:S(2)}, u32[]{:S(2)}) collective-permute-start(bf16[384,768]{1,0:T(8,128)(2,1)S(1)} %get-tuple-element.31), channel_id=1, source_target_pairs={{4,8},{8,4},{5,9},{9,5},{6,10},{10,6},{7,11},{11,7},{20,24},{24,20... | collective-permute-start | bytes 1769480 | tf_op jit(solution)/shard_map/ppermute | solution.py:166
  40.8 17.6 %collective-permute-start.6 = (bf16[384,768]{1,0:T(8,128)(2,1)S(1)}, bf16[384,768]{1,0:T(8,128)(2,1)S(1)}, u32[]{:S(2)}, u32[]{:S(2)}) collective-permute-start(bf16[384,768]{1,0:T(8,128)(2,1)S(1)} %get-tuple-element.34), channel_id=1, source_target_pairs={{0,4},{4,0},{8,12},{12,8},{1,5},{5,1},{9,13},{13,9},{2,6},{6,2},{1... | collective-permute-start | bytes 1769480 | tf_op jit(solution)/shard_map/ppermute | solution.py:166
  42.9 15.5 %collective-permute-start.7 = (bf16[384,768]{1,0:T(8,128)(2,1)S(1)}, bf16[384,768]{1,0:T(8,128)(2,1)S(1)}, u32[]{:S(2)}, u32[]{:S(2)}) collective-permute-start(bf16[384,768]{1,0:T(8,128)(2,1)S(1)} %get-tuple-element.35), channel_id=1, source_target_pairs={{4,8},{8,4},{5,9},{9,5},{6,10},{10,6},{7,11},{11,7},{20,24},{24,20... | collective-permute-start | bytes 1769480 | tf_op jit(solution)/shard_map/ppermute | solution.py:166

commit v4 on v3

v4 whole, which is shorter than its diff:
```python
import math

import jax
import jax.numpy as jnp
from jax import lax
from jax.experimental import pallas as pl
from jax.experimental.pallas import tpu as pltpu
from jax.sharding import PartitionSpec as P

HD = 128
TOK_FRAME = 192
FR_DEV = 2
REACH = 2
NSEL = 3
SB = 4
DEPTH = 3
MOVED = 2
SPLIT = MOVED * HD
ROWS = FR_DEV * TOK_FRAME
WINDOW = FR_DEV + 2 * REACH
SLOTS = NSEL * TOK_FRAME
BLOCK = TOK_FRAME // SB
SCALE = HD ** (-0.5)
SCALE2 = SCALE * math.log2(math.e)
NEG = -1e30
NT = (((1,), (1,)), ((), ()))
NN = (((1,), (0,)), ((), ()))
TN = (((0,), (0,)), ((), ()))
MASKS = WINDOW * NSEL
FIRST = MASKS + WINDOW * NSEL * SB * SB
RANK = FIRST + 1
COUNT = FIRST + 2


def dot(lhs, rhs, dims):
    return lax.dot_general(lhs, rhs, dims, preferred_element_type=jnp.float32)


def column_of(head):
    return slice(head * HD, (head + 1) * HD)


def rows_of(frame):
    return slice(frame * TOK_FRAME, (frame + 1) * TOK_FRAME)


def side_of(table, side):
    return jnp.where(table[RANK] % 2 == 1, side, 2 - side)


def inside(table, place):
    target = table[FIRST] + place
    return (target >= 0) & (target < table[COUNT])


def spot_of(table, frame, slot):
    place = frame + table[(REACH + frame) * NSEL + slot]
    side = (place >= 0).astype(jnp.int32) + (place >= FR_DEV).astype(jnp.int32)
    return side_of(table, side) * FR_DEV + (place + FR_DEV) % FR_DEV


def span(table, frame, slot):
    spot = spot_of(table, frame, slot)
    return pl.ds(pl.multiple_of(spot * TOK_FRAME, TOK_FRAME), TOK_FRAME)


def pair_of(table, query, key):
    index = side_of(table, query // FR_DEV) * FR_DEV + query % FR_DEV
    place = index - REACH
    active = jnp.zeros((), jnp.int32)
    slot = jnp.zeros((), jnp.int32)
    for each in range(NSEL):
        hit = (table[index * NSEL + each] + place == key).astype(jnp.int32)
        active += hit
        slot += hit * each
    active = (active > 0) & inside(table, place)
    return active, MASKS + (index * NSEL + slot) * SB * SB


def write_bias(table, start, seen, bias, row):
    q_block = lax.broadcasted_iota(jnp.int32, (8, TOK_FRAME), 1) // BLOCK
    for k_block in range(SB):
        value = jnp.zeros((8, TOK_FRAME), jnp.float32)
        for block in range(SB):
            keep = (table[start + block * SB + k_block] > 0) & seen
            value = jnp.where(q_block == block, jnp.where(keep, 0.0, NEG), value)
        for step in range(0, BLOCK, 8):
            bias[pl.ds(row + k_block * BLOCK + step, 8), :] = value


def copy_all(pairs, sems):
    moves = [pltpu.make_async_copy(a, b, sems.at[i]) for i, (a, b) in enumerate(pairs)]
    for move in moves:
        move.start()
    return moves


def pack_kernel(queries, grad_out, keys, values, both, k_send, v_send, sems):
    moves = copy_all(
        [
            (queries.at[:, :SPLIT], both.at[0]),
            (grad_out.at[:, :SPLIT], both.at[1]),
            (keys.at[:, SPLIT:], k_send),
            (values.at[:, SPLIT:], v_send),
        ],
        sems,
    )
    for move in moves:
        move.wait()


def stage_kernel(table, *refs):
    arrays, copies, bias, moved_bias, sems = refs[:4], refs[4:8], refs[8], refs[9], refs[10]
    moves = copy_all(list(zip(arrays, copies)), sems)
    for frame in range(FR_DEV):
        for slot in range(NSEL):
            at = (REACH + frame) * NSEL + slot
            seen = inside(table, frame + table[at])
            write_bias(table, MASKS + at * SB * SB, seen, bias.at[frame], slot * TOK_FRAME)
    for query in range(WINDOW):
        for key in range(FR_DEV):
            active, start = pair_of(table, query, key)

            @pl.when(active)
            def _():
                write_bias(table, start, active, moved_bias.at[query, key], 0)

    for move in moves:
        move.wait()


def fill_window(window, one, own, two, column, far_column):
    window[0:ROWS] = one[:, far_column]
    window[ROWS : 2 * ROWS] = own[:, column]
    window[2 * ROWS : 3 * ROWS] = two[:, far_column]


def pick(table, frame, window, chosen):
    for slot in range(NSEL):
        chosen[rows_of(slot)] = window[span(table, frame, slot), :]


def spread(table, frame, accum, parts):
    for slot in range(1, NSEL):
        accum[span(table, frame, slot), :] += parts[rows_of(slot - 1)]


def values_kernel(
    table, queries, grad_out, k_own, bias, k_one, k_two,
    chosen_out, prob_out, own_out, one_out, two_out,
    windows, accums,
):
    for head in range(one_out.shape[1] // HD):
        column = column_of(MOVED + head)
        far_column = column_of(head)
        window = windows.at[head % DEPTH]
        accum = accums.at[head % DEPTH]
        fill_window(window, k_one, k_own, k_two, column, far_column)
        accum[...] = jnp.zeros_like(accum)
        for frame in range(FR_DEV):
            chosen = chosen_out.at[head, frame]
            pick(table, frame, window, chosen)
            scores = dot(chosen[...], queries[rows_of(frame), column], NT)
            masked = scores * SCALE2 + bias[frame]
            raised = jnp.exp2(masked - jnp.max(masked, 0, keepdims=True))
            inverse = 1.0 / jnp.sum(raised, 0, keepdims=True)
            prob_low = (raised * inverse).astype(jnp.bfloat16)
            prob_out[head, frame] = prob_low
            far = dot(prob_low[TOK_FRAME:], grad_out[rows_of(frame), column], NN)
            spread(table, frame, accum, far)
        one_out[:, far_column] = accum[0:ROWS].astype(one_out.dtype)
        own_out[:, far_column] = accum[ROWS : 2 * ROWS]
        two_out[:, far_column] = accum[2 * ROWS : 3 * ROWS].astype(two_out.dtype)


def keys_kernel(
    table, queries, grad_out, v_own, prob_in, v_one, v_two,
    score_out, own_out, one_out, two_out,
    windows, choices, accums,
):
    for head in range(one_out.shape[1] // HD):
        column = column_of(MOVED + head)
        far_column = column_of(head)
        window = windows.at[head % DEPTH]
        accum = accums.at[head % DEPTH]
        fill_window(window, v_one, v_own, v_two, column, far_column)
        accum[...] = jnp.zeros_like(accum)
        for frame in range(FR_DEV):
            chosen = choices.at[head % DEPTH, frame]
            pick(table, frame, window, chosen)
            grad_prob = dot(chosen[...], grad_out[rows_of(frame), column], NT)
            prob = prob_in[head, frame].astype(jnp.float32)
            delta = jnp.sum(prob * grad_prob, 0, keepdims=True)
            score_low = (prob * (grad_prob - delta)).astype(jnp.bfloat16)
            score_out[head, frame] = score_low
            far = dot(score_low[TOK_FRAME:], queries[rows_of(frame), column], NN)
            spread(table, frame, accum, far)
        one_out[:, far_column] = (accum[0:ROWS] * SCALE).astype(one_out.dtype)
        own_out[:, far_column] = accum[ROWS : 2 * ROWS]
        two_out[:, far_column] = (accum[2 * ROWS : 3 * ROWS] * SCALE).astype(two_out.dtype)


def rest_kernel(
    queries, grad_out, chosen_in, prob_in, score_in, gv_own, gk_own, rv_one, rv_two,
    query_out, value_out, key_out,
):
    for head in range(query_out.shape[1] // HD):
        column = column_of(MOVED + head)
        far_column = column_of(head)
        for frame in range(FR_DEV):
            rows = rows_of(frame)
            score_low = score_in[head, frame]
            grad_query = dot(score_low, chosen_in[head, frame], TN)
            query_out[rows, far_column] = (grad_query * SCALE).astype(query_out.dtype)
            near = dot(score_low[:TOK_FRAME], queries[rows, column], NN)
            key_out[rows, far_column] = (gk_own[rows, far_column] + near) * SCALE
            near = dot(prob_in[head, frame, :TOK_FRAME], grad_out[rows, column], NN)
            total = gv_own[rows, far_column] + near
            total += rv_one[rows, far_column].astype(jnp.float32)
            total += rv_two[rows, far_column].astype(jnp.float32)
            value_out[rows, far_column] = total.astype(value_out.dtype)


def view_of(query, own, one, two, part, head):
    rows = rows_of(query % FR_DEV)
    column = column_of(head)
    if query // FR_DEV == 1:
        return own[rows, column]
    return (one if query < FR_DEV else two)[part, rows, column]


def stats_kernel(
    table, queries, grad_out, keys, values, bias, f_one, f_two,
    masked_out, grad_prob_out, mine_out, one_out, two_out, far_out, other_out,
    parts,
):
    for query in range(WINDOW):
        for key in range(FR_DEV):
            active, _ = pair_of(table, query, key)

            @pl.when(active)
            def _():
                for head in range(MOVED):
                    column = column_of(head)
                    row = slice(query * MOVED + head, query * MOVED + head + 1)
                    rows = rows_of(key)
                    scores = dot(
                        keys[rows, column], view_of(query, queries, f_one, f_two, 0, head), NT
                    )
                    masked = scores * SCALE2 + bias[query, key]
                    highest = jnp.max(masked, 0, keepdims=True)
                    raised = jnp.exp2(masked - highest)
                    grad_prob = dot(
                        values[rows, column], view_of(query, grad_out, f_one, f_two, 1, head), NT
                    )
                    masked_out[query, key, head] = masked
                    grad_prob_out[query, key, head] = grad_prob
                    parts[key, 0, row] = highest
                    parts[key, 1, row] = jnp.sum(raised, 0, keepdims=True)
                    parts[key, 2, row] = jnp.sum(raised * grad_prob, 0, keepdims=True)

            @pl.when(jnp.logical_not(active))
            def _():
                rows = slice(query * MOVED, (query + 1) * MOVED)
                parts[key, 0, rows] = jnp.full((MOVED, TOK_FRAME), NEG, jnp.float32)
                parts[key, 1, rows] = jnp.zeros((MOVED, TOK_FRAME), jnp.float32)
                parts[key, 2, rows] = jnp.zeros((MOVED, TOK_FRAME), jnp.float32)

    highest, total, moment = joined_stats([parts[key] for key in range(FR_DEV)])
    mine_out[0] = highest
    mine_out[1] = total
    mine_out[2] = moment
    side = FR_DEV * MOVED
    rank = table[RANK] % 4
    swapped = (rank == 1) | (rank == 2)
    for index in range(3):
        whole = mine_out[index]
        one_out[index] = whole[0 : 2 * side]
        two_out[index] = whole[side : 3 * side]
        far_out[index] = jnp.where(swapped, whole[2 * side :], whole[:side])
        other_out[index] = jnp.where(swapped, whole[:side], whole[2 * side :])


def joined_stats(sources):
    tops = [jnp.where(each[1] > 0, each[0], NEG) for each in sources]
    highest = tops[0]
    for top in tops[1:]:
        highest = jnp.maximum(highest, top)
    weights = [jnp.exp2(top - highest) for top in tops]
    total = sum(weight * each[1] for weight, each in zip(weights, sources))
    moment = sum(weight * each[2] for weight, each in zip(weights, sources))
    return highest, total, moment


def finish_pair(query, key, head, masked, grad_probs, logs, deltas):
    row = slice(query * MOVED + head, query * MOVED + head + 1)
    prob = jnp.exp2(masked[query, key, head] - logs[row])
    score_low = (prob * (grad_probs[query, key, head] - deltas[row])).astype(jnp.bfloat16)
    return prob.astype(jnp.bfloat16), score_low


def back_kernel(
    table, keys, masked, grad_probs, mine, s_one, s_two, s_far, s_other,
    prob_out, score_out, logs, deltas, one_out, two_out,
    accums,
):
    side = FR_DEV * MOVED
    rank = table[RANK] % 4
    swapped = (rank == 1) | (rank == 2)
    far = [jnp.where(swapped, s_other[i], s_far[i]) for i in range(3)]
    other = [jnp.where(swapped, s_far[i], s_other[i]) for i in range(3)]

    def part(ref, start):
        return [ref[i, start : start + side] for i in range(3)]

    groups = (
        (part(mine, 0), part(s_one, side), far),
        (part(mine, side), part(s_one, 0), part(s_two, side)),
        (part(mine, 2 * side), part(s_two, 0), other),
    )
    for index, sources in enumerate(groups):
        highest, total, moment = joined_stats(sources)
        rows = slice(index * side, (index + 1) * side)
        total = jnp.where(total > 0, total, 1.0)
        logs[rows] = highest + jnp.log2(total)
        deltas[rows] = moment / total
    accums[...] = jnp.zeros_like(accums)
    for query in (0, 1, 4, 5):
        for key in range(FR_DEV):
            active, _ = pair_of(table, query, key)

            @pl.when(active)
            def _():
                for head in range(MOVED):
                    prob_low, score_low = finish_pair(
                        query, key, head, masked, grad_probs, logs, deltas
                    )
                    prob_out[query, key, head] = prob_low
                    score_out[query, key, head] = score_low
                    accums[query // 4, rows_of(query % FR_DEV), column_of(head)] += dot(
                        score_low, keys[rows_of(key), column_of(head)], TN
                    )

    one_out[...] = (accums[0] * SCALE).astype(one_out.dtype)
    two_out[...] = (accums[1] * SCALE).astype(two_out.dtype)


def home_kernel(
    table, queries, grad_out, keys, f_one, f_two, masked, grad_probs, prob_in, score_in,
    logs, deltas,
    query_out, key_out, value_out,
    key_accum, value_accum,
):
    query_out[...] = jnp.zeros_like(query_out)
    key_accum[...] = jnp.zeros_like(key_accum)
    value_accum[...] = jnp.zeros_like(value_accum)
    for query in range(WINDOW):
        for key in range(FR_DEV):
            active, _ = pair_of(table, query, key)

            @pl.when(active)
            def _():
                for head in range(MOVED):
                    column = column_of(head)
                    rows = rows_of(key)
                    if query // FR_DEV == 1:
                        prob_low, score_low = finish_pair(
                            query, key, head, masked, grad_probs, logs, deltas
                        )
                        query_out[rows_of(query % FR_DEV), column] += dot(
                            score_low, keys[rows, column], TN
                        )
                    else:
                        prob_low = prob_in[query, key, head]
                        score_low = score_in[query, key, head]
                    key_accum[rows, column] += dot(
                        score_low, view_of(query, queries, f_one, f_two, 0, head), NN
                    )
                    value_accum[rows, column] += dot(
                        prob_low, view_of(query, grad_out, f_one, f_two, 1, head), NN
                    )

    query_out[...] = query_out[...] * SCALE
    key_out[...] = (key_accum[...] * SCALE).astype(key_out.dtype)
    value_out[...] = value_accum[...].astype(value_out.dtype)


def both_ways(pairs):
    return [pair for i, j in pairs for pair in ((i, j), (j, i))]


def swap(one, two):
    count = lax.axis_size("frames")
    first = [(i, i + 1) for i in range(0, count - 1, 2)]
    second = [(i, i + 1) for i in range(1, count - 1, 2)]
    return (
        lax.ppermute(one, "frames", both_ways(first)),
        lax.ppermute(two, "frames", both_ways(second)),
    )


def swap_far(far, other):
    count = lax.axis_size("frames")
    near = [(i, i + 2) for i in range(count - 2) if i % 4 < 2]
    over = [(i, i + 2) for i in range(count - 2) if i % 4 >= 2]
    far = lax.ppermute(far, "frames", both_ways(near))
    other = lax.ppermute(other, "frames", both_ways(over)) if over else jnp.zeros_like(other)
    return far, other


def lookup(offsets, spatial):
    rank = lax.axis_index("frames")
    first = rank * FR_DEV
    frames = offsets.shape[0]
    around = ((REACH, REACH), (0, 0))
    shifts = lax.dynamic_slice_in_dim(jnp.pad(offsets, around), first, WINDOW, 0)
    blocks = lax.dynamic_slice_in_dim(
        jnp.pad(spatial, around + ((0, 0), (0, 0))), first, WINDOW, 0
    )
    ends = jnp.stack([first, rank, jnp.full_like(rank, frames)]).astype(jnp.int32)
    return jnp.concatenate([shifts.reshape(-1), blocks.reshape(-1), ends])


def call(kernel, name, scalars, arrays, outs, scratch, flops, space=pltpu.VMEM):
    arrays = [pltpu.with_memory_space_constraint(array, space) for array in arrays]
    return pl.pallas_call(
        kernel,
        out_shape=outs,
        in_specs=[pl.BlockSpec(memory_space=pltpu.SMEM)] * len(scalars)
        + [pl.BlockSpec(memory_space=space)] * len(arrays),
        out_specs=tuple(pl.BlockSpec(memory_space=pltpu.VMEM) for _ in outs),
        scratch_shapes=scratch,
        compiler_params=pltpu.CompilerParams(vmem_limit_bytes=16 << 20),
        cost_estimate=pl.CostEstimate(flops=flops, bytes_accessed=0, transcendentals=0),
        name=name,
    )(*scalars, *arrays)


def local(queries, keys, values, grad_out, offsets, spatial):
    width = queries.shape[1]
    heads = width // HD - MOVED

    def low(*shape):
        return pltpu.VMEM(shape, jnp.bfloat16)

    def full(*shape):
        return pltpu.VMEM(shape, jnp.float32)

    unit = 2 * FR_DEV * NSEL * TOK_FRAME * TOK_FRAME * HD
    rest = width - SPLIT
    y_send, k_send, v_send = call(
        pack_kernel, "pack", (), (queries, grad_out, keys, values),
        (low(2, ROWS, SPLIT), low(ROWS, rest), low(ROWS, rest)),
        [pltpu.SemaphoreType.DMA((4,))], unit, pltpu.HBM,
    )
    f_one, f_two = swap(y_send, y_send)
    k_one, k_two = swap(k_send, k_send)
    v_one, v_two = swap(v_send, v_send)
    table = lookup(offsets, spatial)
    query, grad, key, value, bias, moved_bias = call(
        stage_kernel, "stage", (table,), (queries, grad_out, keys, values),
        (low(ROWS, width),) * 4
        + (full(FR_DEV, SLOTS, TOK_FRAME), full(WINDOW, FR_DEV, TOK_FRAME, TOK_FRAME)),
        [pltpu.SemaphoreType.DMA((4,))], unit, pltpu.HBM,
    )
    grid = (WINDOW, FR_DEV, MOVED, TOK_FRAME, TOK_FRAME)
    side = FR_DEV * MOVED
    masked, grad_probs, mine, s_one, s_two, s_far, s_other = call(
        stats_kernel, "stats", (table,), (query, grad, key, value, moved_bias, f_one, f_two),
        (full(*grid), full(*grid), full(3, 3 * side, TOK_FRAME))
        + (full(3, 2 * side, TOK_FRAME),) * 2 + (full(3, side, TOK_FRAME),) * 2,
        [full(FR_DEV, 3, 3 * side, TOK_FRAME)], 2 * MOVED * unit,
    )
    s_one, s_two = swap(s_one, s_two)
    s_far, s_other = swap_far(s_far, s_other)
    k_one, k_two, mine = lax.optimization_barrier((k_one, k_two, mine))
    windows = low(DEPTH, 3 * ROWS, HD)
    accums = full(DEPTH, 3 * ROWS, HD)
    pairs = low(heads, FR_DEV, SLOTS, TOK_FRAME)
    chosen, prob_low, gv_own, gv_one, gv_two = call(
        values_kernel, "values_part", (table,), (query, grad, key, bias, k_one, k_two),
        (low(heads, FR_DEV, SLOTS, HD), pairs, full(ROWS, rest), low(ROWS, rest), low(ROWS, rest)),
        [windows, accums], 2 * heads * unit,
    )
    rv_one, rv_two = swap(gv_one, gv_two)
    score_low, gk_own, gk_one, gk_two = call(
        keys_kernel, "keys_part", (table,), (query, grad, value, prob_low, v_one, v_two),
        (pairs, full(ROWS, rest), low(ROWS, rest), low(ROWS, rest)),
        [windows, low(DEPTH, FR_DEV, SLOTS, HD), accums], 2 * heads * unit,
    )
    rk_one, rk_two = swap(gk_one, gk_two)
    gk_own, masked = lax.optimization_barrier((gk_own, masked))
    y_prob, y_score, logs, deltas, gq_one, gq_two = call(
        back_kernel, "back", (table,),
        (key, masked, grad_probs, mine, s_one, s_two, s_far, s_other),
        (low(*grid), low(*grid), full(3 * side, TOK_FRAME), full(3 * side, TOK_FRAME))
        + (low(ROWS, SPLIT),) * 2,
        [full(2, ROWS, SPLIT)], MOVED * unit,
    )
    rq_one, rq_two = swap(gq_one, gq_two)
    gq_near, gk_near, gv_near = call(
        home_kernel, "home", (table,),
        (query, grad, key, f_one, f_two, masked, grad_probs, y_prob, y_score, logs, deltas),
        (full(ROWS, SPLIT), low(ROWS, SPLIT), low(ROWS, SPLIT)),
        [full(ROWS, SPLIT), full(ROWS, SPLIT)], 3 * MOVED * unit,
    )
    gq_rest, gv_rest, gk_own = call(
        rest_kernel, "rest", (),
        (query, grad, chosen, prob_low, score_low, gv_own, gk_own, rv_one, rv_two),
        (low(ROWS, rest), low(ROWS, rest), full(ROWS, rest)), [], 2 * heads * unit,
    )

    def joined(own, one, two):
        total = own + one.astype(jnp.float32) + two.astype(jnp.float32)
        return total.astype(jnp.bfloat16)

    grad_queries = jnp.concatenate([joined(gq_near, rq_one, rq_two), gq_rest], 1)
    grad_keys = jnp.concatenate([gk_near, joined(gk_own, rk_one, rk_two)], 1)
    grad_values = jnp.concatenate([gv_near, gv_rest], 1)
    return grad_queries, grad_keys, grad_values


def solution(mesh):
    rows = P(("clips", "frames"), "heads")
    return jax.shard_map(
        local,
        mesh=mesh,
        in_specs=(rows, rows, rows, rows, P("clips", None), P("clips", None, None, None)),
        out_specs=(rows, rows, rows),
        check_vma=False,
    )
```

time: 59.9 us -> 69.9 us (1.17)
  starting transfers between devices: 14.8 us -> 33.1 us
  waiting for transfers between devices: 17.8 us -> 8.26 us
  Pallas kernels: 16.3 us -> 20.6 us
  local copies, waits for them, and re-layouts: 6.33 us -> 4.16 us
    ppermute x8 -> x15, starting transfers between devices: 14.8 us -> 33.1 us  [the longest x7 25.4 us: swap(): lax.ppermute(one, 'frames', both_ways(first))]
    ppermute x8 -> x15, waiting for transfers between devices: 17.8 us -> 8.26 us  [the longest x7 8.24 us: swap(): lax.ppermute(one, 'frames', both_ways(first))]
    unnamed x10 -> x2, local copies, waits for them, and re-layouts: 5.89 us -> 0.01 us
    pallas_call x4 -> x8, Pallas kernels: 16.3 us -> 20.6 us  [call(): pl.pallas_call(kernel, out_shape=outs, in_specs=[pl.BlockSpec(memory_spac...]
    dynamic_slice x0 -> x4, local copies, waits for them, and re-layouts: none -> 3.11 us  [the longest x2 2.93 us: lookup(): lax.dynamic_slice_in_dim(jnp.pad(spatial, around + ((0, 0), (0, 0))), fir...]
    concatenate x1 -> x3, other arithmetic: 0.08 us -> 2.56 us  [the longest x1 0.85 us: local(): grad_keys = jnp.concatenate([gk_near, joined(gk_own, rk_one, rk_two)], 1)]
    convert_element_type x2, other arithmetic: 1.79 us -> 0.25 us  [joined(): return total.astype(jnp.bfloat16)]
    mul x1 -> x0, other arithmetic: 0.81 us -> none  [lookup(): blocks = blocks * inside[:, :, None, None]]
  transfers between devices with their start and end apart: 8 -> 15, of which waited for: 4 -> 3; matrix products, arithmetic and copies ran while one was open for 8% -> 7% of each run, Pallas kernels for 28% -> 26%
where the time goes in v4:
time: 69.9 us; the launch traced here: 69.8 us
  starting transfers between devices  33.1 us (47%)
  Pallas kernels  20.6 us (29%)
  waiting for transfers between devices  8.26 us (12%)
  local copies, waits for them, and re-layouts  4.16 us (6%)
  other arithmetic  2.81 us (4%)
  between operations  0.85 us (1%)
    ppermute x7, starting transfers between devices, swap(): lax.ppermute(one, 'frames', both_ways(first))  25.4 us
    pallas_call x8, Pallas kernels, call(): pl.pallas_call(kernel, out_shape=outs, in_specs=[pl.BlockSpec(memory_spac...  20.6 us
    ppermute x7, waiting for transfers between devices, swap(): lax.ppermute(one, 'frames', both_ways(first))  8.24 us
    ppermute x7, starting transfers between devices, swap(): lax.ppermute(two, 'frames', both_ways(second))  4.89 us
    dynamic_slice x2, local copies, waits for them, and re-layouts, lookup(): lax.dynamic_slice_in_dim(jnp.pad(spatial, around + ((0, 0), (0, 0))), fir...  2.93 us
    ppermute x1, starting transfers between devices, swap_far(): far = lax.ppermute(far, 'frames', both_ways(near))  2.79 us
  transfers between devices with their start and end apart: 15, of which 3 were waited for; matrix products, arithmetic and copies ran while one was open for 7% of the time, Pallas kernels for 26%

profile of v4, /device:TPU:0, one launch (start us, length us, event | category | flops | bytes accessed | tf_op | source)
XLA Modules:
  0.0 69.8 jit_solution(13241303896971504149)
XLA Ops:
  0.6 0.0 copy-start
  0.6 1.4 %pack.1 = (bf16[2,384,256]{2,1,0:T(8,128)(2,1)S(1)}, bf16[384,512]{1,0:T(8,128)(2,1)S(1)}, bf16[384,512]{1,0:T(8,128)(2,1)S(1)}) custom-call(bf16[384,768]{1,0:T(8,128)(2,1)} %queries.1, bf16[384,768]{1,0:T(8,128)(2,1)} %grad_out.1, bf16[384,768]{1,0:T(8,128)(2,1)} %keys.1, bf16[384,768]{1,0:T(8,128)(2,1)} %values.1), custom_call_target="tpu_custom_call" | custom-call | flops 56623104 | tf_op jit(solution)/shard_map/pack/pallas_call | solution.py:426
  2.0 3.1 %collective-permute-start = (bf16[2,384,256]{2,1,0:T(8,128)(2,1)S(1)}, bf16[2,384,256]{2,1,0:T(8,128)(2,1)S(1)}, u32[]{:S(2)}, u32[]{:S(2)}) collective-permute-start(bf16[2,384,256]{2,1,0:T(8,128)(2,1)S(1)} %get-tuple-element.47), channel_id=1, source_target_pairs={{0,4},{4,0},{8,12},{12,8},{1,5},{5,1},{9,13},{13,9},{2,6},{6,2},{1... | collective-permute-start | bytes 1179656 | tf_op jit(solution)/shard_map/ppermute | solution.py:397
  5.1 0.7 collective-permute-start.1
  5.8 4.4 %collective-permute-start.2 = (bf16[384,512]{1,0:T(8,128)(2,1)S(1)}, bf16[384,512]{1,0:T(8,128)(2,1)S(1)}, u32[]{:S(2)}, u32[]{:S(2)}) collective-permute-start(bf16[384,512]{1,0:T(8,128)(2,1)S(1)} %get-tuple-element.50), channel_id=1, source_target_pairs={{0,4},{4,0},{8,12},{12,8},{1,5},{5,1},{9,13},{13,9},{2,6},{6,2},{1... | collective-permute-start | bytes 1179656 | tf_op jit(solution)/shard_map/ppermute | solution.py:397
  10.2 0.7 collective-permute-start.3
  10.9 1.3 %collective-permute-start.4 = (bf16[384,512]{1,0:T(8,128)(2,1)S(1)}, bf16[384,512]{1,0:T(8,128)(2,1)S(1)}, u32[]{:S(2)}, u32[]{:S(2)}) collective-permute-start(bf16[384,512]{1,0:T(8,128)(2,1)S(1)} %get-tuple-element.56), channel_id=1, source_target_pairs={{0,4},{4,0},{8,12},{12,8},{1,5},{5,1},{9,13},{13,9},{2,6},{6,2},{1... | collective-permute-start | bytes 1179656 | tf_op jit(solution)/shard_map/ppermute | solution.py:397
  12.2 2.8 %collective-permute-done.f_one = bf16[2,384,256]{2,1,0:T(8,128)(2,1)S(1)} collective-permute-done((bf16[2,384,256]{2,1,0:T(8,128)(2,1)S(1)}, bf16[2,384,256]{2,1,0:T(8,128)(2,1)S(1)}, u32[]{:S(2)}, u32[]{:S(2)}) %collective-permute-start) | collective-permute-done | bytes 393248 | tf_op jit(solution)/shard_map/ppermute | solution.py:397
  15.0 0.7 collective-permute-start.5
  15.7 0.0 copy-done
  15.7 0.1 pad_dynamic-slice_fusion.1
  15.8 0.1 copy.10
  15.9 0.1 reshape.12
  16.0 1.4 %pad_dynamic-slice_fusion = s32[6,3,4,4]{0,3,2,1:T(4,128)} fusion(s32[]{:T(128)S(6)} %select_n.4, s32[8,3,4,4]{0,3,2,1:T(4,128)} %param.11), kind=kLoop, calls=%fused_computation.5 | loop fusion | bytes 2692 | tf_op jit(solution)/shard_map/dynamic_slice | solution.py:417
  17.4 1.5 %copy.11 = s32[6,3,4,4]{3,2,1,0:T(4,128)} copy(s32[6,3,4,4]{0,3,2,1:T(4,128)} %pad_dynamic-slice_fusion) | data formatting | bytes 2304 | tf_op jit(solution)/shard_map/dynamic_slice | solution.py:417
  18.9 0.9 %reshape.13 = s32[288]{0:T(512)S(1)} reshape(s32[6,3,4,4]{3,2,1,0:T(4,128)} %copy.11) | data formatting | bytes 2304 | tf_op jit(solution)/shard_map/reshape | solution.py:421
  19.8 0.1 concatenate.12.table
  19.9 2.2 %stage.1 = (bf16[384,768]{1,0:T(8,128)(2,1)S(1)}, bf16[384,768]{1,0:T(8,128)(2,1)S(1)}, bf16[384,768]{1,0:T(8,128)(2,1)S(1)}, bf16[384,768]{1,0:T(8,128)(2,1)S(1...) custom-call(s32[309]{0:T(512)S(1)} %concatenate.12.table, bf16[384,768]{1,0:T(8,128)(2,1)} %queries.1, ...), custom_call_target="tpu_custom_call" | custom-call | flops 56623104 | tf_op jit(solution)/shard_map/stage/pallas_call | solution.py:426
  22.1 0.0 collective-permute-done.1.f_two
  22.1 3.0 %stats.1 = (f32[6,2,2,192,192]{4,3,2,1,0:T(8,128)S(1)}, f32[6,2,2,192,192]{4,3,2,1,0:T(8,128)S(1)}, f32[3,12,192]{2,1,0:T(8,128)S(1)}, f32[3,8,192]{2,1,0:T(8,12...) custom-call(s32[309]{0:T(512)S(1)} %concatenate.12.table, ...), custom_call_target="tpu_custom_call" | custom-call | flops 226492416 | tf_op jit(solution)/shard_map/stats/pallas_call | solution.py:426
  25.1 0.0 collective-permute-done.2.k_one
  25.1 0.0 collective-permute-done.3.k_two
  25.1 6.3 %collective-permute-start.6 = (f32[3,8,192]{2,1,0:T(8,128)S(1)}, f32[3,8,192]{2,1,0:T(8,128)S(1)}, u32[]{:S(2)}, u32[]{:S(2)}) collective-permute-start(f32[3,8,192]{2,1,0:T(8,128)S(1)} %get-tuple-element.62), channel_id=1, source_target_pairs={{0,4},{4,0},{8,12},{12,8},{1,5},{5,1},{9,13},{13,9},{2,6},{6,2},{1... | collective-permute-start | bytes 55304 | tf_op jit(solution)/shard_map/ppermute | solution.py:397
  31.4 0.8 %collective-permute-start.7 = (f32[3,8,192]{2,1,0:T(8,128)S(1)}, f32[3,8,192]{2,1,0:T(8,128)S(1)}, u32[]{:S(2)}, u32[]{:S(2)}) collective-permute-start(f32[3,8,192]{2,1,0:T(8,128)S(1)} %get-tuple-element.63), channel_id=1, source_target_pairs={{4,8},{8,4},{5,9},{9,5},{6,10},{10,6},{7,11},{11,7},{20,24},{24,20... | collective-permute-start | bytes 55304 | tf_op jit(solution)/shard_map/ppermute | solution.py:398
  32.2 2.8 %collective-permute-start.8 = (f32[3,4,192]{2,1,0:T(4,128)S(1)}, f32[3,4,192]{2,1,0:T(4,128)S(1)}, u32[]{:S(2)}, u32[]{:S(2)}) collective-permute-start(f32[3,4,192]{2,1,0:T(4,128)S(1)} %get-tuple-element.64), channel_id=1, source_target_pairs={{0,8},{8,0},{4,12},{12,4},{1,9},{9,1},{5,13},{13,5},{2,10},{10,2},... | collective-permute-start | bytes 27656 | tf_op jit(solution)/shard_map/ppermute | solution.py:406
  35.0 4.9 %values_part.1 = (bf16[4,2,576,128]{3,2,1,0:T(8,128)(2,1)S(1)}, bf16[4,2,576,192]{3,2,1,0:T(8,128)(2,1)S(1)}, f32[384,512]{1,0:T(8,128)S(1)}, bf16[384,512]{1,0:T(8,128)(2,1)S(1)}, bf16[384,512]{1,0:T(8,128)(2,1)S(1)}) custom-call(s32[309]{0:T(512)S(1)} %concatenate.12.table, bf16[384,768]{1,0:T(8,128)(2,1)S(1)} %get-tuple-element.44.queries, ...), custom_call_target="tpu_custom_call" | custom-call | flops 452984832 | tf_op jit(solution)/shard_map/values_part/pallas_call | solution.py:426
  40.0 0.0 collective-permute-done.4.v_one
  40.0 0.0 collective-permute-done.5.v_two
  40.0 4.7 %keys_part.1 = (bf16[4,2,576,192]{3,2,1,0:T(8,128)(2,1)S(1)}, f32[384,512]{1,0:T(8,128)S(1)}, bf16[384,512]{1,0:T(8,128)(2,1)S(1)}, bf16[384,512]{1,0:T(8,128)(2,1)S(1)}) custom-call(s32[309]{0:T(512)S(1)} %concatenate.12.table, bf16[384,768]{1,0:T(8,128)(2,1)S(1)} %get-tuple-element.44.queries, bf16[384,768]{1,0:T(8,128)(2,1)S(1)} %get-tuple-element.45.grad_out, ...), custom_call_target="tpu_custom_call" | custom-call | flops 452984832 | tf_op jit(solution)/shard_map/keys_part/pallas_call | solution.py:426
  44.7 0.0 collective-permute-done.8.s_far
  44.7 0.0 collective-permute-done.6.s_one
  44.7 0.0 collective-permute-done.7.s_two
  44.7 1.1 %back.1 = (bf16[6,2,2,192,192]{4,3,2,1,0:T(8,128)(2,1)S(1)}, bf16[6,2,2,192,192]{4,3,2,1,0:T(8,128)(2,1)S(1)}, f32[12,192]{1,0:T(8,128)S(1)}, f32[12,192]{1,0:T(...) custom-call(s32[309]{0:T(512)S(1)} %concatenate.12.table, ...), custom_call_target="tpu_custom_call" | custom-call | flops 113246208 | tf_op jit(solution)/shard_map/back/pallas_call | solution.py:426
  45.9 0.7 collective-permute-start.10
  46.5 2.6 %collective-permute-start.9 = (bf16[384,256]{1,0:T(8,128)(2,1)S(1)}, bf16[384,256]{1,0:T(8,128)(2,1)S(1)}, u32[]{:S(2)}, u32[]{:S(2)}) collective-permute-start(bf16[384,256]{1,0:T(8,128)(2,1)S(1)} %get-tuple-element.70), channel_id=1, source_target_pairs={{0,4},{4,0},{8,12},{12,8},{1,5},{5,1},{9,13},{13,9},{2,6},{6,2},{1... | collective-permute-start | bytes 589832 | tf_op jit(solution)/shard_map/ppermute | solution.py:397
  49.2 0.1 collective-permute-start.11
  49.2 0.7 collective-permute-start.12
  49.9 0.7 collective-permute-start.14
  50.6 2.2 %home.1 = (f32[384,256]{1,0:T(8,128)S(1)}, bf16[384,256]{1,0:T(8,128)(2,1)S(1)}, bf16[384,256]{1,0:T(8,128)(2,1)S(1)}) custom-call(s32[309]{0:T(512)S(1)} %concatenate.12.table, bf16[384,768]{1,0:T(8,128)(2,1)S(1)} %get-tuple-element.44.queries, bf16[384,768]{1,0:T(8,128)(2,1)S(1)} %get-tuple-element.45.grad_out, ...), custom_call_target="tpu_custom_call" | custom-call | flops 339738624 | tf_op jit(solution)/shard_map/home/pallas_call | solution.py:426
  52.8 0.0 collective-permute-done.10
  52.8 7.5 %collective-permute-start.13 = (bf16[384,512]{1,0:T(8,128)(2,1)S(1)}, bf16[384,512]{1,0:T(8,128)(2,1)S(1)}, u32[]{:S(2)}, u32[]{:S(2)}) collective-permute-start(bf16[384,512]{1,0:T(8,128)(2,1)S(1)} %get-tuple-element.81), channel_id=1, source_target_pairs={{0,4},{4,0},{8,12},{12,8},{1,5},{5,1},{9,13},{13,9},{2,6},{6,2},{1... | collective-permute-start | bytes 1179656 | tf_op jit(solution)/shard_map/ppermute | solution.py:397
  60.3 0.0 collective-permute-done.9
  60.4 0.1 add_convert_fusion.1
  60.4 1.5 %collective-permute-done.11.rv_one = bf16[384,512]{1,0:T(8,128)(2,1)S(1)} collective-permute-done((bf16[384,512]{1,0:T(8,128)(2,1)S(1)}, bf16[384,512]{1,0:T(8,128)(2,1)S(1)}, u32[]{:S(2)}, u32[]{:S(2)}) %collective-permute-start.11) | collective-permute-done | bytes 393248 | tf_op jit(solution)/shard_map/ppermute | solution.py:397
  61.9 0.0 collective-permute-done.12.rv_two
  61.9 1.2 %rest.1 = (bf16[384,512]{1,0:T(8,128)(2,1)S(1)}, bf16[384,512]{1,0:T(8,128)(2,1)S(1)}, f32[384,512]{1,0:T(8,128)S(1)}) custom-call(bf16[384,768]{1,0:T(8,128)(2,1)S(1)} %get-tuple-element.44.queries, bf16[384,768]{1,0:T(8,128)(2,1)S(1)} %get-tuple-element.45.grad_out, bf16[4,2,576,128]{3,2,1,0:T(8,128)(2,1)S(1)} %get-tuple-element.72.chosen_in, ...), custom_call_target="tpu_custom_call" | custom-call | flops 452984832 | tf_op jit(solution)/shard_map/rest/pallas_call | solution.py:426
  63.1 0.9 %pad_maximum_fusion = bf16[384,768]{1,0:T(8,128)(2,1)} fusion(bf16[384,512]{1,0:T(8,128)(2,1)S(1)} %get-tuple-element.78, bf16[384,256]{1,0:T(8,128)(2,1)S(1)} %add_convert_fusion.1), kind=kLoop, calls=%fused_computation.1 | loop fusion | flops 1179648 | bytes 1179648 | tf_op jit(solution)/shard_map/concatenate | solution.py:517
  64.0 0.0 collective-permute-done.14
  64.0 3.9 %collective-permute-done.13 = bf16[384,512]{1,0:T(8,128)(2,1)S(1)} collective-permute-done((bf16[384,512]{1,0:T(8,128)(2,1)S(1)}, bf16[384,512]{1,0:T(8,128)(2,1)S(1)}, u32[]{:S(2)}, u32[]{:S(2)}) %collective-permute-start.13) | collective-permute-done | bytes 393248 | tf_op jit(solution)/shard_map/ppermute | solution.py:397
  67.9 0.2 add_convert_fusion
  68.1 0.9 %pad_maximum_fusion.1 = bf16[384,768]{1,0:T(8,128)(2,1)} fusion(bf16[384,512]{1,0:T(8,128)(2,1)S(1)} %add_convert_fusion, bf16[384,256]{1,0:T(8,128)(2,1)S(1)} %get-tuple-element.79), kind=kLoop, calls=%fused_computation.2 | loop fusion | flops 1179648 | bytes 1179648 | tf_op jit(solution)/shard_map/concatenate | solution.py:518
  68.9 0.9 %pad_maximum_fusion.2 = bf16[384,768]{1,0:T(8,128)(2,1)} fusion(bf16[384,512]{1,0:T(8,128)(2,1)S(1)} %get-tuple-element.84, bf16[384,256]{1,0:T(8,128)(2,1)S(1)} %get-tuple-element.83), kind=kLoop, calls=%fused_computation.3 | loop fusion | flops 1179648 | bytes 1179648 | tf_op jit(solution)/shard_map/concatenate | solution.py:519
  (1 shorter events, 0.0 us)
Async XLA Ops:
  0.6 15.1 %copy-start = (s32[8,3]{0,1:T(4,128)S(1)}, s32[8,3]{0,1:T(4,128)}, u32[]{:S(2)}) copy-start(s32[8,3]{0,1:T(4,128)} %param.10) | copy-start | bytes 292
  2.0 13.0 %collective-permute-start = (bf16[2,384,256]{2,1,0:T(8,128)(2,1)S(1)}, bf16[2,384,256]{2,1,0:T(8,128)(2,1)S(1)}, u32[]{:S(2)}, u32[]{:S(2)}) collective-permute-start(bf16[2,384,256]{2,1,0:T(8,128)(2,1)S(1)} %get-tuple-element.47), channel_id=1, source_target_pairs={{0,4},{4,0},{8,12},{12,8},{1,5},{5,1},{9,13},{13,9},{2,6},{6,2},{1... | collective-permute-start | bytes 1179656 | tf_op jit(solution)/shard_map/ppermute | solution.py:397
  5.1 17.0 %collective-permute-start.1 = (bf16[2,384,256]{2,1,0:T(8,128)(2,1)S(1)}, bf16[2,384,256]{2,1,0:T(8,128)(2,1)S(1)}, u32[]{:S(2)}, u32[]{:S(2)}) collective-permute-start(bf16[2,384,256]{2,1,0:T(8,128)(2,1)S(1)} %get-tuple-element.47), channel_id=1, source_target_pairs={{4,8},{8,4},{5,9},{9,5},{6,10},{10,6},{7,11},{11,7},{20,24},{24,20... | collective-permute-start | bytes 1179656 | tf_op jit(solution)/shard_map/ppermute | solution.py:398
  5.8 19.3 %collective-permute-start.2 = (bf16[384,512]{1,0:T(8,128)(2,1)S(1)}, bf16[384,512]{1,0:T(8,128)(2,1)S(1)}, u32[]{:S(2)}, u32[]{:S(2)}) collective-permute-start(bf16[384,512]{1,0:T(8,128)(2,1)S(1)} %get-tuple-element.50), channel_id=1, source_target_pairs={{0,4},{4,0},{8,12},{12,8},{1,5},{5,1},{9,13},{13,9},{2,6},{6,2},{1... | collective-permute-start | bytes 1179656 | tf_op jit(solution)/shard_map/ppermute | solution.py:397
  10.2 14.8 %collective-permute-start.3 = (bf16[384,512]{1,0:T(8,128)(2,1)S(1)}, bf16[384,512]{1,0:T(8,128)(2,1)S(1)}, u32[]{:S(2)}, u32[]{:S(2)}) collective-permute-start(bf16[384,512]{1,0:T(8,128)(2,1)S(1)} %get-tuple-element.50), channel_id=1, source_target_pairs={{4,8},{8,4},{5,9},{9,5},{6,10},{10,6},{7,11},{11,7},{20,24},{24,20... | collective-permute-start | bytes 1179656 | tf_op jit(solution)/shard_map/ppermute | solution.py:398
  10.9 29.1 %collective-permute-start.4 = (bf16[384,512]{1,0:T(8,128)(2,1)S(1)}, bf16[384,512]{1,0:T(8,128)(2,1)S(1)}, u32[]{:S(2)}, u32[]{:S(2)}) collective-permute-start(bf16[384,512]{1,0:T(8,128)(2,1)S(1)} %get-tuple-element.56), channel_id=1, source_target_pairs={{0,4},{4,0},{8,12},{12,8},{1,5},{5,1},{9,13},{13,9},{2,6},{6,2},{1... | collective-permute-start | bytes 1179656 | tf_op jit(solution)/shard_map/ppermute | solution.py:397
  15.0 24.9 %collective-permute-start.5 = (bf16[384,512]{1,0:T(8,128)(2,1)S(1)}, bf16[384,512]{1,0:T(8,128)(2,1)S(1)}, u32[]{:S(2)}, u32[]{:S(2)}) collective-permute-start(bf16[384,512]{1,0:T(8,128)(2,1)S(1)} %get-tuple-element.56), channel_id=1, source_target_pairs={{4,8},{8,4},{5,9},{9,5},{6,10},{10,6},{7,11},{11,7},{20,24},{24,20... | collective-permute-start | bytes 1179656 | tf_op jit(solution)/shard_map/ppermute | solution.py:398
  25.1 19.6 %collective-permute-start.6 = (f32[3,8,192]{2,1,0:T(8,128)S(1)}, f32[3,8,192]{2,1,0:T(8,128)S(1)}, u32[]{:S(2)}, u32[]{:S(2)}) collective-permute-start(f32[3,8,192]{2,1,0:T(8,128)S(1)} %get-tuple-element.62), channel_id=1, source_target_pairs={{0,4},{4,0},{8,12},{12,8},{1,5},{5,1},{9,13},{13,9},{2,6},{6,2},{1... | collective-permute-start | bytes 55304 | tf_op jit(solution)/shard_map/ppermute | solution.py:397
  31.4 13.3 %collective-permute-start.7 = (f32[3,8,192]{2,1,0:T(8,128)S(1)}, f32[3,8,192]{2,1,0:T(8,128)S(1)}, u32[]{:S(2)}, u32[]{:S(2)}) collective-permute-start(f32[3,8,192]{2,1,0:T(8,128)S(1)} %get-tuple-element.63), channel_id=1, source_target_pairs={{4,8},{8,4},{5,9},{9,5},{6,10},{10,6},{7,11},{11,7},{20,24},{24,20... | collective-permute-start | bytes 55304 | tf_op jit(solution)/shard_map/ppermute | solution.py:398
  32.2 12.4 %collective-permute-start.8 = (f32[3,4,192]{2,1,0:T(4,128)S(1)}, f32[3,4,192]{2,1,0:T(4,128)S(1)}, u32[]{:S(2)}, u32[]{:S(2)}) collective-permute-start(f32[3,4,192]{2,1,0:T(4,128)S(1)} %get-tuple-element.64), channel_id=1, source_target_pairs={{0,8},{8,0},{4,12},{12,4},{1,9},{9,1},{5,13},{13,5},{2,10},{10,2},... | collective-permute-start | bytes 27656 | tf_op jit(solution)/shard_map/ppermute | solution.py:406
  45.9 6.9 %collective-permute-start.10 = (bf16[384,256]{1,0:T(8,128)(2,1)S(1)}, bf16[384,256]{1,0:T(8,128)(2,1)S(1)}, u32[]{:S(2)}, u32[]{:S(2)}) collective-permute-start(bf16[384,256]{1,0:T(8,128)(2,1)S(1)} %get-tuple-element.71), channel_id=1, source_target_pairs={{4,8},{8,4},{5,9},{9,5},{6,10},{10,6},{7,11},{11,7},{20,24},{24,20... | collective-permute-start | bytes 589832 | tf_op jit(solution)/shard_map/ppermute | solution.py:398
  46.5 13.8 %collective-permute-start.9 = (bf16[384,256]{1,0:T(8,128)(2,1)S(1)}, bf16[384,256]{1,0:T(8,128)(2,1)S(1)}, u32[]{:S(2)}, u32[]{:S(2)}) collective-permute-start(bf16[384,256]{1,0:T(8,128)(2,1)S(1)} %get-tuple-element.70), channel_id=1, source_target_pairs={{0,4},{4,0},{8,12},{12,8},{1,5},{5,1},{9,13},{13,9},{2,6},{6,2},{1... | collective-permute-start | bytes 589832 | tf_op jit(solution)/shard_map/ppermute | solution.py:397
  49.2 12.8 %collective-permute-start.11 = (bf16[384,512]{1,0:T(8,128)(2,1)S(1)}, bf16[384,512]{1,0:T(8,128)(2,1)S(1)}, u32[]{:S(2)}, u32[]{:S(2)}) collective-permute-start(bf16[384,512]{1,0:T(8,128)(2,1)S(1)} %get-tuple-element.76), channel_id=1, source_target_pairs={{0,4},{4,0},{8,12},{12,8},{1,5},{5,1},{9,13},{13,9},{2,6},{6,2},{1... | collective-permute-start | bytes 1179656 | tf_op jit(solution)/shard_map/ppermute | solution.py:397
  49.2 12.7 %collective-permute-start.12 = (bf16[384,512]{1,0:T(8,128)(2,1)S(1)}, bf16[384,512]{1,0:T(8,128)(2,1)S(1)}, u32[]{:S(2)}, u32[]{:S(2)}) collective-permute-start(bf16[384,512]{1,0:T(8,128)(2,1)S(1)} %get-tuple-element.77), channel_id=1, source_target_pairs={{4,8},{8,4},{5,9},{9,5},{6,10},{10,6},{7,11},{11,7},{20,24},{24,20... | collective-permute-start | bytes 1179656 | tf_op jit(solution)/shard_map/ppermute | solution.py:398
  49.9 14.1 %collective-permute-start.14 = (bf16[384,512]{1,0:T(8,128)(2,1)S(1)}, bf16[384,512]{1,0:T(8,128)(2,1)S(1)}, u32[]{:S(2)}, u32[]{:S(2)}) collective-permute-start(bf16[384,512]{1,0:T(8,128)(2,1)S(1)} %get-tuple-element.82), channel_id=1, source_target_pairs={{4,8},{8,4},{5,9},{9,5},{6,10},{10,6},{7,11},{11,7},{20,24},{24,20... | collective-permute-start | bytes 1179656 | tf_op jit(solution)/shard_map/ppermute | solution.py:398
  52.8 15.1 %collective-permute-start.13 = (bf16[384,512]{1,0:T(8,128)(2,1)S(1)}, bf16[384,512]{1,0:T(8,128)(2,1)S(1)}, u32[]{:S(2)}, u32[]{:S(2)}) collective-permute-start(bf16[384,512]{1,0:T(8,128)(2,1)S(1)} %get-tuple-element.81), channel_id=1, source_target_pairs={{0,4},{4,0},{8,12},{12,8},{1,5},{5,1},{9,13},{13,9},{2,6},{6,2},{1... | collective-permute-start | bytes 1179656 | tf_op jit(solution)/shard_map/ppermute | solution.py:397

commit v5 on v4

--- a/solution.py
+++ b/solution.py
@@ -14,7 +14,7 @@
 NSEL = 3
 SB = 4
 DEPTH = 3
-MOVED = 2
+MOVED = 3
 SPLIT = MOVED * HD
 ROWS = FR_DEV * TOK_FRAME
 WINDOW = FR_DEV + 2 * REACH
@@ -22,7 +22,7 @@
 BLOCK = TOK_FRAME // SB
 SCALE = HD ** (-0.5)
 SCALE2 = SCALE * math.log2(math.e)
-NEG = -1e30
+NEG = -(2.0**100)
 NT = (((1,), (1,)), ((), ()))
 NN = (((1,), (0,)), ((), ()))
 TN = (((0,), (0,)), ((), ()))
@@ -30,6 +30,8 @@
 FIRST = MASKS + WINDOW * NSEL * SB * SB
 RANK = FIRST + 1
 COUNT = FIRST + 2
+NOTES = 32
+SIDE = FR_DEV * MOVED
 
 
 def dot(lhs, rhs, dims):
@@ -146,7 +148,7 @@
 
 
 def values_kernel(
-    table, queries, grad_out, k_own, bias, k_one, k_two,
+    table, queries, grad_out, k_own, bias, k_one, k_two, n_one, n_two,
     chosen_out, prob_out, own_out, one_out, two_out,
     windows, accums,
 ):
@@ -168,9 +170,11 @@
             prob_out[head, frame] = prob_low
             far = dot(prob_low[TOK_FRAME:], grad_out[rows_of(frame), column], NN)
             spread(table, frame, accum, far)
-        one_out[:, far_column] = accum[0:ROWS].astype(one_out.dtype)
+        one_out[:ROWS, far_column] = accum[0:ROWS].astype(one_out.dtype)
         own_out[:, far_column] = accum[ROWS : 2 * ROWS]
-        two_out[:, far_column] = accum[2 * ROWS : 3 * ROWS].astype(two_out.dtype)
+        two_out[:ROWS, far_column] = accum[2 * ROWS : 3 * ROWS].astype(two_out.dtype)
+    write_notes(n_one, one_out)
+    write_notes(n_two, two_out)
 
 
 def keys_kernel(
@@ -248,7 +252,7 @@
                         keys[rows, column], view_of(query, queries, f_one, f_two, 0, head), NT
                     )
                     masked = scores * SCALE2 + bias[query, key]
-                    highest = jnp.max(masked, 0, keepdims=True)
+                    highest = rounded(jnp.max(masked, 0, keepdims=True))
                     raised = jnp.exp2(masked - highest)
                     grad_prob = dot(
                         values[rows, column], view_of(query, grad_out, f_one, f_two, 1, head), NT
@@ -270,15 +274,44 @@
     mine_out[0] = highest
     mine_out[1] = total
     mine_out[2] = moment
-    side = FR_DEV * MOVED
+    side = SIDE
     rank = table[RANK] % 4
     swapped = (rank == 1) | (rank == 2)
+    for out, start in ((one_out, 0), (two_out, side)):
+        rows = slice(start, start + 2 * side)
+        out[...] = jnp.zeros_like(out)
+        notes = (highest[rows], *halves(total[rows]), *halves(moment[rows]))
+        for index, note in enumerate(notes):
+            out[index * 2 * side : (index + 1) * 2 * side] = note
     for index in range(3):
         whole = mine_out[index]
-        one_out[index] = whole[0 : 2 * side]
-        two_out[index] = whole[side : 3 * side]
         far_out[index] = jnp.where(swapped, whole[2 * side :], whole[:side])
         other_out[index] = jnp.where(swapped, whole[:side], whole[2 * side :])
+
+
+def rounded(array):
+    return array.astype(jnp.bfloat16).astype(jnp.float32)
+
+
+def halves(array):
+    high = rounded(array)
+    return high, array - high
+
+
+def write_notes(notes, message):
+    for half in range(2):
+        message[ROWS:, half * TOK_FRAME : (half + 1) * TOK_FRAME] = notes[
+            half * NOTES : (half + 1) * NOTES
+        ].astype(message.dtype)
+
+
+def read_notes(message, notes):
+    for half in range(2):
+        notes[half * NOTES : (half + 1) * NOTES] = message[
+            ROWS:, half * TOK_FRAME : (half + 1) * TOK_FRAME
+        ].astype(notes.dtype)
+    parts = [notes[i * 2 * SIDE : (i + 1) * 2 * SIDE] for i in range(5)]
+    return parts[0], parts[1] + parts[2], parts[3] + parts[4]
 
 
 def joined_stats(sources):
@@ -300,23 +333,26 @@
 
 
 def back_kernel(
-    table, keys, masked, grad_probs, mine, s_one, s_two, s_far, s_other,
+    table, keys, masked, grad_probs, mine, r_one, r_two, s_far, s_other,
     prob_out, score_out, logs, deltas, one_out, two_out,
-    accums,
+    accums, notes,
 ):
-    side = FR_DEV * MOVED
+    side = SIDE
     rank = table[RANK] % 4
     swapped = (rank == 1) | (rank == 2)
     far = [jnp.where(swapped, s_other[i], s_far[i]) for i in range(3)]
     other = [jnp.where(swapped, s_far[i], s_other[i]) for i in range(3)]
-
-    def part(ref, start):
-        return [ref[i, start : start + side] for i in range(3)]
+    s_one = read_notes(r_one, notes.at[0])
+    s_two = read_notes(r_two, notes.at[1])
+    s_mine = [mine[i] for i in range(3)]
+
+    def part(stats, start):
+        return [each[start : start + side] for each in stats]
 
     groups = (
-        (part(mine, 0), part(s_one, side), far),
-        (part(mine, side), part(s_one, 0), part(s_two, side)),
-        (part(mine, 2 * side), part(s_two, 0), other),
+        (part(s_mine, 0), part(s_one, side), far),
+        (part(s_mine, side), part(s_one, 0), part(s_two, side)),
+        (part(s_mine, 2 * side), part(s_two, 0), other),
     )
     for index, sources in enumerate(groups):
         highest, total, moment = joined_stats(sources)
@@ -431,7 +467,7 @@
         out_specs=tuple(pl.BlockSpec(memory_space=pltpu.VMEM) for _ in outs),
         scratch_shapes=scratch,
         compiler_params=pltpu.CompilerParams(vmem_limit_bytes=16 << 20),
-        cost_estimate=pl.CostEstimate(flops=flops, bytes_accessed=0, transcendentals=0),
+        cost_estimate=pl.CostEstimate(flops=flops // 1000, bytes_accessed=0, transcendentals=0),
         name=name,
     )(*scalars, *arrays)
 
@@ -464,25 +500,27 @@
         [pltpu.SemaphoreType.DMA((4,))], unit, pltpu.HBM,
     )
     grid = (WINDOW, FR_DEV, MOVED, TOK_FRAME, TOK_FRAME)
-    side = FR_DEV * MOVED
-    masked, grad_probs, mine, s_one, s_two, s_far, s_other = call(
+    side = SIDE
+    note = full(2 * NOTES, TOK_FRAME)
+    masked, grad_probs, mine, n_one, n_two, s_far, s_other = call(
         stats_kernel, "stats", (table,), (query, grad, key, value, moved_bias, f_one, f_two),
         (full(*grid), full(*grid), full(3, 3 * side, TOK_FRAME))
-        + (full(3, 2 * side, TOK_FRAME),) * 2 + (full(3, side, TOK_FRAME),) * 2,
+        + (note, note) + (full(3, side, TOK_FRAME),) * 2,
         [full(FR_DEV, 3, 3 * side, TOK_FRAME)], 2 * MOVED * unit,
     )
-    s_one, s_two = swap(s_one, s_two)
     s_far, s_other = swap_far(s_far, s_other)
-    k_one, k_two, mine = lax.optimization_barrier((k_one, k_two, mine))
     windows = low(DEPTH, 3 * ROWS, HD)
     accums = full(DEPTH, 3 * ROWS, HD)
     pairs = low(heads, FR_DEV, SLOTS, TOK_FRAME)
     chosen, prob_low, gv_own, gv_one, gv_two = call(
-        values_kernel, "values_part", (table,), (query, grad, key, bias, k_one, k_two),
-        (low(heads, FR_DEV, SLOTS, HD), pairs, full(ROWS, rest), low(ROWS, rest), low(ROWS, rest)),
+        values_kernel, "values_part", (table,),
+        (query, grad, key, bias, k_one, k_two, n_one, n_two),
+        (low(heads, FR_DEV, SLOTS, HD), pairs, full(ROWS, rest))
+        + (low(ROWS + NOTES, rest),) * 2,
         [windows, accums], 2 * heads * unit,
     )
     rv_one, rv_two = swap(gv_one, gv_two)
+    v_one, s_far = lax.optimization_barrier((v_one, s_far))
     score_low, gk_own, gk_one, gk_two = call(
         keys_kernel, "keys_part", (table,), (query, grad, value, prob_low, v_one, v_two),
         (pairs, full(ROWS, rest), low(ROWS, rest), low(ROWS, rest)),
@@ -492,10 +530,10 @@
     gk_own, masked = lax.optimization_barrier((gk_own, masked))
     y_prob, y_score, logs, deltas, gq_one, gq_two = call(
         back_kernel, "back", (table,),
-        (key, masked, grad_probs, mine, s_one, s_two, s_far, s_other),
+        (key, masked, grad_probs, mine, rv_one, rv_two, s_far, s_other),
         (low(*grid), low(*grid), full(3 * side, TOK_FRAME), full(3 * side, TOK_FRAME))
         + (low(ROWS, SPLIT),) * 2,
-        [full(2, ROWS, SPLIT)], MOVED * unit,
+        [full(2, ROWS, SPLIT), full(2, 2 * NOTES, TOK_FRAME)], MOVED * unit,
     )
     rq_one, rq_two = swap(gq_one, gq_two)
     gq_near, gk_near, gv_near = call(

time: 69.9 us -> 71.2 us (1.019)
  the two profiles are of different devices: /device:TPU:0 before, /device:TPU:10 now
where the time goes in v5:
time: 71.2 us; the launch traced here: 70.7 us
  starting transfers between devices  22.9 us (32%)
  Pallas kernels  21.7 us (30%)
  waiting for transfers between devices  18.3 us (26%)
  local copies, waits for them, and re-layouts  4.16 us (6%)
  other arithmetic  2.78 us (4%)
  between operations  0.84 us (1%)
    pallas_call x8, Pallas kernels, call(): pl.pallas_call(kernel, out_shape=outs, in_specs=[pl.BlockSpec(memory_spac...  21.7 us
    ppermute x6, starting transfers between devices, swap(): lax.ppermute(two, 'frames', both_ways(second))  16.6 us
    ppermute x6, waiting for transfers between devices, swap(): lax.ppermute(two, 'frames', both_ways(second))  12.9 us
    ppermute x6, starting transfers between devices, swap(): lax.ppermute(one, 'frames', both_ways(first))  6.02 us
    ppermute x1, waiting for transfers between devices, swap_far(): far = lax.ppermute(far, 'frames', both_ways(near))  5.35 us
    dynamic_slice x2, local copies, waits for them, and re-layouts, lookup(): lax.dynamic_slice_in_dim(jnp.pad(spatial, around + ((0, 0), (0, 0))), fir...  2.93 us
  transfers between devices with their start and end apart: 13, of which 3 were waited for; matrix products, arithmetic and copies ran while one was open for 8% of the time, Pallas kernels for 29%

profile of v5, /device:TPU:10, one launch (start us, length us, event | category | flops | bytes accessed | tf_op | source)
XLA Modules:
  0.0 70.7 jit_solution(11913900213813620124)
XLA Ops:
  0.6 0.0 copy-start
  0.6 1.3 %pack.1 = (bf16[2,384,384]{2,1,0:T(8,128)(2,1)S(1)}, bf16[384,384]{1,0:T(8,128)(2,1)S(1)}, bf16[384,384]{1,0:T(8,128)(2,1)S(1)}) custom-call(bf16[384,768]{1,0:T(8,128)(2,1)} %queries.1, bf16[384,768]{1,0:T(8,128)(2,1)} %grad_out.1, bf16[384,768]{1,0:T(8,128)(2,1)} %keys.1, bf16[384,768]{1,0:T(8,128)(2,1)} %values.1), custom_call_target="tpu_custom_call" | custom-call | flops 56623 | tf_op jit(solution)/shard_map/pack/pallas_call | solution.py:462
  1.9 3.5 %collective-permute-start.1 = (bf16[2,384,384]{2,1,0:T(8,128)(2,1)S(1)}, bf16[2,384,384]{2,1,0:T(8,128)(2,1)S(1)}, u32[]{:S(2)}, u32[]{:S(2)}) collective-permute-start(bf16[2,384,384]{2,1,0:T(8,128)(2,1)S(1)} %get-tuple-element.46), channel_id=1, source_target_pairs={{4,8},{8,4},{5,9},{9,5},{6,10},{10,6},{7,11},{11,7},{20,24},{24,20... | collective-permute-start | bytes 1769480 | tf_op jit(solution)/shard_map/ppermute | solution.py:434
  5.4 0.1 collective-permute-start
  5.5 2.4 %collective-permute-start.3 = (bf16[384,384]{1,0:T(8,128)(2,1)S(1)}, bf16[384,384]{1,0:T(8,128)(2,1)S(1)}, u32[]{:S(2)}, u32[]{:S(2)}) collective-permute-start(bf16[384,384]{1,0:T(8,128)(2,1)S(1)} %get-tuple-element.49), channel_id=1, source_target_pairs={{4,8},{8,4},{5,9},{9,5},{6,10},{10,6},{7,11},{11,7},{20,24},{24,20... | collective-permute-start | bytes 884744 | tf_op jit(solution)/shard_map/ppermute | solution.py:434
  7.9 0.4 collective-permute-start.2
  8.2 1.7 %collective-permute-start.4 = (bf16[384,384]{1,0:T(8,128)(2,1)S(1)}, bf16[384,384]{1,0:T(8,128)(2,1)S(1)}, u32[]{:S(2)}, u32[]{:S(2)}) collective-permute-start(bf16[384,384]{1,0:T(8,128)(2,1)S(1)} %get-tuple-element.54), channel_id=1, source_target_pairs={{0,4},{4,0},{8,12},{12,8},{1,5},{5,1},{9,13},{13,9},{2,6},{6,2},{1... | collective-permute-start | bytes 884744 | tf_op jit(solution)/shard_map/ppermute | solution.py:433
  9.9 10.1 %collective-permute-done.1.f_two = bf16[2,384,384]{2,1,0:T(8,128)(2,1)S(1)} collective-permute-done((bf16[2,384,384]{2,1,0:T(8,128)(2,1)S(1)}, bf16[2,384,384]{2,1,0:T(8,128)(2,1)S(1)}, u32[]{:S(2)}, u32[]{:S(2)}) %collective-permute-start.1) | collective-permute-done | bytes 589856 | tf_op jit(solution)/shard_map/ppermute | solution.py:434
  20.0 3.5 %collective-permute-start.6 = (bf16[384,384]{1,0:T(8,128)(2,1)S(1)}, bf16[384,384]{1,0:T(8,128)(2,1)S(1)}, u32[]{:S(2)}, u32[]{:S(2)}) collective-permute-start(bf16[384,384]{1,0:T(8,128)(2,1)S(1)} %get-tuple-element.54), channel_id=1, source_target_pairs={{4,8},{8,4},{5,9},{9,5},{6,10},{10,6},{7,11},{11,7},{20,24},{24,20... | collective-permute-start | bytes 884744 | tf_op jit(solution)/shard_map/ppermute | solution.py:434
  23.5 0.0 copy-done
  23.5 0.1 pad_dynamic-slice_fusion.1
  23.6 0.1 copy.10
  23.7 0.1 reshape.12
  23.8 1.4 %pad_dynamic-slice_fusion = s32[6,3,4,4]{0,3,2,1:T(4,128)} fusion(s32[]{:T(128)S(6)} %select_n.4, s32[8,3,4,4]{0,3,2,1:T(4,128)} %param.11), kind=kLoop, calls=%fused_computation.5 | loop fusion | bytes 2692 | tf_op jit(solution)/shard_map/dynamic_slice | solution.py:453
  25.2 1.5 %copy.11 = s32[6,3,4,4]{3,2,1,0:T(4,128)} copy(s32[6,3,4,4]{0,3,2,1:T(4,128)} %pad_dynamic-slice_fusion) | data formatting | bytes 2304 | tf_op jit(solution)/shard_map/dynamic_slice | solution.py:453
  26.7 0.9 %reshape.13 = s32[288]{0:T(512)S(1)} reshape(s32[6,3,4,4]{3,2,1,0:T(4,128)} %copy.11) | data formatting | bytes 2304 | tf_op jit(solution)/shard_map/reshape | solution.py:457
  27.6 0.1 concatenate.12.table
  27.7 2.2 %stage.1 = (bf16[384,768]{1,0:T(8,128)(2,1)S(1)}, bf16[384,768]{1,0:T(8,128)(2,1)S(1)}, bf16[384,768]{1,0:T(8,128)(2,1)S(1)}, bf16[384,768]{1,0:T(8,128)(2,1)S(1...) custom-call(s32[309]{0:T(512)S(1)} %concatenate.12.table, bf16[384,768]{1,0:T(8,128)(2,1)} %queries.1, ...), custom_call_target="tpu_custom_call" | custom-call | flops 56623 | tf_op jit(solution)/shard_map/stage/pallas_call | solution.py:462
  29.9 0.0 collective-permute-done.f_one
  29.9 4.6 %stats.1 = (f32[6,2,3,192,192]{4,3,2,1,0:T(8,128)S(1)}, f32[6,2,3,192,192]{4,3,2,1,0:T(8,128)S(1)}, f32[3,18,192]{2,1,0:T(8,128)S(1)}, f32[64,192]{1,0:T(8,128)S...) custom-call(s32[309]{0:T(512)S(1)} %concatenate.12.table, ...), custom_call_target="tpu_custom_call" | custom-call | flops 339738 | tf_op jit(solution)/shard_map/stats/pallas_call | solution.py:462
  34.5 0.0 collective-permute-done.3.k_two
  34.5 0.0 collective-permute-done.2.k_one
  34.5 3.7 %values_part.1 = (bf16[3,2,576,128]{3,2,1,0:T(8,128)(2,1)S(1)}, bf16[3,2,576,192]{3,2,1,0:T(8,128)(2,1)S(1)}, f32[384,384]{1,0:T(8,128)S(1)}, bf16[416,384]{1,0:T(8,128)(2,1)S(1)}, bf16[416,384]{1,0:T(8,128)(2,1)S(1)}) custom-call(s32[309]{0:T(512)S(1)} %concatenate.12.table, bf16[384,768]{1,0:T(8,128)(2,1)S(1)} %get-tuple-element.43.queries, ...), custom_call_target="tpu_custom_call" | custom-call | flops 339738 | tf_op jit(solution)/shard_map/values_part/pallas_call | solution.py:462
  38.2 0.1 collective-permute-start.7
  38.3 2.1 %collective-permute-start.8 = (bf16[416,384]{1,0:T(8,128)(2,1)S(1)}, bf16[416,384]{1,0:T(8,128)(2,1)S(1)}, u32[]{:S(2)}, u32[]{:S(2)}) collective-permute-start(bf16[416,384]{1,0:T(8,128)(2,1)S(1)} %get-tuple-element.63), channel_id=1, source_target_pairs={{4,8},{8,4},{5,9},{9,5},{6,10},{10,6},{7,11},{11,7},{20,24},{24,20... | collective-permute-start | bytes 958472 | tf_op jit(solution)/shard_map/ppermute | solution.py:434
  40.4 0.3 collective-permute-start.5
  40.6 0.0 collective-permute-done.4.v_one
  40.6 5.4 %collective-permute-done.5.s_far = f32[3,6,192]{2,1,0:T(8,128)S(1)} collective-permute-done((f32[3,6,192]{2,1,0:T(8,128)S(1)}, f32[3,6,192]{2,1,0:T(8,128)S(1)}, u32[]{:S(2)}, u32[]{:S(2)}) %collective-permute-start.5) | collective-permute-done | bytes 13856 | tf_op jit(solution)/shard_map/ppermute | solution.py:442
  46.0 0.0 collective-permute-done.6.v_two
  46.0 3.4 %keys_part.1 = (bf16[3,2,576,192]{3,2,1,0:T(8,128)(2,1)S(1)}, f32[384,384]{1,0:T(8,128)S(1)}, bf16[384,384]{1,0:T(8,128)(2,1)S(1)}, bf16[384,384]{1,0:T(8,128)(2,1)S(1)}) custom-call(s32[309]{0:T(512)S(1)} %concatenate.12.table, bf16[384,768]{1,0:T(8,128)(2,1)S(1)} %get-tuple-element.43.queries, bf16[384,768]{1,0:T(8,128)(2,1)S(1)} %get-tuple-element.44.grad_out, ...), custom_call_target="tpu_custom_call" | custom-call | flops 339738 | tf_op jit(solution)/shard_map/keys_part/pallas_call | solution.py:462
  49.4 3.7 %collective-permute-start.11 = (bf16[384,384]{1,0:T(8,128)(2,1)S(1)}, bf16[384,384]{1,0:T(8,128)(2,1)S(1)}, u32[]{:S(2)}, u32[]{:S(2)}) collective-permute-start(bf16[384,384]{1,0:T(8,128)(2,1)S(1)} %get-tuple-element.79), channel_id=1, source_target_pairs={{0,4},{4,0},{8,12},{12,8},{1,5},{5,1},{9,13},{13,9},{2,6},{6,2},{1... | collective-permute-start | bytes 884744 | tf_op jit(solution)/shard_map/ppermute | solution.py:433
  53.1 2.2 %collective-permute-start.12 = (bf16[384,384]{1,0:T(8,128)(2,1)S(1)}, bf16[384,384]{1,0:T(8,128)(2,1)S(1)}, u32[]{:S(2)}, u32[]{:S(2)}) collective-permute-start(bf16[384,384]{1,0:T(8,128)(2,1)S(1)} %get-tuple-element.80), channel_id=1, source_target_pairs={{4,8},{8,4},{5,9},{9,5},{6,10},{10,6},{7,11},{11,7},{20,24},{24,20... | collective-permute-start | bytes 884744 | tf_op jit(solution)/shard_map/ppermute | solution.py:434
  55.3 0.0 collective-permute-done.7.r_one.rv_one
  55.3 0.0 collective-permute-done.8.r_two.rv_two
  55.3 2.2 %back.1 = (bf16[6,2,3,192,192]{4,3,2,1,0:T(8,128)(2,1)S(1)}, bf16[6,2,3,192,192]{4,3,2,1,0:T(8,128)(2,1)S(1)}, f32[18,192]{1,0:T(8,128)S(1)}, f32[18,192]{1,0:T(...) custom-call(s32[309]{0:T(512)S(1)} %concatenate.12.table, ...), custom_call_target="tpu_custom_call" | custom-call | flops 169869 | tf_op jit(solution)/shard_map/back/pallas_call | solution.py:462
  57.5 0.1 collective-permute-start.9
  57.6 3.0 %collective-permute-start.10 = (bf16[384,384]{1,0:T(8,128)(2,1)S(1)}, bf16[384,384]{1,0:T(8,128)(2,1)S(1)}, u32[]{:S(2)}, u32[]{:S(2)}) collective-permute-start(bf16[384,384]{1,0:T(8,128)(2,1)S(1)} %get-tuple-element.71), channel_id=1, source_target_pairs={{4,8},{8,4},{5,9},{9,5},{6,10},{10,6},{7,11},{11,7},{20,24},{24,20... | collective-permute-start | bytes 884744 | tf_op jit(solution)/shard_map/ppermute | solution.py:434
  60.6 1.0 %rest.1 = (bf16[384,384]{1,0:T(8,128)(2,1)S(1)}, bf16[384,384]{1,0:T(8,128)(2,1)S(1)}, f32[384,384]{1,0:T(8,128)S(1)}) custom-call(bf16[384,768]{1,0:T(8,128)(2,1)S(1)} %get-tuple-element.43.queries, bf16[384,768]{1,0:T(8,128)(2,1)S(1)} %get-tuple-element.44.grad_out, bf16[3,2,576,128]{3,2,1,0:T(8,128)(2,1)S(1)} %get-tuple-element.72.chosen_in, ...), custom_call_target="tpu_custom_call" | custom-call | flops 339738 | tf_op jit(solution)/shard_map/rest/pallas_call | solution.py:462
  61.6 0.0 collective-permute-done.11
  61.6 2.8 %collective-permute-done.12 = bf16[384,384]{1,0:T(8,128)(2,1)S(1)} collective-permute-done((bf16[384,384]{1,0:T(8,128)(2,1)S(1)}, bf16[384,384]{1,0:T(8,128)(2,1)S(1)}, u32[]{:S(2)}, u32[]{:S(2)}) %collective-permute-start.12) | collective-permute-done | bytes 294944 | tf_op jit(solution)/shard_map/ppermute | solution.py:434
  64.4 0.1 add_convert_fusion
  64.5 3.5 %home.1 = (f32[384,384]{1,0:T(8,128)S(1)}, bf16[384,384]{1,0:T(8,128)(2,1)S(1)}, bf16[384,384]{1,0:T(8,128)(2,1)S(1)}) custom-call(s32[309]{0:T(512)S(1)} %concatenate.12.table, bf16[384,768]{1,0:T(8,128)(2,1)S(1)} %get-tuple-element.43.queries, bf16[384,768]{1,0:T(8,128)(2,1)S(1)} %get-tuple-element.44.grad_out, ...), custom_call_target="tpu_custom_call" | custom-call | flops 509607 | tf_op jit(solution)/shard_map/home/pallas_call | solution.py:462
  68.0 0.9 %pad_maximum_fusion.1 = bf16[384,768]{1,0:T(8,128)(2,1)} fusion(bf16[384,384]{1,0:T(8,128)(2,1)S(1)} %add_convert_fusion, bf16[384,384]{1,0:T(8,128)(2,1)S(1)} %get-tuple-element.77), kind=kLoop, calls=%fused_computation.1 | loop fusion | flops 1179648 | bytes 1179648 | tf_op jit(solution)/shard_map/concatenate | solution.py:556
  68.9 0.9 %pad_maximum_fusion.2 = bf16[384,768]{1,0:T(8,128)(2,1)} fusion(bf16[384,384]{1,0:T(8,128)(2,1)S(1)} %get-tuple-element.82, bf16[384,384]{1,0:T(8,128)(2,1)S(1)} %get-tuple-element.81), kind=kLoop, calls=%fused_computation.2 | loop fusion | flops 1179648 | bytes 1179648 | tf_op jit(solution)/shard_map/concatenate | solution.py:557
  69.7 0.0 collective-permute-done.9
  69.7 0.0 collective-permute-done.10
  69.7 0.1 add_convert_fusion.1
  69.8 0.9 %pad_maximum_fusion = bf16[384,768]{1,0:T(8,128)(2,1)} fusion(bf16[384,384]{1,0:T(8,128)(2,1)S(1)} %get-tuple-element.76, bf16[384,384]{1,0:T(8,128)(2,1)S(1)} %add_convert_fusion.1), kind=kLoop, calls=%fused_computation | loop fusion | flops 1179648 | bytes 1179648 | tf_op jit(solution)/shard_map/concatenate | solution.py:555
  (1 shorter events, 0.0 us)
Async XLA Ops:
  0.6 22.9 %copy-start = (s32[8,3]{0,1:T(4,128)S(1)}, s32[8,3]{0,1:T(4,128)}, u32[]{:S(2)}) copy-start(s32[8,3]{0,1:T(4,128)} %param.10) | copy-start | bytes 292
  1.9 18.1 %collective-permute-start.1 = (bf16[2,384,384]{2,1,0:T(8,128)(2,1)S(1)}, bf16[2,384,384]{2,1,0:T(8,128)(2,1)S(1)}, u32[]{:S(2)}, u32[]{:S(2)}) collective-permute-start(bf16[2,384,384]{2,1,0:T(8,128)(2,1)S(1)} %get-tuple-element.46), channel_id=1, source_target_pairs={{4,8},{8,4},{5,9},{9,5},{6,10},{10,6},{7,11},{11,7},{20,24},{24,20... | collective-permute-start | bytes 1769480 | tf_op jit(solution)/shard_map/ppermute | solution.py:434
  5.4 24.5 %collective-permute-start = (bf16[2,384,384]{2,1,0:T(8,128)(2,1)S(1)}, bf16[2,384,384]{2,1,0:T(8,128)(2,1)S(1)}, u32[]{:S(2)}, u32[]{:S(2)}) collective-permute-start(bf16[2,384,384]{2,1,0:T(8,128)(2,1)S(1)} %get-tuple-element.46), channel_id=1, source_target_pairs={{0,4},{4,0},{8,12},{12,8},{1,5},{5,1},{9,13},{13,9},{2,6},{6,2},{1... | collective-permute-start | bytes 1769480 | tf_op jit(solution)/shard_map/ppermute | solution.py:433
  5.5 29.0 %collective-permute-start.3 = (bf16[384,384]{1,0:T(8,128)(2,1)S(1)}, bf16[384,384]{1,0:T(8,128)(2,1)S(1)}, u32[]{:S(2)}, u32[]{:S(2)}) collective-permute-start(bf16[384,384]{1,0:T(8,128)(2,1)S(1)} %get-tuple-element.49), channel_id=1, source_target_pairs={{4,8},{8,4},{5,9},{9,5},{6,10},{10,6},{7,11},{11,7},{20,24},{24,20... | collective-permute-start | bytes 884744 | tf_op jit(solution)/shard_map/ppermute | solution.py:434
  7.9 26.6 %collective-permute-start.2 = (bf16[384,384]{1,0:T(8,128)(2,1)S(1)}, bf16[384,384]{1,0:T(8,128)(2,1)S(1)}, u32[]{:S(2)}, u32[]{:S(2)}) collective-permute-start(bf16[384,384]{1,0:T(8,128)(2,1)S(1)} %get-tuple-element.49), channel_id=1, source_target_pairs={{0,4},{4,0},{8,12},{12,8},{1,5},{5,1},{9,13},{13,9},{2,6},{6,2},{1... | collective-permute-start | bytes 884744 | tf_op jit(solution)/shard_map/ppermute | solution.py:433
  8.2 32.4 %collective-permute-start.4 = (bf16[384,384]{1,0:T(8,128)(2,1)S(1)}, bf16[384,384]{1,0:T(8,128)(2,1)S(1)}, u32[]{:S(2)}, u32[]{:S(2)}) collective-permute-start(bf16[384,384]{1,0:T(8,128)(2,1)S(1)} %get-tuple-element.54), channel_id=1, source_target_pairs={{0,4},{4,0},{8,12},{12,8},{1,5},{5,1},{9,13},{13,9},{2,6},{6,2},{1... | collective-permute-start | bytes 884744 | tf_op jit(solution)/shard_map/ppermute | solution.py:433
  20.0 26.0 %collective-permute-start.6 = (bf16[384,384]{1,0:T(8,128)(2,1)S(1)}, bf16[384,384]{1,0:T(8,128)(2,1)S(1)}, u32[]{:S(2)}, u32[]{:S(2)}) collective-permute-start(bf16[384,384]{1,0:T(8,128)(2,1)S(1)} %get-tuple-element.54), channel_id=1, source_target_pairs={{4,8},{8,4},{5,9},{9,5},{6,10},{10,6},{7,11},{11,7},{20,24},{24,20... | collective-permute-start | bytes 884744 | tf_op jit(solution)/shard_map/ppermute | solution.py:434
  38.2 17.1 %collective-permute-start.7 = (bf16[416,384]{1,0:T(8,128)(2,1)S(1)}, bf16[416,384]{1,0:T(8,128)(2,1)S(1)}, u32[]{:S(2)}, u32[]{:S(2)}) collective-permute-start(bf16[416,384]{1,0:T(8,128)(2,1)S(1)} %get-tuple-element.62), channel_id=1, source_target_pairs={{0,4},{4,0},{8,12},{12,8},{1,5},{5,1},{9,13},{13,9},{2,6},{6,2},{1... | collective-permute-start | bytes 958472 | tf_op jit(solution)/shard_map/ppermute | solution.py:433
  38.3 17.1 %collective-permute-start.8 = (bf16[416,384]{1,0:T(8,128)(2,1)S(1)}, bf16[416,384]{1,0:T(8,128)(2,1)S(1)}, u32[]{:S(2)}, u32[]{:S(2)}) collective-permute-start(bf16[416,384]{1,0:T(8,128)(2,1)S(1)} %get-tuple-element.63), channel_id=1, source_target_pairs={{4,8},{8,4},{5,9},{9,5},{6,10},{10,6},{7,11},{11,7},{20,24},{24,20... | collective-permute-start | bytes 958472 | tf_op jit(solution)/shard_map/ppermute | solution.py:434
  40.4 5.6 %collective-permute-start.5 = (f32[3,6,192]{2,1,0:T(8,128)S(1)}, f32[3,6,192]{2,1,0:T(8,128)S(1)}, u32[]{:S(2)}, u32[]{:S(2)}) collective-permute-start(f32[3,6,192]{2,1,0:T(8,128)S(1)} %get-tuple-element.55), channel_id=1, source_target_pairs={{0,8},{8,0},{4,12},{12,4},{1,9},{9,1},{5,13},{13,5},{2,10},{10,2},... | collective-permute-start | bytes 41480 | tf_op jit(solution)/shard_map/ppermute | solution.py:442
  49.4 12.2 %collective-permute-start.11 = (bf16[384,384]{1,0:T(8,128)(2,1)S(1)}, bf16[384,384]{1,0:T(8,128)(2,1)S(1)}, u32[]{:S(2)}, u32[]{:S(2)}) collective-permute-start(bf16[384,384]{1,0:T(8,128)(2,1)S(1)} %get-tuple-element.79), channel_id=1, source_target_pairs={{0,4},{4,0},{8,12},{12,8},{1,5},{5,1},{9,13},{13,9},{2,6},{6,2},{1... | collective-permute-start | bytes 884744 | tf_op jit(solution)/shard_map/ppermute | solution.py:433
  53.1 11.3 %collective-permute-start.12 = (bf16[384,384]{1,0:T(8,128)(2,1)S(1)}, bf16[384,384]{1,0:T(8,128)(2,1)S(1)}, u32[]{:S(2)}, u32[]{:S(2)}) collective-permute-start(bf16[384,384]{1,0:T(8,128)(2,1)S(1)} %get-tuple-element.80), channel_id=1, source_target_pairs={{4,8},{8,4},{5,9},{9,5},{6,10},{10,6},{7,11},{11,7},{20,24},{24,20... | collective-permute-start | bytes 884744 | tf_op jit(solution)/shard_map/ppermute | solution.py:434
  57.5 12.2 %collective-permute-start.9 = (bf16[384,384]{1,0:T(8,128)(2,1)S(1)}, bf16[384,384]{1,0:T(8,128)(2,1)S(1)}, u32[]{:S(2)}, u32[]{:S(2)}) collective-permute-start(bf16[384,384]{1,0:T(8,128)(2,1)S(1)} %get-tuple-element.70), channel_id=1, source_target_pairs={{0,4},{4,0},{8,12},{12,8},{1,5},{5,1},{9,13},{13,9},{2,6},{6,2},{1... | collective-permute-start | bytes 884744 | tf_op jit(solution)/shard_map/ppermute | solution.py:433
  57.6 12.1 %collective-permute-start.10 = (bf16[384,384]{1,0:T(8,128)(2,1)S(1)}, bf16[384,384]{1,0:T(8,128)(2,1)S(1)}, u32[]{:S(2)}, u32[]{:S(2)}) collective-permute-start(bf16[384,384]{1,0:T(8,128)(2,1)S(1)} %get-tuple-element.71), channel_id=1, source_target_pairs={{4,8},{8,4},{5,9},{9,5},{6,10},{10,6},{7,11},{11,7},{20,24},{24,20... | collective-permute-start | bytes 884744 | tf_op jit(solution)/shard_map/ppermute | solution.py:434

commit v6 on v5

--- a/solution.py
+++ b/solution.py
@@ -14,7 +14,7 @@
 NSEL = 3
 SB = 4
 DEPTH = 3
-MOVED = 3
+MOVED = 2
 SPLIT = MOVED * HD
 ROWS = FR_DEV * TOK_FRAME
 WINDOW = FR_DEV + 2 * REACH
@@ -467,7 +467,7 @@
         out_specs=tuple(pl.BlockSpec(memory_space=pltpu.VMEM) for _ in outs),
         scratch_shapes=scratch,
         compiler_params=pltpu.CompilerParams(vmem_limit_bytes=16 << 20),
-        cost_estimate=pl.CostEstimate(flops=flops // 1000, bytes_accessed=0, transcendentals=0),
+        cost_estimate=pl.CostEstimate(flops=flops, bytes_accessed=0, transcendentals=0),
         name=name,
     )(*scalars, *arrays)
 
@@ -491,7 +491,6 @@
     )
     f_one, f_two = swap(y_send, y_send)
     k_one, k_two = swap(k_send, k_send)
-    v_one, v_two = swap(v_send, v_send)
     table = lookup(offsets, spatial)
     query, grad, key, value, bias, moved_bias = call(
         stage_kernel, "stage", (table,), (queries, grad_out, keys, values),
@@ -509,6 +508,9 @@
         [full(FR_DEV, 3, 3 * side, TOK_FRAME)], 2 * MOVED * unit,
     )
     s_far, s_other = swap_far(s_far, s_other)
+    v_send, mine = lax.optimization_barrier((v_send, mine))
+    v_one, v_two = swap(v_send, v_send)
+    k_one, k_two, s_far, s_other = lax.optimization_barrier((k_one, k_two, s_far, s_other))
     windows = low(DEPTH, 3 * ROWS, HD)
     accums = full(DEPTH, 3 * ROWS, HD)
     pairs = low(heads, FR_DEV, SLOTS, TOK_FRAME)
@@ -520,7 +522,6 @@
         [windows, accums], 2 * heads * unit,
     )
     rv_one, rv_two = swap(gv_one, gv_two)
-    v_one, s_far = lax.optimization_barrier((v_one, s_far))
     score_low, gk_own, gk_one, gk_two = call(
         keys_kernel, "keys_part", (table,), (query, grad, value, prob_low, v_one, v_two),
         (pairs, full(ROWS, rest), low(ROWS, rest), low(ROWS, rest)),

time: 71.2 us -> 58.6 us (0.82)
  the two profiles are of different devices: /device:TPU:10 before, /device:TPU:0 now
where the time goes in v6:
time: 58.6 us; the launch traced here: 58.3 us
  starting transfers between devices  23.6 us (40%)
  Pallas kernels  19.9 us (34%)
  waiting for transfers between devices  10.5 us (18%)
  other arithmetic  2.84 us (5%)
  between operations  0.79 us (1%)
  local copies, waits for them, and re-layouts  0.73 us (1%)
    pallas_call x8, Pallas kernels, call(): pl.pallas_call(kernel, out_shape=outs, in_specs=[pl.BlockSpec(memory_spac...  19.9 us
    ppermute x6, starting transfers between devices, swap(): lax.ppermute(one, 'frames', both_ways(first))  15.9 us
    ppermute x6, waiting for transfers between devices, swap(): lax.ppermute(one, 'frames', both_ways(first))  10.5 us
    ppermute x6, starting transfers between devices, swap(): lax.ppermute(two, 'frames', both_ways(second))  4.22 us
    ppermute x1, starting transfers between devices, swap_far(): far = lax.ppermute(far, 'frames', both_ways(near))  3.43 us
  transfers between devices with their start and end apart: 13, of which 4 were waited for; matrix products, arithmetic and copies ran while one was open for 4% of the time, Pallas kernels for 32%

profile of v6, /device:TPU:0, one launch (start us, length us, event | category | flops | bytes accessed | tf_op | source)
XLA Modules:
  0.0 58.3 jit_solution(8194168032930396057)
XLA Ops:
  0.6 0.0 copy-start.1
  0.6 0.0 copy-start
  0.7 1.4 %pack.1 = (bf16[2,384,256]{2,1,0:T(8,128)(2,1)S(1)}, bf16[384,512]{1,0:T(8,128)(2,1)S(1)}, bf16[384,512]{1,0:T(8,128)(2,1)S(1)}) custom-call(bf16[384,768]{1,0:T(8,128)(2,1)} %queries.1, bf16[384,768]{1,0:T(8,128)(2,1)} %grad_out.1, bf16[384,768]{1,0:T(8,128)(2,1)} %keys.1, bf16[384,768]{1,0:T(8,128)(2,1)} %values.1), custom_call_target="tpu_custom_call" | custom-call | flops 56623104 | tf_op jit(solution)/shard_map/pack/pallas_call | solution.py:462
  2.0 0.7 %collective-permute-start.1 = (bf16[2,384,256]{2,1,0:T(8,128)(2,1)S(1)}, bf16[2,384,256]{2,1,0:T(8,128)(2,1)S(1)}, u32[]{:S(2)}, u32[]{:S(2)}) collective-permute-start(bf16[2,384,256]{2,1,0:T(8,128)(2,1)S(1)} %get-tuple-element.50), channel_id=1, source_target_pairs={{4,8},{8,4},{5,9},{9,5},{6,10},{10,6},{7,11},{11,7},{20,24},{24,20... | collective-permute-start | bytes 1179656 | tf_op jit(solution)/shard_map/ppermute | solution.py:434
  2.7 5.9 %collective-permute-start = (bf16[2,384,256]{2,1,0:T(8,128)(2,1)S(1)}, bf16[2,384,256]{2,1,0:T(8,128)(2,1)S(1)}, u32[]{:S(2)}, u32[]{:S(2)}) collective-permute-start(bf16[2,384,256]{2,1,0:T(8,128)(2,1)S(1)} %get-tuple-element.50), channel_id=1, source_target_pairs={{0,4},{4,0},{8,12},{12,8},{1,5},{5,1},{9,13},{13,9},{2,6},{6,2},{1... | collective-permute-start | bytes 1179656 | tf_op jit(solution)/shard_map/ppermute | solution.py:433
  8.6 0.7 %collective-permute-start.3 = (bf16[384,512]{1,0:T(8,128)(2,1)S(1)}, bf16[384,512]{1,0:T(8,128)(2,1)S(1)}, u32[]{:S(2)}, u32[]{:S(2)}) collective-permute-start(bf16[384,512]{1,0:T(8,128)(2,1)S(1)} %get-tuple-element.53), channel_id=1, source_target_pairs={{4,8},{8,4},{5,9},{9,5},{6,10},{10,6},{7,11},{11,7},{20,24},{24,20... | collective-permute-start | bytes 1179656 | tf_op jit(solution)/shard_map/ppermute | solution.py:434
  9.3 1.8 %collective-permute-start.2 = (bf16[384,512]{1,0:T(8,128)(2,1)S(1)}, bf16[384,512]{1,0:T(8,128)(2,1)S(1)}, u32[]{:S(2)}, u32[]{:S(2)}) collective-permute-start(bf16[384,512]{1,0:T(8,128)(2,1)S(1)} %get-tuple-element.53), channel_id=1, source_target_pairs={{0,4},{4,0},{8,12},{12,8},{1,5},{5,1},{9,13},{13,9},{2,6},{6,2},{1... | collective-permute-start | bytes 1179656 | tf_op jit(solution)/shard_map/ppermute | solution.py:433
  11.0 0.0 copy-done.1
  11.1 0.1 pad_dynamic-slice_fusion.1
  11.1 0.1 copy.10
  11.2 0.1 reshape.12
  11.3 0.0 copy-done
  11.3 0.1 pad_dynamic-slice_fusion
  11.4 0.2 copy.11
  11.6 0.1 reshape.13
  11.7 0.1 concatenate.12.table
  11.8 2.2 %stage.1 = (bf16[384,768]{1,0:T(8,128)(2,1)S(1)}, bf16[384,768]{1,0:T(8,128)(2,1)S(1)}, bf16[384,768]{1,0:T(8,128)(2,1)S(1)}, bf16[384,768]{1,0:T(8,128)(2,1)S(1...) custom-call(s32[309]{0:T(512)S(1)} %concatenate.12.table, bf16[384,768]{1,0:T(8,128)(2,1)} %queries.1, ...), custom_call_target="tpu_custom_call" | custom-call | flops 56623104 | tf_op jit(solution)/shard_map/stage/pallas_call | solution.py:462
  14.0 0.0 collective-permute-done.1.f_two
  14.0 4.6 %collective-permute-done.f_one = bf16[2,384,256]{2,1,0:T(8,128)(2,1)S(1)} collective-permute-done((bf16[2,384,256]{2,1,0:T(8,128)(2,1)S(1)}, bf16[2,384,256]{2,1,0:T(8,128)(2,1)S(1)}, u32[]{:S(2)}, u32[]{:S(2)}) %collective-permute-start) | collective-permute-done | bytes 393248 | tf_op jit(solution)/shard_map/ppermute | solution.py:433
  18.6 2.6 %stats.1 = (f32[6,2,2,192,192]{4,3,2,1,0:T(8,128)S(1)}, f32[6,2,2,192,192]{4,3,2,1,0:T(8,128)S(1)}, f32[3,12,192]{2,1,0:T(8,128)S(1)}, f32[64,192]{1,0:T(8,128)S...) custom-call(s32[309]{0:T(512)S(1)} %concatenate.12.table, ...), custom_call_target="tpu_custom_call" | custom-call | flops 226492416 | tf_op jit(solution)/shard_map/stats/pallas_call | solution.py:462
  21.2 3.4 %collective-permute-start.4 = (f32[3,4,192]{2,1,0:T(4,128)S(1)}, f32[3,4,192]{2,1,0:T(4,128)S(1)}, u32[]{:S(2)}, u32[]{:S(2)}) collective-permute-start(f32[3,4,192]{2,1,0:T(4,128)S(1)} %get-tuple-element.55), channel_id=1, source_target_pairs={{0,8},{8,0},{4,12},{12,4},{1,9},{9,1},{5,13},{13,5},{2,10},{10,2},... | collective-permute-start | bytes 27656 | tf_op jit(solution)/shard_map/ppermute | solution.py:442
  24.6 0.7 %collective-permute-start.6 = (bf16[384,512]{1,0:T(8,128)(2,1)S(1)}, bf16[384,512]{1,0:T(8,128)(2,1)S(1)}, u32[]{:S(2)}, u32[]{:S(2)}) collective-permute-start(bf16[384,512]{1,0:T(8,128)(2,1)S(1)} %get-tuple-element.63), channel_id=1, source_target_pairs={{4,8},{8,4},{5,9},{9,5},{6,10},{10,6},{7,11},{11,7},{20,24},{24,20... | collective-permute-start | bytes 1179656 | tf_op jit(solution)/shard_map/ppermute | solution.py:434
  25.3 1.9 %collective-permute-start.5 = (bf16[384,512]{1,0:T(8,128)(2,1)S(1)}, bf16[384,512]{1,0:T(8,128)(2,1)S(1)}, u32[]{:S(2)}, u32[]{:S(2)}) collective-permute-start(bf16[384,512]{1,0:T(8,128)(2,1)S(1)} %get-tuple-element.63), channel_id=1, source_target_pairs={{0,4},{4,0},{8,12},{12,8},{1,5},{5,1},{9,13},{13,9},{2,6},{6,2},{1... | collective-permute-start | bytes 1179656 | tf_op jit(solution)/shard_map/ppermute | solution.py:433
  27.1 0.0 collective-permute-done.3.k_two
  27.1 0.0 collective-permute-done.2.k_one
  27.1 0.0 collective-permute-done.4.s_far
  27.1 4.9 %values_part.1 = (bf16[4,2,576,128]{3,2,1,0:T(8,128)(2,1)S(1)}, bf16[4,2,576,192]{3,2,1,0:T(8,128)(2,1)S(1)}, f32[384,512]{1,0:T(8,128)S(1)}, bf16[416,512]{1,0:T(8,128)(2,1)S(1)}, bf16[416,512]{1,0:T(8,128)(2,1)S(1)}) custom-call(s32[309]{0:T(512)S(1)} %concatenate.12.table, bf16[384,768]{1,0:T(8,128)(2,1)S(1)} %get-tuple-element.47.queries, ...), custom_call_target="tpu_custom_call" | custom-call | flops 452984832 | tf_op jit(solution)/shard_map/values_part/pallas_call | solution.py:462
  32.1 1.6 %collective-permute-start.7 = (bf16[416,512]{1,0:T(8,128)(2,1)S(1)}, bf16[416,512]{1,0:T(8,128)(2,1)S(1)}, u32[]{:S(2)}, u32[]{:S(2)}) collective-permute-start(bf16[416,512]{1,0:T(8,128)(2,1)S(1)} %get-tuple-element.69), channel_id=1, source_target_pairs={{0,4},{4,0},{8,12},{12,8},{1,5},{5,1},{9,13},{13,9},{2,6},{6,2},{1... | collective-permute-start | bytes 1277960 | tf_op jit(solution)/shard_map/ppermute | solution.py:433
  33.7 0.9 %collective-permute-start.8 = (bf16[416,512]{1,0:T(8,128)(2,1)S(1)}, bf16[416,512]{1,0:T(8,128)(2,1)S(1)}, u32[]{:S(2)}, u32[]{:S(2)}) collective-permute-start(bf16[416,512]{1,0:T(8,128)(2,1)S(1)} %get-tuple-element.70), channel_id=1, source_target_pairs={{4,8},{8,4},{5,9},{9,5},{6,10},{10,6},{7,11},{11,7},{20,24},{24,20... | collective-permute-start | bytes 1277960 | tf_op jit(solution)/shard_map/ppermute | solution.py:434
  34.6 0.0 collective-permute-done.6.v_two
  34.6 1.9 %collective-permute-done.5.v_one = bf16[384,512]{1,0:T(8,128)(2,1)S(1)} collective-permute-done((bf16[384,512]{1,0:T(8,128)(2,1)S(1)}, bf16[384,512]{1,0:T(8,128)(2,1)S(1)}, u32[]{:S(2)}, u32[]{:S(2)}) %collective-permute-start.5) | collective-permute-done | bytes 393248 | tf_op jit(solution)/shard_map/ppermute | solution.py:433
  36.5 4.7 %keys_part.1 = (bf16[4,2,576,192]{3,2,1,0:T(8,128)(2,1)S(1)}, f32[384,512]{1,0:T(8,128)S(1)}, bf16[384,512]{1,0:T(8,128)(2,1)S(1)}, bf16[384,512]{1,0:T(8,128)(2,1)S(1)}) custom-call(s32[309]{0:T(512)S(1)} %concatenate.12.table, bf16[384,768]{1,0:T(8,128)(2,1)S(1)} %get-tuple-element.47.queries, bf16[384,768]{1,0:T(8,128)(2,1)S(1)} %get-tuple-element.48.grad_out, ...), custom_call_target="tpu_custom_call" | custom-call | flops 452984832 | tf_op jit(solution)/shard_map/keys_part/pallas_call | solution.py:462
  41.2 2.3 %collective-permute-start.11 = (bf16[384,512]{1,0:T(8,128)(2,1)S(1)}, bf16[384,512]{1,0:T(8,128)(2,1)S(1)}, u32[]{:S(2)}, u32[]{:S(2)}) collective-permute-start(bf16[384,512]{1,0:T(8,128)(2,1)S(1)} %get-tuple-element.87), channel_id=1, source_target_pairs={{0,4},{4,0},{8,12},{12,8},{1,5},{5,1},{9,13},{13,9},{2,6},{6,2},{1... | collective-permute-start | bytes 1179656 | tf_op jit(solution)/shard_map/ppermute | solution.py:433
  43.4 0.7 %collective-permute-start.12 = (bf16[384,512]{1,0:T(8,128)(2,1)S(1)}, bf16[384,512]{1,0:T(8,128)(2,1)S(1)}, u32[]{:S(2)}, u32[]{:S(2)}) collective-permute-start(bf16[384,512]{1,0:T(8,128)(2,1)S(1)} %get-tuple-element.88), channel_id=1, source_target_pairs={{4,8},{8,4},{5,9},{9,5},{6,10},{10,6},{7,11},{11,7},{20,24},{24,20... | collective-permute-start | bytes 1179656 | tf_op jit(solution)/shard_map/ppermute | solution.py:434
  44.1 1.5 %collective-permute-done.7.r_one.rv_one = bf16[416,512]{1,0:T(8,128)(2,1)S(1)} collective-permute-done((bf16[416,512]{1,0:T(8,128)(2,1)S(1)}, bf16[416,512]{1,0:T(8,128)(2,1)S(1)}, u32[]{:S(2)}, u32[]{:S(2)}) %collective-permute-start.7) | collective-permute-done | bytes 426016 | tf_op jit(solution)/shard_map/ppermute | solution.py:433
  45.6 0.0 collective-permute-done.8.r_two.rv_two
  45.6 1.1 %back.1 = (bf16[6,2,2,192,192]{4,3,2,1,0:T(8,128)(2,1)S(1)}, bf16[6,2,2,192,192]{4,3,2,1,0:T(8,128)(2,1)S(1)}, f32[12,192]{1,0:T(8,128)S(1)}, f32[12,192]{1,0:T(...) custom-call(s32[309]{0:T(512)S(1)} %concatenate.12.table, ...), custom_call_target="tpu_custom_call" | custom-call | flops 113246208 | tf_op jit(solution)/shard_map/back/pallas_call | solution.py:462
  46.8 2.5 %collective-permute-start.9 = (bf16[384,256]{1,0:T(8,128)(2,1)S(1)}, bf16[384,256]{1,0:T(8,128)(2,1)S(1)}, u32[]{:S(2)}, u32[]{:S(2)}) collective-permute-start(bf16[384,256]{1,0:T(8,128)(2,1)S(1)} %get-tuple-element.78), channel_id=1, source_target_pairs={{0,4},{4,0},{8,12},{12,8},{1,5},{5,1},{9,13},{13,9},{2,6},{6,2},{1... | collective-permute-start | bytes 589832 | tf_op jit(solution)/shard_map/ppermute | solution.py:433
  49.3 0.7 %collective-permute-start.10 = (bf16[384,256]{1,0:T(8,128)(2,1)S(1)}, bf16[384,256]{1,0:T(8,128)(2,1)S(1)}, u32[]{:S(2)}, u32[]{:S(2)}) collective-permute-start(bf16[384,256]{1,0:T(8,128)(2,1)S(1)} %get-tuple-element.79), channel_id=1, source_target_pairs={{4,8},{8,4},{5,9},{9,5},{6,10},{10,6},{7,11},{11,7},{20,24},{24,20... | collective-permute-start | bytes 589832 | tf_op jit(solution)/shard_map/ppermute | solution.py:434
  50.0 1.9 %home.1 = (f32[384,256]{1,0:T(8,128)S(1)}, bf16[384,256]{1,0:T(8,128)(2,1)S(1)}, bf16[384,256]{1,0:T(8,128)(2,1)S(1)}) custom-call(s32[309]{0:T(512)S(1)} %concatenate.12.table, bf16[384,768]{1,0:T(8,128)(2,1)S(1)} %get-tuple-element.47.queries, bf16[384,768]{1,0:T(8,128)(2,1)S(1)} %get-tuple-element.48.grad_out, ...), custom_call_target="tpu_custom_call" | custom-call | flops 339738624 | tf_op jit(solution)/shard_map/home/pallas_call | solution.py:462
  51.8 1.2 %rest.1 = (bf16[384,512]{1,0:T(8,128)(2,1)S(1)}, bf16[384,512]{1,0:T(8,128)(2,1)S(1)}, f32[384,512]{1,0:T(8,128)S(1)}) custom-call(bf16[384,768]{1,0:T(8,128)(2,1)S(1)} %get-tuple-element.47.queries, bf16[384,768]{1,0:T(8,128)(2,1)S(1)} %get-tuple-element.48.grad_out, bf16[4,2,576,128]{3,2,1,0:T(8,128)(2,1)S(1)} %get-tuple-element.80.chosen_in, ...), custom_call_target="tpu_custom_call" | custom-call | flops 452984832 | tf_op jit(solution)/shard_map/rest/pallas_call | solution.py:462
  53.0 0.9 %pad_maximum_fusion.2 = bf16[384,768]{1,0:T(8,128)(2,1)} fusion(bf16[384,512]{1,0:T(8,128)(2,1)S(1)} %get-tuple-element.90, bf16[384,256]{1,0:T(8,128)(2,1)S(1)} %get-tuple-element.89), kind=kLoop, calls=%fused_computation.3 | loop fusion | flops 1179648 | bytes 1179648 | tf_op jit(solution)/shard_map/concatenate | solution.py:558
  53.8 2.5 %collective-permute-done.9 = bf16[384,256]{1,0:T(8,128)(2,1)S(1)} collective-permute-done((bf16[384,256]{1,0:T(8,128)(2,1)S(1)}, bf16[384,256]{1,0:T(8,128)(2,1)S(1)}, u32[]{:S(2)}, u32[]{:S(2)}) %collective-permute-start.9) | collective-permute-done | bytes 196640 | tf_op jit(solution)/shard_map/ppermute | solution.py:433
  56.3 0.0 collective-permute-done.10
  56.3 0.1 add_convert_fusion.1
  56.4 0.9 %pad_maximum_fusion = bf16[384,768]{1,0:T(8,128)(2,1)} fusion(bf16[384,512]{1,0:T(8,128)(2,1)S(1)} %get-tuple-element.84, bf16[384,256]{1,0:T(8,128)(2,1)S(1)} %add_convert_fusion.1), kind=kLoop, calls=%fused_computation.1 | loop fusion | flops 1179648 | bytes 1179648 | tf_op jit(solution)/shard_map/concatenate | solution.py:556
  57.3 0.0 collective-permute-done.11
  57.3 0.0 collective-permute-done.12
  57.3 0.2 add_convert_fusion
  57.5 0.9 %pad_maximum_fusion.1 = bf16[384,768]{1,0:T(8,128)(2,1)} fusion(bf16[384,512]{1,0:T(8,128)(2,1)S(1)} %add_convert_fusion, bf16[384,256]{1,0:T(8,128)(2,1)S(1)} %get-tuple-element.85), kind=kLoop, calls=%fused_computation.2 | loop fusion | flops 1179648 | bytes 1179648 | tf_op jit(solution)/shard_map/concatenate | solution.py:557
  (1 shorter events, 0.0 us)
Async XLA Ops:
  0.6 10.4 %copy-start.1 = (s32[8,3]{0,1:T(4,128)S(1)}, s32[8,3]{0,1:T(4,128)}, u32[]{:S(2)}) copy-start(s32[8,3]{0,1:T(4,128)} %param.10) | copy-start | bytes 292
  0.6 10.7 %copy-start = (s32[8,3,4,4]{0,3,2,1:T(4,128)S(1)}, s32[8,3,4,4]{0,3,2,1:T(4,128)}, u32[]{:S(2)}) copy-start(s32[8,3,4,4]{0,3,2,1:T(4,128)} %param.11) | copy-start | bytes 4612
  2.0 12.0 %collective-permute-start.1 = (bf16[2,384,256]{2,1,0:T(8,128)(2,1)S(1)}, bf16[2,384,256]{2,1,0:T(8,128)(2,1)S(1)}, u32[]{:S(2)}, u32[]{:S(2)}) collective-permute-start(bf16[2,384,256]{2,1,0:T(8,128)(2,1)S(1)} %get-tuple-element.50), channel_id=1, source_target_pairs={{4,8},{8,4},{5,9},{9,5},{6,10},{10,6},{7,11},{11,7},{20,24},{24,20... | collective-permute-start | bytes 1179656 | tf_op jit(solution)/shard_map/ppermute | solution.py:434
  2.7 15.9 %collective-permute-start = (bf16[2,384,256]{2,1,0:T(8,128)(2,1)S(1)}, bf16[2,384,256]{2,1,0:T(8,128)(2,1)S(1)}, u32[]{:S(2)}, u32[]{:S(2)}) collective-permute-start(bf16[2,384,256]{2,1,0:T(8,128)(2,1)S(1)} %get-tuple-element.50), channel_id=1, source_target_pairs={{0,4},{4,0},{8,12},{12,8},{1,5},{5,1},{9,13},{13,9},{2,6},{6,2},{1... | collective-permute-start | bytes 1179656 | tf_op jit(solution)/shard_map/ppermute | solution.py:433
  8.6 18.5 %collective-permute-start.3 = (bf16[384,512]{1,0:T(8,128)(2,1)S(1)}, bf16[384,512]{1,0:T(8,128)(2,1)S(1)}, u32[]{:S(2)}, u32[]{:S(2)}) collective-permute-start(bf16[384,512]{1,0:T(8,128)(2,1)S(1)} %get-tuple-element.53), channel_id=1, source_target_pairs={{4,8},{8,4},{5,9},{9,5},{6,10},{10,6},{7,11},{11,7},{20,24},{24,20... | collective-permute-start | bytes 1179656 | tf_op jit(solution)/shard_map/ppermute | solution.py:434
  9.3 17.8 %collective-permute-start.2 = (bf16[384,512]{1,0:T(8,128)(2,1)S(1)}, bf16[384,512]{1,0:T(8,128)(2,1)S(1)}, u32[]{:S(2)}, u32[]{:S(2)}) collective-permute-start(bf16[384,512]{1,0:T(8,128)(2,1)S(1)} %get-tuple-element.53), channel_id=1, source_target_pairs={{0,4},{4,0},{8,12},{12,8},{1,5},{5,1},{9,13},{13,9},{2,6},{6,2},{1... | collective-permute-start | bytes 1179656 | tf_op jit(solution)/shard_map/ppermute | solution.py:433
  21.2 6.0 %collective-permute-start.4 = (f32[3,4,192]{2,1,0:T(4,128)S(1)}, f32[3,4,192]{2,1,0:T(4,128)S(1)}, u32[]{:S(2)}, u32[]{:S(2)}) collective-permute-start(f32[3,4,192]{2,1,0:T(4,128)S(1)} %get-tuple-element.55), channel_id=1, source_target_pairs={{0,8},{8,0},{4,12},{12,4},{1,9},{9,1},{5,13},{13,5},{2,10},{10,2},... | collective-permute-start | bytes 27656 | tf_op jit(solution)/shard_map/ppermute | solution.py:442
  24.6 10.0 %collective-permute-start.6 = (bf16[384,512]{1,0:T(8,128)(2,1)S(1)}, bf16[384,512]{1,0:T(8,128)(2,1)S(1)}, u32[]{:S(2)}, u32[]{:S(2)}) collective-permute-start(bf16[384,512]{1,0:T(8,128)(2,1)S(1)} %get-tuple-element.63), channel_id=1, source_target_pairs={{4,8},{8,4},{5,9},{9,5},{6,10},{10,6},{7,11},{11,7},{20,24},{24,20... | collective-permute-start | bytes 1179656 | tf_op jit(solution)/shard_map/ppermute | solution.py:434
  25.3 11.2 %collective-permute-start.5 = (bf16[384,512]{1,0:T(8,128)(2,1)S(1)}, bf16[384,512]{1,0:T(8,128)(2,1)S(1)}, u32[]{:S(2)}, u32[]{:S(2)}) collective-permute-start(bf16[384,512]{1,0:T(8,128)(2,1)S(1)} %get-tuple-element.63), channel_id=1, source_target_pairs={{0,4},{4,0},{8,12},{12,8},{1,5},{5,1},{9,13},{13,9},{2,6},{6,2},{1... | collective-permute-start | bytes 1179656 | tf_op jit(solution)/shard_map/ppermute | solution.py:433
  32.1 13.5 %collective-permute-start.7 = (bf16[416,512]{1,0:T(8,128)(2,1)S(1)}, bf16[416,512]{1,0:T(8,128)(2,1)S(1)}, u32[]{:S(2)}, u32[]{:S(2)}) collective-permute-start(bf16[416,512]{1,0:T(8,128)(2,1)S(1)} %get-tuple-element.69), channel_id=1, source_target_pairs={{0,4},{4,0},{8,12},{12,8},{1,5},{5,1},{9,13},{13,9},{2,6},{6,2},{1... | collective-permute-start | bytes 1277960 | tf_op jit(solution)/shard_map/ppermute | solution.py:433
  33.7 11.9 %collective-permute-start.8 = (bf16[416,512]{1,0:T(8,128)(2,1)S(1)}, bf16[416,512]{1,0:T(8,128)(2,1)S(1)}, u32[]{:S(2)}, u32[]{:S(2)}) collective-permute-start(bf16[416,512]{1,0:T(8,128)(2,1)S(1)} %get-tuple-element.70), channel_id=1, source_target_pairs={{4,8},{8,4},{5,9},{9,5},{6,10},{10,6},{7,11},{11,7},{20,24},{24,20... | collective-permute-start | bytes 1277960 | tf_op jit(solution)/shard_map/ppermute | solution.py:434
  41.2 16.1 %collective-permute-start.11 = (bf16[384,512]{1,0:T(8,128)(2,1)S(1)}, bf16[384,512]{1,0:T(8,128)(2,1)S(1)}, u32[]{:S(2)}, u32[]{:S(2)}) collective-permute-start(bf16[384,512]{1,0:T(8,128)(2,1)S(1)} %get-tuple-element.87), channel_id=1, source_target_pairs={{0,4},{4,0},{8,12},{12,8},{1,5},{5,1},{9,13},{13,9},{2,6},{6,2},{1... | collective-permute-start | bytes 1179656 | tf_op jit(solution)/shard_map/ppermute | solution.py:433
  43.4 13.9 %collective-permute-start.12 = (bf16[384,512]{1,0:T(8,128)(2,1)S(1)}, bf16[384,512]{1,0:T(8,128)(2,1)S(1)}, u32[]{:S(2)}, u32[]{:S(2)}) collective-permute-start(bf16[384,512]{1,0:T(8,128)(2,1)S(1)} %get-tuple-element.88), channel_id=1, source_target_pairs={{4,8},{8,4},{5,9},{9,5},{6,10},{10,6},{7,11},{11,7},{20,24},{24,20... | collective-permute-start | bytes 1179656 | tf_op jit(solution)/shard_map/ppermute | solution.py:434
  46.8 9.6 %collective-permute-start.9 = (bf16[384,256]{1,0:T(8,128)(2,1)S(1)}, bf16[384,256]{1,0:T(8,128)(2,1)S(1)}, u32[]{:S(2)}, u32[]{:S(2)}) collective-permute-start(bf16[384,256]{1,0:T(8,128)(2,1)S(1)} %get-tuple-element.78), channel_id=1, source_target_pairs={{0,4},{4,0},{8,12},{12,8},{1,5},{5,1},{9,13},{13,9},{2,6},{6,2},{1... | collective-permute-start | bytes 589832 | tf_op jit(solution)/shard_map/ppermute | solution.py:433
  49.3 7.0 %collective-permute-start.10 = (bf16[384,256]{1,0:T(8,128)(2,1)S(1)}, bf16[384,256]{1,0:T(8,128)(2,1)S(1)}, u32[]{:S(2)}, u32[]{:S(2)}) collective-permute-start(bf16[384,256]{1,0:T(8,128)(2,1)S(1)} %get-tuple-element.79), channel_id=1, source_target_pairs={{4,8},{8,4},{5,9},{9,5},{6,10},{10,6},{7,11},{11,7},{20,24},{24,20... | collective-permute-start | bytes 589832 | tf_op jit(solution)/shard_map/ppermute | solution.py:434

commit v7 on v6

--- a/solution.py
+++ b/solution.py
@@ -32,6 +32,7 @@
 COUNT = FIRST + 2
 NOTES = 32
 SIDE = FR_DEV * MOVED
+FAR = (0, 1, 4, 5)
 
 
 def dot(lhs, rhs, dims):
@@ -225,68 +226,82 @@
             value_out[rows, far_column] = total.astype(value_out.dtype)
 
 
-def view_of(query, own, one, two, part, head):
-    rows = rows_of(query % FR_DEV)
-    column = column_of(head)
-    if query // FR_DEV == 1:
-        return own[rows, column]
-    return (one if query < FR_DEV else two)[part, rows, column]
+def pair_stats(table, window, key, index, query, grad, keys, values, bias, outs):
+    masked_out, grad_prob_out, parts = outs
+    active, _ = pair_of(table, window, key)
+
+    @pl.when(active)
+    def _():
+        for head in range(MOVED):
+            column = column_of(head)
+            row = slice(index * MOVED + head, index * MOVED + head + 1)
+            rows = rows_of(key)
+            masked = dot(keys[rows, column], query(head), NT) * SCALE2 + bias[window, key]
+            highest = rounded(jnp.max(masked, 0, keepdims=True))
+            raised = jnp.exp2(masked - highest)
+            grad_prob = dot(values[rows, column], grad(head), NT)
+            masked_out[index, key, head] = masked
+            grad_prob_out[index, key, head] = grad_prob
+            parts[key, 0, row] = highest
+            parts[key, 1, row] = jnp.sum(raised, 0, keepdims=True)
+            parts[key, 2, row] = jnp.sum(raised * grad_prob, 0, keepdims=True)
+
+    @pl.when(jnp.logical_not(active))
+    def _():
+        rows = slice(index * MOVED, (index + 1) * MOVED)
+        parts[key, 0, rows] = jnp.full((MOVED, TOK_FRAME), NEG, jnp.float32)
+        parts[key, 1, rows] = jnp.zeros((MOVED, TOK_FRAME), jnp.float32)
+        parts[key, 2, rows] = jnp.zeros((MOVED, TOK_FRAME), jnp.float32)
+
+
+def own_stats_kernel(
+    table, queries, grad_out, keys, values, bias,
+    masked_out, grad_prob_out, stats_out,
+    parts,
+):
+    for index in range(FR_DEV):
+        for key in range(FR_DEV):
+            rows = rows_of(index)
+            pair_stats(
+                table, FR_DEV + index, key, index,
+                lambda head: queries[rows, column_of(head)],
+                lambda head: grad_out[rows, column_of(head)],
+                keys, values, bias, (masked_out, grad_prob_out, parts),
+            )
+    for index, each in enumerate(joined_stats([parts[key] for key in range(FR_DEV)])):
+        stats_out[index] = each
 
 
 def stats_kernel(
-    table, queries, grad_out, keys, values, bias, f_one, f_two,
+    table, keys, values, bias, own, f_one, f_two,
     masked_out, grad_prob_out, mine_out, one_out, two_out, far_out, other_out,
     parts,
 ):
-    for query in range(WINDOW):
+    for index, window in enumerate(FAR):
+        sent = f_one if window < FR_DEV else f_two
         for key in range(FR_DEV):
-            active, _ = pair_of(table, query, key)
-
-            @pl.when(active)
-            def _():
-                for head in range(MOVED):
-                    column = column_of(head)
-                    row = slice(query * MOVED + head, query * MOVED + head + 1)
-                    rows = rows_of(key)
-                    scores = dot(
-                        keys[rows, column], view_of(query, queries, f_one, f_two, 0, head), NT
-                    )
-                    masked = scores * SCALE2 + bias[query, key]
-                    highest = rounded(jnp.max(masked, 0, keepdims=True))
-                    raised = jnp.exp2(masked - highest)
-                    grad_prob = dot(
-                        values[rows, column], view_of(query, grad_out, f_one, f_two, 1, head), NT
-                    )
-                    masked_out[query, key, head] = masked
-                    grad_prob_out[query, key, head] = grad_prob
-                    parts[key, 0, row] = highest
-                    parts[key, 1, row] = jnp.sum(raised, 0, keepdims=True)
-                    parts[key, 2, row] = jnp.sum(raised * grad_prob, 0, keepdims=True)
-
-            @pl.when(jnp.logical_not(active))
-            def _():
-                rows = slice(query * MOVED, (query + 1) * MOVED)
-                parts[key, 0, rows] = jnp.full((MOVED, TOK_FRAME), NEG, jnp.float32)
-                parts[key, 1, rows] = jnp.zeros((MOVED, TOK_FRAME), jnp.float32)
-                parts[key, 2, rows] = jnp.zeros((MOVED, TOK_FRAME), jnp.float32)
-
-    highest, total, moment = joined_stats([parts[key] for key in range(FR_DEV)])
-    mine_out[0] = highest
-    mine_out[1] = total
-    mine_out[2] = moment
-    side = SIDE
+            rows = rows_of(window % FR_DEV)
+            pair_stats(
+                table, window, key, index,
+                lambda head: sent[0, rows, column_of(head)],
+                lambda head: sent[1, rows, column_of(head)],
+                keys, values, bias, (masked_out, grad_prob_out, parts),
+            )
+    far = joined_stats([parts[key] for key in range(FR_DEV)])
     rank = table[RANK] % 4
     swapped = (rank == 1) | (rank == 2)
-    for out, start in ((one_out, 0), (two_out, side)):
-        rows = slice(start, start + 2 * side)
+    for index in range(3):
+        mine_out[index, :SIDE] = far[index][:SIDE]
+        mine_out[index, SIDE : 2 * SIDE] = own[index]
+        mine_out[index, 2 * SIDE :] = far[index][SIDE:]
+        far_out[index] = jnp.where(swapped, far[index][SIDE:], far[index][:SIDE])
+        other_out[index] = jnp.where(swapped, far[index][:SIDE], far[index][SIDE:])
+    for out, start in ((one_out, 0), (two_out, SIDE)):
+        rows = slice(start, start + 2 * SIDE)
         out[...] = jnp.zeros_like(out)
-        notes = (highest[rows], *halves(total[rows]), *halves(moment[rows]))
+        notes = (mine_out[0, rows], *halves(mine_out[1, rows]), *halves(mine_out[2, rows]))
         for index, note in enumerate(notes):
-            out[index * 2 * side : (index + 1) * 2 * side] = note
-    for index in range(3):
-        whole = mine_out[index]
-        far_out[index] = jnp.where(swapped, whole[2 * side :], whole[:side])
-        other_out[index] = jnp.where(swapped, whole[:side], whole[2 * side :])
+            out[index * 2 * SIDE : (index + 1) * 2 * SIDE] = note
 
 
 def rounded(array):
@@ -325,10 +340,10 @@
     return highest, total, moment
 
 
-def finish_pair(query, key, head, masked, grad_probs, logs, deltas):
-    row = slice(query * MOVED + head, query * MOVED + head + 1)
-    prob = jnp.exp2(masked[query, key, head] - logs[row])
-    score_low = (prob * (grad_probs[query, key, head] - deltas[row])).astype(jnp.bfloat16)
+def finish_pair(window, index, key, head, masked, grad_probs, logs, deltas):
+    row = slice(window * MOVED + head, window * MOVED + head + 1)
+    prob = jnp.exp2(masked[index, key, head] - logs[row])
+    score_low = (prob * (grad_probs[index, key, head] - deltas[row])).astype(jnp.bfloat16)
     return prob.astype(jnp.bfloat16), score_low
 
 
@@ -361,19 +376,19 @@
         logs[rows] = highest + jnp.log2(total)
         deltas[rows] = moment / total
     accums[...] = jnp.zeros_like(accums)
-    for query in (0, 1, 4, 5):
+    for index, window in enumerate(FAR):
         for key in range(FR_DEV):
-            active, _ = pair_of(table, query, key)
+            active, _ = pair_of(table, window, key)
 
             @pl.when(active)
             def _():
                 for head in range(MOVED):
                     prob_low, score_low = finish_pair(
-                        query, key, head, masked, grad_probs, logs, deltas
+                        window, index, key, head, masked, grad_probs, logs, deltas
                     )
-                    prob_out[query, key, head] = prob_low
-                    score_out[query, key, head] = score_low
-                    accums[query // 4, rows_of(query % FR_DEV), column_of(head)] += dot(
+                    prob_out[index, key, head] = prob_low
+                    score_out[index, key, head] = score_low
+                    accums[index // FR_DEV, rows_of(index % FR_DEV), column_of(head)] += dot(
                         score_low, keys[rows_of(key), column_of(head)], TN
                     )
 
@@ -390,31 +405,33 @@
     query_out[...] = jnp.zeros_like(query_out)
     key_accum[...] = jnp.zeros_like(key_accum)
     value_accum[...] = jnp.zeros_like(value_accum)
-    for query in range(WINDOW):
+    for window in range(WINDOW):
+        rows = rows_of(window % FR_DEV)
+        near = window // FR_DEV == 1
+        sent = f_one if window < FR_DEV else f_two
         for key in range(FR_DEV):
-            active, _ = pair_of(table, query, key)
+            active, _ = pair_of(table, window, key)
 
             @pl.when(active)
             def _():
                 for head in range(MOVED):
                     column = column_of(head)
-                    rows = rows_of(key)
-                    if query // FR_DEV == 1:
+                    if near:
+                        query = queries[rows, column]
+                        grad = grad_out[rows, column]
                         prob_low, score_low = finish_pair(
-                            query, key, head, masked, grad_probs, logs, deltas
+                            window, window - FR_DEV, key, head, masked, grad_probs, logs, deltas
                         )
-                        query_out[rows_of(query % FR_DEV), column] += dot(
-                            score_low, keys[rows, column], TN
+                        query_out[rows, column] += dot(
+                            score_low, keys[rows_of(key), column], TN
                         )
                     else:
-                        prob_low = prob_in[query, key, head]
-                        score_low = score_in[query, key, head]
-                    key_accum[rows, column] += dot(
-                        score_low, view_of(query, queries, f_one, f_two, 0, head), NN
-                    )
-                    value_accum[rows, column] += dot(
-                        prob_low, view_of(query, grad_out, f_one, f_two, 1, head), NN
-                    )
+                        query = sent[0, rows, column]
+                        grad = sent[1, rows, column]
+                        prob_low = prob_in[FAR.index(window), key, head]
+                        score_low = score_in[FAR.index(window), key, head]
+                    key_accum[rows_of(key), column] += dot(score_low, query, NN)
+                    value_accum[rows_of(key), column] += dot(prob_low, grad, NN)
 
     query_out[...] = query_out[...] * SCALE
     key_out[...] = (key_accum[...] * SCALE).astype(key_out.dtype)
@@ -498,19 +515,25 @@
         + (full(FR_DEV, SLOTS, TOK_FRAME), full(WINDOW, FR_DEV, TOK_FRAME, TOK_FRAME)),
         [pltpu.SemaphoreType.DMA((4,))], unit, pltpu.HBM,
     )
-    grid = (WINDOW, FR_DEV, MOVED, TOK_FRAME, TOK_FRAME)
-    side = SIDE
+    near_grid = (FR_DEV, FR_DEV, MOVED, TOK_FRAME, TOK_FRAME)
+    far_grid = (len(FAR), FR_DEV, MOVED, TOK_FRAME, TOK_FRAME)
+    near_masked, near_grads, own_stats = call(
+        own_stats_kernel, "own_stats", (table,), (query, grad, key, value, moved_bias),
+        (full(*near_grid), full(*near_grid), full(3, SIDE, TOK_FRAME)),
+        [full(FR_DEV, 3, SIDE, TOK_FRAME)], MOVED * unit,
+    )
+    v_send, f_one, f_two, own_stats = lax.optimization_barrier(
+        (v_send, f_one, f_two, own_stats)
+    )
+    v_one, v_two = swap(v_send, v_send)
     note = full(2 * NOTES, TOK_FRAME)
     masked, grad_probs, mine, n_one, n_two, s_far, s_other = call(
-        stats_kernel, "stats", (table,), (query, grad, key, value, moved_bias, f_one, f_two),
-        (full(*grid), full(*grid), full(3, 3 * side, TOK_FRAME))
-        + (note, note) + (full(3, side, TOK_FRAME),) * 2,
-        [full(FR_DEV, 3, 3 * side, TOK_FRAME)], 2 * MOVED * unit,
+        stats_kernel, "stats", (table,), (key, value, moved_bias, own_stats, f_one, f_two),
+        (full(*far_grid), full(*far_grid), full(3, 3 * SIDE, TOK_FRAME), note, note)
+        + (full(3, SIDE, TOK_FRAME),) * 2,
+        [full(FR_DEV, 3, 2 * SIDE, TOK_FRAME)], 2 * MOVED * unit,
     )
     s_far, s_other = swap_far(s_far, s_other)
-    v_send, mine = lax.optimization_barrier((v_send, mine))
-    v_one, v_two = swap(v_send, v_send)
-    k_one, k_two, s_far, s_other = lax.optimization_barrier((k_one, k_two, s_far, s_other))
     windows = low(DEPTH, 3 * ROWS, HD)
     accums = full(DEPTH, 3 * ROWS, HD)
     pairs = low(heads, FR_DEV, SLOTS, TOK_FRAME)
@@ -527,19 +550,20 @@
         (pairs, full(ROWS, rest), low(ROWS, rest), low(ROWS, rest)),
         [windows, low(DEPTH, FR_DEV, SLOTS, HD), accums], 2 * heads * unit,
     )
+    gk_one, gk_two, s_far, s_other = lax.optimization_barrier((gk_one, gk_two, s_far, s_other))
     rk_one, rk_two = swap(gk_one, gk_two)
     gk_own, masked = lax.optimization_barrier((gk_own, masked))
     y_prob, y_score, logs, deltas, gq_one, gq_two = call(
         back_kernel, "back", (table,),
         (key, masked, grad_probs, mine, rv_one, rv_two, s_far, s_other),
-        (low(*grid), low(*grid), full(3 * side, TOK_FRAME), full(3 * side, TOK_FRAME))
+        (low(*far_grid), low(*far_grid)) + (full(3 * SIDE, TOK_FRAME),) * 2
         + (low(ROWS, SPLIT),) * 2,
         [full(2, ROWS, SPLIT), full(2, 2 * NOTES, TOK_FRAME)], MOVED * unit,
     )
     rq_one, rq_two = swap(gq_one, gq_two)
     gq_near, gk_near, gv_near = call(
         home_kernel, "home", (table,),
-        (query, grad, key, f_one, f_two, masked, grad_probs, y_prob, y_score, logs, deltas),
+        (query, grad, key, f_one, f_two, near_masked, near_grads, y_prob, y_score, logs, deltas),
         (full(ROWS, SPLIT), low(ROWS, SPLIT), low(ROWS, SPLIT)),
         [full(ROWS, SPLIT), full(ROWS, SPLIT)], 3 * MOVED * unit,
     )
@@ -553,8 +577,9 @@
         total = own + one.astype(jnp.float32) + two.astype(jnp.float32)
         return total.astype(jnp.bfloat16)
 
+    grad_keys = jnp.concatenate([gk_near, joined(gk_own, rk_one, rk_two)], 1)
+    grad_keys, gq_near = lax.optimization_barrier((grad_keys, gq_near))
     grad_queries = jnp.concatenate([joined(gq_near, rq_one, rq_two), gq_rest], 1)
-    grad_keys = jnp.concatenate([gk_near, joined(gk_own, rk_one, rk_two)], 1)
     grad_values = jnp.concatenate([gv_near, gv_rest], 1)
     return grad_queries, grad_keys, grad_values
 

time: 58.6 us -> 60.2 us (1.027)
  starting transfers between devices: 23.6 us -> 30.5 us
  waiting for transfers between devices: 10.5 us -> 3.71 us
  Pallas kernels: 19.9 us -> 21.3 us
    ppermute x6, waiting for transfers between devices: 10.5 us -> 0.54 us  [swap(): lax.ppermute(one, 'frames', both_ways(first))]
    ppermute x6, starting transfers between devices: 15.9 us -> 23.4 us  [swap(): lax.ppermute(one, 'frames', both_ways(first))]
    ppermute x1, waiting for transfers between devices: 0.01 us -> 3.16 us  [swap_far(): far = lax.ppermute(far, 'frames', both_ways(near))]
    pallas_call x8 -> x9, Pallas kernels: 19.9 us -> 21.3 us  [call(): pl.pallas_call(kernel, out_shape=outs, in_specs=[pl.BlockSpec(memory_spac...]
    ppermute x1, starting transfers between devices: 3.43 us -> 2.81 us  [swap_far(): far = lax.ppermute(far, 'frames', both_ways(near))]
  transfers between devices with their start and end apart: 13 -> 13, of which waited for: 4 -> 2; matrix products, arithmetic and copies ran while one was open for 4% -> 4% of each run, Pallas kernels for 32% -> 33%
where the time goes in v7:
time: 60.2 us; the launch traced here: 59.9 us
  starting transfers between devices  30.5 us (51%)
  Pallas kernels  21.3 us (35%)
  waiting for transfers between devices  3.71 us (6%)
  other arithmetic  2.82 us (5%)
  between operations  0.81 us (1%)
  local copies, waits for them, and re-layouts  0.73 us (1%)
    ppermute x6, starting transfers between devices, swap(): lax.ppermute(one, 'frames', both_ways(first))  23.4 us
    pallas_call x9, Pallas kernels, call(): pl.pallas_call(kernel, out_shape=outs, in_specs=[pl.BlockSpec(memory_spac...  21.3 us
    ppermute x6, starting transfers between devices, swap(): lax.ppermute(two, 'frames', both_ways(second))  4.22 us
    ppermute x1, waiting for transfers between devices, swap_far(): far = lax.ppermute(far, 'frames', both_ways(near))  3.16 us
    ppermute x1, starting transfers between devices, swap_far(): far = lax.ppermute(far, 'frames', both_ways(near))  2.81 us
  transfers between devices with their start and end apart: 13, of which 2 were waited for; matrix products, arithmetic and copies ran while one was open for 4% of the time, Pallas kernels for 33%

profile of v7, /device:TPU:0, one launch (start us, length us, event | category | flops | bytes accessed | tf_op | source)
XLA Modules:
  0.0 59.9 jit_solution(5226242144589889322)
XLA Ops:
  0.6 0.0 copy-start.1
  0.6 0.0 copy-start
  0.7 1.4 %pack.1 = (bf16[2,384,256]{2,1,0:T(8,128)(2,1)S(1)}, bf16[384,512]{1,0:T(8,128)(2,1)S(1)}, bf16[384,512]{1,0:T(8,128)(2,1)S(1)}) custom-call(bf16[384,768]{1,0:T(8,128)(2,1)} %queries.1, bf16[384,768]{1,0:T(8,128)(2,1)} %grad_out.1, bf16[384,768]{1,0:T(8,128)(2,1)} %keys.1, bf16[384,768]{1,0:T(8,128)(2,1)} %values.1), custom_call_target="tpu_custom_call" | custom-call | flops 56623104 | tf_op jit(solution)/shard_map/pack/pallas_call | solution.py:479
  2.0 3.1 %collective-permute-start = (bf16[2,384,256]{2,1,0:T(8,128)(2,1)S(1)}, bf16[2,384,256]{2,1,0:T(8,128)(2,1)S(1)}, u32[]{:S(2)}, u32[]{:S(2)}) collective-permute-start(bf16[2,384,256]{2,1,0:T(8,128)(2,1)S(1)} %get-tuple-element.58), channel_id=1, source_target_pairs={{0,4},{4,0},{8,12},{12,8},{1,5},{5,1},{9,13},{13,9},{2,6},{6,2},{1... | collective-permute-start | bytes 1179656 | tf_op jit(solution)/shard_map/ppermute | solution.py:450
  5.1 0.7 %collective-permute-start.1 = (bf16[2,384,256]{2,1,0:T(8,128)(2,1)S(1)}, bf16[2,384,256]{2,1,0:T(8,128)(2,1)S(1)}, u32[]{:S(2)}, u32[]{:S(2)}) collective-permute-start(bf16[2,384,256]{2,1,0:T(8,128)(2,1)S(1)} %get-tuple-element.58), channel_id=1, source_target_pairs={{4,8},{8,4},{5,9},{9,5},{6,10},{10,6},{7,11},{11,7},{20,24},{24,20... | collective-permute-start | bytes 1179656 | tf_op jit(solution)/shard_map/ppermute | solution.py:451
  5.8 4.4 %collective-permute-start.2 = (bf16[384,512]{1,0:T(8,128)(2,1)S(1)}, bf16[384,512]{1,0:T(8,128)(2,1)S(1)}, u32[]{:S(2)}, u32[]{:S(2)}) collective-permute-start(bf16[384,512]{1,0:T(8,128)(2,1)S(1)} %get-tuple-element.67), channel_id=1, source_target_pairs={{0,4},{4,0},{8,12},{12,8},{1,5},{5,1},{9,13},{13,9},{2,6},{6,2},{1... | collective-permute-start | bytes 1179656 | tf_op jit(solution)/shard_map/ppermute | solution.py:450
  10.2 0.7 %collective-permute-start.3 = (bf16[384,512]{1,0:T(8,128)(2,1)S(1)}, bf16[384,512]{1,0:T(8,128)(2,1)S(1)}, u32[]{:S(2)}, u32[]{:S(2)}) collective-permute-start(bf16[384,512]{1,0:T(8,128)(2,1)S(1)} %get-tuple-element.67), channel_id=1, source_target_pairs={{4,8},{8,4},{5,9},{9,5},{6,10},{10,6},{7,11},{11,7},{20,24},{24,20... | collective-permute-start | bytes 1179656 | tf_op jit(solution)/shard_map/ppermute | solution.py:451
  10.9 0.0 copy-done.1
  10.9 0.1 pad_dynamic-slice_fusion.1
  11.0 0.1 copy.10
  11.1 0.1 reshape.12
  11.2 0.0 copy-done
  11.2 0.1 pad_dynamic-slice_fusion
  11.3 0.2 copy.11
  11.4 0.1 reshape.13
  11.6 0.1 concatenate.12.table
  11.7 2.2 %stage.1 = (bf16[384,768]{1,0:T(8,128)(2,1)S(1)}, bf16[384,768]{1,0:T(8,128)(2,1)S(1)}, bf16[384,768]{1,0:T(8,128)(2,1)S(1)}, bf16[384,768]{1,0:T(8,128)(2,1)S(1...) custom-call(s32[309]{0:T(512)S(1)} %concatenate.12.table, bf16[384,768]{1,0:T(8,128)(2,1)} %queries.1, ...), custom_call_target="tpu_custom_call" | custom-call | flops 56623104 | tf_op jit(solution)/shard_map/stage/pallas_call | solution.py:479
  13.9 1.4 %own_stats.1 = (f32[2,2,2,192,192]{4,3,2,1,0:T(8,128)S(1)}, f32[2,2,2,192,192]{4,3,2,1,0:T(8,128)S(1)}, f32[3,4,192]{2,1,0:T(4,128)S(1)}) custom-call(s32[309]{0:T(512)S(1)} %concatenate.12.table, bf16[384,768]{1,0:T(8,128)(2,1)S(1)} %get-tuple-element.54.queries, bf16[384,768]{1,0:T(8,128)(2,1)S(1)} %get-tuple-element.55.grad_out, ...), custom_call_target="tpu_custom_call" | custom-call | flops 113246208 | tf_op jit(solution)/shard_map/own_stats/pallas_call | solution.py:479
  15.2 0.0 collective-permute-done.f_one
  15.2 0.0 collective-permute-done.1.f_two
  15.3 4.9 %collective-permute-start.4 = (bf16[384,512]{1,0:T(8,128)(2,1)S(1)}, bf16[384,512]{1,0:T(8,128)(2,1)S(1)}, u32[]{:S(2)}, u32[]{:S(2)}) collective-permute-start(bf16[384,512]{1,0:T(8,128)(2,1)S(1)} %get-tuple-element.72), channel_id=1, source_target_pairs={{0,4},{4,0},{8,12},{12,8},{1,5},{5,1},{9,13},{13,9},{2,6},{6,2},{1... | collective-permute-start | bytes 1179656 | tf_op jit(solution)/shard_map/ppermute | solution.py:450
  20.1 0.7 %collective-permute-start.5 = (bf16[384,512]{1,0:T(8,128)(2,1)S(1)}, bf16[384,512]{1,0:T(8,128)(2,1)S(1)}, u32[]{:S(2)}, u32[]{:S(2)}) collective-permute-start(bf16[384,512]{1,0:T(8,128)(2,1)S(1)} %get-tuple-element.72), channel_id=1, source_target_pairs={{4,8},{8,4},{5,9},{9,5},{6,10},{10,6},{7,11},{11,7},{20,24},{24,20... | collective-permute-start | bytes 1179656 | tf_op jit(solution)/shard_map/ppermute | solution.py:451
  20.8 2.1 %stats.1 = (f32[4,2,2,192,192]{4,3,2,1,0:T(8,128)S(1)}, f32[4,2,2,192,192]{4,3,2,1,0:T(8,128)S(1)}, f32[3,12,192]{2,1,0:T(8,128)S(1)}, f32[64,192]{1,0:T(8,128)S...) custom-call(s32[309]{0:T(512)S(1)} %concatenate.12.table, ...), custom_call_target="tpu_custom_call" | custom-call | flops 226492416 | tf_op jit(solution)/shard_map/stats/pallas_call | solution.py:479
  23.0 0.5 collective-permute-done.2.k_one
  23.5 0.0 collective-permute-done.3.k_two
  23.5 4.9 %values_part.1 = (bf16[4,2,576,128]{3,2,1,0:T(8,128)(2,1)S(1)}, bf16[4,2,576,192]{3,2,1,0:T(8,128)(2,1)S(1)}, f32[384,512]{1,0:T(8,128)S(1)}, bf16[416,512]{1,0:T(8,128)(2,1)S(1)}, bf16[416,512]{1,0:T(8,128)(2,1)S(1)}) custom-call(s32[309]{0:T(512)S(1)} %concatenate.12.table, bf16[384,768]{1,0:T(8,128)(2,1)S(1)} %get-tuple-element.54.queries, ...), custom_call_target="tpu_custom_call" | custom-call | flops 452984832 | tf_op jit(solution)/shard_map/values_part/pallas_call | solution.py:479
  28.4 5.1 %collective-permute-start.6 = (bf16[416,512]{1,0:T(8,128)(2,1)S(1)}, bf16[416,512]{1,0:T(8,128)(2,1)S(1)}, u32[]{:S(2)}, u32[]{:S(2)}) collective-permute-start(bf16[416,512]{1,0:T(8,128)(2,1)S(1)} %get-tuple-element.78), channel_id=1, source_target_pairs={{0,4},{4,0},{8,12},{12,8},{1,5},{5,1},{9,13},{13,9},{2,6},{6,2},{1... | collective-permute-start | bytes 1277960 | tf_op jit(solution)/shard_map/ppermute | solution.py:450
  33.6 0.9 %collective-permute-start.7 = (bf16[416,512]{1,0:T(8,128)(2,1)S(1)}, bf16[416,512]{1,0:T(8,128)(2,1)S(1)}, u32[]{:S(2)}, u32[]{:S(2)}) collective-permute-start(bf16[416,512]{1,0:T(8,128)(2,1)S(1)} %get-tuple-element.79), channel_id=1, source_target_pairs={{4,8},{8,4},{5,9},{9,5},{6,10},{10,6},{7,11},{11,7},{20,24},{24,20... | collective-permute-start | bytes 1277960 | tf_op jit(solution)/shard_map/ppermute | solution.py:451
  34.4 2.8 %collective-permute-start.8 = (f32[3,4,192]{2,1,0:T(4,128)S(1)}, f32[3,4,192]{2,1,0:T(4,128)S(1)}, u32[]{:S(2)}, u32[]{:S(2)}) collective-permute-start(f32[3,4,192]{2,1,0:T(4,128)S(1)} %get-tuple-element.82), channel_id=1, source_target_pairs={{0,8},{8,0},{4,12},{12,4},{1,9},{9,1},{5,13},{13,5},{2,10},{10,2},... | collective-permute-start | bytes 27656 | tf_op jit(solution)/shard_map/ppermute | solution.py:459
  37.2 0.0 collective-permute-done.4.v_one
  37.2 0.0 collective-permute-done.5.v_two
  37.2 4.7 %keys_part.1 = (bf16[4,2,576,192]{3,2,1,0:T(8,128)(2,1)S(1)}, f32[384,512]{1,0:T(8,128)S(1)}, bf16[384,512]{1,0:T(8,128)(2,1)S(1)}, bf16[384,512]{1,0:T(8,128)(2,1)S(1)}) custom-call(s32[309]{0:T(512)S(1)} %concatenate.12.table, bf16[384,768]{1,0:T(8,128)(2,1)S(1)} %get-tuple-element.54.queries, bf16[384,768]{1,0:T(8,128)(2,1)S(1)} %get-tuple-element.55.grad_out, ...), custom_call_target="tpu_custom_call" | custom-call | flops 452984832 | tf_op jit(solution)/shard_map/keys_part/pallas_call | solution.py:479
  41.9 3.2 %collective-permute-done.8.s_far = f32[3,4,192]{2,1,0:T(4,128)S(1)} collective-permute-done((f32[3,4,192]{2,1,0:T(4,128)S(1)}, f32[3,4,192]{2,1,0:T(4,128)S(1)}, u32[]{:S(2)}, u32[]{:S(2)}) %collective-permute-start.8) | collective-permute-done | bytes 9248 | tf_op jit(solution)/shard_map/ppermute | solution.py:459
  45.1 0.7 %collective-permute-start.10 = (bf16[384,512]{1,0:T(8,128)(2,1)S(1)}, bf16[384,512]{1,0:T(8,128)(2,1)S(1)}, u32[]{:S(2)}, u32[]{:S(2)}) collective-permute-start(bf16[384,512]{1,0:T(8,128)(2,1)S(1)} %get-tuple-element.96), channel_id=1, source_target_pairs={{4,8},{8,4},{5,9},{9,5},{6,10},{10,6},{7,11},{11,7},{20,24},{24,20... | collective-permute-start | bytes 1179656 | tf_op jit(solution)/shard_map/ppermute | solution.py:451
  45.8 1.9 %collective-permute-start.9 = (bf16[384,512]{1,0:T(8,128)(2,1)S(1)}, bf16[384,512]{1,0:T(8,128)(2,1)S(1)}, u32[]{:S(2)}, u32[]{:S(2)}) collective-permute-start(bf16[384,512]{1,0:T(8,128)(2,1)S(1)} %get-tuple-element.95), channel_id=1, source_target_pairs={{0,4},{4,0},{8,12},{12,8},{1,5},{5,1},{9,13},{13,9},{2,6},{6,2},{1... | collective-permute-start | bytes 1179656 | tf_op jit(solution)/shard_map/ppermute | solution.py:450
  47.6 0.0 collective-permute-done.6.r_one.rv_one
  47.6 0.0 collective-permute-done.7.r_two.rv_two
  47.6 1.4 %back.1 = (bf16[4,2,2,192,192]{4,3,2,1,0:T(8,128)(2,1)S(1)}, bf16[4,2,2,192,192]{4,3,2,1,0:T(8,128)(2,1)S(1)}, f32[12,192]{1,0:T(8,128)S(1)}, f32[12,192]{1,0:T(...) custom-call(s32[309]{0:T(512)S(1)} %concatenate.12.table, ...), custom_call_target="tpu_custom_call" | custom-call | flops 113246208 | tf_op jit(solution)/shard_map/back/pallas_call | solution.py:479
  49.1 0.7 %collective-permute-start.12 = (bf16[384,256]{1,0:T(8,128)(2,1)S(1)}, bf16[384,256]{1,0:T(8,128)(2,1)S(1)}, u32[]{:S(2)}, u32[]{:S(2)}) collective-permute-start(bf16[384,256]{1,0:T(8,128)(2,1)S(1)} %get-tuple-element.100), channel_id=1, source_target_pairs={{4,8},{8,4},{5,9},{9,5},{6,10},{10,6},{7,11},{11,7},{20,24},{24,20... | collective-permute-start | bytes 589832 | tf_op jit(solution)/shard_map/ppermute | solution.py:451
  49.7 4.0 %collective-permute-start.11 = (bf16[384,256]{1,0:T(8,128)(2,1)S(1)}, bf16[384,256]{1,0:T(8,128)(2,1)S(1)}, u32[]{:S(2)}, u32[]{:S(2)}) collective-permute-start(bf16[384,256]{1,0:T(8,128)(2,1)S(1)} %get-tuple-element.99), channel_id=1, source_target_pairs={{0,4},{4,0},{8,12},{12,8},{1,5},{5,1},{9,13},{13,9},{2,6},{6,2},{1... | collective-permute-start | bytes 589832 | tf_op jit(solution)/shard_map/ppermute | solution.py:450
  53.8 2.1 %home.1 = (f32[384,256]{1,0:T(8,128)S(1)}, bf16[384,256]{1,0:T(8,128)(2,1)S(1)}, bf16[384,256]{1,0:T(8,128)(2,1)S(1)}) custom-call(s32[309]{0:T(512)S(1)} %concatenate.12.table, bf16[384,768]{1,0:T(8,128)(2,1)S(1)} %get-tuple-element.54.queries, bf16[384,768]{1,0:T(8,128)(2,1)S(1)} %get-tuple-element.55.grad_out, ...), custom_call_target="tpu_custom_call" | custom-call | flops 339738624 | tf_op jit(solution)/shard_map/home/pallas_call | solution.py:479
  55.8 1.2 %rest.1 = (bf16[384,512]{1,0:T(8,128)(2,1)S(1)}, bf16[384,512]{1,0:T(8,128)(2,1)S(1)}, f32[384,512]{1,0:T(8,128)S(1)}) custom-call(bf16[384,768]{1,0:T(8,128)(2,1)S(1)} %get-tuple-element.54.queries, bf16[384,768]{1,0:T(8,128)(2,1)S(1)} %get-tuple-element.55.grad_out, bf16[4,2,576,128]{3,2,1,0:T(8,128)(2,1)S(1)} %get-tuple-element.90.chosen_in, ...), custom_call_target="tpu_custom_call" | custom-call | flops 452984832 | tf_op jit(solution)/shard_map/rest/pallas_call | solution.py:479
  57.0 0.9 %pad_maximum_fusion.2 = bf16[384,768]{1,0:T(8,128)(2,1)} fusion(bf16[384,512]{1,0:T(8,128)(2,1)S(1)} %get-tuple-element.104, bf16[384,256]{1,0:T(8,128)(2,1)S(1)} %get-tuple-element.103), kind=kLoop, calls=%fused_computation.3 | loop fusion | flops 1179648 | bytes 1179648 | tf_op jit(solution)/shard_map/concatenate | solution.py:583
  57.9 0.0 collective-permute-done.10
  57.9 0.0 collective-permute-done.9
  57.9 0.2 add_convert_fusion
  58.1 0.9 %pad_maximum_fusion = bf16[384,768]{1,0:T(8,128)(2,1)} fusion(bf16[384,512]{1,0:T(8,128)(2,1)S(1)} %add_convert_fusion, bf16[384,256]{1,0:T(8,128)(2,1)S(1)} %get-tuple-element.89), kind=kLoop, calls=%fused_computation.1 | loop fusion | flops 1179648 | bytes 1179648 | tf_op jit(solution)/shard_map/concatenate | solution.py:580
  58.9 0.0 collective-permute-done.12
  58.9 0.0 collective-permute-done.11
  58.9 0.1 add_convert_fusion.1
  59.0 0.9 %pad_maximum_fusion.1 = bf16[384,768]{1,0:T(8,128)(2,1)} fusion(bf16[384,512]{1,0:T(8,128)(2,1)S(1)} %get-tuple-element.101, bf16[384,256]{1,0:T(8,128)(2,1)S(1)} %add_convert_fusion.1), kind=kLoop, calls=%fused_computation.2 | loop fusion | flops 1179648 | bytes 1179648 | tf_op jit(solution)/shard_map/concatenate | solution.py:582
  (1 shorter events, 0.0 us)
Async XLA Ops:
  0.6 10.3 %copy-start.1 = (s32[8,3]{0,1:T(4,128)S(1)}, s32[8,3]{0,1:T(4,128)}, u32[]{:S(2)}) copy-start(s32[8,3]{0,1:T(4,128)} %param.10) | copy-start | bytes 292
  0.6 10.6 %copy-start = (s32[8,3,4,4]{0,3,2,1:T(4,128)S(1)}, s32[8,3,4,4]{0,3,2,1:T(4,128)}, u32[]{:S(2)}) copy-start(s32[8,3,4,4]{0,3,2,1:T(4,128)} %param.11) | copy-start | bytes 4612
  2.0 13.2 %collective-permute-start = (bf16[2,384,256]{2,1,0:T(8,128)(2,1)S(1)}, bf16[2,384,256]{2,1,0:T(8,128)(2,1)S(1)}, u32[]{:S(2)}, u32[]{:S(2)}) collective-permute-start(bf16[2,384,256]{2,1,0:T(8,128)(2,1)S(1)} %get-tuple-element.58), channel_id=1, source_target_pairs={{0,4},{4,0},{8,12},{12,8},{1,5},{5,1},{9,13},{13,9},{2,6},{6,2},{1... | collective-permute-start | bytes 1179656 | tf_op jit(solution)/shard_map/ppermute | solution.py:450
  5.1 10.1 %collective-permute-start.1 = (bf16[2,384,256]{2,1,0:T(8,128)(2,1)S(1)}, bf16[2,384,256]{2,1,0:T(8,128)(2,1)S(1)}, u32[]{:S(2)}, u32[]{:S(2)}) collective-permute-start(bf16[2,384,256]{2,1,0:T(8,128)(2,1)S(1)} %get-tuple-element.58), channel_id=1, source_target_pairs={{4,8},{8,4},{5,9},{9,5},{6,10},{10,6},{7,11},{11,7},{20,24},{24,20... | collective-permute-start | bytes 1179656 | tf_op jit(solution)/shard_map/ppermute | solution.py:451
  5.8 17.7 %collective-permute-start.2 = (bf16[384,512]{1,0:T(8,128)(2,1)S(1)}, bf16[384,512]{1,0:T(8,128)(2,1)S(1)}, u32[]{:S(2)}, u32[]{:S(2)}) collective-permute-start(bf16[384,512]{1,0:T(8,128)(2,1)S(1)} %get-tuple-element.67), channel_id=1, source_target_pairs={{0,4},{4,0},{8,12},{12,8},{1,5},{5,1},{9,13},{13,9},{2,6},{6,2},{1... | collective-permute-start | bytes 1179656 | tf_op jit(solution)/shard_map/ppermute | solution.py:450
  10.2 13.2 %collective-permute-start.3 = (bf16[384,512]{1,0:T(8,128)(2,1)S(1)}, bf16[384,512]{1,0:T(8,128)(2,1)S(1)}, u32[]{:S(2)}, u32[]{:S(2)}) collective-permute-start(bf16[384,512]{1,0:T(8,128)(2,1)S(1)} %get-tuple-element.67), channel_id=1, source_target_pairs={{4,8},{8,4},{5,9},{9,5},{6,10},{10,6},{7,11},{11,7},{20,24},{24,20... | collective-permute-start | bytes 1179656 | tf_op jit(solution)/shard_map/ppermute | solution.py:451
  15.3 22.0 %collective-permute-start.4 = (bf16[384,512]{1,0:T(8,128)(2,1)S(1)}, bf16[384,512]{1,0:T(8,128)(2,1)S(1)}, u32[]{:S(2)}, u32[]{:S(2)}) collective-permute-start(bf16[384,512]{1,0:T(8,128)(2,1)S(1)} %get-tuple-element.72), channel_id=1, source_target_pairs={{0,4},{4,0},{8,12},{12,8},{1,5},{5,1},{9,13},{13,9},{2,6},{6,2},{1... | collective-permute-start | bytes 1179656 | tf_op jit(solution)/shard_map/ppermute | solution.py:450
  20.1 17.1 %collective-permute-start.5 = (bf16[384,512]{1,0:T(8,128)(2,1)S(1)}, bf16[384,512]{1,0:T(8,128)(2,1)S(1)}, u32[]{:S(2)}, u32[]{:S(2)}) collective-permute-start(bf16[384,512]{1,0:T(8,128)(2,1)S(1)} %get-tuple-element.72), channel_id=1, source_target_pairs={{4,8},{8,4},{5,9},{9,5},{6,10},{10,6},{7,11},{11,7},{20,24},{24,20... | collective-permute-start | bytes 1179656 | tf_op jit(solution)/shard_map/ppermute | solution.py:451
  28.4 19.2 %collective-permute-start.6 = (bf16[416,512]{1,0:T(8,128)(2,1)S(1)}, bf16[416,512]{1,0:T(8,128)(2,1)S(1)}, u32[]{:S(2)}, u32[]{:S(2)}) collective-permute-start(bf16[416,512]{1,0:T(8,128)(2,1)S(1)} %get-tuple-element.78), channel_id=1, source_target_pairs={{0,4},{4,0},{8,12},{12,8},{1,5},{5,1},{9,13},{13,9},{2,6},{6,2},{1... | collective-permute-start | bytes 1277960 | tf_op jit(solution)/shard_map/ppermute | solution.py:450
  33.6 14.1 %collective-permute-start.7 = (bf16[416,512]{1,0:T(8,128)(2,1)S(1)}, bf16[416,512]{1,0:T(8,128)(2,1)S(1)}, u32[]{:S(2)}, u32[]{:S(2)}) collective-permute-start(bf16[416,512]{1,0:T(8,128)(2,1)S(1)} %get-tuple-element.79), channel_id=1, source_target_pairs={{4,8},{8,4},{5,9},{9,5},{6,10},{10,6},{7,11},{11,7},{20,24},{24,20... | collective-permute-start | bytes 1277960 | tf_op jit(solution)/shard_map/ppermute | solution.py:451
  34.4 10.7 %collective-permute-start.8 = (f32[3,4,192]{2,1,0:T(4,128)S(1)}, f32[3,4,192]{2,1,0:T(4,128)S(1)}, u32[]{:S(2)}, u32[]{:S(2)}) collective-permute-start(f32[3,4,192]{2,1,0:T(4,128)S(1)} %get-tuple-element.82), channel_id=1, source_target_pairs={{0,8},{8,0},{4,12},{12,4},{1,9},{9,1},{5,13},{13,5},{2,10},{10,2},... | collective-permute-start | bytes 27656 | tf_op jit(solution)/shard_map/ppermute | solution.py:459
  45.1 12.8 %collective-permute-start.10 = (bf16[384,512]{1,0:T(8,128)(2,1)S(1)}, bf16[384,512]{1,0:T(8,128)(2,1)S(1)}, u32[]{:S(2)}, u32[]{:S(2)}) collective-permute-start(bf16[384,512]{1,0:T(8,128)(2,1)S(1)} %get-tuple-element.96), channel_id=1, source_target_pairs={{4,8},{8,4},{5,9},{9,5},{6,10},{10,6},{7,11},{11,7},{20,24},{24,20... | collective-permute-start | bytes 1179656 | tf_op jit(solution)/shard_map/ppermute | solution.py:451
  45.8 12.1 %collective-permute-start.9 = (bf16[384,512]{1,0:T(8,128)(2,1)S(1)}, bf16[384,512]{1,0:T(8,128)(2,1)S(1)}, u32[]{:S(2)}, u32[]{:S(2)}) collective-permute-start(bf16[384,512]{1,0:T(8,128)(2,1)S(1)} %get-tuple-element.95), channel_id=1, source_target_pairs={{0,4},{4,0},{8,12},{12,8},{1,5},{5,1},{9,13},{13,9},{2,6},{6,2},{1... | collective-permute-start | bytes 1179656 | tf_op jit(solution)/shard_map/ppermute | solution.py:450
  49.1 9.9 %collective-permute-start.12 = (bf16[384,256]{1,0:T(8,128)(2,1)S(1)}, bf16[384,256]{1,0:T(8,128)(2,1)S(1)}, u32[]{:S(2)}, u32[]{:S(2)}) collective-permute-start(bf16[384,256]{1,0:T(8,128)(2,1)S(1)} %get-tuple-element.100), channel_id=1, source_target_pairs={{4,8},{8,4},{5,9},{9,5},{6,10},{10,6},{7,11},{11,7},{20,24},{24,20... | collective-permute-start | bytes 589832 | tf_op jit(solution)/shard_map/ppermute | solution.py:451
  49.7 9.2 %collective-permute-start.11 = (bf16[384,256]{1,0:T(8,128)(2,1)S(1)}, bf16[384,256]{1,0:T(8,128)(2,1)S(1)}, u32[]{:S(2)}, u32[]{:S(2)}) collective-permute-start(bf16[384,256]{1,0:T(8,128)(2,1)S(1)} %get-tuple-element.99), channel_id=1, source_target_pairs={{0,4},{4,0},{8,12},{12,8},{1,5},{5,1},{9,13},{13,9},{2,6},{6,2},{1... | collective-permute-start | bytes 589832 | tf_op jit(solution)/shard_map/ppermute | solution.py:450

commit v8 on v7

--- a/solution.py
+++ b/solution.py
@@ -206,7 +206,7 @@
 
 
 def rest_kernel(
-    queries, grad_out, chosen_in, prob_in, score_in, gv_own, gk_own, rv_one, rv_two,
+    queries, grad_out, chosen_in, prob_in, score_in, gv_own, gk_own,
     query_out, value_out, key_out,
 ):
     for head in range(query_out.shape[1] // HD):
@@ -220,10 +220,28 @@
             near = dot(score_low[:TOK_FRAME], queries[rows, column], NN)
             key_out[rows, far_column] = (gk_own[rows, far_column] + near) * SCALE
             near = dot(prob_in[head, frame, :TOK_FRAME], grad_out[rows, column], NN)
-            total = gv_own[rows, far_column] + near
-            total += rv_one[rows, far_column].astype(jnp.float32)
-            total += rv_two[rows, far_column].astype(jnp.float32)
-            value_out[rows, far_column] = total.astype(value_out.dtype)
+            value_out[rows, far_column] = gv_own[rows, far_column] + near
+
+
+def joined(own, one, two):
+    total = own[...] + one[...].astype(jnp.float32) + two[...].astype(jnp.float32)
+    return total.astype(jnp.bfloat16)
+
+
+def last_kernel(
+    gq_rest, gk_near, gq_near, rq_one, rq_two, gk_own, rk_one, rk_two,
+    query_out, key_out,
+    query_done, key_done, sems,
+):
+    moves = copy_all(
+        [(gq_rest, query_out.at[:, SPLIT:]), (gk_near, key_out.at[:, :SPLIT])], sems
+    )
+    key_done[...] = joined(gk_own, rk_one, rk_two)
+    moves += copy_all([(key_done, key_out.at[:, SPLIT:])], sems.at[2:3])
+    query_done[...] = joined(gq_near, rq_one, rq_two)
+    moves += copy_all([(query_done, query_out.at[:, :SPLIT])], sems.at[3:4])
+    for move in moves:
+        move.wait()
 
 
 def pair_stats(table, window, key, index, query, grad, keys, values, bias, outs):
@@ -474,14 +492,14 @@
     return jnp.concatenate([shifts.reshape(-1), blocks.reshape(-1), ends])
 
 
-def call(kernel, name, scalars, arrays, outs, scratch, flops, space=pltpu.VMEM):
+def call(kernel, name, scalars, arrays, outs, scratch, flops, space=pltpu.VMEM, out_space=pltpu.VMEM):
     arrays = [pltpu.with_memory_space_constraint(array, space) for array in arrays]
     return pl.pallas_call(
         kernel,
         out_shape=outs,
         in_specs=[pl.BlockSpec(memory_space=pltpu.SMEM)] * len(scalars)
         + [pl.BlockSpec(memory_space=space)] * len(arrays),
-        out_specs=tuple(pl.BlockSpec(memory_space=pltpu.VMEM) for _ in outs),
+        out_specs=tuple(pl.BlockSpec(memory_space=out_space) for _ in outs),
         scratch_shapes=scratch,
         compiler_params=pltpu.CompilerParams(vmem_limit_bytes=16 << 20),
         cost_estimate=pl.CostEstimate(flops=flops, bytes_accessed=0, transcendentals=0),
@@ -522,10 +540,7 @@
         (full(*near_grid), full(*near_grid), full(3, SIDE, TOK_FRAME)),
         [full(FR_DEV, 3, SIDE, TOK_FRAME)], MOVED * unit,
     )
-    v_send, f_one, f_two, own_stats = lax.optimization_barrier(
-        (v_send, f_one, f_two, own_stats)
-    )
-    v_one, v_two = swap(v_send, v_send)
+    f_one, f_two, own_stats = lax.optimization_barrier((f_one, f_two, own_stats))
     note = full(2 * NOTES, TOK_FRAME)
     masked, grad_probs, mine, n_one, n_two, s_far, s_other = call(
         stats_kernel, "stats", (table,), (key, value, moved_bias, own_stats, f_one, f_two),
@@ -534,6 +549,9 @@
         [full(FR_DEV, 3, 2 * SIDE, TOK_FRAME)], 2 * MOVED * unit,
     )
     s_far, s_other = swap_far(s_far, s_other)
+    v_send, mine = lax.optimization_barrier((v_send, mine))
+    v_one, v_two = swap(v_send, v_send)
+    k_one, k_two, s_far, s_other = lax.optimization_barrier((k_one, k_two, s_far, s_other))
     windows = low(DEPTH, 3 * ROWS, HD)
     accums = full(DEPTH, 3 * ROWS, HD)
     pairs = low(heads, FR_DEV, SLOTS, TOK_FRAME)
@@ -550,9 +568,13 @@
         (pairs, full(ROWS, rest), low(ROWS, rest), low(ROWS, rest)),
         [windows, low(DEPTH, FR_DEV, SLOTS, HD), accums], 2 * heads * unit,
     )
-    gk_one, gk_two, s_far, s_other = lax.optimization_barrier((gk_one, gk_two, s_far, s_other))
     rk_one, rk_two = swap(gk_one, gk_two)
-    gk_own, masked = lax.optimization_barrier((gk_own, masked))
+    gq_rest, gv_own, gk_own = call(
+        rest_kernel, "rest", (),
+        (query, grad, chosen, prob_low, score_low, gv_own, gk_own),
+        (low(ROWS, rest), full(ROWS, rest), full(ROWS, rest)), [], heads * unit,
+    )
+    rv_one, rv_two, gv_own = lax.optimization_barrier((rv_one, rv_two, gv_own))
     y_prob, y_score, logs, deltas, gq_one, gq_two = call(
         back_kernel, "back", (table,),
         (key, masked, grad_probs, mine, rv_one, rv_two, s_far, s_other),
@@ -567,20 +589,14 @@
         (full(ROWS, SPLIT), low(ROWS, SPLIT), low(ROWS, SPLIT)),
         [full(ROWS, SPLIT), full(ROWS, SPLIT)], 3 * MOVED * unit,
     )
-    gq_rest, gv_rest, gk_own = call(
-        rest_kernel, "rest", (),
-        (query, grad, chosen, prob_low, score_low, gv_own, gk_own, rv_one, rv_two),
-        (low(ROWS, rest), low(ROWS, rest), full(ROWS, rest)), [], 2 * heads * unit,
-    )
-
-    def joined(own, one, two):
-        total = own + one.astype(jnp.float32) + two.astype(jnp.float32)
-        return total.astype(jnp.bfloat16)
-
-    grad_keys = jnp.concatenate([gk_near, joined(gk_own, rk_one, rk_two)], 1)
-    grad_keys, gq_near = lax.optimization_barrier((grad_keys, gq_near))
-    grad_queries = jnp.concatenate([joined(gq_near, rq_one, rq_two), gq_rest], 1)
-    grad_values = jnp.concatenate([gv_near, gv_rest], 1)
+    grad_values = jnp.concatenate([gv_near, joined(gv_own, rv_one[:ROWS], rv_two[:ROWS])], 1)
+    grad_queries, grad_keys = call(
+        last_kernel, "last", (),
+        (gq_rest, gk_near, gq_near, rq_one, rq_two, gk_own, rk_one, rk_two),
+        (pltpu.HBM((ROWS, width), jnp.bfloat16),) * 2,
+        [low(ROWS, SPLIT), low(ROWS, rest), pltpu.SemaphoreType.DMA((4,))],
+        unit, pltpu.VMEM, pltpu.HBM,
+    )
     return grad_queries, grad_keys, grad_values
 
 

time: 60.2 us -> 57.8 us (0.960)
  starting transfers between devices: 30.5 us -> 23.2 us
  waiting for transfers between devices: 3.71 us -> 9.44 us
  other arithmetic: 2.82 us -> 1.04 us
  Pallas kernels: 21.3 us -> 22.2 us
    ppermute x6, waiting for transfers between devices: 0.54 us -> 9.42 us  [swap(): lax.ppermute(one, 'frames', both_ways(first))]
    ppermute x6, starting transfers between devices: 23.4 us -> 16.3 us  [swap(): lax.ppermute(one, 'frames', both_ways(first))]
    ppermute x1, waiting for transfers between devices: 3.16 us -> 0.01 us  [swap_far(): far = lax.ppermute(far, 'frames', both_ways(near))]
    concatenate x3 -> x1, other arithmetic: 2.56 us -> 0.85 us  [local(): jnp.concatenate([gv_near, joined(gv_own, rv_one[:ROWS], rv_two[:ROWS])], 1)]
    pallas_call x9 -> x10, Pallas kernels: 21.3 us -> 22.2 us  [call(): pl.pallas_call(kernel, out_shape=outs, in_specs=[pl.BlockSpec(memory_spac...]
  transfers between devices with their start and end apart: 13 -> 13, of which waited for: 2 -> 5; matrix products, arithmetic and copies ran while one was open for 4% -> 3% of each run, Pallas kernels for 33% -> 34%
where the time goes in v8:
time: 57.8 us; the launch traced here: 57.5 us
  starting transfers between devices  23.2 us (40%)
  Pallas kernels  22.2 us (38%)
  waiting for transfers between devices  9.44 us (16%)
  other arithmetic  1.04 us (2%)
  between operations  0.95 us (2%)
  local copies, waits for them, and re-layouts  0.73 us (1%)
    pallas_call x10, Pallas kernels, call(): pl.pallas_call(kernel, out_shape=outs, in_specs=[pl.BlockSpec(memory_spac...  22.2 us
    ppermute x6, starting transfers between devices, swap(): lax.ppermute(one, 'frames', both_ways(first))  16.3 us
    ppermute x6, waiting for transfers between devices, swap(): lax.ppermute(one, 'frames', both_ways(first))  9.42 us
    ppermute x6, starting transfers between devices, swap(): lax.ppermute(two, 'frames', both_ways(second))  4.22 us
    ppermute x1, starting transfers between devices, swap_far(): far = lax.ppermute(far, 'frames', both_ways(near))  2.69 us
  transfers between devices with their start and end apart: 13, of which 5 were waited for; matrix products, arithmetic and copies ran while one was open for 3% of the time, Pallas kernels for 34%

profile of v8, /device:TPU:0, one launch (start us, length us, event | category | flops | bytes accessed | tf_op | source)
XLA Modules:
  0.0 57.5 jit_solution(8996337481586682866)
XLA Ops:
  0.6 0.0 copy-start.1
  0.6 0.0 copy-start
  0.7 1.4 %pack.1 = (bf16[2,384,256]{2,1,0:T(8,128)(2,1)S(1)}, bf16[384,512]{1,0:T(8,128)(2,1)S(1)}, bf16[384,512]{1,0:T(8,128)(2,1)S(1)}) custom-call(bf16[384,768]{1,0:T(8,128)(2,1)} %queries.1, bf16[384,768]{1,0:T(8,128)(2,1)} %grad_out.1, bf16[384,768]{1,0:T(8,128)(2,1)} %keys.1, bf16[384,768]{1,0:T(8,128)(2,1)} %values.1), custom_call_target="tpu_custom_call" | custom-call | flops 56623104 | tf_op jit(solution)/shard_map/pack/pallas_call | solution.py:497
  2.0 0.7 %collective-permute-start.3 = (bf16[2,384,256]{2,1,0:T(8,128)(2,1)S(1)}, bf16[2,384,256]{2,1,0:T(8,128)(2,1)S(1)}, u32[]{:S(2)}, u32[]{:S(2)}) collective-permute-start(bf16[2,384,256]{2,1,0:T(8,128)(2,1)S(1)} %get-tuple-element.63), channel_id=1, source_target_pairs={{4,8},{8,4},{5,9},{9,5},{6,10},{10,6},{7,11},{11,7},{20,24},{24,20... | collective-permute-start | bytes 1179656 | tf_op jit(solution)/shard_map/ppermute | solution.py:469
  2.7 5.9 %collective-permute-start.2 = (bf16[2,384,256]{2,1,0:T(8,128)(2,1)S(1)}, bf16[2,384,256]{2,1,0:T(8,128)(2,1)S(1)}, u32[]{:S(2)}, u32[]{:S(2)}) collective-permute-start(bf16[2,384,256]{2,1,0:T(8,128)(2,1)S(1)} %get-tuple-element.63), channel_id=1, source_target_pairs={{0,4},{4,0},{8,12},{12,8},{1,5},{5,1},{9,13},{13,9},{2,6},{6,2},{1... | collective-permute-start | bytes 1179656 | tf_op jit(solution)/shard_map/ppermute | solution.py:468
  8.6 0.7 %collective-permute-start.1 = (bf16[384,512]{1,0:T(8,128)(2,1)S(1)}, bf16[384,512]{1,0:T(8,128)(2,1)S(1)}, u32[]{:S(2)}, u32[]{:S(2)}) collective-permute-start(bf16[384,512]{1,0:T(8,128)(2,1)S(1)} %get-tuple-element.60), channel_id=1, source_target_pairs={{4,8},{8,4},{5,9},{9,5},{6,10},{10,6},{7,11},{11,7},{20,24},{24,20... | collective-permute-start | bytes 1179656 | tf_op jit(solution)/shard_map/ppermute | solution.py:469
  9.3 1.8 %collective-permute-start = (bf16[384,512]{1,0:T(8,128)(2,1)S(1)}, bf16[384,512]{1,0:T(8,128)(2,1)S(1)}, u32[]{:S(2)}, u32[]{:S(2)}) collective-permute-start(bf16[384,512]{1,0:T(8,128)(2,1)S(1)} %get-tuple-element.60), channel_id=1, source_target_pairs={{0,4},{4,0},{8,12},{12,8},{1,5},{5,1},{9,13},{13,9},{2,6},{6,2},{1... | collective-permute-start | bytes 1179656 | tf_op jit(solution)/shard_map/ppermute | solution.py:468
  11.0 0.0 copy-done.1
  11.1 0.1 pad_dynamic-slice_fusion.1
  11.1 0.1 copy.10
  11.2 0.1 reshape.12
  11.3 0.0 copy-done
  11.3 0.1 pad_dynamic-slice_fusion
  11.4 0.2 copy.11
  11.6 0.1 reshape.13
  11.7 0.1 concatenate.6.table
  11.8 2.2 %stage.1 = (bf16[384,768]{1,0:T(8,128)(2,1)S(1)}, bf16[384,768]{1,0:T(8,128)(2,1)S(1)}, bf16[384,768]{1,0:T(8,128)(2,1)S(1)}, bf16[384,768]{1,0:T(8,128)(2,1)S(1...) custom-call(s32[309]{0:T(512)S(1)} %concatenate.6.table, bf16[384,768]{1,0:T(8,128)(2,1)} %queries.1, ...), custom_call_target="tpu_custom_call" | custom-call | flops 56623104 | tf_op jit(solution)/shard_map/stage/pallas_call | solution.py:497
  14.0 1.7 %own_stats.1 = (f32[2,2,2,192,192]{4,3,2,1,0:T(8,128)S(1)}, f32[2,2,2,192,192]{4,3,2,1,0:T(8,128)S(1)}, f32[3,4,192]{2,1,0:T(4,128)S(1)}) custom-call(s32[309]{0:T(512)S(1)} %concatenate.6.table, bf16[384,768]{1,0:T(8,128)(2,1)S(1)} %get-tuple-element.56.queries, bf16[384,768]{1,0:T(8,128)(2,1)S(1)} %get-tuple-element.57.grad_out, ...), custom_call_target="tpu_custom_call" | custom-call | flops 113246208 | tf_op jit(solution)/shard_map/own_stats/pallas_call | solution.py:497
  15.7 0.0 collective-permute-done.3.f_two
  15.7 2.9 %collective-permute-done.2.f_one = bf16[2,384,256]{2,1,0:T(8,128)(2,1)S(1)} collective-permute-done((bf16[2,384,256]{2,1,0:T(8,128)(2,1)S(1)}, bf16[2,384,256]{2,1,0:T(8,128)(2,1)S(1)}, u32[]{:S(2)}, u32[]{:S(2)}) %collective-permute-start.2) | collective-permute-done | bytes 393248 | tf_op jit(solution)/shard_map/ppermute | solution.py:468
  18.6 1.8 %stats.1 = (f32[4,2,2,192,192]{4,3,2,1,0:T(8,128)S(1)}, f32[4,2,2,192,192]{4,3,2,1,0:T(8,128)S(1)}, f32[3,12,192]{2,1,0:T(8,128)S(1)}, f32[64,192]{1,0:T(8,128)S...) custom-call(s32[309]{0:T(512)S(1)} %concatenate.6.table, ...), custom_call_target="tpu_custom_call" | custom-call | flops 226492416 | tf_op jit(solution)/shard_map/stats/pallas_call | solution.py:497
  20.4 2.7 %collective-permute-start.4 = (f32[3,4,192]{2,1,0:T(4,128)S(1)}, f32[3,4,192]{2,1,0:T(4,128)S(1)}, u32[]{:S(2)}, u32[]{:S(2)}) collective-permute-start(f32[3,4,192]{2,1,0:T(4,128)S(1)} %get-tuple-element.68), channel_id=1, source_target_pairs={{0,8},{8,0},{4,12},{12,4},{1,9},{9,1},{5,13},{13,5},{2,10},{10,2},... | collective-permute-start | bytes 27656 | tf_op jit(solution)/shard_map/ppermute | solution.py:477
  23.0 0.7 %collective-permute-start.6 = (bf16[384,512]{1,0:T(8,128)(2,1)S(1)}, bf16[384,512]{1,0:T(8,128)(2,1)S(1)}, u32[]{:S(2)}, u32[]{:S(2)}) collective-permute-start(bf16[384,512]{1,0:T(8,128)(2,1)S(1)} %get-tuple-element.77), channel_id=1, source_target_pairs={{4,8},{8,4},{5,9},{9,5},{6,10},{10,6},{7,11},{11,7},{20,24},{24,20... | collective-permute-start | bytes 1179656 | tf_op jit(solution)/shard_map/ppermute | solution.py:469
  23.7 2.1 %collective-permute-start.5 = (bf16[384,512]{1,0:T(8,128)(2,1)S(1)}, bf16[384,512]{1,0:T(8,128)(2,1)S(1)}, u32[]{:S(2)}, u32[]{:S(2)}) collective-permute-start(bf16[384,512]{1,0:T(8,128)(2,1)S(1)} %get-tuple-element.77), channel_id=1, source_target_pairs={{0,4},{4,0},{8,12},{12,8},{1,5},{5,1},{9,13},{13,9},{2,6},{6,2},{1... | collective-permute-start | bytes 1179656 | tf_op jit(solution)/shard_map/ppermute | solution.py:468
  25.8 0.0 collective-permute-done.1.k_two
  25.8 1.5 %collective-permute-done.k_one = bf16[384,512]{1,0:T(8,128)(2,1)S(1)} collective-permute-done((bf16[384,512]{1,0:T(8,128)(2,1)S(1)}, bf16[384,512]{1,0:T(8,128)(2,1)S(1)}, u32[]{:S(2)}, u32[]{:S(2)}) %collective-permute-start) | collective-permute-done | bytes 393248 | tf_op jit(solution)/shard_map/ppermute | solution.py:468
  27.3 0.0 collective-permute-done.4.s_far
  27.3 4.9 %values_part.1 = (bf16[4,2,576,128]{3,2,1,0:T(8,128)(2,1)S(1)}, bf16[4,2,576,192]{3,2,1,0:T(8,128)(2,1)S(1)}, f32[384,512]{1,0:T(8,128)S(1)}, bf16[416,512]{1,0:T(8,128)(2,1)S(1)}, bf16[416,512]{1,0:T(8,128)(2,1)S(1)}) custom-call(s32[309]{0:T(512)S(1)} %concatenate.6.table, bf16[384,768]{1,0:T(8,128)(2,1)S(1)} %get-tuple-element.56.queries, ...), custom_call_target="tpu_custom_call" | custom-call | flops 452984832 | tf_op jit(solution)/shard_map/values_part/pallas_call | solution.py:497
  32.2 2.0 %collective-permute-start.7 = (bf16[416,512]{1,0:T(8,128)(2,1)S(1)}, bf16[416,512]{1,0:T(8,128)(2,1)S(1)}, u32[]{:S(2)}, u32[]{:S(2)}) collective-permute-start(bf16[416,512]{1,0:T(8,128)(2,1)S(1)} %get-tuple-element.87), channel_id=1, source_target_pairs={{0,4},{4,0},{8,12},{12,8},{1,5},{5,1},{9,13},{13,9},{2,6},{6,2},{1... | collective-permute-start | bytes 1277960 | tf_op jit(solution)/shard_map/ppermute | solution.py:468
  34.2 0.9 %collective-permute-start.8 = (bf16[416,512]{1,0:T(8,128)(2,1)S(1)}, bf16[416,512]{1,0:T(8,128)(2,1)S(1)}, u32[]{:S(2)}, u32[]{:S(2)}) collective-permute-start(bf16[416,512]{1,0:T(8,128)(2,1)S(1)} %get-tuple-element.88), channel_id=1, source_target_pairs={{4,8},{8,4},{5,9},{9,5},{6,10},{10,6},{7,11},{11,7},{20,24},{24,20... | collective-permute-start | bytes 1277960 | tf_op jit(solution)/shard_map/ppermute | solution.py:469
  35.1 0.0 collective-permute-done.6.v_two
  35.1 0.8 %collective-permute-done.5.v_one = bf16[384,512]{1,0:T(8,128)(2,1)S(1)} collective-permute-done((bf16[384,512]{1,0:T(8,128)(2,1)S(1)}, bf16[384,512]{1,0:T(8,128)(2,1)S(1)}, u32[]{:S(2)}, u32[]{:S(2)}) %collective-permute-start.5) | collective-permute-done | bytes 393248 | tf_op jit(solution)/shard_map/ppermute | solution.py:468
  35.8 4.7 %keys_part.1 = (bf16[4,2,576,192]{3,2,1,0:T(8,128)(2,1)S(1)}, f32[384,512]{1,0:T(8,128)S(1)}, bf16[384,512]{1,0:T(8,128)(2,1)S(1)}, bf16[384,512]{1,0:T(8,128)(2,1)S(1)}) custom-call(s32[309]{0:T(512)S(1)} %concatenate.6.table, bf16[384,768]{1,0:T(8,128)(2,1)S(1)} %get-tuple-element.56.queries, bf16[384,768]{1,0:T(8,128)(2,1)S(1)} %get-tuple-element.57.grad_out, ...), custom_call_target="tpu_custom_call" | custom-call | flops 452984832 | tf_op jit(solution)/shard_map/keys_part/pallas_call | solution.py:497
  40.5 2.1 %collective-permute-start.11 = (bf16[384,512]{1,0:T(8,128)(2,1)S(1)}, bf16[384,512]{1,0:T(8,128)(2,1)S(1)}, u32[]{:S(2)}, u32[]{:S(2)}) collective-permute-start(bf16[384,512]{1,0:T(8,128)(2,1)S(1)} %get-tuple-element.103), channel_id=1, source_target_pairs={{0,4},{4,0},{8,12},{12,8},{1,5},{5,1},{9,13},{13,9},{2,6},{6,2},{1... | collective-permute-start | bytes 1179656 | tf_op jit(solution)/shard_map/ppermute | solution.py:468
  42.7 0.7 %collective-permute-start.12 = (bf16[384,512]{1,0:T(8,128)(2,1)S(1)}, bf16[384,512]{1,0:T(8,128)(2,1)S(1)}, u32[]{:S(2)}, u32[]{:S(2)}) collective-permute-start(bf16[384,512]{1,0:T(8,128)(2,1)S(1)} %get-tuple-element.104), channel_id=1, source_target_pairs={{4,8},{8,4},{5,9},{9,5},{6,10},{10,6},{7,11},{11,7},{20,24},{24,20... | collective-permute-start | bytes 1179656 | tf_op jit(solution)/shard_map/ppermute | solution.py:469
  43.3 1.2 %rest.1 = (bf16[384,512]{1,0:T(8,128)(2,1)S(1)}, f32[384,512]{1,0:T(8,128)S(1)}, f32[384,512]{1,0:T(8,128)S(1)}) custom-call(bf16[384,768]{1,0:T(8,128)(2,1)S(1)} %get-tuple-element.56.queries, bf16[384,768]{1,0:T(8,128)(2,1)S(1)} %get-tuple-element.57.grad_out, bf16[4,2,576,128]{3,2,1,0:T(8,128)(2,1)S(1)} %get-tuple-element.73.chosen_in, ...), custom_call_target="tpu_custom_call" | custom-call | flops 226492416 | tf_op jit(solution)/shard_map/rest/pallas_call | solution.py:497
  44.5 0.4 collective-permute-done.7.r_one
  45.0 0.0 collective-permute-done.8.r_two
  45.0 1.1 %back.1 = (bf16[4,2,2,192,192]{4,3,2,1,0:T(8,128)(2,1)S(1)}, bf16[4,2,2,192,192]{4,3,2,1,0:T(8,128)(2,1)S(1)}, f32[12,192]{1,0:T(8,128)S(1)}, f32[12,192]{1,0:T(...) custom-call(s32[309]{0:T(512)S(1)} %concatenate.6.table, ...), custom_call_target="tpu_custom_call" | custom-call | flops 113246208 | tf_op jit(solution)/shard_map/back/pallas_call | solution.py:497
  46.1 2.4 %collective-permute-start.9 = (bf16[384,256]{1,0:T(8,128)(2,1)S(1)}, bf16[384,256]{1,0:T(8,128)(2,1)S(1)}, u32[]{:S(2)}, u32[]{:S(2)}) collective-permute-start(bf16[384,256]{1,0:T(8,128)(2,1)S(1)} %get-tuple-element.100), channel_id=1, source_target_pairs={{0,4},{4,0},{8,12},{12,8},{1,5},{5,1},{9,13},{13,9},{2,6},{6,2},{1... | collective-permute-start | bytes 589832 | tf_op jit(solution)/shard_map/ppermute | solution.py:468
  48.5 0.7 %collective-permute-start.10 = (bf16[384,256]{1,0:T(8,128)(2,1)S(1)}, bf16[384,256]{1,0:T(8,128)(2,1)S(1)}, u32[]{:S(2)}, u32[]{:S(2)}) collective-permute-start(bf16[384,256]{1,0:T(8,128)(2,1)S(1)} %get-tuple-element.101), channel_id=1, source_target_pairs={{4,8},{8,4},{5,9},{9,5},{6,10},{10,6},{7,11},{11,7},{20,24},{24,20... | collective-permute-start | bytes 589832 | tf_op jit(solution)/shard_map/ppermute | solution.py:469
  49.2 0.2 add_convert_fusion
  49.3 2.2 %home.1 = (f32[384,256]{1,0:T(8,128)S(1)}, bf16[384,256]{1,0:T(8,128)(2,1)S(1)}, bf16[384,256]{1,0:T(8,128)(2,1)S(1)}) custom-call(s32[309]{0:T(512)S(1)} %concatenate.6.table, bf16[384,768]{1,0:T(8,128)(2,1)S(1)} %get-tuple-element.56.queries, bf16[384,768]{1,0:T(8,128)(2,1)S(1)} %get-tuple-element.57.grad_out, ...), custom_call_target="tpu_custom_call" | custom-call | flops 339738624 | tf_op jit(solution)/shard_map/home/pallas_call | solution.py:497
  51.6 0.9 %pad_maximum_fusion = bf16[384,768]{1,0:T(8,128)(2,1)} fusion(bf16[384,512]{1,0:T(8,128)(2,1)S(1)} %add_convert_fusion, bf16[384,256]{1,0:T(8,128)(2,1)S(1)} %get-tuple-element.107), kind=kLoop, calls=%fused_computation.1 | loop fusion | flops 1179648 | bytes 1179648 | tf_op jit(solution)/shard_map/concatenate | solution.py:592
  52.4 3.9 %collective-permute-done.9.rq_one = bf16[384,256]{1,0:T(8,128)(2,1)S(1)} collective-permute-done((bf16[384,256]{1,0:T(8,128)(2,1)S(1)}, bf16[384,256]{1,0:T(8,128)(2,1)S(1)}, u32[]{:S(2)}, u32[]{:S(2)}) %collective-permute-start.9) | collective-permute-done | bytes 196640 | tf_op jit(solution)/shard_map/ppermute | solution.py:468
  56.3 0.0 collective-permute-done.10.rq_two
  56.3 0.0 collective-permute-done.11.rk_one
  56.3 0.0 collective-permute-done.12.rk_two
  56.3 1.0 %last.1 = (bf16[384,768]{1,0:T(8,128)(2,1)}, bf16[384,768]{1,0:T(8,128)(2,1)}) custom-call(bf16[384,512]{1,0:T(8,128)(2,1)S(1)} %get-tuple-element.81.gq_rest, bf16[384,256]{1,0:T(8,128)(2,1)S(1)} %get-tuple-element.98.gk_near, f32[384,256]{1,0:T(8,128)S(1)} %get-tuple-element.99.gq_near, bf16[384,256]{1,0:T(8,128)(2,1)S(1)} %collective-permute-done.9.rq_one, ...), custom_call_target="tpu_custom_call" | custom-call | flops 56623104 | tf_op jit(solution)/shard_map/last/pallas_call | solution.py:497
  (1 shorter events, 0.0 us)
Async XLA Ops:
  0.6 10.4 %copy-start.1 = (s32[8,3]{0,1:T(4,128)S(1)}, s32[8,3]{0,1:T(4,128)}, u32[]{:S(2)}) copy-start(s32[8,3]{0,1:T(4,128)} %param.10) | copy-start | bytes 292
  0.6 10.7 %copy-start = (s32[8,3,4,4]{0,3,2,1:T(4,128)S(1)}, s32[8,3,4,4]{0,3,2,1:T(4,128)}, u32[]{:S(2)}) copy-start(s32[8,3,4,4]{0,3,2,1:T(4,128)} %param.11) | copy-start | bytes 4612
  2.0 13.7 %collective-permute-start.3 = (bf16[2,384,256]{2,1,0:T(8,128)(2,1)S(1)}, bf16[2,384,256]{2,1,0:T(8,128)(2,1)S(1)}, u32[]{:S(2)}, u32[]{:S(2)}) collective-permute-start(bf16[2,384,256]{2,1,0:T(8,128)(2,1)S(1)} %get-tuple-element.63), channel_id=1, source_target_pairs={{4,8},{8,4},{5,9},{9,5},{6,10},{10,6},{7,11},{11,7},{20,24},{24,20... | collective-permute-start | bytes 1179656 | tf_op jit(solution)/shard_map/ppermute | solution.py:469
  2.7 15.9 %collective-permute-start.2 = (bf16[2,384,256]{2,1,0:T(8,128)(2,1)S(1)}, bf16[2,384,256]{2,1,0:T(8,128)(2,1)S(1)}, u32[]{:S(2)}, u32[]{:S(2)}) collective-permute-start(bf16[2,384,256]{2,1,0:T(8,128)(2,1)S(1)} %get-tuple-element.63), channel_id=1, source_target_pairs={{0,4},{4,0},{8,12},{12,8},{1,5},{5,1},{9,13},{13,9},{2,6},{6,2},{1... | collective-permute-start | bytes 1179656 | tf_op jit(solution)/shard_map/ppermute | solution.py:468
  8.6 17.2 %collective-permute-start.1 = (bf16[384,512]{1,0:T(8,128)(2,1)S(1)}, bf16[384,512]{1,0:T(8,128)(2,1)S(1)}, u32[]{:S(2)}, u32[]{:S(2)}) collective-permute-start(bf16[384,512]{1,0:T(8,128)(2,1)S(1)} %get-tuple-element.60), channel_id=1, source_target_pairs={{4,8},{8,4},{5,9},{9,5},{6,10},{10,6},{7,11},{11,7},{20,24},{24,20... | collective-permute-start | bytes 1179656 | tf_op jit(solution)/shard_map/ppermute | solution.py:469
  9.3 18.0 %collective-permute-start = (bf16[384,512]{1,0:T(8,128)(2,1)S(1)}, bf16[384,512]{1,0:T(8,128)(2,1)S(1)}, u32[]{:S(2)}, u32[]{:S(2)}) collective-permute-start(bf16[384,512]{1,0:T(8,128)(2,1)S(1)} %get-tuple-element.60), channel_id=1, source_target_pairs={{0,4},{4,0},{8,12},{12,8},{1,5},{5,1},{9,13},{13,9},{2,6},{6,2},{1... | collective-permute-start | bytes 1179656 | tf_op jit(solution)/shard_map/ppermute | solution.py:468
  20.4 6.9 %collective-permute-start.4 = (f32[3,4,192]{2,1,0:T(4,128)S(1)}, f32[3,4,192]{2,1,0:T(4,128)S(1)}, u32[]{:S(2)}, u32[]{:S(2)}) collective-permute-start(f32[3,4,192]{2,1,0:T(4,128)S(1)} %get-tuple-element.68), channel_id=1, source_target_pairs={{0,8},{8,0},{4,12},{12,4},{1,9},{9,1},{5,13},{13,5},{2,10},{10,2},... | collective-permute-start | bytes 27656 | tf_op jit(solution)/shard_map/ppermute | solution.py:477
  23.0 12.0 %collective-permute-start.6 = (bf16[384,512]{1,0:T(8,128)(2,1)S(1)}, bf16[384,512]{1,0:T(8,128)(2,1)S(1)}, u32[]{:S(2)}, u32[]{:S(2)}) collective-permute-start(bf16[384,512]{1,0:T(8,128)(2,1)S(1)} %get-tuple-element.77), channel_id=1, source_target_pairs={{4,8},{8,4},{5,9},{9,5},{6,10},{10,6},{7,11},{11,7},{20,24},{24,20... | collective-permute-start | bytes 1179656 | tf_op jit(solution)/shard_map/ppermute | solution.py:469
  23.7 12.1 %collective-permute-start.5 = (bf16[384,512]{1,0:T(8,128)(2,1)S(1)}, bf16[384,512]{1,0:T(8,128)(2,1)S(1)}, u32[]{:S(2)}, u32[]{:S(2)}) collective-permute-start(bf16[384,512]{1,0:T(8,128)(2,1)S(1)} %get-tuple-element.77), channel_id=1, source_target_pairs={{0,4},{4,0},{8,12},{12,8},{1,5},{5,1},{9,13},{13,9},{2,6},{6,2},{1... | collective-permute-start | bytes 1179656 | tf_op jit(solution)/shard_map/ppermute | solution.py:468
  32.2 12.8 %collective-permute-start.7 = (bf16[416,512]{1,0:T(8,128)(2,1)S(1)}, bf16[416,512]{1,0:T(8,128)(2,1)S(1)}, u32[]{:S(2)}, u32[]{:S(2)}) collective-permute-start(bf16[416,512]{1,0:T(8,128)(2,1)S(1)} %get-tuple-element.87), channel_id=1, source_target_pairs={{0,4},{4,0},{8,12},{12,8},{1,5},{5,1},{9,13},{13,9},{2,6},{6,2},{1... | collective-permute-start | bytes 1277960 | tf_op jit(solution)/shard_map/ppermute | solution.py:468
  34.2 10.8 %collective-permute-start.8 = (bf16[416,512]{1,0:T(8,128)(2,1)S(1)}, bf16[416,512]{1,0:T(8,128)(2,1)S(1)}, u32[]{:S(2)}, u32[]{:S(2)}) collective-permute-start(bf16[416,512]{1,0:T(8,128)(2,1)S(1)} %get-tuple-element.88), channel_id=1, source_target_pairs={{4,8},{8,4},{5,9},{9,5},{6,10},{10,6},{7,11},{11,7},{20,24},{24,20... | collective-permute-start | bytes 1277960 | tf_op jit(solution)/shard_map/ppermute | solution.py:469
  40.5 15.8 %collective-permute-start.11 = (bf16[384,512]{1,0:T(8,128)(2,1)S(1)}, bf16[384,512]{1,0:T(8,128)(2,1)S(1)}, u32[]{:S(2)}, u32[]{:S(2)}) collective-permute-start(bf16[384,512]{1,0:T(8,128)(2,1)S(1)} %get-tuple-element.103), channel_id=1, source_target_pairs={{0,4},{4,0},{8,12},{12,8},{1,5},{5,1},{9,13},{13,9},{2,6},{6,2},{1... | collective-permute-start | bytes 1179656 | tf_op jit(solution)/shard_map/ppermute | solution.py:468
  42.7 13.7 %collective-permute-start.12 = (bf16[384,512]{1,0:T(8,128)(2,1)S(1)}, bf16[384,512]{1,0:T(8,128)(2,1)S(1)}, u32[]{:S(2)}, u32[]{:S(2)}) collective-permute-start(bf16[384,512]{1,0:T(8,128)(2,1)S(1)} %get-tuple-element.104), channel_id=1, source_target_pairs={{4,8},{8,4},{5,9},{9,5},{6,10},{10,6},{7,11},{11,7},{20,24},{24,20... | collective-permute-start | bytes 1179656 | tf_op jit(solution)/shard_map/ppermute | solution.py:469
  46.1 10.2 %collective-permute-start.9 = (bf16[384,256]{1,0:T(8,128)(2,1)S(1)}, bf16[384,256]{1,0:T(8,128)(2,1)S(1)}, u32[]{:S(2)}, u32[]{:S(2)}) collective-permute-start(bf16[384,256]{1,0:T(8,128)(2,1)S(1)} %get-tuple-element.100), channel_id=1, source_target_pairs={{0,4},{4,0},{8,12},{12,8},{1,5},{5,1},{9,13},{13,9},{2,6},{6,2},{1... | collective-permute-start | bytes 589832 | tf_op jit(solution)/shard_map/ppermute | solution.py:468
  48.5 7.8 %collective-permute-start.10 = (bf16[384,256]{1,0:T(8,128)(2,1)S(1)}, bf16[384,256]{1,0:T(8,128)(2,1)S(1)}, u32[]{:S(2)}, u32[]{:S(2)}) collective-permute-start(bf16[384,256]{1,0:T(8,128)(2,1)S(1)} %get-tuple-element.101), channel_id=1, source_target_pairs={{4,8},{8,4},{5,9},{9,5},{6,10},{10,6},{7,11},{11,7},{20,24},{24,20... | collective-permute-start | bytes 589832 | tf_op jit(solution)/shard_map/ppermute | solution.py:469

commit v9 on v8

--- a/solution.py
+++ b/solution.py
@@ -540,7 +540,7 @@
         (full(*near_grid), full(*near_grid), full(3, SIDE, TOK_FRAME)),
         [full(FR_DEV, 3, SIDE, TOK_FRAME)], MOVED * unit,
     )
-    f_one, f_two, own_stats = lax.optimization_barrier((f_one, f_two, own_stats))
+    f_two, f_one, own_stats = lax.optimization_barrier((f_two, f_one, own_stats))
     note = full(2 * NOTES, TOK_FRAME)
     masked, grad_probs, mine, n_one, n_two, s_far, s_other = call(
         stats_kernel, "stats", (table,), (key, value, moved_bias, own_stats, f_one, f_two),
@@ -551,7 +551,7 @@
     s_far, s_other = swap_far(s_far, s_other)
     v_send, mine = lax.optimization_barrier((v_send, mine))
     v_one, v_two = swap(v_send, v_send)
-    k_one, k_two, s_far, s_other = lax.optimization_barrier((k_one, k_two, s_far, s_other))
+    k_two, k_one, s_far, s_other = lax.optimization_barrier((k_two, k_one, s_far, s_other))
     windows = low(DEPTH, 3 * ROWS, HD)
     accums = full(DEPTH, 3 * ROWS, HD)
     pairs = low(heads, FR_DEV, SLOTS, TOK_FRAME)

time: 57.8 us -> 57.4 us (level)
  waiting for transfers between devices: 9.44 us -> 4.53 us
  starting transfers between devices: 23.2 us -> 27.1 us
    ppermute x6, waiting for transfers between devices: 9.42 us -> 2.66 us  [swap(): lax.ppermute(one, 'frames', both_ways(first))]
    ppermute x1, starting transfers between devices: 2.69 us -> 6.74 us  [swap_far(): far = lax.ppermute(far, 'frames', both_ways(near))]
    ppermute x1, waiting for transfers between devices: 0.01 us -> 1.85 us  [swap_far(): far = lax.ppermute(far, 'frames', both_ways(near))]
  transfers between devices with their start and end apart: 13 -> 13, of which waited for: 5 -> 2; matrix products, arithmetic and copies ran while one was open for 3% -> 3% of each run, Pallas kernels for 34% -> 35%
where the time goes in v9:
time: 57.4 us; the launch traced here: 56.6 us
  starting transfers between devices  27.1 us (47%)
  Pallas kernels  22.2 us (39%)
  waiting for transfers between devices  4.53 us (8%)
  other arithmetic  1.04 us (2%)
  between operations  1 us (2%)
  local copies, waits for them, and re-layouts  0.73 us (1%)
    pallas_call x10, Pallas kernels, call(): pl.pallas_call(kernel, out_shape=outs, in_specs=[pl.BlockSpec(memory_spac...  22.2 us
    ppermute x6, starting transfers between devices, swap(): lax.ppermute(one, 'frames', both_ways(first))  16.1 us
    ppermute x1, starting transfers between devices, swap_far(): far = lax.ppermute(far, 'frames', both_ways(near))  6.74 us
    ppermute x6, starting transfers between devices, swap(): lax.ppermute(two, 'frames', both_ways(second))  4.21 us
    ppermute x6, waiting for transfers between devices, swap(): lax.ppermute(one, 'frames', both_ways(first))  2.66 us
    ppermute x1, waiting for transfers between devices, swap_far(): far = lax.ppermute(far, 'frames', both_ways(near))  1.85 us
  transfers between devices with their start and end apart: 13, of which 2 were waited for; matrix products, arithmetic and copies ran while one was open for 3% of the time, Pallas kernels for 35%

profile of v9, /device:TPU:0, one launch (start us, length us, event | category | flops | bytes accessed | tf_op | source)
XLA Modules:
  0.0 56.6 jit_solution(7730745236632746254)
XLA Ops:
  0.6 0.0 copy-start.1
  0.6 0.0 copy-start
  0.7 1.4 %pack.1 = (bf16[2,384,256]{2,1,0:T(8,128)(2,1)S(1)}, bf16[384,512]{1,0:T(8,128)(2,1)S(1)}, bf16[384,512]{1,0:T(8,128)(2,1)S(1)}) custom-call(bf16[384,768]{1,0:T(8,128)(2,1)} %queries.1, bf16[384,768]{1,0:T(8,128)(2,1)} %grad_out.1, bf16[384,768]{1,0:T(8,128)(2,1)} %keys.1, bf16[384,768]{1,0:T(8,128)(2,1)} %values.1), custom_call_target="tpu_custom_call" | custom-call | flops 56623104 | tf_op jit(solution)/shard_map/pack/pallas_call | solution.py:497
  2.0 3.1 %collective-permute-start.3 = (bf16[2,384,256]{2,1,0:T(8,128)(2,1)S(1)}, bf16[2,384,256]{2,1,0:T(8,128)(2,1)S(1)}, u32[]{:S(2)}, u32[]{:S(2)}) collective-permute-start(bf16[2,384,256]{2,1,0:T(8,128)(2,1)S(1)} %get-tuple-element.63), channel_id=1, source_target_pairs={{0,4},{4,0},{8,12},{12,8},{1,5},{5,1},{9,13},{13,9},{2,6},{6,2},{1... | collective-permute-start | bytes 1179656 | tf_op jit(solution)/shard_map/ppermute | solution.py:468
  5.1 0.7 %collective-permute-start.2 = (bf16[2,384,256]{2,1,0:T(8,128)(2,1)S(1)}, bf16[2,384,256]{2,1,0:T(8,128)(2,1)S(1)}, u32[]{:S(2)}, u32[]{:S(2)}) collective-permute-start(bf16[2,384,256]{2,1,0:T(8,128)(2,1)S(1)} %get-tuple-element.63), channel_id=1, source_target_pairs={{4,8},{8,4},{5,9},{9,5},{6,10},{10,6},{7,11},{11,7},{20,24},{24,20... | collective-permute-start | bytes 1179656 | tf_op jit(solution)/shard_map/ppermute | solution.py:469
  5.8 4.4 %collective-permute-start.1 = (bf16[384,512]{1,0:T(8,128)(2,1)S(1)}, bf16[384,512]{1,0:T(8,128)(2,1)S(1)}, u32[]{:S(2)}, u32[]{:S(2)}) collective-permute-start(bf16[384,512]{1,0:T(8,128)(2,1)S(1)} %get-tuple-element.60), channel_id=1, source_target_pairs={{0,4},{4,0},{8,12},{12,8},{1,5},{5,1},{9,13},{13,9},{2,6},{6,2},{1... | collective-permute-start | bytes 1179656 | tf_op jit(solution)/shard_map/ppermute | solution.py:468
  10.2 0.7 %collective-permute-start = (bf16[384,512]{1,0:T(8,128)(2,1)S(1)}, bf16[384,512]{1,0:T(8,128)(2,1)S(1)}, u32[]{:S(2)}, u32[]{:S(2)}) collective-permute-start(bf16[384,512]{1,0:T(8,128)(2,1)S(1)} %get-tuple-element.60), channel_id=1, source_target_pairs={{4,8},{8,4},{5,9},{9,5},{6,10},{10,6},{7,11},{11,7},{20,24},{24,20... | collective-permute-start | bytes 1179656 | tf_op jit(solution)/shard_map/ppermute | solution.py:469
  10.9 0.0 copy-done.1
  10.9 0.1 pad_dynamic-slice_fusion.1
  11.0 0.1 copy.10
  11.1 0.1 reshape.12
  11.2 0.0 copy-done
  11.2 0.1 pad_dynamic-slice_fusion
  11.3 0.2 copy.11
  11.4 0.1 reshape.13
  11.6 0.1 concatenate.6.table
  11.7 2.2 %stage.1 = (bf16[384,768]{1,0:T(8,128)(2,1)S(1)}, bf16[384,768]{1,0:T(8,128)(2,1)S(1)}, bf16[384,768]{1,0:T(8,128)(2,1)S(1)}, bf16[384,768]{1,0:T(8,128)(2,1)S(1...) custom-call(s32[309]{0:T(512)S(1)} %concatenate.6.table, bf16[384,768]{1,0:T(8,128)(2,1)} %queries.1, ...), custom_call_target="tpu_custom_call" | custom-call | flops 56623104 | tf_op jit(solution)/shard_map/stage/pallas_call | solution.py:497
  13.9 1.7 %own_stats.1 = (f32[2,2,2,192,192]{4,3,2,1,0:T(8,128)S(1)}, f32[2,2,2,192,192]{4,3,2,1,0:T(8,128)S(1)}, f32[3,4,192]{2,1,0:T(4,128)S(1)}) custom-call(s32[309]{0:T(512)S(1)} %concatenate.6.table, bf16[384,768]{1,0:T(8,128)(2,1)S(1)} %get-tuple-element.56.queries, bf16[384,768]{1,0:T(8,128)(2,1)S(1)} %get-tuple-element.57.grad_out, ...), custom_call_target="tpu_custom_call" | custom-call | flops 113246208 | tf_op jit(solution)/shard_map/own_stats/pallas_call | solution.py:497
  15.6 0.0 collective-permute-done.3.f_one
  15.6 0.0 collective-permute-done.2.f_two
  15.6 1.8 %stats.1 = (f32[4,2,2,192,192]{4,3,2,1,0:T(8,128)S(1)}, f32[4,2,2,192,192]{4,3,2,1,0:T(8,128)S(1)}, f32[3,12,192]{2,1,0:T(8,128)S(1)}, f32[64,192]{1,0:T(8,128)S...) custom-call(s32[309]{0:T(512)S(1)} %concatenate.6.table, ...), custom_call_target="tpu_custom_call" | custom-call | flops 226492416 | tf_op jit(solution)/shard_map/stats/pallas_call | solution.py:497
  17.4 6.7 %collective-permute-start.4 = (f32[3,4,192]{2,1,0:T(4,128)S(1)}, f32[3,4,192]{2,1,0:T(4,128)S(1)}, u32[]{:S(2)}, u32[]{:S(2)}) collective-permute-start(f32[3,4,192]{2,1,0:T(4,128)S(1)} %get-tuple-element.68), channel_id=1, source_target_pairs={{0,8},{8,0},{4,12},{12,4},{1,9},{9,1},{5,13},{13,5},{2,10},{10,2},... | collective-permute-start | bytes 27656 | tf_op jit(solution)/shard_map/ppermute | solution.py:477
  24.1 0.7 %collective-permute-start.6 = (bf16[384,512]{1,0:T(8,128)(2,1)S(1)}, bf16[384,512]{1,0:T(8,128)(2,1)S(1)}, u32[]{:S(2)}, u32[]{:S(2)}) collective-permute-start(bf16[384,512]{1,0:T(8,128)(2,1)S(1)} %get-tuple-element.77), channel_id=1, source_target_pairs={{4,8},{8,4},{5,9},{9,5},{6,10},{10,6},{7,11},{11,7},{20,24},{24,20... | collective-permute-start | bytes 1179656 | tf_op jit(solution)/shard_map/ppermute | solution.py:469
  24.8 1.9 %collective-permute-start.5 = (bf16[384,512]{1,0:T(8,128)(2,1)S(1)}, bf16[384,512]{1,0:T(8,128)(2,1)S(1)}, u32[]{:S(2)}, u32[]{:S(2)}) collective-permute-start(bf16[384,512]{1,0:T(8,128)(2,1)S(1)} %get-tuple-element.77), channel_id=1, source_target_pairs={{0,4},{4,0},{8,12},{12,8},{1,5},{5,1},{9,13},{13,9},{2,6},{6,2},{1... | collective-permute-start | bytes 1179656 | tf_op jit(solution)/shard_map/ppermute | solution.py:468
  26.7 0.0 collective-permute-done.1.k_one
  26.7 0.0 collective-permute-done.k_two
  26.7 1.9 %collective-permute-done.4.s_far = f32[3,4,192]{2,1,0:T(4,128)S(1)} collective-permute-done((f32[3,4,192]{2,1,0:T(4,128)S(1)}, f32[3,4,192]{2,1,0:T(4,128)S(1)}, u32[]{:S(2)}, u32[]{:S(2)}) %collective-permute-start.4) | collective-permute-done | bytes 9248 | tf_op jit(solution)/shard_map/ppermute | solution.py:477
  28.5 4.9 %values_part.1 = (bf16[4,2,576,128]{3,2,1,0:T(8,128)(2,1)S(1)}, bf16[4,2,576,192]{3,2,1,0:T(8,128)(2,1)S(1)}, f32[384,512]{1,0:T(8,128)S(1)}, bf16[416,512]{1,0:T(8,128)(2,1)S(1)}, bf16[416,512]{1,0:T(8,128)(2,1)S(1)}) custom-call(s32[309]{0:T(512)S(1)} %concatenate.6.table, bf16[384,768]{1,0:T(8,128)(2,1)S(1)} %get-tuple-element.56.queries, ...), custom_call_target="tpu_custom_call" | custom-call | flops 452984832 | tf_op jit(solution)/shard_map/values_part/pallas_call | solution.py:497
  33.5 0.4 collective-permute-start.7
  33.8 0.9 %collective-permute-start.8 = (bf16[416,512]{1,0:T(8,128)(2,1)S(1)}, bf16[416,512]{1,0:T(8,128)(2,1)S(1)}, u32[]{:S(2)}, u32[]{:S(2)}) collective-permute-start(bf16[416,512]{1,0:T(8,128)(2,1)S(1)} %get-tuple-element.88), channel_id=1, source_target_pairs={{4,8},{8,4},{5,9},{9,5},{6,10},{10,6},{7,11},{11,7},{20,24},{24,20... | collective-permute-start | bytes 1277960 | tf_op jit(solution)/shard_map/ppermute | solution.py:469
  34.7 0.0 collective-permute-done.6.v_two
  34.7 0.0 collective-permute-done.5.v_one
  34.7 4.7 %keys_part.1 = (bf16[4,2,576,192]{3,2,1,0:T(8,128)(2,1)S(1)}, f32[384,512]{1,0:T(8,128)S(1)}, bf16[384,512]{1,0:T(8,128)(2,1)S(1)}, bf16[384,512]{1,0:T(8,128)(2,1)S(1)}) custom-call(s32[309]{0:T(512)S(1)} %concatenate.6.table, bf16[384,768]{1,0:T(8,128)(2,1)S(1)} %get-tuple-element.56.queries, bf16[384,768]{1,0:T(8,128)(2,1)S(1)} %get-tuple-element.57.grad_out, ...), custom_call_target="tpu_custom_call" | custom-call | flops 452984832 | tf_op jit(solution)/shard_map/keys_part/pallas_call | solution.py:497
  39.4 5.1 %collective-permute-start.11 = (bf16[384,512]{1,0:T(8,128)(2,1)S(1)}, bf16[384,512]{1,0:T(8,128)(2,1)S(1)}, u32[]{:S(2)}, u32[]{:S(2)}) collective-permute-start(bf16[384,512]{1,0:T(8,128)(2,1)S(1)} %get-tuple-element.103), channel_id=1, source_target_pairs={{0,4},{4,0},{8,12},{12,8},{1,5},{5,1},{9,13},{13,9},{2,6},{6,2},{1... | collective-permute-start | bytes 1179656 | tf_op jit(solution)/shard_map/ppermute | solution.py:468
  44.4 0.7 %collective-permute-start.12 = (bf16[384,512]{1,0:T(8,128)(2,1)S(1)}, bf16[384,512]{1,0:T(8,128)(2,1)S(1)}, u32[]{:S(2)}, u32[]{:S(2)}) collective-permute-start(bf16[384,512]{1,0:T(8,128)(2,1)S(1)} %get-tuple-element.104), channel_id=1, source_target_pairs={{4,8},{8,4},{5,9},{9,5},{6,10},{10,6},{7,11},{11,7},{20,24},{24,20... | collective-permute-start | bytes 1179656 | tf_op jit(solution)/shard_map/ppermute | solution.py:469
  45.1 1.2 %rest.1 = (bf16[384,512]{1,0:T(8,128)(2,1)S(1)}, f32[384,512]{1,0:T(8,128)S(1)}, f32[384,512]{1,0:T(8,128)S(1)}) custom-call(bf16[384,768]{1,0:T(8,128)(2,1)S(1)} %get-tuple-element.56.queries, bf16[384,768]{1,0:T(8,128)(2,1)S(1)} %get-tuple-element.57.grad_out, bf16[4,2,576,128]{3,2,1,0:T(8,128)(2,1)S(1)} %get-tuple-element.73.chosen_in, ...), custom_call_target="tpu_custom_call" | custom-call | flops 226492416 | tf_op jit(solution)/shard_map/rest/pallas_call | solution.py:497
  46.3 0.0 collective-permute-done.7.r_one
  46.3 0.0 collective-permute-done.8.r_two
  46.3 1.1 %back.1 = (bf16[4,2,2,192,192]{4,3,2,1,0:T(8,128)(2,1)S(1)}, bf16[4,2,2,192,192]{4,3,2,1,0:T(8,128)(2,1)S(1)}, f32[12,192]{1,0:T(8,128)S(1)}, f32[12,192]{1,0:T(...) custom-call(s32[309]{0:T(512)S(1)} %concatenate.6.table, ...), custom_call_target="tpu_custom_call" | custom-call | flops 113246208 | tf_op jit(solution)/shard_map/back/pallas_call | solution.py:497
  47.5 1.3 %collective-permute-start.9 = (bf16[384,256]{1,0:T(8,128)(2,1)S(1)}, bf16[384,256]{1,0:T(8,128)(2,1)S(1)}, u32[]{:S(2)}, u32[]{:S(2)}) collective-permute-start(bf16[384,256]{1,0:T(8,128)(2,1)S(1)} %get-tuple-element.100), channel_id=1, source_target_pairs={{0,4},{4,0},{8,12},{12,8},{1,5},{5,1},{9,13},{13,9},{2,6},{6,2},{1... | collective-permute-start | bytes 589832 | tf_op jit(solution)/shard_map/ppermute | solution.py:468
  48.8 0.7 %collective-permute-start.10 = (bf16[384,256]{1,0:T(8,128)(2,1)S(1)}, bf16[384,256]{1,0:T(8,128)(2,1)S(1)}, u32[]{:S(2)}, u32[]{:S(2)}) collective-permute-start(bf16[384,256]{1,0:T(8,128)(2,1)S(1)} %get-tuple-element.101), channel_id=1, source_target_pairs={{4,8},{8,4},{5,9},{9,5},{6,10},{10,6},{7,11},{11,7},{20,24},{24,20... | collective-permute-start | bytes 589832 | tf_op jit(solution)/shard_map/ppermute | solution.py:469
  49.5 0.2 add_convert_fusion
  49.7 2.2 %home.1 = (f32[384,256]{1,0:T(8,128)S(1)}, bf16[384,256]{1,0:T(8,128)(2,1)S(1)}, bf16[384,256]{1,0:T(8,128)(2,1)S(1)}) custom-call(s32[309]{0:T(512)S(1)} %concatenate.6.table, bf16[384,768]{1,0:T(8,128)(2,1)S(1)} %get-tuple-element.56.queries, bf16[384,768]{1,0:T(8,128)(2,1)S(1)} %get-tuple-element.57.grad_out, ...), custom_call_target="tpu_custom_call" | custom-call | flops 339738624 | tf_op jit(solution)/shard_map/home/pallas_call | solution.py:497
  51.9 0.9 %pad_maximum_fusion = bf16[384,768]{1,0:T(8,128)(2,1)} fusion(bf16[384,512]{1,0:T(8,128)(2,1)S(1)} %add_convert_fusion, bf16[384,256]{1,0:T(8,128)(2,1)S(1)} %get-tuple-element.107), kind=kLoop, calls=%fused_computation.1 | loop fusion | flops 1179648 | bytes 1179648 | tf_op jit(solution)/shard_map/concatenate | solution.py:592
  52.8 2.6 %collective-permute-done.9.rq_one = bf16[384,256]{1,0:T(8,128)(2,1)S(1)} collective-permute-done((bf16[384,256]{1,0:T(8,128)(2,1)S(1)}, bf16[384,256]{1,0:T(8,128)(2,1)S(1)}, u32[]{:S(2)}, u32[]{:S(2)}) %collective-permute-start.9) | collective-permute-done | bytes 196640 | tf_op jit(solution)/shard_map/ppermute | solution.py:468
  55.4 0.0 collective-permute-done.10.rq_two
  55.4 0.0 collective-permute-done.11.rk_one
  55.4 0.0 collective-permute-done.12.rk_two
  55.4 1.0 %last.1 = (bf16[384,768]{1,0:T(8,128)(2,1)}, bf16[384,768]{1,0:T(8,128)(2,1)}) custom-call(bf16[384,512]{1,0:T(8,128)(2,1)S(1)} %get-tuple-element.81.gq_rest, bf16[384,256]{1,0:T(8,128)(2,1)S(1)} %get-tuple-element.98.gk_near, f32[384,256]{1,0:T(8,128)S(1)} %get-tuple-element.99.gq_near, bf16[384,256]{1,0:T(8,128)(2,1)S(1)} %collective-permute-done.9.rq_one, ...), custom_call_target="tpu_custom_call" | custom-call | flops 56623104 | tf_op jit(solution)/shard_map/last/pallas_call | solution.py:497
  (1 shorter events, 0.0 us)
Async XLA Ops:
  0.6 10.3 %copy-start.1 = (s32[8,3]{0,1:T(4,128)S(1)}, s32[8,3]{0,1:T(4,128)}, u32[]{:S(2)}) copy-start(s32[8,3]{0,1:T(4,128)} %param.10) | copy-start | bytes 292
  0.6 10.6 %copy-start = (s32[8,3,4,4]{0,3,2,1:T(4,128)S(1)}, s32[8,3,4,4]{0,3,2,1:T(4,128)}, u32[]{:S(2)}) copy-start(s32[8,3,4,4]{0,3,2,1:T(4,128)} %param.11) | copy-start | bytes 4612
  2.0 13.6 %collective-permute-start.3 = (bf16[2,384,256]{2,1,0:T(8,128)(2,1)S(1)}, bf16[2,384,256]{2,1,0:T(8,128)(2,1)S(1)}, u32[]{:S(2)}, u32[]{:S(2)}) collective-permute-start(bf16[2,384,256]{2,1,0:T(8,128)(2,1)S(1)} %get-tuple-element.63), channel_id=1, source_target_pairs={{0,4},{4,0},{8,12},{12,8},{1,5},{5,1},{9,13},{13,9},{2,6},{6,2},{1... | collective-permute-start | bytes 1179656 | tf_op jit(solution)/shard_map/ppermute | solution.py:468
  5.1 10.5 %collective-permute-start.2 = (bf16[2,384,256]{2,1,0:T(8,128)(2,1)S(1)}, bf16[2,384,256]{2,1,0:T(8,128)(2,1)S(1)}, u32[]{:S(2)}, u32[]{:S(2)}) collective-permute-start(bf16[2,384,256]{2,1,0:T(8,128)(2,1)S(1)} %get-tuple-element.63), channel_id=1, source_target_pairs={{4,8},{8,4},{5,9},{9,5},{6,10},{10,6},{7,11},{11,7},{20,24},{24,20... | collective-permute-start | bytes 1179656 | tf_op jit(solution)/shard_map/ppermute | solution.py:469
  5.8 20.9 %collective-permute-start.1 = (bf16[384,512]{1,0:T(8,128)(2,1)S(1)}, bf16[384,512]{1,0:T(8,128)(2,1)S(1)}, u32[]{:S(2)}, u32[]{:S(2)}) collective-permute-start(bf16[384,512]{1,0:T(8,128)(2,1)S(1)} %get-tuple-element.60), channel_id=1, source_target_pairs={{0,4},{4,0},{8,12},{12,8},{1,5},{5,1},{9,13},{13,9},{2,6},{6,2},{1... | collective-permute-start | bytes 1179656 | tf_op jit(solution)/shard_map/ppermute | solution.py:468
  10.2 16.4 %collective-permute-start = (bf16[384,512]{1,0:T(8,128)(2,1)S(1)}, bf16[384,512]{1,0:T(8,128)(2,1)S(1)}, u32[]{:S(2)}, u32[]{:S(2)}) collective-permute-start(bf16[384,512]{1,0:T(8,128)(2,1)S(1)} %get-tuple-element.60), channel_id=1, source_target_pairs={{4,8},{8,4},{5,9},{9,5},{6,10},{10,6},{7,11},{11,7},{20,24},{24,20... | collective-permute-start | bytes 1179656 | tf_op jit(solution)/shard_map/ppermute | solution.py:469
  17.4 11.1 %collective-permute-start.4 = (f32[3,4,192]{2,1,0:T(4,128)S(1)}, f32[3,4,192]{2,1,0:T(4,128)S(1)}, u32[]{:S(2)}, u32[]{:S(2)}) collective-permute-start(f32[3,4,192]{2,1,0:T(4,128)S(1)} %get-tuple-element.68), channel_id=1, source_target_pairs={{0,8},{8,0},{4,12},{12,4},{1,9},{9,1},{5,13},{13,5},{2,10},{10,2},... | collective-permute-start | bytes 27656 | tf_op jit(solution)/shard_map/ppermute | solution.py:477
  24.1 10.6 %collective-permute-start.6 = (bf16[384,512]{1,0:T(8,128)(2,1)S(1)}, bf16[384,512]{1,0:T(8,128)(2,1)S(1)}, u32[]{:S(2)}, u32[]{:S(2)}) collective-permute-start(bf16[384,512]{1,0:T(8,128)(2,1)S(1)} %get-tuple-element.77), channel_id=1, source_target_pairs={{4,8},{8,4},{5,9},{9,5},{6,10},{10,6},{7,11},{11,7},{20,24},{24,20... | collective-permute-start | bytes 1179656 | tf_op jit(solution)/shard_map/ppermute | solution.py:469
  24.8 9.9 %collective-permute-start.5 = (bf16[384,512]{1,0:T(8,128)(2,1)S(1)}, bf16[384,512]{1,0:T(8,128)(2,1)S(1)}, u32[]{:S(2)}, u32[]{:S(2)}) collective-permute-start(bf16[384,512]{1,0:T(8,128)(2,1)S(1)} %get-tuple-element.77), channel_id=1, source_target_pairs={{0,4},{4,0},{8,12},{12,8},{1,5},{5,1},{9,13},{13,9},{2,6},{6,2},{1... | collective-permute-start | bytes 1179656 | tf_op jit(solution)/shard_map/ppermute | solution.py:468
  33.5 12.9 %collective-permute-start.7 = (bf16[416,512]{1,0:T(8,128)(2,1)S(1)}, bf16[416,512]{1,0:T(8,128)(2,1)S(1)}, u32[]{:S(2)}, u32[]{:S(2)}) collective-permute-start(bf16[416,512]{1,0:T(8,128)(2,1)S(1)} %get-tuple-element.87), channel_id=1, source_target_pairs={{0,4},{4,0},{8,12},{12,8},{1,5},{5,1},{9,13},{13,9},{2,6},{6,2},{1... | collective-permute-start | bytes 1277960 | tf_op jit(solution)/shard_map/ppermute | solution.py:468
  33.8 12.5 %collective-permute-start.8 = (bf16[416,512]{1,0:T(8,128)(2,1)S(1)}, bf16[416,512]{1,0:T(8,128)(2,1)S(1)}, u32[]{:S(2)}, u32[]{:S(2)}) collective-permute-start(bf16[416,512]{1,0:T(8,128)(2,1)S(1)} %get-tuple-element.88), channel_id=1, source_target_pairs={{4,8},{8,4},{5,9},{9,5},{6,10},{10,6},{7,11},{11,7},{20,24},{24,20... | collective-permute-start | bytes 1277960 | tf_op jit(solution)/shard_map/ppermute | solution.py:469
  39.4 16.0 %collective-permute-start.11 = (bf16[384,512]{1,0:T(8,128)(2,1)S(1)}, bf16[384,512]{1,0:T(8,128)(2,1)S(1)}, u32[]{:S(2)}, u32[]{:S(2)}) collective-permute-start(bf16[384,512]{1,0:T(8,128)(2,1)S(1)} %get-tuple-element.103), channel_id=1, source_target_pairs={{0,4},{4,0},{8,12},{12,8},{1,5},{5,1},{9,13},{13,9},{2,6},{6,2},{1... | collective-permute-start | bytes 1179656 | tf_op jit(solution)/shard_map/ppermute | solution.py:468
  44.4 11.0 %collective-permute-start.12 = (bf16[384,512]{1,0:T(8,128)(2,1)S(1)}, bf16[384,512]{1,0:T(8,128)(2,1)S(1)}, u32[]{:S(2)}, u32[]{:S(2)}) collective-permute-start(bf16[384,512]{1,0:T(8,128)(2,1)S(1)} %get-tuple-element.104), channel_id=1, source_target_pairs={{4,8},{8,4},{5,9},{9,5},{6,10},{10,6},{7,11},{11,7},{20,24},{24,20... | collective-permute-start | bytes 1179656 | tf_op jit(solution)/shard_map/ppermute | solution.py:469
  47.5 7.9 %collective-permute-start.9 = (bf16[384,256]{1,0:T(8,128)(2,1)S(1)}, bf16[384,256]{1,0:T(8,128)(2,1)S(1)}, u32[]{:S(2)}, u32[]{:S(2)}) collective-permute-start(bf16[384,256]{1,0:T(8,128)(2,1)S(1)} %get-tuple-element.100), channel_id=1, source_target_pairs={{0,4},{4,0},{8,12},{12,8},{1,5},{5,1},{9,13},{13,9},{2,6},{6,2},{1... | collective-permute-start | bytes 589832 | tf_op jit(solution)/shard_map/ppermute | solution.py:468
  48.8 6.6 %collective-permute-start.10 = (bf16[384,256]{1,0:T(8,128)(2,1)S(1)}, bf16[384,256]{1,0:T(8,128)(2,1)S(1)}, u32[]{:S(2)}, u32[]{:S(2)}) collective-permute-start(bf16[384,256]{1,0:T(8,128)(2,1)S(1)} %get-tuple-element.101), channel_id=1, source_target_pairs={{4,8},{8,4},{5,9},{9,5},{6,10},{10,6},{7,11},{11,7},{20,24},{24,20... | collective-permute-start | bytes 589832 | tf_op jit(solution)/shard_map/ppermute | solution.py:469

commit v10 on v9

--- a/solution.py
+++ b/solution.py
@@ -98,17 +98,15 @@
     return moves
 
 
-def pack_kernel(queries, grad_out, keys, values, both, k_send, v_send, sems):
-    moves = copy_all(
-        [
-            (queries.at[:, :SPLIT], both.at[0]),
-            (grad_out.at[:, :SPLIT], both.at[1]),
-            (keys.at[:, SPLIT:], k_send),
-            (values.at[:, SPLIT:], v_send),
-        ],
-        sems,
-    )
-    for move in moves:
+def pack_queries_kernel(queries, grad_out, both, sems):
+    pairs = [(queries.at[:, :SPLIT], both.at[0]), (grad_out.at[:, :SPLIT], both.at[1])]
+    for move in copy_all(pairs, sems):
+        move.wait()
+
+
+def pack_keys_kernel(keys, values, k_send, v_send, sems):
+    pairs = [(keys.at[:, SPLIT:], k_send), (values.at[:, SPLIT:], v_send)]
+    for move in copy_all(pairs, sems):
         move.wait()
 
 
@@ -148,8 +146,17 @@
         accum[span(table, frame, slot), :] += parts[rows_of(slot - 1)]
 
 
+def own_scores_kernel(queries, k_own, bias, masked_out):
+    for head in range(masked_out.shape[0]):
+        column = column_of(MOVED + head)
+        for frame in range(FR_DEV):
+            rows = rows_of(frame)
+            scores = dot(k_own[rows, column], queries[rows, column], NT)
+            masked_out[head, frame] = scores * SCALE2 + bias[frame, :TOK_FRAME]
+
+
 def values_kernel(
-    table, queries, grad_out, k_own, bias, k_one, k_two, n_one, n_two,
+    table, queries, grad_out, k_own, bias, near_masked, k_one, k_two, n_one, n_two,
     chosen_out, prob_out, own_out, one_out, two_out,
     windows, accums,
 ):
@@ -161,16 +168,21 @@
         fill_window(window, k_one, k_own, k_two, column, far_column)
         accum[...] = jnp.zeros_like(accum)
         for frame in range(FR_DEV):
+            rows = rows_of(frame)
             chosen = chosen_out.at[head, frame]
-            pick(table, frame, window, chosen)
-            scores = dot(chosen[...], queries[rows_of(frame), column], NT)
-            masked = scores * SCALE2 + bias[frame]
-            raised = jnp.exp2(masked - jnp.max(masked, 0, keepdims=True))
-            inverse = 1.0 / jnp.sum(raised, 0, keepdims=True)
-            prob_low = (raised * inverse).astype(jnp.bfloat16)
-            prob_out[head, frame] = prob_low
-            far = dot(prob_low[TOK_FRAME:], grad_out[rows_of(frame), column], NN)
-            spread(table, frame, accum, far)
+            chosen[:TOK_FRAME] = k_own[rows, column]
+            for slot in range(1, NSEL):
+                chosen[rows_of(slot)] = window[span(table, frame, slot), :]
+            scores = dot(chosen[TOK_FRAME:], queries[rows, column], NT)
+            masked = (near_masked[head, frame], scores * SCALE2 + bias[frame, TOK_FRAME:])
+            highest = jnp.maximum(*(jnp.max(each, 0, keepdims=True) for each in masked))
+            near, far = (jnp.exp2(each - highest) for each in masked)
+            total = jnp.sum(near, 0, keepdims=True) + jnp.sum(far, 0, keepdims=True)
+            inverse = 1.0 / total
+            far_low = (far * inverse).astype(jnp.bfloat16)
+            prob_out[head, frame, :TOK_FRAME] = (near * inverse).astype(jnp.bfloat16)
+            prob_out[head, frame, TOK_FRAME:] = far_low
+            spread(table, frame, accum, dot(far_low, grad_out[rows, column], NN))
         one_out[:ROWS, far_column] = accum[0:ROWS].astype(one_out.dtype)
         own_out[:, far_column] = accum[ROWS : 2 * ROWS]
         two_out[:ROWS, far_column] = accum[2 * ROWS : 3 * ROWS].astype(two_out.dtype)
@@ -519,10 +531,13 @@
 
     unit = 2 * FR_DEV * NSEL * TOK_FRAME * TOK_FRAME * HD
     rest = width - SPLIT
-    y_send, k_send, v_send = call(
-        pack_kernel, "pack", (), (queries, grad_out, keys, values),
-        (low(2, ROWS, SPLIT), low(ROWS, rest), low(ROWS, rest)),
-        [pltpu.SemaphoreType.DMA((4,))], unit, pltpu.HBM,
+    (y_send,) = call(
+        pack_queries_kernel, "pack_queries", (), (queries, grad_out),
+        (low(2, ROWS, SPLIT),), [pltpu.SemaphoreType.DMA((2,))], unit, pltpu.HBM,
+    )
+    k_send, v_send = call(
+        pack_keys_kernel, "pack_keys", (), (keys, values),
+        (low(ROWS, rest), low(ROWS, rest)), [pltpu.SemaphoreType.DMA((2,))], unit, pltpu.HBM,
     )
     f_one, f_two = swap(y_send, y_send)
     k_one, k_two = swap(k_send, k_send)
@@ -540,7 +555,13 @@
         (full(*near_grid), full(*near_grid), full(3, SIDE, TOK_FRAME)),
         [full(FR_DEV, 3, SIDE, TOK_FRAME)], MOVED * unit,
     )
-    f_two, f_one, own_stats = lax.optimization_barrier((f_two, f_one, own_stats))
+    (near_scores,) = call(
+        own_scores_kernel, "own_scores", (), (query, key, bias),
+        (full(heads, FR_DEV, TOK_FRAME, TOK_FRAME),), [], heads * unit // 3,
+    )
+    f_two, f_one, own_stats, near_scores = lax.optimization_barrier(
+        (f_two, f_one, own_stats, near_scores)
+    )
     note = full(2 * NOTES, TOK_FRAME)
     masked, grad_probs, mine, n_one, n_two, s_far, s_other = call(
         stats_kernel, "stats", (table,), (key, value, moved_bias, own_stats, f_one, f_two),
@@ -557,7 +578,7 @@
     pairs = low(heads, FR_DEV, SLOTS, TOK_FRAME)
     chosen, prob_low, gv_own, gv_one, gv_two = call(
         values_kernel, "values_part", (table,),
-        (query, grad, key, bias, k_one, k_two, n_one, n_two),
+        (query, grad, key, bias, near_scores, k_one, k_two, n_one, n_two),
         (low(heads, FR_DEV, SLOTS, HD), pairs, full(ROWS, rest))
         + (low(ROWS + NOTES, rest),) * 2,
         [windows, accums], 2 * heads * unit,
@@ -569,12 +590,6 @@
         [windows, low(DEPTH, FR_DEV, SLOTS, HD), accums], 2 * heads * unit,
     )
     rk_one, rk_two = swap(gk_one, gk_two)
-    gq_rest, gv_own, gk_own = call(
-        rest_kernel, "rest", (),
-        (query, grad, chosen, prob_low, score_low, gv_own, gk_own),
-        (low(ROWS, rest), full(ROWS, rest), full(ROWS, rest)), [], heads * unit,
-    )
-    rv_one, rv_two, gv_own = lax.optimization_barrier((rv_one, rv_two, gv_own))
     y_prob, y_score, logs, deltas, gq_one, gq_two = call(
         back_kernel, "back", (table,),
         (key, masked, grad_probs, mine, rv_one, rv_two, s_far, s_other),
@@ -583,6 +598,12 @@
         [full(2, ROWS, SPLIT), full(2, 2 * NOTES, TOK_FRAME)], MOVED * unit,
     )
     rq_one, rq_two = swap(gq_one, gq_two)
+    score_low, logs = lax.optimization_barrier((score_low, logs))
+    gq_rest, gv_own, gk_own = call(
+        rest_kernel, "rest", (),
+        (query, grad, chosen, prob_low, score_low, gv_own, gk_own),
+        (low(ROWS, rest), full(ROWS, rest), full(ROWS, rest)), [], heads * unit,
+    )
     gq_near, gk_near, gv_near = call(
         home_kernel, "home", (table,),
         (query, grad, key, f_one, f_two, near_masked, near_grads, y_prob, y_score, logs, deltas),

time: 57.4 us -> 57.5 us (level)
  waiting for transfers between devices: 4.53 us -> 8.31 us
  starting transfers between devices: 27.1 us -> 24.2 us
    ppermute x6, waiting for transfers between devices: 2.66 us -> 8.29 us  [swap(): lax.ppermute(one, 'frames', both_ways(first))]
    ppermute x1, starting transfers between devices: 6.74 us -> 2.69 us  [swap_far(): far = lax.ppermute(far, 'frames', both_ways(near))]
    ppermute x1, waiting for transfers between devices: 1.85 us -> 0.01 us  [swap_far(): far = lax.ppermute(far, 'frames', both_ways(near))]
    ppermute x6, starting transfers between devices: 16.1 us -> 17.3 us  [swap(): lax.ppermute(one, 'frames', both_ways(first))]
    pallas_call x10 -> x12, Pallas kernels: 22.2 us -> 22 us  [call(): pl.pallas_call(kernel, out_shape=outs, in_specs=[pl.BlockSpec(memory_spac...]
  transfers between devices with their start and end apart: 13 -> 13, of which waited for: 2 -> 5; matrix products, arithmetic and copies ran while one was open for 3% -> 3% of each run, Pallas kernels for 35% -> 35%
where the time goes in v10:
time: 57.5 us; the launch traced here: 57.2 us
  starting transfers between devices  24.2 us (42%)
  Pallas kernels  22 us (38%)
  waiting for transfers between devices  8.31 us (14%)
  other arithmetic  1.04 us (2%)
  between operations  0.97 us (2%)
  local copies, waits for them, and re-layouts  0.73 us (1%)
    pallas_call x12, Pallas kernels, call(): pl.pallas_call(kernel, out_shape=outs, in_specs=[pl.BlockSpec(memory_spac...  22 us
    ppermute x6, starting transfers between devices, swap(): lax.ppermute(one, 'frames', both_ways(first))  17.3 us
    ppermute x6, waiting for transfers between devices, swap(): lax.ppermute(one, 'frames', both_ways(first))  8.29 us
    ppermute x6, starting transfers between devices, swap(): lax.ppermute(two, 'frames', both_ways(second))  4.25 us
    ppermute x1, starting transfers between devices, swap_far(): far = lax.ppermute(far, 'frames', both_ways(near))  2.69 us
  transfers between devices with their start and end apart: 13, of which 5 were waited for; matrix products, arithmetic and copies ran while one was open for 3% of the time, Pallas kernels for 35%

profile of v10, /device:TPU:0, one launch (start us, length us, event | category | flops | bytes accessed | tf_op | source)
XLA Modules:
  0.0 57.2 jit_solution(4442627633241865844)
XLA Ops:
  0.6 0.0 copy-start
  0.6 0.0 copy-start.1
  0.7 1.1 %pack_queries.1 = bf16[2,384,256]{2,1,0:T(8,128)(2,1)S(1)} custom-call(bf16[384,768]{1,0:T(8,128)(2,1)} %queries.1, bf16[384,768]{1,0:T(8,128)(2,1)} %grad_out.1), custom_call_target="tpu_custom_call" | custom-call | flops 56623104 | tf_op jit(solution)/shard_map/pack_queries/pallas_call | solution.py:509
  1.7 0.7 %collective-permute-start = (bf16[2,384,256]{2,1,0:T(8,128)(2,1)S(1)}, bf16[2,384,256]{2,1,0:T(8,128)(2,1)S(1)}, u32[]{:S(2)}, u32[]{:S(2)}) collective-permute-start(bf16[2,384,256]{2,1,0:T(8,128)(2,1)S(1)} %pack_queries.1), channel_id=1, source_target_pairs={{4,8},{8,4},{5,9},{9,5},{6,10},{10,6},{7,11},{11,7},{20,24},{24,20... | collective-permute-start | bytes 1179656 | tf_op jit(solution)/shard_map/ppermute | solution.py:481
  2.4 5.9 %collective-permute-start.1 = (bf16[2,384,256]{2,1,0:T(8,128)(2,1)S(1)}, bf16[2,384,256]{2,1,0:T(8,128)(2,1)S(1)}, u32[]{:S(2)}, u32[]{:S(2)}) collective-permute-start(bf16[2,384,256]{2,1,0:T(8,128)(2,1)S(1)} %pack_queries.1), channel_id=1, source_target_pairs={{0,4},{4,0},{8,12},{12,8},{1,5},{5,1},{9,13},{13,9},{2,6},{6,2},{1... | collective-permute-start | bytes 1179656 | tf_op jit(solution)/shard_map/ppermute | solution.py:480
  8.3 1.1 %pack_keys.1 = (bf16[384,512]{1,0:T(8,128)(2,1)S(1)}, bf16[384,512]{1,0:T(8,128)(2,1)S(1)}) custom-call(bf16[384,768]{1,0:T(8,128)(2,1)} %keys.1, bf16[384,768]{1,0:T(8,128)(2,1)} %values.1), custom_call_target="tpu_custom_call" | custom-call | flops 56623104 | tf_op jit(solution)/shard_map/pack_keys/pallas_call | solution.py:509
  9.4 0.7 %collective-permute-start.2 = (bf16[384,512]{1,0:T(8,128)(2,1)S(1)}, bf16[384,512]{1,0:T(8,128)(2,1)S(1)}, u32[]{:S(2)}, u32[]{:S(2)}) collective-permute-start(bf16[384,512]{1,0:T(8,128)(2,1)S(1)} %get-tuple-element.63), channel_id=1, source_target_pairs={{4,8},{8,4},{5,9},{9,5},{6,10},{10,6},{7,11},{11,7},{20,24},{24,20... | collective-permute-start | bytes 1179656 | tf_op jit(solution)/shard_map/ppermute | solution.py:481
  10.1 1.8 %collective-permute-start.3 = (bf16[384,512]{1,0:T(8,128)(2,1)S(1)}, bf16[384,512]{1,0:T(8,128)(2,1)S(1)}, u32[]{:S(2)}, u32[]{:S(2)}) collective-permute-start(bf16[384,512]{1,0:T(8,128)(2,1)S(1)} %get-tuple-element.63), channel_id=1, source_target_pairs={{0,4},{4,0},{8,12},{12,8},{1,5},{5,1},{9,13},{13,9},{2,6},{6,2},{1... | collective-permute-start | bytes 1179656 | tf_op jit(solution)/shard_map/ppermute | solution.py:480
  11.9 0.0 copy-done
  11.9 0.1 pad_dynamic-slice_fusion
  12.0 0.2 copy.11
  12.1 0.1 reshape.13
  12.3 0.0 copy-done.1
  12.3 0.1 pad_dynamic-slice_fusion.1
  12.4 0.1 copy.10
  12.4 0.1 reshape.12
  12.5 0.1 concatenate.6.table
  12.6 2.2 %stage.1 = (bf16[384,768]{1,0:T(8,128)(2,1)S(1)}, bf16[384,768]{1,0:T(8,128)(2,1)S(1)}, bf16[384,768]{1,0:T(8,128)(2,1)S(1)}, bf16[384,768]{1,0:T(8,128)(2,1)S(1...) custom-call(s32[309]{0:T(512)S(1)} %concatenate.6.table, bf16[384,768]{1,0:T(8,128)(2,1)} %queries.1, ...), custom_call_target="tpu_custom_call" | custom-call | flops 56623104 | tf_op jit(solution)/shard_map/stage/pallas_call | solution.py:509
  14.8 0.4 own_scores.1.near_masked
  15.2 1.7 %own_stats.1 = (f32[2,2,2,192,192]{4,3,2,1,0:T(8,128)S(1)}, f32[2,2,2,192,192]{4,3,2,1,0:T(8,128)S(1)}, f32[3,4,192]{2,1,0:T(4,128)S(1)}) custom-call(s32[309]{0:T(512)S(1)} %concatenate.6.table, bf16[384,768]{1,0:T(8,128)(2,1)S(1)} %get-tuple-element.55.queries, bf16[384,768]{1,0:T(8,128)(2,1)S(1)} %get-tuple-element.56.grad_out, ...), custom_call_target="tpu_custom_call" | custom-call | flops 113246208 | tf_op jit(solution)/shard_map/own_stats/pallas_call | solution.py:509
  17.0 0.0 collective-permute-done.f_two
  17.0 1.3 %collective-permute-done.1.f_one = bf16[2,384,256]{2,1,0:T(8,128)(2,1)S(1)} collective-permute-done((bf16[2,384,256]{2,1,0:T(8,128)(2,1)S(1)}, bf16[2,384,256]{2,1,0:T(8,128)(2,1)S(1)}, u32[]{:S(2)}, u32[]{:S(2)}) %collective-permute-start.1) | collective-permute-done | bytes 393248 | tf_op jit(solution)/shard_map/ppermute | solution.py:480
  18.3 1.8 %stats.1 = (f32[4,2,2,192,192]{4,3,2,1,0:T(8,128)S(1)}, f32[4,2,2,192,192]{4,3,2,1,0:T(8,128)S(1)}, f32[3,12,192]{2,1,0:T(8,128)S(1)}, f32[64,192]{1,0:T(8,128)S...) custom-call(s32[309]{0:T(512)S(1)} %concatenate.6.table, ...), custom_call_target="tpu_custom_call" | custom-call | flops 226492416 | tf_op jit(solution)/shard_map/stats/pallas_call | solution.py:509
  20.0 2.7 %collective-permute-start.4 = (f32[3,4,192]{2,1,0:T(4,128)S(1)}, f32[3,4,192]{2,1,0:T(4,128)S(1)}, u32[]{:S(2)}, u32[]{:S(2)}) collective-permute-start(f32[3,4,192]{2,1,0:T(4,128)S(1)} %get-tuple-element.67), channel_id=1, source_target_pairs={{0,8},{8,0},{4,12},{12,4},{1,9},{9,1},{5,13},{13,5},{2,10},{10,2},... | collective-permute-start | bytes 27656 | tf_op jit(solution)/shard_map/ppermute | solution.py:489
  22.7 0.9 %collective-permute-start.5 = (bf16[384,512]{1,0:T(8,128)(2,1)S(1)}, bf16[384,512]{1,0:T(8,128)(2,1)S(1)}, u32[]{:S(2)}, u32[]{:S(2)}) collective-permute-start(bf16[384,512]{1,0:T(8,128)(2,1)S(1)} %get-tuple-element.76), channel_id=1, source_target_pairs={{0,4},{4,0},{8,12},{12,8},{1,5},{5,1},{9,13},{13,9},{2,6},{6,2},{1... | collective-permute-start | bytes 1179656 | tf_op jit(solution)/shard_map/ppermute | solution.py:480
  23.6 0.7 %collective-permute-start.6 = (bf16[384,512]{1,0:T(8,128)(2,1)S(1)}, bf16[384,512]{1,0:T(8,128)(2,1)S(1)}, u32[]{:S(2)}, u32[]{:S(2)}) collective-permute-start(bf16[384,512]{1,0:T(8,128)(2,1)S(1)} %get-tuple-element.76), channel_id=1, source_target_pairs={{4,8},{8,4},{5,9},{9,5},{6,10},{10,6},{7,11},{11,7},{20,24},{24,20... | collective-permute-start | bytes 1179656 | tf_op jit(solution)/shard_map/ppermute | solution.py:481
  24.3 0.0 collective-permute-done.2.k_two
  24.3 2.7 %collective-permute-done.3.k_one = bf16[384,512]{1,0:T(8,128)(2,1)S(1)} collective-permute-done((bf16[384,512]{1,0:T(8,128)(2,1)S(1)}, bf16[384,512]{1,0:T(8,128)(2,1)S(1)}, u32[]{:S(2)}, u32[]{:S(2)}) %collective-permute-start.3) | collective-permute-done | bytes 393248 | tf_op jit(solution)/shard_map/ppermute | solution.py:480
  27.0 0.0 collective-permute-done.4.s_far
  27.0 3.5 %values_part.1 = (bf16[4,2,576,128]{3,2,1,0:T(8,128)(2,1)S(1)}, bf16[4,2,576,192]{3,2,1,0:T(8,128)(2,1)S(1)}, f32[384,512]{1,0:T(8,128)S(1)}, bf16[416,512]{1,0:T(8,128)(2,1)S(1)}, bf16[416,512]{1,0:T(8,128)(2,1)S(1)}) custom-call(s32[309]{0:T(512)S(1)} %concatenate.6.table, bf16[384,768]{1,0:T(8,128)(2,1)S(1)} %get-tuple-element.55.queries, ...), custom_call_target="tpu_custom_call" | custom-call | flops 452984832 | tf_op jit(solution)/shard_map/values_part/pallas_call | solution.py:509
  30.5 2.1 %collective-permute-start.7 = (bf16[416,512]{1,0:T(8,128)(2,1)S(1)}, bf16[416,512]{1,0:T(8,128)(2,1)S(1)}, u32[]{:S(2)}, u32[]{:S(2)}) collective-permute-start(bf16[416,512]{1,0:T(8,128)(2,1)S(1)} %get-tuple-element.81), channel_id=1, source_target_pairs={{0,4},{4,0},{8,12},{12,8},{1,5},{5,1},{9,13},{13,9},{2,6},{6,2},{1... | collective-permute-start | bytes 1277960 | tf_op jit(solution)/shard_map/ppermute | solution.py:480
  32.6 0.9 %collective-permute-start.8 = (bf16[416,512]{1,0:T(8,128)(2,1)S(1)}, bf16[416,512]{1,0:T(8,128)(2,1)S(1)}, u32[]{:S(2)}, u32[]{:S(2)}) collective-permute-start(bf16[416,512]{1,0:T(8,128)(2,1)S(1)} %get-tuple-element.82), channel_id=1, source_target_pairs={{4,8},{8,4},{5,9},{9,5},{6,10},{10,6},{7,11},{11,7},{20,24},{24,20... | collective-permute-start | bytes 1277960 | tf_op jit(solution)/shard_map/ppermute | solution.py:481
  33.4 1.9 %collective-permute-done.5.v_one = bf16[384,512]{1,0:T(8,128)(2,1)S(1)} collective-permute-done((bf16[384,512]{1,0:T(8,128)(2,1)S(1)}, bf16[384,512]{1,0:T(8,128)(2,1)S(1)}, u32[]{:S(2)}, u32[]{:S(2)}) %collective-permute-start.5) | collective-permute-done | bytes 393248 | tf_op jit(solution)/shard_map/ppermute | solution.py:480
  35.4 0.0 collective-permute-done.6.v_two
  35.4 4.7 %keys_part.1 = (bf16[4,2,576,192]{3,2,1,0:T(8,128)(2,1)S(1)}, f32[384,512]{1,0:T(8,128)S(1)}, bf16[384,512]{1,0:T(8,128)(2,1)S(1)}, bf16[384,512]{1,0:T(8,128)(2,1)S(1)}) custom-call(s32[309]{0:T(512)S(1)} %concatenate.6.table, bf16[384,768]{1,0:T(8,128)(2,1)S(1)} %get-tuple-element.55.queries, bf16[384,768]{1,0:T(8,128)(2,1)S(1)} %get-tuple-element.56.grad_out, ...), custom_call_target="tpu_custom_call" | custom-call | flops 452984832 | tf_op jit(solution)/shard_map/keys_part/pallas_call | solution.py:509
  40.1 2.1 %collective-permute-start.11 = (bf16[384,512]{1,0:T(8,128)(2,1)S(1)}, bf16[384,512]{1,0:T(8,128)(2,1)S(1)}, u32[]{:S(2)}, u32[]{:S(2)}) collective-permute-start(bf16[384,512]{1,0:T(8,128)(2,1)S(1)} %get-tuple-element.101), channel_id=1, source_target_pairs={{0,4},{4,0},{8,12},{12,8},{1,5},{5,1},{9,13},{13,9},{2,6},{6,2},{1... | collective-permute-start | bytes 1179656 | tf_op jit(solution)/shard_map/ppermute | solution.py:480
  42.2 0.7 %collective-permute-start.12 = (bf16[384,512]{1,0:T(8,128)(2,1)S(1)}, bf16[384,512]{1,0:T(8,128)(2,1)S(1)}, u32[]{:S(2)}, u32[]{:S(2)}) collective-permute-start(bf16[384,512]{1,0:T(8,128)(2,1)S(1)} %get-tuple-element.102), channel_id=1, source_target_pairs={{4,8},{8,4},{5,9},{9,5},{6,10},{10,6},{7,11},{11,7},{20,24},{24,20... | collective-permute-start | bytes 1179656 | tf_op jit(solution)/shard_map/ppermute | solution.py:481
  42.9 1.6 %collective-permute-done.7.r_one = bf16[416,512]{1,0:T(8,128)(2,1)S(1)} collective-permute-done((bf16[416,512]{1,0:T(8,128)(2,1)S(1)}, bf16[416,512]{1,0:T(8,128)(2,1)S(1)}, u32[]{:S(2)}, u32[]{:S(2)}) %collective-permute-start.7) | collective-permute-done | bytes 426016 | tf_op jit(solution)/shard_map/ppermute | solution.py:480
  44.5 0.0 collective-permute-done.8.r_two
  44.5 1.1 %back.1 = (bf16[4,2,2,192,192]{4,3,2,1,0:T(8,128)(2,1)S(1)}, bf16[4,2,2,192,192]{4,3,2,1,0:T(8,128)(2,1)S(1)}, f32[12,192]{1,0:T(8,128)S(1)}, f32[12,192]{1,0:T(...) custom-call(s32[309]{0:T(512)S(1)} %concatenate.6.table, ...), custom_call_target="tpu_custom_call" | custom-call | flops 113246208 | tf_op jit(solution)/shard_map/back/pallas_call | solution.py:509
  45.7 0.7 %collective-permute-start.10 = (bf16[384,256]{1,0:T(8,128)(2,1)S(1)}, bf16[384,256]{1,0:T(8,128)(2,1)S(1)}, u32[]{:S(2)}, u32[]{:S(2)}) collective-permute-start(bf16[384,256]{1,0:T(8,128)(2,1)S(1)} %get-tuple-element.99), channel_id=1, source_target_pairs={{4,8},{8,4},{5,9},{9,5},{6,10},{10,6},{7,11},{11,7},{20,24},{24,20... | collective-permute-start | bytes 589832 | tf_op jit(solution)/shard_map/ppermute | solution.py:481
  46.4 4.5 %collective-permute-start.9 = (bf16[384,256]{1,0:T(8,128)(2,1)S(1)}, bf16[384,256]{1,0:T(8,128)(2,1)S(1)}, u32[]{:S(2)}, u32[]{:S(2)}) collective-permute-start(bf16[384,256]{1,0:T(8,128)(2,1)S(1)} %get-tuple-element.98), channel_id=1, source_target_pairs={{0,4},{4,0},{8,12},{12,8},{1,5},{5,1},{9,13},{13,9},{2,6},{6,2},{1... | collective-permute-start | bytes 589832 | tf_op jit(solution)/shard_map/ppermute | solution.py:480
  50.9 1.2 %rest.1 = (bf16[384,512]{1,0:T(8,128)(2,1)S(1)}, f32[384,512]{1,0:T(8,128)S(1)}, f32[384,512]{1,0:T(8,128)S(1)}) custom-call(bf16[384,768]{1,0:T(8,128)(2,1)S(1)} %get-tuple-element.55.queries, bf16[384,768]{1,0:T(8,128)(2,1)S(1)} %get-tuple-element.56.grad_out, bf16[4,2,576,128]{3,2,1,0:T(8,128)(2,1)S(1)} %get-tuple-element.72.chosen_in, ...), custom_call_target="tpu_custom_call" | custom-call | flops 226492416 | tf_op jit(solution)/shard_map/rest/pallas_call | solution.py:509
  52.0 0.2 add_convert_fusion
  52.2 2.2 %home.1 = (f32[384,256]{1,0:T(8,128)S(1)}, bf16[384,256]{1,0:T(8,128)(2,1)S(1)}, bf16[384,256]{1,0:T(8,128)(2,1)S(1)}) custom-call(s32[309]{0:T(512)S(1)} %concatenate.6.table, bf16[384,768]{1,0:T(8,128)(2,1)S(1)} %get-tuple-element.55.queries, bf16[384,768]{1,0:T(8,128)(2,1)S(1)} %get-tuple-element.56.grad_out, ...), custom_call_target="tpu_custom_call" | custom-call | flops 339738624 | tf_op jit(solution)/shard_map/home/pallas_call | solution.py:509
  54.4 0.9 %pad_maximum_fusion = bf16[384,768]{1,0:T(8,128)(2,1)} fusion(bf16[384,512]{1,0:T(8,128)(2,1)S(1)} %add_convert_fusion, bf16[384,256]{1,0:T(8,128)(2,1)S(1)} %get-tuple-element.105), kind=kLoop, calls=%fused_computation.1 | loop fusion | flops 1179648 | bytes 1179648 | tf_op jit(solution)/shard_map/concatenate | solution.py:613
  55.3 0.0 collective-permute-done.10.rq_two
  55.3 0.7 %collective-permute-done.9.rq_one = bf16[384,256]{1,0:T(8,128)(2,1)S(1)} collective-permute-done((bf16[384,256]{1,0:T(8,128)(2,1)S(1)}, bf16[384,256]{1,0:T(8,128)(2,1)S(1)}, u32[]{:S(2)}, u32[]{:S(2)}) %collective-permute-start.9) | collective-permute-done | bytes 196640 | tf_op jit(solution)/shard_map/ppermute | solution.py:480
  56.0 0.0 collective-permute-done.11.rk_one
  56.0 0.0 collective-permute-done.12.rk_two
  56.0 1.0 %last.1 = (bf16[384,768]{1,0:T(8,128)(2,1)}, bf16[384,768]{1,0:T(8,128)(2,1)}) custom-call(bf16[384,512]{1,0:T(8,128)(2,1)S(1)} %get-tuple-element.89.gq_rest, bf16[384,256]{1,0:T(8,128)(2,1)S(1)} %get-tuple-element.96.gk_near, f32[384,256]{1,0:T(8,128)S(1)} %get-tuple-element.97.gq_near, bf16[384,256]{1,0:T(8,128)(2,1)S(1)} %collective-permute-done.9.rq_one, ...), custom_call_target="tpu_custom_call" | custom-call | flops 56623104 | tf_op jit(solution)/shard_map/last/pallas_call | solution.py:509
  (1 shorter events, 0.0 us)
Async XLA Ops:
  0.6 11.3 %copy-start = (s32[8,3,4,4]{0,3,2,1:T(4,128)S(1)}, s32[8,3,4,4]{0,3,2,1:T(4,128)}, u32[]{:S(2)}) copy-start(s32[8,3,4,4]{0,3,2,1:T(4,128)} %param.11) | copy-start | bytes 4612
  0.6 11.6 %copy-start.1 = (s32[8,3]{0,1:T(4,128)S(1)}, s32[8,3]{0,1:T(4,128)}, u32[]{:S(2)}) copy-start(s32[8,3]{0,1:T(4,128)} %param.10) | copy-start | bytes 292
  1.7 15.3 %collective-permute-start = (bf16[2,384,256]{2,1,0:T(8,128)(2,1)S(1)}, bf16[2,384,256]{2,1,0:T(8,128)(2,1)S(1)}, u32[]{:S(2)}, u32[]{:S(2)}) collective-permute-start(bf16[2,384,256]{2,1,0:T(8,128)(2,1)S(1)} %pack_queries.1), channel_id=1, source_target_pairs={{4,8},{8,4},{5,9},{9,5},{6,10},{10,6},{7,11},{11,7},{20,24},{24,20... | collective-permute-start | bytes 1179656 | tf_op jit(solution)/shard_map/ppermute | solution.py:481
  2.4 15.9 %collective-permute-start.1 = (bf16[2,384,256]{2,1,0:T(8,128)(2,1)S(1)}, bf16[2,384,256]{2,1,0:T(8,128)(2,1)S(1)}, u32[]{:S(2)}, u32[]{:S(2)}) collective-permute-start(bf16[2,384,256]{2,1,0:T(8,128)(2,1)S(1)} %pack_queries.1), channel_id=1, source_target_pairs={{0,4},{4,0},{8,12},{12,8},{1,5},{5,1},{9,13},{13,9},{2,6},{6,2},{1... | collective-permute-start | bytes 1179656 | tf_op jit(solution)/shard_map/ppermute | solution.py:480
  9.4 14.8 %collective-permute-start.2 = (bf16[384,512]{1,0:T(8,128)(2,1)S(1)}, bf16[384,512]{1,0:T(8,128)(2,1)S(1)}, u32[]{:S(2)}, u32[]{:S(2)}) collective-permute-start(bf16[384,512]{1,0:T(8,128)(2,1)S(1)} %get-tuple-element.63), channel_id=1, source_target_pairs={{4,8},{8,4},{5,9},{9,5},{6,10},{10,6},{7,11},{11,7},{20,24},{24,20... | collective-permute-start | bytes 1179656 | tf_op jit(solution)/shard_map/ppermute | solution.py:481
  10.1 16.8 %collective-permute-start.3 = (bf16[384,512]{1,0:T(8,128)(2,1)S(1)}, bf16[384,512]{1,0:T(8,128)(2,1)S(1)}, u32[]{:S(2)}, u32[]{:S(2)}) collective-permute-start(bf16[384,512]{1,0:T(8,128)(2,1)S(1)} %get-tuple-element.63), channel_id=1, source_target_pairs={{0,4},{4,0},{8,12},{12,8},{1,5},{5,1},{9,13},{13,9},{2,6},{6,2},{1... | collective-permute-start | bytes 1179656 | tf_op jit(solution)/shard_map/ppermute | solution.py:480
  20.0 6.9 %collective-permute-start.4 = (f32[3,4,192]{2,1,0:T(4,128)S(1)}, f32[3,4,192]{2,1,0:T(4,128)S(1)}, u32[]{:S(2)}, u32[]{:S(2)}) collective-permute-start(f32[3,4,192]{2,1,0:T(4,128)S(1)} %get-tuple-element.67), channel_id=1, source_target_pairs={{0,8},{8,0},{4,12},{12,4},{1,9},{9,1},{5,13},{13,5},{2,10},{10,2},... | collective-permute-start | bytes 27656 | tf_op jit(solution)/shard_map/ppermute | solution.py:489
  22.7 12.7 %collective-permute-start.5 = (bf16[384,512]{1,0:T(8,128)(2,1)S(1)}, bf16[384,512]{1,0:T(8,128)(2,1)S(1)}, u32[]{:S(2)}, u32[]{:S(2)}) collective-permute-start(bf16[384,512]{1,0:T(8,128)(2,1)S(1)} %get-tuple-element.76), channel_id=1, source_target_pairs={{0,4},{4,0},{8,12},{12,8},{1,5},{5,1},{9,13},{13,9},{2,6},{6,2},{1... | collective-permute-start | bytes 1179656 | tf_op jit(solution)/shard_map/ppermute | solution.py:480
  23.6 11.8 %collective-permute-start.6 = (bf16[384,512]{1,0:T(8,128)(2,1)S(1)}, bf16[384,512]{1,0:T(8,128)(2,1)S(1)}, u32[]{:S(2)}, u32[]{:S(2)}) collective-permute-start(bf16[384,512]{1,0:T(8,128)(2,1)S(1)} %get-tuple-element.76), channel_id=1, source_target_pairs={{4,8},{8,4},{5,9},{9,5},{6,10},{10,6},{7,11},{11,7},{20,24},{24,20... | collective-permute-start | bytes 1179656 | tf_op jit(solution)/shard_map/ppermute | solution.py:481
  30.5 14.1 %collective-permute-start.7 = (bf16[416,512]{1,0:T(8,128)(2,1)S(1)}, bf16[416,512]{1,0:T(8,128)(2,1)S(1)}, u32[]{:S(2)}, u32[]{:S(2)}) collective-permute-start(bf16[416,512]{1,0:T(8,128)(2,1)S(1)} %get-tuple-element.81), channel_id=1, source_target_pairs={{0,4},{4,0},{8,12},{12,8},{1,5},{5,1},{9,13},{13,9},{2,6},{6,2},{1... | collective-permute-start | bytes 1277960 | tf_op jit(solution)/shard_map/ppermute | solution.py:480
  32.6 11.9 %collective-permute-start.8 = (bf16[416,512]{1,0:T(8,128)(2,1)S(1)}, bf16[416,512]{1,0:T(8,128)(2,1)S(1)}, u32[]{:S(2)}, u32[]{:S(2)}) collective-permute-start(bf16[416,512]{1,0:T(8,128)(2,1)S(1)} %get-tuple-element.82), channel_id=1, source_target_pairs={{4,8},{8,4},{5,9},{9,5},{6,10},{10,6},{7,11},{11,7},{20,24},{24,20... | collective-permute-start | bytes 1277960 | tf_op jit(solution)/shard_map/ppermute | solution.py:481
  40.1 16.0 %collective-permute-start.11 = (bf16[384,512]{1,0:T(8,128)(2,1)S(1)}, bf16[384,512]{1,0:T(8,128)(2,1)S(1)}, u32[]{:S(2)}, u32[]{:S(2)}) collective-permute-start(bf16[384,512]{1,0:T(8,128)(2,1)S(1)} %get-tuple-element.101), channel_id=1, source_target_pairs={{0,4},{4,0},{8,12},{12,8},{1,5},{5,1},{9,13},{13,9},{2,6},{6,2},{1... | collective-permute-start | bytes 1179656 | tf_op jit(solution)/shard_map/ppermute | solution.py:480
  42.2 13.8 %collective-permute-start.12 = (bf16[384,512]{1,0:T(8,128)(2,1)S(1)}, bf16[384,512]{1,0:T(8,128)(2,1)S(1)}, u32[]{:S(2)}, u32[]{:S(2)}) collective-permute-start(bf16[384,512]{1,0:T(8,128)(2,1)S(1)} %get-tuple-element.102), channel_id=1, source_target_pairs={{4,8},{8,4},{5,9},{9,5},{6,10},{10,6},{7,11},{11,7},{20,24},{24,20... | collective-permute-start | bytes 1179656 | tf_op jit(solution)/shard_map/ppermute | solution.py:481
  45.7 9.6 %collective-permute-start.10 = (bf16[384,256]{1,0:T(8,128)(2,1)S(1)}, bf16[384,256]{1,0:T(8,128)(2,1)S(1)}, u32[]{:S(2)}, u32[]{:S(2)}) collective-permute-start(bf16[384,256]{1,0:T(8,128)(2,1)S(1)} %get-tuple-element.99), channel_id=1, source_target_pairs={{4,8},{8,4},{5,9},{9,5},{6,10},{10,6},{7,11},{11,7},{20,24},{24,20... | collective-permute-start | bytes 589832 | tf_op jit(solution)/shard_map/ppermute | solution.py:481
  46.4 9.7 %collective-permute-start.9 = (bf16[384,256]{1,0:T(8,128)(2,1)S(1)}, bf16[384,256]{1,0:T(8,128)(2,1)S(1)}, u32[]{:S(2)}, u32[]{:S(2)}) collective-permute-start(bf16[384,256]{1,0:T(8,128)(2,1)S(1)} %get-tuple-element.98), channel_id=1, source_target_pairs={{0,4},{4,0},{8,12},{12,8},{1,5},{5,1},{9,13},{13,9},{2,6},{6,2},{1... | collective-permute-start | bytes 589832 | tf_op jit(solution)/shard_map/ppermute | solution.py:480

commit v11 on v10

--- a/solution.py
+++ b/solution.py
@@ -1,3 +1,4 @@
+import functools
 import math
 
 import jax
@@ -240,18 +241,11 @@
     return total.astype(jnp.bfloat16)
 
 
-def last_kernel(
-    gq_rest, gk_near, gq_near, rq_one, rq_two, gk_own, rk_one, rk_two,
-    query_out, key_out,
-    query_done, key_done, sems,
-):
-    moves = copy_all(
-        [(gq_rest, query_out.at[:, SPLIT:]), (gk_near, key_out.at[:, :SPLIT])], sems
-    )
-    key_done[...] = joined(gk_own, rk_one, rk_two)
-    moves += copy_all([(key_done, key_out.at[:, SPLIT:])], sems.at[2:3])
-    query_done[...] = joined(gq_near, rq_one, rq_two)
-    moves += copy_all([(query_done, query_out.at[:, :SPLIT])], sems.at[3:4])
+def finish_kernel(order, ready, own, one, two, out, done, sems):
+    ready_at, done_at = order
+    moves = copy_all([(ready, out.at[:, ready_at])], sems.at[0:1])
+    done[...] = joined(own, one, two)
+    moves += copy_all([(done, out.at[:, done_at])], sems.at[1:2])
     for move in moves:
         move.wait()
 
@@ -611,12 +605,18 @@
         [full(ROWS, SPLIT), full(ROWS, SPLIT)], 3 * MOVED * unit,
     )
     grad_values = jnp.concatenate([gv_near, joined(gv_own, rv_one[:ROWS], rv_two[:ROWS])], 1)
-    grad_queries, grad_keys = call(
-        last_kernel, "last", (),
-        (gq_rest, gk_near, gq_near, rq_one, rq_two, gk_own, rk_one, rk_two),
-        (pltpu.HBM((ROWS, width), jnp.bfloat16),) * 2,
-        [low(ROWS, SPLIT), low(ROWS, rest), pltpu.SemaphoreType.DMA((4,))],
-        unit, pltpu.VMEM, pltpu.HBM,
+    moved, kept = slice(0, SPLIT), slice(SPLIT, width)
+    result = (pltpu.HBM((ROWS, width), jnp.bfloat16),)
+    (grad_keys,) = call(
+        functools.partial(finish_kernel, (moved, kept)), "last_keys", (),
+        (gk_near, gk_own, rk_one, rk_two), result,
+        [low(ROWS, rest), pltpu.SemaphoreType.DMA((2,))], unit, pltpu.VMEM, pltpu.HBM,
+    )
+    grad_keys, gq_near = lax.optimization_barrier((grad_keys, gq_near))
+    (grad_queries,) = call(
+        functools.partial(finish_kernel, (kept, moved)), "last_queries", (),
+        (gq_rest, gq_near, rq_one, rq_two), result,
+        [low(ROWS, SPLIT), pltpu.SemaphoreType.DMA((2,))], unit, pltpu.VMEM, pltpu.HBM,
     )
     return grad_queries, grad_keys, grad_values
 

time: 57.5 us -> 57.3 us (level)
  waiting for transfers between devices: 8.31 us -> 9.64 us
  Pallas kernels: 22 us -> 21.1 us
  starting transfers between devices: 24.2 us -> 23.6 us
    ppermute x6, starting transfers between devices: 17.3 us -> 15.9 us  [swap(): lax.ppermute(one, 'frames', both_ways(first))]
    ppermute x6, waiting for transfers between devices: 8.29 us -> 9.62 us  [swap(): lax.ppermute(one, 'frames', both_ways(first))]
    pallas_call x12 -> x13, Pallas kernels: 22 us -> 21.1 us  [call(): pl.pallas_call(kernel, out_shape=outs, in_specs=[pl.BlockSpec(memory_spac...]
    ppermute x1, starting transfers between devices: 2.69 us -> 3.43 us  [swap_far(): far = lax.ppermute(far, 'frames', both_ways(near))]
  transfers between devices with their start and end apart: 13 -> 13, of which waited for: 5 -> 5; matrix products, arithmetic and copies ran while one was open for 3% -> 3% of each run, Pallas kernels for 35% -> 34%
where the time goes in v11:
time: 57.3 us; the launch traced here: 57 us
  starting transfers between devices  23.6 us (41%)
  Pallas kernels  21.1 us (37%)
  waiting for transfers between devices  9.64 us (17%)
  other arithmetic  1.04 us (2%)
  between operations  0.98 us (2%)
  local copies, waits for them, and re-layouts  0.73 us (1%)
    pallas_call x13, Pallas kernels, call(): pl.pallas_call(kernel, out_shape=outs, in_specs=[pl.BlockSpec(memory_spac...  21.1 us
    ppermute x6, starting transfers between devices, swap(): lax.ppermute(one, 'frames', both_ways(first))  15.9 us
    ppermute x6, waiting for transfers between devices, swap(): lax.ppermute(one, 'frames', both_ways(first))  9.62 us
    ppermute x6, starting transfers between devices, swap(): lax.ppermute(two, 'frames', both_ways(second))  4.25 us
    ppermute x1, starting transfers between devices, swap_far(): far = lax.ppermute(far, 'frames', both_ways(near))  3.43 us
  transfers between devices with their start and end apart: 13, of which 5 were waited for; matrix products, arithmetic and copies ran while one was open for 3% of the time, Pallas kernels for 34%

profile of v11, /device:TPU:0, one launch (start us, length us, event | category | flops | bytes accessed | tf_op | source)
XLA Modules:
  0.0 57.0 jit_solution(1293866056144674044)
XLA Ops:
  0.6 0.0 copy-start
  0.6 0.0 copy-start.1
  0.7 1.1 %pack_queries.1 = bf16[2,384,256]{2,1,0:T(8,128)(2,1)S(1)} custom-call(bf16[384,768]{1,0:T(8,128)(2,1)} %queries.1, bf16[384,768]{1,0:T(8,128)(2,1)} %grad_out.1), custom_call_target="tpu_custom_call" | custom-call | flops 56623104 | tf_op jit(solution)/shard_map/pack_queries/pallas_call | solution.py:503
  1.7 0.7 %collective-permute-start = (bf16[2,384,256]{2,1,0:T(8,128)(2,1)S(1)}, bf16[2,384,256]{2,1,0:T(8,128)(2,1)S(1)}, u32[]{:S(2)}, u32[]{:S(2)}) collective-permute-start(bf16[2,384,256]{2,1,0:T(8,128)(2,1)S(1)} %pack_queries.1), channel_id=1, source_target_pairs={{4,8},{8,4},{5,9},{9,5},{6,10},{10,6},{7,11},{11,7},{20,24},{24,20... | collective-permute-start | bytes 1179656 | tf_op jit(solution)/shard_map/ppermute | solution.py:475
  2.4 5.9 %collective-permute-start.1 = (bf16[2,384,256]{2,1,0:T(8,128)(2,1)S(1)}, bf16[2,384,256]{2,1,0:T(8,128)(2,1)S(1)}, u32[]{:S(2)}, u32[]{:S(2)}) collective-permute-start(bf16[2,384,256]{2,1,0:T(8,128)(2,1)S(1)} %pack_queries.1), channel_id=1, source_target_pairs={{0,4},{4,0},{8,12},{12,8},{1,5},{5,1},{9,13},{13,9},{2,6},{6,2},{1... | collective-permute-start | bytes 1179656 | tf_op jit(solution)/shard_map/ppermute | solution.py:474
  8.3 1.1 %pack_keys.1 = (bf16[384,512]{1,0:T(8,128)(2,1)S(1)}, bf16[384,512]{1,0:T(8,128)(2,1)S(1)}) custom-call(bf16[384,768]{1,0:T(8,128)(2,1)} %keys.1, bf16[384,768]{1,0:T(8,128)(2,1)} %values.1), custom_call_target="tpu_custom_call" | custom-call | flops 56623104 | tf_op jit(solution)/shard_map/pack_keys/pallas_call | solution.py:503
  9.4 0.7 %collective-permute-start.2 = (bf16[384,512]{1,0:T(8,128)(2,1)S(1)}, bf16[384,512]{1,0:T(8,128)(2,1)S(1)}, u32[]{:S(2)}, u32[]{:S(2)}) collective-permute-start(bf16[384,512]{1,0:T(8,128)(2,1)S(1)} %get-tuple-element.63), channel_id=1, source_target_pairs={{4,8},{8,4},{5,9},{9,5},{6,10},{10,6},{7,11},{11,7},{20,24},{24,20... | collective-permute-start | bytes 1179656 | tf_op jit(solution)/shard_map/ppermute | solution.py:475
  10.1 1.8 %collective-permute-start.3 = (bf16[384,512]{1,0:T(8,128)(2,1)S(1)}, bf16[384,512]{1,0:T(8,128)(2,1)S(1)}, u32[]{:S(2)}, u32[]{:S(2)}) collective-permute-start(bf16[384,512]{1,0:T(8,128)(2,1)S(1)} %get-tuple-element.63), channel_id=1, source_target_pairs={{0,4},{4,0},{8,12},{12,8},{1,5},{5,1},{9,13},{13,9},{2,6},{6,2},{1... | collective-permute-start | bytes 1179656 | tf_op jit(solution)/shard_map/ppermute | solution.py:474
  11.9 0.0 copy-done
  11.9 0.1 pad_dynamic-slice_fusion
  12.0 0.2 copy.11
  12.1 0.1 reshape.13
  12.3 0.0 copy-done.1
  12.3 0.1 pad_dynamic-slice_fusion.1
  12.4 0.1 copy.10
  12.4 0.1 reshape.12
  12.5 0.1 concatenate.6.table
  12.6 2.2 %stage.1 = (bf16[384,768]{1,0:T(8,128)(2,1)S(1)}, bf16[384,768]{1,0:T(8,128)(2,1)S(1)}, bf16[384,768]{1,0:T(8,128)(2,1)S(1)}, bf16[384,768]{1,0:T(8,128)(2,1)S(1...) custom-call(s32[309]{0:T(512)S(1)} %concatenate.6.table, bf16[384,768]{1,0:T(8,128)(2,1)} %queries.1, ...), custom_call_target="tpu_custom_call" | custom-call | flops 56623104 | tf_op jit(solution)/shard_map/stage/pallas_call | solution.py:503
  14.8 0.4 own_scores.1.near_masked
  15.2 1.4 %own_stats.1 = (f32[2,2,2,192,192]{4,3,2,1,0:T(8,128)S(1)}, f32[2,2,2,192,192]{4,3,2,1,0:T(8,128)S(1)}, f32[3,4,192]{2,1,0:T(4,128)S(1)}) custom-call(s32[309]{0:T(512)S(1)} %concatenate.6.table, bf16[384,768]{1,0:T(8,128)(2,1)S(1)} %get-tuple-element.55.queries, bf16[384,768]{1,0:T(8,128)(2,1)S(1)} %get-tuple-element.56.grad_out, ...), custom_call_target="tpu_custom_call" | custom-call | flops 113246208 | tf_op jit(solution)/shard_map/own_stats/pallas_call | solution.py:503
  16.6 0.0 collective-permute-done.f_two
  16.6 1.7 %collective-permute-done.1.f_one = bf16[2,384,256]{2,1,0:T(8,128)(2,1)S(1)} collective-permute-done((bf16[2,384,256]{2,1,0:T(8,128)(2,1)S(1)}, bf16[2,384,256]{2,1,0:T(8,128)(2,1)S(1)}, u32[]{:S(2)}, u32[]{:S(2)}) %collective-permute-start.1) | collective-permute-done | bytes 393248 | tf_op jit(solution)/shard_map/ppermute | solution.py:474
  18.3 1.4 %stats.1 = (f32[4,2,2,192,192]{4,3,2,1,0:T(8,128)S(1)}, f32[4,2,2,192,192]{4,3,2,1,0:T(8,128)S(1)}, f32[3,12,192]{2,1,0:T(8,128)S(1)}, f32[64,192]{1,0:T(8,128)S...) custom-call(s32[309]{0:T(512)S(1)} %concatenate.6.table, ...), custom_call_target="tpu_custom_call" | custom-call | flops 226492416 | tf_op jit(solution)/shard_map/stats/pallas_call | solution.py:503
  19.7 3.4 %collective-permute-start.4 = (f32[3,4,192]{2,1,0:T(4,128)S(1)}, f32[3,4,192]{2,1,0:T(4,128)S(1)}, u32[]{:S(2)}, u32[]{:S(2)}) collective-permute-start(f32[3,4,192]{2,1,0:T(4,128)S(1)} %get-tuple-element.67), channel_id=1, source_target_pairs={{0,8},{8,0},{4,12},{12,4},{1,9},{9,1},{5,13},{13,5},{2,10},{10,2},... | collective-permute-start | bytes 27656 | tf_op jit(solution)/shard_map/ppermute | solution.py:483
  23.1 0.0 collective-permute-start.5
  23.1 0.7 %collective-permute-start.6 = (bf16[384,512]{1,0:T(8,128)(2,1)S(1)}, bf16[384,512]{1,0:T(8,128)(2,1)S(1)}, u32[]{:S(2)}, u32[]{:S(2)}) collective-permute-start(bf16[384,512]{1,0:T(8,128)(2,1)S(1)} %get-tuple-element.76), channel_id=1, source_target_pairs={{4,8},{8,4},{5,9},{9,5},{6,10},{10,6},{7,11},{11,7},{20,24},{24,20... | collective-permute-start | bytes 1179656 | tf_op jit(solution)/shard_map/ppermute | solution.py:475
  23.8 0.0 collective-permute-done.2.k_two
  23.8 3.2 %collective-permute-done.3.k_one = bf16[384,512]{1,0:T(8,128)(2,1)S(1)} collective-permute-done((bf16[384,512]{1,0:T(8,128)(2,1)S(1)}, bf16[384,512]{1,0:T(8,128)(2,1)S(1)}, u32[]{:S(2)}, u32[]{:S(2)}) %collective-permute-start.3) | collective-permute-done | bytes 393248 | tf_op jit(solution)/shard_map/ppermute | solution.py:474
  27.0 0.0 collective-permute-done.4.s_far
  27.0 3.5 %values_part.1 = (bf16[4,2,576,128]{3,2,1,0:T(8,128)(2,1)S(1)}, bf16[4,2,576,192]{3,2,1,0:T(8,128)(2,1)S(1)}, f32[384,512]{1,0:T(8,128)S(1)}, bf16[416,512]{1,0:T(8,128)(2,1)S(1)}, bf16[416,512]{1,0:T(8,128)(2,1)S(1)}) custom-call(s32[309]{0:T(512)S(1)} %concatenate.6.table, bf16[384,768]{1,0:T(8,128)(2,1)S(1)} %get-tuple-element.55.queries, ...), custom_call_target="tpu_custom_call" | custom-call | flops 452984832 | tf_op jit(solution)/shard_map/values_part/pallas_call | solution.py:503
  30.5 2.0 %collective-permute-start.7 = (bf16[416,512]{1,0:T(8,128)(2,1)S(1)}, bf16[416,512]{1,0:T(8,128)(2,1)S(1)}, u32[]{:S(2)}, u32[]{:S(2)}) collective-permute-start(bf16[416,512]{1,0:T(8,128)(2,1)S(1)} %get-tuple-element.81), channel_id=1, source_target_pairs={{0,4},{4,0},{8,12},{12,8},{1,5},{5,1},{9,13},{13,9},{2,6},{6,2},{1... | collective-permute-start | bytes 1277960 | tf_op jit(solution)/shard_map/ppermute | solution.py:474
  32.5 0.9 %collective-permute-start.8 = (bf16[416,512]{1,0:T(8,128)(2,1)S(1)}, bf16[416,512]{1,0:T(8,128)(2,1)S(1)}, u32[]{:S(2)}, u32[]{:S(2)}) collective-permute-start(bf16[416,512]{1,0:T(8,128)(2,1)S(1)} %get-tuple-element.82), channel_id=1, source_target_pairs={{4,8},{8,4},{5,9},{9,5},{6,10},{10,6},{7,11},{11,7},{20,24},{24,20... | collective-permute-start | bytes 1277960 | tf_op jit(solution)/shard_map/ppermute | solution.py:475
  33.3 2.1 %collective-permute-done.5.v_one = bf16[384,512]{1,0:T(8,128)(2,1)S(1)} collective-permute-done((bf16[384,512]{1,0:T(8,128)(2,1)S(1)}, bf16[384,512]{1,0:T(8,128)(2,1)S(1)}, u32[]{:S(2)}, u32[]{:S(2)}) %collective-permute-start.5) | collective-permute-done | bytes 393248 | tf_op jit(solution)/shard_map/ppermute | solution.py:474
  35.4 0.0 collective-permute-done.6.v_two
  35.4 4.7 %keys_part.1 = (bf16[4,2,576,192]{3,2,1,0:T(8,128)(2,1)S(1)}, f32[384,512]{1,0:T(8,128)S(1)}, bf16[384,512]{1,0:T(8,128)(2,1)S(1)}, bf16[384,512]{1,0:T(8,128)(2,1)S(1)}) custom-call(s32[309]{0:T(512)S(1)} %concatenate.6.table, bf16[384,768]{1,0:T(8,128)(2,1)S(1)} %get-tuple-element.55.queries, bf16[384,768]{1,0:T(8,128)(2,1)S(1)} %get-tuple-element.56.grad_out, ...), custom_call_target="tpu_custom_call" | custom-call | flops 452984832 | tf_op jit(solution)/shard_map/keys_part/pallas_call | solution.py:503
  40.1 0.7 %collective-permute-start.10 = (bf16[384,512]{1,0:T(8,128)(2,1)S(1)}, bf16[384,512]{1,0:T(8,128)(2,1)S(1)}, u32[]{:S(2)}, u32[]{:S(2)}) collective-permute-start(bf16[384,512]{1,0:T(8,128)(2,1)S(1)} %get-tuple-element.99), channel_id=1, source_target_pairs={{4,8},{8,4},{5,9},{9,5},{6,10},{10,6},{7,11},{11,7},{20,24},{24,20... | collective-permute-start | bytes 1179656 | tf_op jit(solution)/shard_map/ppermute | solution.py:475
  40.8 3.8 %collective-permute-start.9 = (bf16[384,512]{1,0:T(8,128)(2,1)S(1)}, bf16[384,512]{1,0:T(8,128)(2,1)S(1)}, u32[]{:S(2)}, u32[]{:S(2)}) collective-permute-start(bf16[384,512]{1,0:T(8,128)(2,1)S(1)} %get-tuple-element.98), channel_id=1, source_target_pairs={{0,4},{4,0},{8,12},{12,8},{1,5},{5,1},{9,13},{13,9},{2,6},{6,2},{1... | collective-permute-start | bytes 1179656 | tf_op jit(solution)/shard_map/ppermute | solution.py:474
  44.6 0.0 collective-permute-done.7.r_one
  44.6 0.0 collective-permute-done.8.r_two
  44.6 0.9 %back.1 = (bf16[4,2,2,192,192]{4,3,2,1,0:T(8,128)(2,1)S(1)}, bf16[4,2,2,192,192]{4,3,2,1,0:T(8,128)(2,1)S(1)}, f32[12,192]{1,0:T(8,128)S(1)}, f32[12,192]{1,0:T(...) custom-call(s32[309]{0:T(512)S(1)} %concatenate.6.table, ...), custom_call_target="tpu_custom_call" | custom-call | flops 113246208 | tf_op jit(solution)/shard_map/back/pallas_call | solution.py:503
  45.4 2.4 %collective-permute-start.11 = (bf16[384,256]{1,0:T(8,128)(2,1)S(1)}, bf16[384,256]{1,0:T(8,128)(2,1)S(1)}, u32[]{:S(2)}, u32[]{:S(2)}) collective-permute-start(bf16[384,256]{1,0:T(8,128)(2,1)S(1)} %get-tuple-element.102), channel_id=1, source_target_pairs={{0,4},{4,0},{8,12},{12,8},{1,5},{5,1},{9,13},{13,9},{2,6},{6,2},{1... | collective-permute-start | bytes 589832 | tf_op jit(solution)/shard_map/ppermute | solution.py:474
  47.9 0.7 %collective-permute-start.12 = (bf16[384,256]{1,0:T(8,128)(2,1)S(1)}, bf16[384,256]{1,0:T(8,128)(2,1)S(1)}, u32[]{:S(2)}, u32[]{:S(2)}) collective-permute-start(bf16[384,256]{1,0:T(8,128)(2,1)S(1)} %get-tuple-element.103), channel_id=1, source_target_pairs={{4,8},{8,4},{5,9},{9,5},{6,10},{10,6},{7,11},{11,7},{20,24},{24,20... | collective-permute-start | bytes 589832 | tf_op jit(solution)/shard_map/ppermute | solution.py:475
  48.5 1.2 %rest.1 = (bf16[384,512]{1,0:T(8,128)(2,1)S(1)}, f32[384,512]{1,0:T(8,128)S(1)}, f32[384,512]{1,0:T(8,128)S(1)}) custom-call(bf16[384,768]{1,0:T(8,128)(2,1)S(1)} %get-tuple-element.55.queries, bf16[384,768]{1,0:T(8,128)(2,1)S(1)} %get-tuple-element.56.grad_out, bf16[4,2,576,128]{3,2,1,0:T(8,128)(2,1)S(1)} %get-tuple-element.72.chosen_in, ...), custom_call_target="tpu_custom_call" | custom-call | flops 226492416 | tf_op jit(solution)/shard_map/rest/pallas_call | solution.py:503
  49.7 0.2 add_convert_fusion
  49.9 1.6 %home.1 = (f32[384,256]{1,0:T(8,128)S(1)}, bf16[384,256]{1,0:T(8,128)(2,1)S(1)}, bf16[384,256]{1,0:T(8,128)(2,1)S(1)}) custom-call(s32[309]{0:T(512)S(1)} %concatenate.6.table, bf16[384,768]{1,0:T(8,128)(2,1)S(1)} %get-tuple-element.55.queries, bf16[384,768]{1,0:T(8,128)(2,1)S(1)} %get-tuple-element.56.grad_out, ...), custom_call_target="tpu_custom_call" | custom-call | flops 339738624 | tf_op jit(solution)/shard_map/home/pallas_call | solution.py:503
  51.5 0.9 %pad_maximum_fusion = bf16[384,768]{1,0:T(8,128)(2,1)} fusion(bf16[384,512]{1,0:T(8,128)(2,1)S(1)} %add_convert_fusion, bf16[384,256]{1,0:T(8,128)(2,1)S(1)} %get-tuple-element.105), kind=kLoop, calls=%fused_computation.1 | loop fusion | flops 1179648 | bytes 1179648 | tf_op jit(solution)/shard_map/concatenate | solution.py:607
  52.4 0.0 collective-permute-done.10.two
  52.4 1.5 %collective-permute-done.9.one = bf16[384,512]{1,0:T(8,128)(2,1)S(1)} collective-permute-done((bf16[384,512]{1,0:T(8,128)(2,1)S(1)}, bf16[384,512]{1,0:T(8,128)(2,1)S(1)}, u32[]{:S(2)}, u32[]{:S(2)}) %collective-permute-start.9) | collective-permute-done | bytes 393248 | tf_op jit(solution)/shard_map/ppermute | solution.py:474
  53.9 0.9 %last_keys.1 = bf16[384,768]{1,0:T(8,128)(2,1)} custom-call(bf16[384,256]{1,0:T(8,128)(2,1)S(1)} %get-tuple-element.96.ready, f32[384,512]{1,0:T(8,128)S(1)} %get-tuple-element.97.own, bf16[384,512]{1,0:T(8,128)(2,1)S(1)} %collective-permute-done.9.one, bf16[384,512]{1,0:T(8,128)(2,1)S(1)} %collective-permute-done.10.two), custom_call_target="tpu_custom_call" | custom-call | flops 56623104 | tf_op jit(solution)/shard_map/last_keys/pallas_call | solution.py:503
  54.8 1.2 %collective-permute-done.11.one = bf16[384,256]{1,0:T(8,128)(2,1)S(1)} collective-permute-done((bf16[384,256]{1,0:T(8,128)(2,1)S(1)}, bf16[384,256]{1,0:T(8,128)(2,1)S(1)}, u32[]{:S(2)}, u32[]{:S(2)}) %collective-permute-start.11) | collective-permute-done | bytes 196640 | tf_op jit(solution)/shard_map/ppermute | solution.py:474
  56.0 0.0 collective-permute-done.12.two
  56.0 0.8 %last_queries.1 = bf16[384,768]{1,0:T(8,128)(2,1)} custom-call(bf16[384,512]{1,0:T(8,128)(2,1)S(1)} %get-tuple-element.89.ready, f32[384,256]{1,0:T(8,128)S(1)} %get-tuple-element.101.own, bf16[384,256]{1,0:T(8,128)(2,1)S(1)} %collective-permute-done.11.one, bf16[384,256]{1,0:T(8,128)(2,1)S(1)} %collective-permute-done.12.two), custom_call_target="tpu_custom_call" | custom-call | flops 56623104 | tf_op jit(solution)/shard_map/last_queries/pallas_call | solution.py:503
  (1 shorter events, 0.0 us)
Async XLA Ops:
  0.6 11.3 %copy-start = (s32[8,3,4,4]{0,3,2,1:T(4,128)S(1)}, s32[8,3,4,4]{0,3,2,1:T(4,128)}, u32[]{:S(2)}) copy-start(s32[8,3,4,4]{0,3,2,1:T(4,128)} %param.11) | copy-start | bytes 4612
  0.6 11.6 %copy-start.1 = (s32[8,3]{0,1:T(4,128)S(1)}, s32[8,3]{0,1:T(4,128)}, u32[]{:S(2)}) copy-start(s32[8,3]{0,1:T(4,128)} %param.10) | copy-start | bytes 292
  1.7 14.9 %collective-permute-start = (bf16[2,384,256]{2,1,0:T(8,128)(2,1)S(1)}, bf16[2,384,256]{2,1,0:T(8,128)(2,1)S(1)}, u32[]{:S(2)}, u32[]{:S(2)}) collective-permute-start(bf16[2,384,256]{2,1,0:T(8,128)(2,1)S(1)} %pack_queries.1), channel_id=1, source_target_pairs={{4,8},{8,4},{5,9},{9,5},{6,10},{10,6},{7,11},{11,7},{20,24},{24,20... | collective-permute-start | bytes 1179656 | tf_op jit(solution)/shard_map/ppermute | solution.py:475
  2.4 15.9 %collective-permute-start.1 = (bf16[2,384,256]{2,1,0:T(8,128)(2,1)S(1)}, bf16[2,384,256]{2,1,0:T(8,128)(2,1)S(1)}, u32[]{:S(2)}, u32[]{:S(2)}) collective-permute-start(bf16[2,384,256]{2,1,0:T(8,128)(2,1)S(1)} %pack_queries.1), channel_id=1, source_target_pairs={{0,4},{4,0},{8,12},{12,8},{1,5},{5,1},{9,13},{13,9},{2,6},{6,2},{1... | collective-permute-start | bytes 1179656 | tf_op jit(solution)/shard_map/ppermute | solution.py:474
  9.4 14.4 %collective-permute-start.2 = (bf16[384,512]{1,0:T(8,128)(2,1)S(1)}, bf16[384,512]{1,0:T(8,128)(2,1)S(1)}, u32[]{:S(2)}, u32[]{:S(2)}) collective-permute-start(bf16[384,512]{1,0:T(8,128)(2,1)S(1)} %get-tuple-element.63), channel_id=1, source_target_pairs={{4,8},{8,4},{5,9},{9,5},{6,10},{10,6},{7,11},{11,7},{20,24},{24,20... | collective-permute-start | bytes 1179656 | tf_op jit(solution)/shard_map/ppermute | solution.py:475
  10.1 16.8 %collective-permute-start.3 = (bf16[384,512]{1,0:T(8,128)(2,1)S(1)}, bf16[384,512]{1,0:T(8,128)(2,1)S(1)}, u32[]{:S(2)}, u32[]{:S(2)}) collective-permute-start(bf16[384,512]{1,0:T(8,128)(2,1)S(1)} %get-tuple-element.63), channel_id=1, source_target_pairs={{0,4},{4,0},{8,12},{12,8},{1,5},{5,1},{9,13},{13,9},{2,6},{6,2},{1... | collective-permute-start | bytes 1179656 | tf_op jit(solution)/shard_map/ppermute | solution.py:474
  19.7 7.3 %collective-permute-start.4 = (f32[3,4,192]{2,1,0:T(4,128)S(1)}, f32[3,4,192]{2,1,0:T(4,128)S(1)}, u32[]{:S(2)}, u32[]{:S(2)}) collective-permute-start(f32[3,4,192]{2,1,0:T(4,128)S(1)} %get-tuple-element.67), channel_id=1, source_target_pairs={{0,8},{8,0},{4,12},{12,4},{1,9},{9,1},{5,13},{13,5},{2,10},{10,2},... | collective-permute-start | bytes 27656 | tf_op jit(solution)/shard_map/ppermute | solution.py:483
  23.1 12.3 %collective-permute-start.5 = (bf16[384,512]{1,0:T(8,128)(2,1)S(1)}, bf16[384,512]{1,0:T(8,128)(2,1)S(1)}, u32[]{:S(2)}, u32[]{:S(2)}) collective-permute-start(bf16[384,512]{1,0:T(8,128)(2,1)S(1)} %get-tuple-element.76), channel_id=1, source_target_pairs={{0,4},{4,0},{8,12},{12,8},{1,5},{5,1},{9,13},{13,9},{2,6},{6,2},{1... | collective-permute-start | bytes 1179656 | tf_op jit(solution)/shard_map/ppermute | solution.py:474
  23.1 12.3 %collective-permute-start.6 = (bf16[384,512]{1,0:T(8,128)(2,1)S(1)}, bf16[384,512]{1,0:T(8,128)(2,1)S(1)}, u32[]{:S(2)}, u32[]{:S(2)}) collective-permute-start(bf16[384,512]{1,0:T(8,128)(2,1)S(1)} %get-tuple-element.76), channel_id=1, source_target_pairs={{4,8},{8,4},{5,9},{9,5},{6,10},{10,6},{7,11},{11,7},{20,24},{24,20... | collective-permute-start | bytes 1179656 | tf_op jit(solution)/shard_map/ppermute | solution.py:475
  30.5 14.1 %collective-permute-start.7 = (bf16[416,512]{1,0:T(8,128)(2,1)S(1)}, bf16[416,512]{1,0:T(8,128)(2,1)S(1)}, u32[]{:S(2)}, u32[]{:S(2)}) collective-permute-start(bf16[416,512]{1,0:T(8,128)(2,1)S(1)} %get-tuple-element.81), channel_id=1, source_target_pairs={{0,4},{4,0},{8,12},{12,8},{1,5},{5,1},{9,13},{13,9},{2,6},{6,2},{1... | collective-permute-start | bytes 1277960 | tf_op jit(solution)/shard_map/ppermute | solution.py:474
  32.5 12.1 %collective-permute-start.8 = (bf16[416,512]{1,0:T(8,128)(2,1)S(1)}, bf16[416,512]{1,0:T(8,128)(2,1)S(1)}, u32[]{:S(2)}, u32[]{:S(2)}) collective-permute-start(bf16[416,512]{1,0:T(8,128)(2,1)S(1)} %get-tuple-element.82), channel_id=1, source_target_pairs={{4,8},{8,4},{5,9},{9,5},{6,10},{10,6},{7,11},{11,7},{20,24},{24,20... | collective-permute-start | bytes 1277960 | tf_op jit(solution)/shard_map/ppermute | solution.py:475
  40.1 12.3 %collective-permute-start.10 = (bf16[384,512]{1,0:T(8,128)(2,1)S(1)}, bf16[384,512]{1,0:T(8,128)(2,1)S(1)}, u32[]{:S(2)}, u32[]{:S(2)}) collective-permute-start(bf16[384,512]{1,0:T(8,128)(2,1)S(1)} %get-tuple-element.99), channel_id=1, source_target_pairs={{4,8},{8,4},{5,9},{9,5},{6,10},{10,6},{7,11},{11,7},{20,24},{24,20... | collective-permute-start | bytes 1179656 | tf_op jit(solution)/shard_map/ppermute | solution.py:475
  40.8 13.1 %collective-permute-start.9 = (bf16[384,512]{1,0:T(8,128)(2,1)S(1)}, bf16[384,512]{1,0:T(8,128)(2,1)S(1)}, u32[]{:S(2)}, u32[]{:S(2)}) collective-permute-start(bf16[384,512]{1,0:T(8,128)(2,1)S(1)} %get-tuple-element.98), channel_id=1, source_target_pairs={{0,4},{4,0},{8,12},{12,8},{1,5},{5,1},{9,13},{13,9},{2,6},{6,2},{1... | collective-permute-start | bytes 1179656 | tf_op jit(solution)/shard_map/ppermute | solution.py:474
  45.4 10.6 %collective-permute-start.11 = (bf16[384,256]{1,0:T(8,128)(2,1)S(1)}, bf16[384,256]{1,0:T(8,128)(2,1)S(1)}, u32[]{:S(2)}, u32[]{:S(2)}) collective-permute-start(bf16[384,256]{1,0:T(8,128)(2,1)S(1)} %get-tuple-element.102), channel_id=1, source_target_pairs={{0,4},{4,0},{8,12},{12,8},{1,5},{5,1},{9,13},{13,9},{2,6},{6,2},{1... | collective-permute-start | bytes 589832 | tf_op jit(solution)/shard_map/ppermute | solution.py:474
  47.9 8.1 %collective-permute-start.12 = (bf16[384,256]{1,0:T(8,128)(2,1)S(1)}, bf16[384,256]{1,0:T(8,128)(2,1)S(1)}, u32[]{:S(2)}, u32[]{:S(2)}) collective-permute-start(bf16[384,256]{1,0:T(8,128)(2,1)S(1)} %get-tuple-element.103), channel_id=1, source_target_pairs={{4,8},{8,4},{5,9},{9,5},{6,10},{10,6},{7,11},{11,7},{20,24},{24,20... | collective-permute-start | bytes 589832 | tf_op jit(solution)/shard_map/ppermute | solution.py:475

commit v12 on v11

--- a/solution.py
+++ b/solution.py
@@ -31,7 +31,7 @@
 FIRST = MASKS + WINDOW * NSEL * SB * SB
 RANK = FIRST + 1
 COUNT = FIRST + 2
-NOTES = 32
+NOTES = 24
 SIDE = FR_DEV * MOVED
 FAR = (0, 1, 4, 5)
 
@@ -137,23 +137,19 @@
     window[2 * ROWS : 3 * ROWS] = two[:, far_column]
 
 
-def pick(table, frame, window, chosen):
-    for slot in range(NSEL):
-        chosen[rows_of(slot)] = window[span(table, frame, slot), :]
-
-
 def spread(table, frame, accum, parts):
     for slot in range(1, NSEL):
         accum[span(table, frame, slot), :] += parts[rows_of(slot - 1)]
 
 
-def own_scores_kernel(queries, k_own, bias, masked_out):
+def own_scores_kernel(queries, grad_out, k_own, v_own, bias, masked_out, grad_prob_out):
     for head in range(masked_out.shape[0]):
         column = column_of(MOVED + head)
         for frame in range(FR_DEV):
             rows = rows_of(frame)
             scores = dot(k_own[rows, column], queries[rows, column], NT)
             masked_out[head, frame] = scores * SCALE2 + bias[frame, :TOK_FRAME]
+            grad_prob_out[head, frame] = dot(v_own[rows, column], grad_out[rows, column], NT)
 
 
 def values_kernel(
@@ -192,7 +188,7 @@
 
 
 def keys_kernel(
-    table, queries, grad_out, v_own, prob_in, v_one, v_two,
+    table, queries, grad_out, v_own, near_grads, prob_in, v_one, v_two,
     score_out, own_out, one_out, two_out,
     windows, choices, accums,
 ):
@@ -204,15 +200,20 @@
         fill_window(window, v_one, v_own, v_two, column, far_column)
         accum[...] = jnp.zeros_like(accum)
         for frame in range(FR_DEV):
+            rows = rows_of(frame)
             chosen = choices.at[head % DEPTH, frame]
-            pick(table, frame, window, chosen)
-            grad_prob = dot(chosen[...], grad_out[rows_of(frame), column], NT)
-            prob = prob_in[head, frame].astype(jnp.float32)
-            delta = jnp.sum(prob * grad_prob, 0, keepdims=True)
-            score_low = (prob * (grad_prob - delta)).astype(jnp.bfloat16)
-            score_out[head, frame] = score_low
-            far = dot(score_low[TOK_FRAME:], queries[rows_of(frame), column], NN)
-            spread(table, frame, accum, far)
+            for slot in range(1, NSEL):
+                chosen[rows_of(slot - 1)] = window[span(table, frame, slot), :]
+            near_grad = near_grads[head, frame]
+            far_grad = dot(chosen[...], grad_out[rows, column], NT)
+            near = prob_in[head, frame, :TOK_FRAME].astype(jnp.float32)
+            far = prob_in[head, frame, TOK_FRAME:].astype(jnp.float32)
+            delta = jnp.sum(near * near_grad, 0, keepdims=True)
+            delta += jnp.sum(far * far_grad, 0, keepdims=True)
+            far_low = (far * (far_grad - delta)).astype(jnp.bfloat16)
+            score_out[head, frame, :TOK_FRAME] = (near * (near_grad - delta)).astype(jnp.bfloat16)
+            score_out[head, frame, TOK_FRAME:] = far_low
+            spread(table, frame, accum, dot(far_low, queries[rows, column], NN))
         one_out[:, far_column] = (accum[0:ROWS] * SCALE).astype(one_out.dtype)
         own_out[:, far_column] = accum[ROWS : 2 * ROWS]
         two_out[:, far_column] = (accum[2 * ROWS : 3 * ROWS] * SCALE).astype(two_out.dtype)
@@ -549,9 +550,9 @@
         (full(*near_grid), full(*near_grid), full(3, SIDE, TOK_FRAME)),
         [full(FR_DEV, 3, SIDE, TOK_FRAME)], MOVED * unit,
     )
-    (near_scores,) = call(
-        own_scores_kernel, "own_scores", (), (query, key, bias),
-        (full(heads, FR_DEV, TOK_FRAME, TOK_FRAME),), [], heads * unit // 3,
+    near_scores, rest_grads = call(
+        own_scores_kernel, "own_scores", (), (query, grad, key, value, bias),
+        (full(heads, FR_DEV, TOK_FRAME, TOK_FRAME),) * 2, [], heads * unit // 2,
     )
     f_two, f_one, own_stats, near_scores = lax.optimization_barrier(
         (f_two, f_one, own_stats, near_scores)
@@ -579,9 +580,10 @@
     )
     rv_one, rv_two = swap(gv_one, gv_two)
     score_low, gk_own, gk_one, gk_two = call(
-        keys_kernel, "keys_part", (table,), (query, grad, value, prob_low, v_one, v_two),
+        keys_kernel, "keys_part", (table,),
+        (query, grad, value, rest_grads, prob_low, v_one, v_two),
         (pairs, full(ROWS, rest), low(ROWS, rest), low(ROWS, rest)),
-        [windows, low(DEPTH, FR_DEV, SLOTS, HD), accums], 2 * heads * unit,
+        [windows, low(DEPTH, FR_DEV, SLOTS - TOK_FRAME, HD), accums], 2 * heads * unit,
     )
     rk_one, rk_two = swap(gk_one, gk_two)
     y_prob, y_score, logs, deltas, gq_one, gq_two = call(

time: 57.3 us -> 57.1 us (level)
  starting transfers between devices: 23.6 us -> 22 us
  Pallas kernels: 21.1 us -> 22.6 us
    pallas_call x13, Pallas kernels: 21.1 us -> 22.6 us  [call(): pl.pallas_call(kernel, out_shape=outs, in_specs=[pl.BlockSpec(memory_spac...]
    ppermute x1, starting transfers between devices: 3.43 us -> 2.31 us  [swap_far(): far = lax.ppermute(far, 'frames', both_ways(near))]
  transfers between devices with their start and end apart: 13 -> 13, of which waited for: 5 -> 5; matrix products, arithmetic and copies ran while one was open for 3% -> 3% of each run, Pallas kernels for 34% -> 36%
where the time goes in v12:
time: 57.1 us; the launch traced here: 56.8 us
  Pallas kernels  22.6 us (40%)
  starting transfers between devices  22 us (39%)
  waiting for transfers between devices  9.5 us (17%)
  other arithmetic  1.06 us (2%)
  between operations  0.98 us (2%)
  local copies, waits for them, and re-layouts  0.73 us (1%)
    pallas_call x13, Pallas kernels, call(): pl.pallas_call(kernel, out_shape=outs, in_specs=[pl.BlockSpec(memory_spac...  22.6 us
    ppermute x6, starting transfers between devices, swap(): lax.ppermute(one, 'frames', both_ways(first))  15.6 us
    ppermute x6, waiting for transfers between devices, swap(): lax.ppermute(one, 'frames', both_ways(first))  9.48 us
    ppermute x6, starting transfers between devices, swap(): lax.ppermute(two, 'frames', both_ways(second))  4.07 us
    ppermute x1, starting transfers between devices, swap_far(): far = lax.ppermute(far, 'frames', both_ways(near))  2.31 us
  transfers between devices with their start and end apart: 13, of which 5 were waited for; matrix products, arithmetic and copies ran while one was open for 3% of the time, Pallas kernels for 36%

profile of v12, /device:TPU:0, one launch (start us, length us, event | category | flops | bytes accessed | tf_op | source)
XLA Modules:
  0.0 56.8 jit_solution(8110551776636541073)
XLA Ops:
  0.6 0.0 copy-start
  0.6 0.0 copy-start.1
  0.7 1.1 %pack_queries.1 = bf16[2,384,256]{2,1,0:T(8,128)(2,1)S(1)} custom-call(bf16[384,768]{1,0:T(8,128)(2,1)} %queries.1, bf16[384,768]{1,0:T(8,128)(2,1)} %grad_out.1), custom_call_target="tpu_custom_call" | custom-call | flops 56623104 | tf_op jit(solution)/shard_map/pack_queries/pallas_call | solution.py:504
  1.7 0.7 %collective-permute-start = (bf16[2,384,256]{2,1,0:T(8,128)(2,1)S(1)}, bf16[2,384,256]{2,1,0:T(8,128)(2,1)S(1)}, u32[]{:S(2)}, u32[]{:S(2)}) collective-permute-start(bf16[2,384,256]{2,1,0:T(8,128)(2,1)S(1)} %pack_queries.1), channel_id=1, source_target_pairs={{4,8},{8,4},{5,9},{9,5},{6,10},{10,6},{7,11},{11,7},{20,24},{24,20... | collective-permute-start | bytes 1179656 | tf_op jit(solution)/shard_map/ppermute | solution.py:476
  2.4 5.9 %collective-permute-start.1 = (bf16[2,384,256]{2,1,0:T(8,128)(2,1)S(1)}, bf16[2,384,256]{2,1,0:T(8,128)(2,1)S(1)}, u32[]{:S(2)}, u32[]{:S(2)}) collective-permute-start(bf16[2,384,256]{2,1,0:T(8,128)(2,1)S(1)} %pack_queries.1), channel_id=1, source_target_pairs={{0,4},{4,0},{8,12},{12,8},{1,5},{5,1},{9,13},{13,9},{2,6},{6,2},{1... | collective-permute-start | bytes 1179656 | tf_op jit(solution)/shard_map/ppermute | solution.py:475
  8.3 1.1 %pack_keys.1 = (bf16[384,512]{1,0:T(8,128)(2,1)S(1)}, bf16[384,512]{1,0:T(8,128)(2,1)S(1)}) custom-call(bf16[384,768]{1,0:T(8,128)(2,1)} %keys.1, bf16[384,768]{1,0:T(8,128)(2,1)} %values.1), custom_call_target="tpu_custom_call" | custom-call | flops 56623104 | tf_op jit(solution)/shard_map/pack_keys/pallas_call | solution.py:504
  9.4 0.7 %collective-permute-start.2 = (bf16[384,512]{1,0:T(8,128)(2,1)S(1)}, bf16[384,512]{1,0:T(8,128)(2,1)S(1)}, u32[]{:S(2)}, u32[]{:S(2)}) collective-permute-start(bf16[384,512]{1,0:T(8,128)(2,1)S(1)} %get-tuple-element.66), channel_id=1, source_target_pairs={{4,8},{8,4},{5,9},{9,5},{6,10},{10,6},{7,11},{11,7},{20,24},{24,20... | collective-permute-start | bytes 1179656 | tf_op jit(solution)/shard_map/ppermute | solution.py:476
  10.1 1.8 %collective-permute-start.3 = (bf16[384,512]{1,0:T(8,128)(2,1)S(1)}, bf16[384,512]{1,0:T(8,128)(2,1)S(1)}, u32[]{:S(2)}, u32[]{:S(2)}) collective-permute-start(bf16[384,512]{1,0:T(8,128)(2,1)S(1)} %get-tuple-element.66), channel_id=1, source_target_pairs={{0,4},{4,0},{8,12},{12,8},{1,5},{5,1},{9,13},{13,9},{2,6},{6,2},{1... | collective-permute-start | bytes 1179656 | tf_op jit(solution)/shard_map/ppermute | solution.py:475
  11.9 0.0 copy-done
  11.9 0.1 pad_dynamic-slice_fusion
  12.0 0.2 copy.11
  12.1 0.1 reshape.13
  12.3 0.0 copy-done.1
  12.3 0.1 pad_dynamic-slice_fusion.1
  12.4 0.1 copy.10
  12.4 0.1 reshape.12
  12.5 0.1 concatenate.6.table
  12.6 2.2 %stage.1 = (bf16[384,768]{1,0:T(8,128)(2,1)S(1)}, bf16[384,768]{1,0:T(8,128)(2,1)S(1)}, bf16[384,768]{1,0:T(8,128)(2,1)S(1)}, bf16[384,768]{1,0:T(8,128)(2,1)S(1...) custom-call(s32[309]{0:T(512)S(1)} %concatenate.6.table, bf16[384,768]{1,0:T(8,128)(2,1)} %queries.1, ...), custom_call_target="tpu_custom_call" | custom-call | flops 56623104 | tf_op jit(solution)/shard_map/stage/pallas_call | solution.py:504
  14.8 0.6 %own_scores.1 = (f32[4,2,192,192]{3,2,1,0:T(8,128)S(1)}, f32[4,2,192,192]{3,2,1,0:T(8,128)S(1)}) custom-call(bf16[384,768]{1,0:T(8,128)(2,1)S(1)} %get-tuple-element.57.queries, bf16[384,768]{1,0:T(8,128)(2,1)S(1)} %get-tuple-element.58.grad_out, bf16[384,768]{1,0:T(8,128)(2,1)S(1)} %get-tuple-element.59.keys.k_own, ...), custom_call_target="tpu_custom_call" | custom-call | flops 113246208 | tf_op jit(solution)/shard_map/own_scores/pallas_call | solution.py:504
  15.4 1.7 %own_stats.1 = (f32[2,2,2,192,192]{4,3,2,1,0:T(8,128)S(1)}, f32[2,2,2,192,192]{4,3,2,1,0:T(8,128)S(1)}, f32[3,4,192]{2,1,0:T(4,128)S(1)}) custom-call(s32[309]{0:T(512)S(1)} %concatenate.6.table, bf16[384,768]{1,0:T(8,128)(2,1)S(1)} %get-tuple-element.57.queries, bf16[384,768]{1,0:T(8,128)(2,1)S(1)} %get-tuple-element.58.grad_out, ...), custom_call_target="tpu_custom_call" | custom-call | flops 113246208 | tf_op jit(solution)/shard_map/own_stats/pallas_call | solution.py:504
  17.2 0.0 collective-permute-done.f_two
  17.2 1.1 %collective-permute-done.1.f_one = bf16[2,384,256]{2,1,0:T(8,128)(2,1)S(1)} collective-permute-done((bf16[2,384,256]{2,1,0:T(8,128)(2,1)S(1)}, bf16[2,384,256]{2,1,0:T(8,128)(2,1)S(1)}, u32[]{:S(2)}, u32[]{:S(2)}) %collective-permute-start.1) | collective-permute-done | bytes 393248 | tf_op jit(solution)/shard_map/ppermute | solution.py:475
  18.3 2.1 %stats.1 = (f32[4,2,2,192,192]{4,3,2,1,0:T(8,128)S(1)}, f32[4,2,2,192,192]{4,3,2,1,0:T(8,128)S(1)}, f32[3,12,192]{2,1,0:T(8,128)S(1)}, f32[48,192]{1,0:T(8,128)S...) custom-call(s32[309]{0:T(512)S(1)} %concatenate.6.table, ...), custom_call_target="tpu_custom_call" | custom-call | flops 226492416 | tf_op jit(solution)/shard_map/stats/pallas_call | solution.py:504
  20.4 2.3 %collective-permute-start.4 = (f32[3,4,192]{2,1,0:T(4,128)S(1)}, f32[3,4,192]{2,1,0:T(4,128)S(1)}, u32[]{:S(2)}, u32[]{:S(2)}) collective-permute-start(f32[3,4,192]{2,1,0:T(4,128)S(1)} %get-tuple-element.70), channel_id=1, source_target_pairs={{0,8},{8,0},{4,12},{12,4},{1,9},{9,1},{5,13},{13,5},{2,10},{10,2},... | collective-permute-start | bytes 27656 | tf_op jit(solution)/shard_map/ppermute | solution.py:484
  22.7 0.0 collective-permute-start.5
  22.7 0.7 %collective-permute-start.6 = (bf16[384,512]{1,0:T(8,128)(2,1)S(1)}, bf16[384,512]{1,0:T(8,128)(2,1)S(1)}, u32[]{:S(2)}, u32[]{:S(2)}) collective-permute-start(bf16[384,512]{1,0:T(8,128)(2,1)S(1)} %get-tuple-element.80), channel_id=1, source_target_pairs={{4,8},{8,4},{5,9},{9,5},{6,10},{10,6},{7,11},{11,7},{20,24},{24,20... | collective-permute-start | bytes 1179656 | tf_op jit(solution)/shard_map/ppermute | solution.py:476
  23.4 0.0 collective-permute-done.2.k_two
  23.4 3.5 %collective-permute-done.3.k_one = bf16[384,512]{1,0:T(8,128)(2,1)S(1)} collective-permute-done((bf16[384,512]{1,0:T(8,128)(2,1)S(1)}, bf16[384,512]{1,0:T(8,128)(2,1)S(1)}, u32[]{:S(2)}, u32[]{:S(2)}) %collective-permute-start.3) | collective-permute-done | bytes 393248 | tf_op jit(solution)/shard_map/ppermute | solution.py:475
  27.0 0.0 collective-permute-done.4.s_far
  27.0 3.5 %values_part.1 = (bf16[4,2,576,128]{3,2,1,0:T(8,128)(2,1)S(1)}, bf16[4,2,576,192]{3,2,1,0:T(8,128)(2,1)S(1)}, f32[384,512]{1,0:T(8,128)S(1)}, bf16[408,512]{1,0:T(8,128)(2,1)S(1)}, bf16[408,512]{1,0:T(8,128)(2,1)S(1)}) custom-call(s32[309]{0:T(512)S(1)} %concatenate.6.table, bf16[384,768]{1,0:T(8,128)(2,1)S(1)} %get-tuple-element.57.queries, ...), custom_call_target="tpu_custom_call" | custom-call | flops 452984832 | tf_op jit(solution)/shard_map/values_part/pallas_call | solution.py:504
  30.5 2.0 %collective-permute-start.7 = (bf16[408,512]{1,0:T(8,128)(2,1)S(1)}, bf16[408,512]{1,0:T(8,128)(2,1)S(1)}, u32[]{:S(2)}, u32[]{:S(2)}) collective-permute-start(bf16[408,512]{1,0:T(8,128)(2,1)S(1)} %get-tuple-element.85), channel_id=1, source_target_pairs={{0,4},{4,0},{8,12},{12,8},{1,5},{5,1},{9,13},{13,9},{2,6},{6,2},{1... | collective-permute-start | bytes 1253384 | tf_op jit(solution)/shard_map/ppermute | solution.py:475
  32.5 0.7 %collective-permute-start.8 = (bf16[408,512]{1,0:T(8,128)(2,1)S(1)}, bf16[408,512]{1,0:T(8,128)(2,1)S(1)}, u32[]{:S(2)}, u32[]{:S(2)}) collective-permute-start(bf16[408,512]{1,0:T(8,128)(2,1)S(1)} %get-tuple-element.86), channel_id=1, source_target_pairs={{4,8},{8,4},{5,9},{9,5},{6,10},{10,6},{7,11},{11,7},{20,24},{24,20... | collective-permute-start | bytes 1253384 | tf_op jit(solution)/shard_map/ppermute | solution.py:476
  33.2 2.2 %collective-permute-done.5.v_one = bf16[384,512]{1,0:T(8,128)(2,1)S(1)} collective-permute-done((bf16[384,512]{1,0:T(8,128)(2,1)S(1)}, bf16[384,512]{1,0:T(8,128)(2,1)S(1)}, u32[]{:S(2)}, u32[]{:S(2)}) %collective-permute-start.5) | collective-permute-done | bytes 393248 | tf_op jit(solution)/shard_map/ppermute | solution.py:475
  35.4 0.0 collective-permute-done.6.v_two
  35.4 3.4 %keys_part.1 = (bf16[4,2,576,192]{3,2,1,0:T(8,128)(2,1)S(1)}, f32[384,512]{1,0:T(8,128)S(1)}, bf16[384,512]{1,0:T(8,128)(2,1)S(1)}, bf16[384,512]{1,0:T(8,128)(2,1)S(1)}) custom-call(s32[309]{0:T(512)S(1)} %concatenate.6.table, bf16[384,768]{1,0:T(8,128)(2,1)S(1)} %get-tuple-element.57.queries, bf16[384,768]{1,0:T(8,128)(2,1)S(1)} %get-tuple-element.58.grad_out, ...), custom_call_target="tpu_custom_call" | custom-call | flops 452984832 | tf_op jit(solution)/shard_map/keys_part/pallas_call | solution.py:504
  38.8 0.7 %collective-permute-start.10 = (bf16[384,512]{1,0:T(8,128)(2,1)S(1)}, bf16[384,512]{1,0:T(8,128)(2,1)S(1)}, u32[]{:S(2)}, u32[]{:S(2)}) collective-permute-start(bf16[384,512]{1,0:T(8,128)(2,1)S(1)} %get-tuple-element.103), channel_id=1, source_target_pairs={{4,8},{8,4},{5,9},{9,5},{6,10},{10,6},{7,11},{11,7},{20,24},{24,20... | collective-permute-start | bytes 1179656 | tf_op jit(solution)/shard_map/ppermute | solution.py:476
  39.5 3.8 %collective-permute-start.9 = (bf16[384,512]{1,0:T(8,128)(2,1)S(1)}, bf16[384,512]{1,0:T(8,128)(2,1)S(1)}, u32[]{:S(2)}, u32[]{:S(2)}) collective-permute-start(bf16[384,512]{1,0:T(8,128)(2,1)S(1)} %get-tuple-element.102), channel_id=1, source_target_pairs={{0,4},{4,0},{8,12},{12,8},{1,5},{5,1},{9,13},{13,9},{2,6},{6,2},{1... | collective-permute-start | bytes 1179656 | tf_op jit(solution)/shard_map/ppermute | solution.py:475
  43.3 1.1 %collective-permute-done.7.r_one = bf16[408,512]{1,0:T(8,128)(2,1)S(1)} collective-permute-done((bf16[408,512]{1,0:T(8,128)(2,1)S(1)}, bf16[408,512]{1,0:T(8,128)(2,1)S(1)}, u32[]{:S(2)}, u32[]{:S(2)}) %collective-permute-start.7) | collective-permute-done | bytes 417824 | tf_op jit(solution)/shard_map/ppermute | solution.py:475
  44.3 0.0 collective-permute-done.8.r_two
  44.4 1.6 %back.1 = (bf16[4,2,2,192,192]{4,3,2,1,0:T(8,128)(2,1)S(1)}, bf16[4,2,2,192,192]{4,3,2,1,0:T(8,128)(2,1)S(1)}, f32[12,192]{1,0:T(8,128)S(1)}, f32[12,192]{1,0:T(...) custom-call(s32[309]{0:T(512)S(1)} %concatenate.6.table, ...), custom_call_target="tpu_custom_call" | custom-call | flops 113246208 | tf_op jit(solution)/shard_map/back/pallas_call | solution.py:504
  45.9 2.1 %collective-permute-start.11 = (bf16[384,256]{1,0:T(8,128)(2,1)S(1)}, bf16[384,256]{1,0:T(8,128)(2,1)S(1)}, u32[]{:S(2)}, u32[]{:S(2)}) collective-permute-start(bf16[384,256]{1,0:T(8,128)(2,1)S(1)} %get-tuple-element.106), channel_id=1, source_target_pairs={{0,4},{4,0},{8,12},{12,8},{1,5},{5,1},{9,13},{13,9},{2,6},{6,2},{1... | collective-permute-start | bytes 589832 | tf_op jit(solution)/shard_map/ppermute | solution.py:475
  48.1 0.7 %collective-permute-start.12 = (bf16[384,256]{1,0:T(8,128)(2,1)S(1)}, bf16[384,256]{1,0:T(8,128)(2,1)S(1)}, u32[]{:S(2)}, u32[]{:S(2)}) collective-permute-start(bf16[384,256]{1,0:T(8,128)(2,1)S(1)} %get-tuple-element.107), channel_id=1, source_target_pairs={{4,8},{8,4},{5,9},{9,5},{6,10},{10,6},{7,11},{11,7},{20,24},{24,20... | collective-permute-start | bytes 589832 | tf_op jit(solution)/shard_map/ppermute | solution.py:476
  48.7 1.1 %rest.1 = (bf16[384,512]{1,0:T(8,128)(2,1)S(1)}, f32[384,512]{1,0:T(8,128)S(1)}, f32[384,512]{1,0:T(8,128)S(1)}) custom-call(bf16[384,768]{1,0:T(8,128)(2,1)S(1)} %get-tuple-element.57.queries, bf16[384,768]{1,0:T(8,128)(2,1)S(1)} %get-tuple-element.58.grad_out, bf16[4,2,576,128]{3,2,1,0:T(8,128)(2,1)S(1)} %get-tuple-element.75.chosen_in, ...), custom_call_target="tpu_custom_call" | custom-call | flops 226492416 | tf_op jit(solution)/shard_map/rest/pallas_call | solution.py:504
  49.9 0.2 add_convert_fusion
  50.1 2.4 %home.1 = (f32[384,256]{1,0:T(8,128)S(1)}, bf16[384,256]{1,0:T(8,128)(2,1)S(1)}, bf16[384,256]{1,0:T(8,128)(2,1)S(1)}) custom-call(s32[309]{0:T(512)S(1)} %concatenate.6.table, bf16[384,768]{1,0:T(8,128)(2,1)S(1)} %get-tuple-element.57.queries, bf16[384,768]{1,0:T(8,128)(2,1)S(1)} %get-tuple-element.58.grad_out, ...), custom_call_target="tpu_custom_call" | custom-call | flops 339738624 | tf_op jit(solution)/shard_map/home/pallas_call | solution.py:504
  52.5 0.9 %pad_maximum_fusion = bf16[384,768]{1,0:T(8,128)(2,1)} fusion(bf16[384,512]{1,0:T(8,128)(2,1)S(1)} %add_convert_fusion, bf16[384,256]{1,0:T(8,128)(2,1)S(1)} %get-tuple-element.109), kind=kLoop, calls=%fused_computation.1 | loop fusion | flops 1179648 | bytes 1179648 | tf_op jit(solution)/shard_map/concatenate | solution.py:609
  53.3 0.0 collective-permute-done.10.two
  53.3 0.0 collective-permute-done.9.one
  53.3 0.9 %last_keys.1 = bf16[384,768]{1,0:T(8,128)(2,1)} custom-call(bf16[384,256]{1,0:T(8,128)(2,1)S(1)} %get-tuple-element.100.ready, f32[384,512]{1,0:T(8,128)S(1)} %get-tuple-element.101.own, bf16[384,512]{1,0:T(8,128)(2,1)S(1)} %collective-permute-done.9.one, bf16[384,512]{1,0:T(8,128)(2,1)S(1)} %collective-permute-done.10.two), custom_call_target="tpu_custom_call" | custom-call | flops 56623104 | tf_op jit(solution)/shard_map/last_keys/pallas_call | solution.py:504
  54.3 1.6 %collective-permute-done.11.one = bf16[384,256]{1,0:T(8,128)(2,1)S(1)} collective-permute-done((bf16[384,256]{1,0:T(8,128)(2,1)S(1)}, bf16[384,256]{1,0:T(8,128)(2,1)S(1)}, u32[]{:S(2)}, u32[]{:S(2)}) %collective-permute-start.11) | collective-permute-done | bytes 196640 | tf_op jit(solution)/shard_map/ppermute | solution.py:475
  55.8 0.0 collective-permute-done.12.two
  55.8 0.8 %last_queries.1 = bf16[384,768]{1,0:T(8,128)(2,1)} custom-call(bf16[384,512]{1,0:T(8,128)(2,1)S(1)} %get-tuple-element.93.ready, f32[384,256]{1,0:T(8,128)S(1)} %get-tuple-element.105.own, bf16[384,256]{1,0:T(8,128)(2,1)S(1)} %collective-permute-done.11.one, bf16[384,256]{1,0:T(8,128)(2,1)S(1)} %collective-permute-done.12.two), custom_call_target="tpu_custom_call" | custom-call | flops 56623104 | tf_op jit(solution)/shard_map/last_queries/pallas_call | solution.py:504
  (1 shorter events, 0.0 us)
Async XLA Ops:
  0.6 11.3 %copy-start = (s32[8,3,4,4]{0,3,2,1:T(4,128)S(1)}, s32[8,3,4,4]{0,3,2,1:T(4,128)}, u32[]{:S(2)}) copy-start(s32[8,3,4,4]{0,3,2,1:T(4,128)} %param.11) | copy-start | bytes 4612
  0.6 11.6 %copy-start.1 = (s32[8,3]{0,1:T(4,128)S(1)}, s32[8,3]{0,1:T(4,128)}, u32[]{:S(2)}) copy-start(s32[8,3]{0,1:T(4,128)} %param.10) | copy-start | bytes 292
  1.7 15.5 %collective-permute-start = (bf16[2,384,256]{2,1,0:T(8,128)(2,1)S(1)}, bf16[2,384,256]{2,1,0:T(8,128)(2,1)S(1)}, u32[]{:S(2)}, u32[]{:S(2)}) collective-permute-start(bf16[2,384,256]{2,1,0:T(8,128)(2,1)S(1)} %pack_queries.1), channel_id=1, source_target_pairs={{4,8},{8,4},{5,9},{9,5},{6,10},{10,6},{7,11},{11,7},{20,24},{24,20... | collective-permute-start | bytes 1179656 | tf_op jit(solution)/shard_map/ppermute | solution.py:476
  2.4 15.9 %collective-permute-start.1 = (bf16[2,384,256]{2,1,0:T(8,128)(2,1)S(1)}, bf16[2,384,256]{2,1,0:T(8,128)(2,1)S(1)}, u32[]{:S(2)}, u32[]{:S(2)}) collective-permute-start(bf16[2,384,256]{2,1,0:T(8,128)(2,1)S(1)} %pack_queries.1), channel_id=1, source_target_pairs={{0,4},{4,0},{8,12},{12,8},{1,5},{5,1},{9,13},{13,9},{2,6},{6,2},{1... | collective-permute-start | bytes 1179656 | tf_op jit(solution)/shard_map/ppermute | solution.py:475
  9.4 14.0 %collective-permute-start.2 = (bf16[384,512]{1,0:T(8,128)(2,1)S(1)}, bf16[384,512]{1,0:T(8,128)(2,1)S(1)}, u32[]{:S(2)}, u32[]{:S(2)}) collective-permute-start(bf16[384,512]{1,0:T(8,128)(2,1)S(1)} %get-tuple-element.66), channel_id=1, source_target_pairs={{4,8},{8,4},{5,9},{9,5},{6,10},{10,6},{7,11},{11,7},{20,24},{24,20... | collective-permute-start | bytes 1179656 | tf_op jit(solution)/shard_map/ppermute | solution.py:476
  10.1 16.8 %collective-permute-start.3 = (bf16[384,512]{1,0:T(8,128)(2,1)S(1)}, bf16[384,512]{1,0:T(8,128)(2,1)S(1)}, u32[]{:S(2)}, u32[]{:S(2)}) collective-permute-start(bf16[384,512]{1,0:T(8,128)(2,1)S(1)} %get-tuple-element.66), channel_id=1, source_target_pairs={{0,4},{4,0},{8,12},{12,8},{1,5},{5,1},{9,13},{13,9},{2,6},{6,2},{1... | collective-permute-start | bytes 1179656 | tf_op jit(solution)/shard_map/ppermute | solution.py:475
  20.4 6.6 %collective-permute-start.4 = (f32[3,4,192]{2,1,0:T(4,128)S(1)}, f32[3,4,192]{2,1,0:T(4,128)S(1)}, u32[]{:S(2)}, u32[]{:S(2)}) collective-permute-start(f32[3,4,192]{2,1,0:T(4,128)S(1)} %get-tuple-element.70), channel_id=1, source_target_pairs={{0,8},{8,0},{4,12},{12,4},{1,9},{9,1},{5,13},{13,5},{2,10},{10,2},... | collective-permute-start | bytes 27656 | tf_op jit(solution)/shard_map/ppermute | solution.py:484
  22.7 12.7 %collective-permute-start.5 = (bf16[384,512]{1,0:T(8,128)(2,1)S(1)}, bf16[384,512]{1,0:T(8,128)(2,1)S(1)}, u32[]{:S(2)}, u32[]{:S(2)}) collective-permute-start(bf16[384,512]{1,0:T(8,128)(2,1)S(1)} %get-tuple-element.80), channel_id=1, source_target_pairs={{0,4},{4,0},{8,12},{12,8},{1,5},{5,1},{9,13},{13,9},{2,6},{6,2},{1... | collective-permute-start | bytes 1179656 | tf_op jit(solution)/shard_map/ppermute | solution.py:475
  22.7 12.7 %collective-permute-start.6 = (bf16[384,512]{1,0:T(8,128)(2,1)S(1)}, bf16[384,512]{1,0:T(8,128)(2,1)S(1)}, u32[]{:S(2)}, u32[]{:S(2)}) collective-permute-start(bf16[384,512]{1,0:T(8,128)(2,1)S(1)} %get-tuple-element.80), channel_id=1, source_target_pairs={{4,8},{8,4},{5,9},{9,5},{6,10},{10,6},{7,11},{11,7},{20,24},{24,20... | collective-permute-start | bytes 1179656 | tf_op jit(solution)/shard_map/ppermute | solution.py:476
  30.5 13.9 %collective-permute-start.7 = (bf16[408,512]{1,0:T(8,128)(2,1)S(1)}, bf16[408,512]{1,0:T(8,128)(2,1)S(1)}, u32[]{:S(2)}, u32[]{:S(2)}) collective-permute-start(bf16[408,512]{1,0:T(8,128)(2,1)S(1)} %get-tuple-element.85), channel_id=1, source_target_pairs={{0,4},{4,0},{8,12},{12,8},{1,5},{5,1},{9,13},{13,9},{2,6},{6,2},{1... | collective-permute-start | bytes 1253384 | tf_op jit(solution)/shard_map/ppermute | solution.py:475
  32.5 11.9 %collective-permute-start.8 = (bf16[408,512]{1,0:T(8,128)(2,1)S(1)}, bf16[408,512]{1,0:T(8,128)(2,1)S(1)}, u32[]{:S(2)}, u32[]{:S(2)}) collective-permute-start(bf16[408,512]{1,0:T(8,128)(2,1)S(1)} %get-tuple-element.86), channel_id=1, source_target_pairs={{4,8},{8,4},{5,9},{9,5},{6,10},{10,6},{7,11},{11,7},{20,24},{24,20... | collective-permute-start | bytes 1253384 | tf_op jit(solution)/shard_map/ppermute | solution.py:476
  38.8 14.5 %collective-permute-start.10 = (bf16[384,512]{1,0:T(8,128)(2,1)S(1)}, bf16[384,512]{1,0:T(8,128)(2,1)S(1)}, u32[]{:S(2)}, u32[]{:S(2)}) collective-permute-start(bf16[384,512]{1,0:T(8,128)(2,1)S(1)} %get-tuple-element.103), channel_id=1, source_target_pairs={{4,8},{8,4},{5,9},{9,5},{6,10},{10,6},{7,11},{11,7},{20,24},{24,20... | collective-permute-start | bytes 1179656 | tf_op jit(solution)/shard_map/ppermute | solution.py:476
  39.5 13.8 %collective-permute-start.9 = (bf16[384,512]{1,0:T(8,128)(2,1)S(1)}, bf16[384,512]{1,0:T(8,128)(2,1)S(1)}, u32[]{:S(2)}, u32[]{:S(2)}) collective-permute-start(bf16[384,512]{1,0:T(8,128)(2,1)S(1)} %get-tuple-element.102), channel_id=1, source_target_pairs={{0,4},{4,0},{8,12},{12,8},{1,5},{5,1},{9,13},{13,9},{2,6},{6,2},{1... | collective-permute-start | bytes 1179656 | tf_op jit(solution)/shard_map/ppermute | solution.py:475
  45.9 9.9 %collective-permute-start.11 = (bf16[384,256]{1,0:T(8,128)(2,1)S(1)}, bf16[384,256]{1,0:T(8,128)(2,1)S(1)}, u32[]{:S(2)}, u32[]{:S(2)}) collective-permute-start(bf16[384,256]{1,0:T(8,128)(2,1)S(1)} %get-tuple-element.106), channel_id=1, source_target_pairs={{0,4},{4,0},{8,12},{12,8},{1,5},{5,1},{9,13},{13,9},{2,6},{6,2},{1... | collective-permute-start | bytes 589832 | tf_op jit(solution)/shard_map/ppermute | solution.py:475
  48.1 7.8 %collective-permute-start.12 = (bf16[384,256]{1,0:T(8,128)(2,1)S(1)}, bf16[384,256]{1,0:T(8,128)(2,1)S(1)}, u32[]{:S(2)}, u32[]{:S(2)}) collective-permute-start(bf16[384,256]{1,0:T(8,128)(2,1)S(1)} %get-tuple-element.107), channel_id=1, source_target_pairs={{4,8},{8,4},{5,9},{9,5},{6,10},{10,6},{7,11},{11,7},{20,24},{24,20... | collective-permute-start | bytes 589832 | tf_op jit(solution)/shard_map/ppermute | solution.py:476

commit v13 on v12

--- a/solution.py
+++ b/solution.py
@@ -586,6 +586,12 @@
         [windows, low(DEPTH, FR_DEV, SLOTS - TOK_FRAME, HD), accums], 2 * heads * unit,
     )
     rk_one, rk_two = swap(gk_one, gk_two)
+    gq_rest, gv_own, gk_own = call(
+        rest_kernel, "rest", (),
+        (query, grad, chosen, prob_low, score_low, gv_own, gk_own),
+        (low(ROWS, rest), full(ROWS, rest), full(ROWS, rest)), [], heads * unit,
+    )
+    rv_one, rv_two, gv_own = lax.optimization_barrier((rv_one, rv_two, gv_own))
     y_prob, y_score, logs, deltas, gq_one, gq_two = call(
         back_kernel, "back", (table,),
         (key, masked, grad_probs, mine, rv_one, rv_two, s_far, s_other),
@@ -594,12 +600,6 @@
         [full(2, ROWS, SPLIT), full(2, 2 * NOTES, TOK_FRAME)], MOVED * unit,
     )
     rq_one, rq_two = swap(gq_one, gq_two)
-    score_low, logs = lax.optimization_barrier((score_low, logs))
-    gq_rest, gv_own, gk_own = call(
-        rest_kernel, "rest", (),
-        (query, grad, chosen, prob_low, score_low, gv_own, gk_own),
-        (low(ROWS, rest), full(ROWS, rest), full(ROWS, rest)), [], heads * unit,
-    )
     gq_near, gk_near, gv_near = call(
         home_kernel, "home", (table,),
         (query, grad, key, f_one, f_two, near_masked, near_grads, y_prob, y_score, logs, deltas),

time: 57.1 us -> 56.4 us (0.988)
  starting transfers between devices: 22 us -> 25.7 us
  waiting for transfers between devices: 9.5 us -> 6.64 us
  Pallas kernels: 22.6 us -> 21 us
    ppermute x6, waiting for transfers between devices: 9.48 us -> 5.15 us  [swap(): lax.ppermute(one, 'frames', both_ways(first))]
    ppermute x1, starting transfers between devices: 2.31 us -> 5.71 us  [swap_far(): far = lax.ppermute(far, 'frames', both_ways(near))]
    pallas_call x13, Pallas kernels: 22.6 us -> 21 us  [call(): pl.pallas_call(kernel, out_shape=outs, in_specs=[pl.BlockSpec(memory_spac...]
    ppermute x1, waiting for transfers between devices: 0.01 us -> 1.48 us  [swap_far(): far = lax.ppermute(far, 'frames', both_ways(near))]
  transfers between devices with their start and end apart: 13 -> 13, of which waited for: 5 -> 5; matrix products, arithmetic and copies ran while one was open for 3% -> 3% of each run, Pallas kernels for 36% -> 34%
where the time goes in v13:
time: 56.4 us; the launch traced here: 56.1 us
  starting transfers between devices  25.7 us (46%)
  Pallas kernels  21 us (37%)
  waiting for transfers between devices  6.64 us (12%)
  other arithmetic  1.02 us (2%)
  between operations  1 us (2%)
  local copies, waits for them, and re-layouts  0.73 us (1%)
    pallas_call x13, Pallas kernels, call(): pl.pallas_call(kernel, out_shape=outs, in_specs=[pl.BlockSpec(memory_spac...  21 us
    ppermute x6, starting transfers between devices, swap(): lax.ppermute(one, 'frames', both_ways(first))  15.8 us
    ppermute x1, starting transfers between devices, swap_far(): far = lax.ppermute(far, 'frames', both_ways(near))  5.71 us
    ppermute x6, waiting for transfers between devices, swap(): lax.ppermute(one, 'frames', both_ways(first))  5.15 us
    ppermute x6, starting transfers between devices, swap(): lax.ppermute(two, 'frames', both_ways(second))  4.21 us
    ppermute x1, waiting for transfers between devices, swap_far(): far = lax.ppermute(far, 'frames', both_ways(near))  1.48 us
  transfers between devices with their start and end apart: 13, of which 5 were waited for; matrix products, arithmetic and copies ran while one was open for 3% of the time, Pallas kernels for 34%

profile of v13, /device:TPU:0, one launch (start us, length us, event | category | flops | bytes accessed | tf_op | source)
XLA Modules:
  0.0 56.1 jit_solution(7074452357468144987)
XLA Ops:
  0.6 0.0 copy-start.1
  0.6 0.0 copy-start
  0.7 1.1 %pack_queries.1 = bf16[2,384,256]{2,1,0:T(8,128)(2,1)S(1)} custom-call(bf16[384,768]{1,0:T(8,128)(2,1)} %queries.1, bf16[384,768]{1,0:T(8,128)(2,1)} %grad_out.1), custom_call_target="tpu_custom_call" | custom-call | flops 56623104 | tf_op jit(solution)/shard_map/pack_queries/pallas_call | solution.py:504
  1.7 3.1 %collective-permute-start.1 = (bf16[2,384,256]{2,1,0:T(8,128)(2,1)S(1)}, bf16[2,384,256]{2,1,0:T(8,128)(2,1)S(1)}, u32[]{:S(2)}, u32[]{:S(2)}) collective-permute-start(bf16[2,384,256]{2,1,0:T(8,128)(2,1)S(1)} %pack_queries.1), channel_id=1, source_target_pairs={{0,4},{4,0},{8,12},{12,8},{1,5},{5,1},{9,13},{13,9},{2,6},{6,2},{1... | collective-permute-start | bytes 1179656 | tf_op jit(solution)/shard_map/ppermute | solution.py:475
  4.8 0.7 %collective-permute-start = (bf16[2,384,256]{2,1,0:T(8,128)(2,1)S(1)}, bf16[2,384,256]{2,1,0:T(8,128)(2,1)S(1)}, u32[]{:S(2)}, u32[]{:S(2)}) collective-permute-start(bf16[2,384,256]{2,1,0:T(8,128)(2,1)S(1)} %pack_queries.1), channel_id=1, source_target_pairs={{4,8},{8,4},{5,9},{9,5},{6,10},{10,6},{7,11},{11,7},{20,24},{24,20... | collective-permute-start | bytes 1179656 | tf_op jit(solution)/shard_map/ppermute | solution.py:476
  5.5 1.1 %pack_keys.1 = (bf16[384,512]{1,0:T(8,128)(2,1)S(1)}, bf16[384,512]{1,0:T(8,128)(2,1)S(1)}) custom-call(bf16[384,768]{1,0:T(8,128)(2,1)} %keys.1, bf16[384,768]{1,0:T(8,128)(2,1)} %values.1), custom_call_target="tpu_custom_call" | custom-call | flops 56623104 | tf_op jit(solution)/shard_map/pack_keys/pallas_call | solution.py:504
  6.6 4.4 %collective-permute-start.3 = (bf16[384,512]{1,0:T(8,128)(2,1)S(1)}, bf16[384,512]{1,0:T(8,128)(2,1)S(1)}, u32[]{:S(2)}, u32[]{:S(2)}) collective-permute-start(bf16[384,512]{1,0:T(8,128)(2,1)S(1)} %get-tuple-element.67), channel_id=1, source_target_pairs={{0,4},{4,0},{8,12},{12,8},{1,5},{5,1},{9,13},{13,9},{2,6},{6,2},{1... | collective-permute-start | bytes 1179656 | tf_op jit(solution)/shard_map/ppermute | solution.py:475
  11.1 0.7 %collective-permute-start.2 = (bf16[384,512]{1,0:T(8,128)(2,1)S(1)}, bf16[384,512]{1,0:T(8,128)(2,1)S(1)}, u32[]{:S(2)}, u32[]{:S(2)}) collective-permute-start(bf16[384,512]{1,0:T(8,128)(2,1)S(1)} %get-tuple-element.67), channel_id=1, source_target_pairs={{4,8},{8,4},{5,9},{9,5},{6,10},{10,6},{7,11},{11,7},{20,24},{24,20... | collective-permute-start | bytes 1179656 | tf_op jit(solution)/shard_map/ppermute | solution.py:476
  11.8 0.0 copy-done.1
  11.8 0.1 pad_dynamic-slice_fusion.1
  11.8 0.1 copy.10
  11.9 0.1 reshape.12
  12.0 0.0 copy-done
  12.0 0.1 pad_dynamic-slice_fusion
  12.1 0.2 copy.11
  12.3 0.1 reshape.13
  12.4 0.1 concatenate.6.table
  12.5 2.2 %stage.1 = (bf16[384,768]{1,0:T(8,128)(2,1)S(1)}, bf16[384,768]{1,0:T(8,128)(2,1)S(1)}, bf16[384,768]{1,0:T(8,128)(2,1)S(1)}, bf16[384,768]{1,0:T(8,128)(2,1)S(1...) custom-call(s32[309]{0:T(512)S(1)} %concatenate.6.table, bf16[384,768]{1,0:T(8,128)(2,1)} %queries.1, ...), custom_call_target="tpu_custom_call" | custom-call | flops 56623104 | tf_op jit(solution)/shard_map/stage/pallas_call | solution.py:504
  14.7 0.6 %own_scores.1 = (f32[4,2,192,192]{3,2,1,0:T(8,128)S(1)}, f32[4,2,192,192]{3,2,1,0:T(8,128)S(1)}) custom-call(bf16[384,768]{1,0:T(8,128)(2,1)S(1)} %get-tuple-element.58.queries, bf16[384,768]{1,0:T(8,128)(2,1)S(1)} %get-tuple-element.59.grad_out, bf16[384,768]{1,0:T(8,128)(2,1)S(1)} %get-tuple-element.60.keys.k_own, ...), custom_call_target="tpu_custom_call" | custom-call | flops 113246208 | tf_op jit(solution)/shard_map/own_scores/pallas_call | solution.py:504
  15.3 1.4 %own_stats.1 = (f32[2,2,2,192,192]{4,3,2,1,0:T(8,128)S(1)}, f32[2,2,2,192,192]{4,3,2,1,0:T(8,128)S(1)}, f32[3,4,192]{2,1,0:T(4,128)S(1)}) custom-call(s32[309]{0:T(512)S(1)} %concatenate.6.table, bf16[384,768]{1,0:T(8,128)(2,1)S(1)} %get-tuple-element.58.queries, bf16[384,768]{1,0:T(8,128)(2,1)S(1)} %get-tuple-element.59.grad_out, ...), custom_call_target="tpu_custom_call" | custom-call | flops 113246208 | tf_op jit(solution)/shard_map/own_stats/pallas_call | solution.py:504
  16.7 0.0 collective-permute-done.1.f_one
  16.7 0.0 collective-permute-done.f_two
  16.7 1.8 %stats.1 = (f32[4,2,2,192,192]{4,3,2,1,0:T(8,128)S(1)}, f32[4,2,2,192,192]{4,3,2,1,0:T(8,128)S(1)}, f32[3,12,192]{2,1,0:T(8,128)S(1)}, f32[48,192]{1,0:T(8,128)S...) custom-call(s32[309]{0:T(512)S(1)} %concatenate.6.table, ...), custom_call_target="tpu_custom_call" | custom-call | flops 226492416 | tf_op jit(solution)/shard_map/stats/pallas_call | solution.py:504
  18.5 5.7 %collective-permute-start.4 = (f32[3,4,192]{2,1,0:T(4,128)S(1)}, f32[3,4,192]{2,1,0:T(4,128)S(1)}, u32[]{:S(2)}, u32[]{:S(2)}) collective-permute-start(f32[3,4,192]{2,1,0:T(4,128)S(1)} %get-tuple-element.71), channel_id=1, source_target_pairs={{0,8},{8,0},{4,12},{12,4},{1,9},{9,1},{5,13},{13,5},{2,10},{10,2},... | collective-permute-start | bytes 27656 | tf_op jit(solution)/shard_map/ppermute | solution.py:484
  24.2 0.7 %collective-permute-start.6 = (bf16[384,512]{1,0:T(8,128)(2,1)S(1)}, bf16[384,512]{1,0:T(8,128)(2,1)S(1)}, u32[]{:S(2)}, u32[]{:S(2)}) collective-permute-start(bf16[384,512]{1,0:T(8,128)(2,1)S(1)} %get-tuple-element.81), channel_id=1, source_target_pairs={{4,8},{8,4},{5,9},{9,5},{6,10},{10,6},{7,11},{11,7},{20,24},{24,20... | collective-permute-start | bytes 1179656 | tf_op jit(solution)/shard_map/ppermute | solution.py:476
  24.9 1.9 %collective-permute-start.5 = (bf16[384,512]{1,0:T(8,128)(2,1)S(1)}, bf16[384,512]{1,0:T(8,128)(2,1)S(1)}, u32[]{:S(2)}, u32[]{:S(2)}) collective-permute-start(bf16[384,512]{1,0:T(8,128)(2,1)S(1)} %get-tuple-element.81), channel_id=1, source_target_pairs={{0,4},{4,0},{8,12},{12,8},{1,5},{5,1},{9,13},{13,9},{2,6},{6,2},{1... | collective-permute-start | bytes 1179656 | tf_op jit(solution)/shard_map/ppermute | solution.py:475
  26.7 0.0 collective-permute-done.3.k_one
  26.7 0.0 collective-permute-done.2.k_two
  26.7 1.5 %collective-permute-done.4.s_far = f32[3,4,192]{2,1,0:T(4,128)S(1)} collective-permute-done((f32[3,4,192]{2,1,0:T(4,128)S(1)}, f32[3,4,192]{2,1,0:T(4,128)S(1)}, u32[]{:S(2)}, u32[]{:S(2)}) %collective-permute-start.4) | collective-permute-done | bytes 9248 | tf_op jit(solution)/shard_map/ppermute | solution.py:484
  28.2 3.5 %values_part.1 = (bf16[4,2,576,128]{3,2,1,0:T(8,128)(2,1)S(1)}, bf16[4,2,576,192]{3,2,1,0:T(8,128)(2,1)S(1)}, f32[384,512]{1,0:T(8,128)S(1)}, bf16[408,512]{1,0:T(8,128)(2,1)S(1)}, bf16[408,512]{1,0:T(8,128)(2,1)S(1)}) custom-call(s32[309]{0:T(512)S(1)} %concatenate.6.table, bf16[384,768]{1,0:T(8,128)(2,1)S(1)} %get-tuple-element.58.queries, ...), custom_call_target="tpu_custom_call" | custom-call | flops 452984832 | tf_op jit(solution)/shard_map/values_part/pallas_call | solution.py:504
  31.7 0.4 collective-permute-start.7
  32.1 0.7 %collective-permute-start.8 = (bf16[408,512]{1,0:T(8,128)(2,1)S(1)}, bf16[408,512]{1,0:T(8,128)(2,1)S(1)}, u32[]{:S(2)}, u32[]{:S(2)}) collective-permute-start(bf16[408,512]{1,0:T(8,128)(2,1)S(1)} %get-tuple-element.92), channel_id=1, source_target_pairs={{4,8},{8,4},{5,9},{9,5},{6,10},{10,6},{7,11},{11,7},{20,24},{24,20... | collective-permute-start | bytes 1253384 | tf_op jit(solution)/shard_map/ppermute | solution.py:476
  32.8 0.0 collective-permute-done.6.v_two
  32.8 2.5 %collective-permute-done.5.v_one = bf16[384,512]{1,0:T(8,128)(2,1)S(1)} collective-permute-done((bf16[384,512]{1,0:T(8,128)(2,1)S(1)}, bf16[384,512]{1,0:T(8,128)(2,1)S(1)}, u32[]{:S(2)}, u32[]{:S(2)}) %collective-permute-start.5) | collective-permute-done | bytes 393248 | tf_op jit(solution)/shard_map/ppermute | solution.py:475
  35.2 3.4 %keys_part.1 = (bf16[4,2,576,192]{3,2,1,0:T(8,128)(2,1)S(1)}, f32[384,512]{1,0:T(8,128)S(1)}, bf16[384,512]{1,0:T(8,128)(2,1)S(1)}, bf16[384,512]{1,0:T(8,128)(2,1)S(1)}) custom-call(s32[309]{0:T(512)S(1)} %concatenate.6.table, bf16[384,768]{1,0:T(8,128)(2,1)S(1)} %get-tuple-element.58.queries, bf16[384,768]{1,0:T(8,128)(2,1)S(1)} %get-tuple-element.59.grad_out, ...), custom_call_target="tpu_custom_call" | custom-call | flops 452984832 | tf_op jit(solution)/shard_map/keys_part/pallas_call | solution.py:504
  38.7 2.6 %collective-permute-start.9 = (bf16[384,512]{1,0:T(8,128)(2,1)S(1)}, bf16[384,512]{1,0:T(8,128)(2,1)S(1)}, u32[]{:S(2)}, u32[]{:S(2)}) collective-permute-start(bf16[384,512]{1,0:T(8,128)(2,1)S(1)} %get-tuple-element.104), channel_id=1, source_target_pairs={{0,4},{4,0},{8,12},{12,8},{1,5},{5,1},{9,13},{13,9},{2,6},{6,2},{1... | collective-permute-start | bytes 1179656 | tf_op jit(solution)/shard_map/ppermute | solution.py:475
  41.3 0.9 %collective-permute-start.10 = (bf16[384,512]{1,0:T(8,128)(2,1)S(1)}, bf16[384,512]{1,0:T(8,128)(2,1)S(1)}, u32[]{:S(2)}, u32[]{:S(2)}) collective-permute-start(bf16[384,512]{1,0:T(8,128)(2,1)S(1)} %get-tuple-element.105), channel_id=1, source_target_pairs={{4,8},{8,4},{5,9},{9,5},{6,10},{10,6},{7,11},{11,7},{20,24},{24,20... | collective-permute-start | bytes 1179656 | tf_op jit(solution)/shard_map/ppermute | solution.py:476
  42.1 1.2 %rest.1 = (bf16[384,512]{1,0:T(8,128)(2,1)S(1)}, f32[384,512]{1,0:T(8,128)S(1)}, f32[384,512]{1,0:T(8,128)S(1)}) custom-call(bf16[384,768]{1,0:T(8,128)(2,1)S(1)} %get-tuple-element.58.queries, bf16[384,768]{1,0:T(8,128)(2,1)S(1)} %get-tuple-element.59.grad_out, bf16[4,2,576,128]{3,2,1,0:T(8,128)(2,1)S(1)} %get-tuple-element.76.chosen_in, ...), custom_call_target="tpu_custom_call" | custom-call | flops 226492416 | tf_op jit(solution)/shard_map/rest/pallas_call | solution.py:504
  43.4 1.0 %collective-permute-done.7.r_one = bf16[408,512]{1,0:T(8,128)(2,1)S(1)} collective-permute-done((bf16[408,512]{1,0:T(8,128)(2,1)S(1)}, bf16[408,512]{1,0:T(8,128)(2,1)S(1)}, u32[]{:S(2)}, u32[]{:S(2)}) %collective-permute-start.7) | collective-permute-done | bytes 417824 | tf_op jit(solution)/shard_map/ppermute | solution.py:475
  44.4 0.0 collective-permute-done.8.r_two
  44.4 1.1 %back.1 = (bf16[4,2,2,192,192]{4,3,2,1,0:T(8,128)(2,1)S(1)}, bf16[4,2,2,192,192]{4,3,2,1,0:T(8,128)(2,1)S(1)}, f32[12,192]{1,0:T(8,128)S(1)}, f32[12,192]{1,0:T(...) custom-call(s32[309]{0:T(512)S(1)} %concatenate.6.table, ...), custom_call_target="tpu_custom_call" | custom-call | flops 113246208 | tf_op jit(solution)/shard_map/back/pallas_call | solution.py:504
  45.5 3.4 %collective-permute-start.11 = (bf16[384,256]{1,0:T(8,128)(2,1)S(1)}, bf16[384,256]{1,0:T(8,128)(2,1)S(1)}, u32[]{:S(2)}, u32[]{:S(2)}) collective-permute-start(bf16[384,256]{1,0:T(8,128)(2,1)S(1)} %get-tuple-element.108), channel_id=1, source_target_pairs={{0,4},{4,0},{8,12},{12,8},{1,5},{5,1},{9,13},{13,9},{2,6},{6,2},{1... | collective-permute-start | bytes 589832 | tf_op jit(solution)/shard_map/ppermute | solution.py:475
  49.0 0.7 %collective-permute-start.12 = (bf16[384,256]{1,0:T(8,128)(2,1)S(1)}, bf16[384,256]{1,0:T(8,128)(2,1)S(1)}, u32[]{:S(2)}, u32[]{:S(2)}) collective-permute-start(bf16[384,256]{1,0:T(8,128)(2,1)S(1)} %get-tuple-element.109), channel_id=1, source_target_pairs={{4,8},{8,4},{5,9},{9,5},{6,10},{10,6},{7,11},{11,7},{20,24},{24,20... | collective-permute-start | bytes 589832 | tf_op jit(solution)/shard_map/ppermute | solution.py:476
  49.6 0.2 add_convert_fusion
  49.8 1.8 %home.1 = (f32[384,256]{1,0:T(8,128)S(1)}, bf16[384,256]{1,0:T(8,128)(2,1)S(1)}, bf16[384,256]{1,0:T(8,128)(2,1)S(1)}) custom-call(s32[309]{0:T(512)S(1)} %concatenate.6.table, bf16[384,768]{1,0:T(8,128)(2,1)S(1)} %get-tuple-element.58.queries, bf16[384,768]{1,0:T(8,128)(2,1)S(1)} %get-tuple-element.59.grad_out, ...), custom_call_target="tpu_custom_call" | custom-call | flops 339738624 | tf_op jit(solution)/shard_map/home/pallas_call | solution.py:504
  51.6 0.9 %pad_maximum_fusion = bf16[384,768]{1,0:T(8,128)(2,1)} fusion(bf16[384,512]{1,0:T(8,128)(2,1)S(1)} %add_convert_fusion, bf16[384,256]{1,0:T(8,128)(2,1)S(1)} %get-tuple-element.111), kind=kLoop, calls=%fused_computation.1 | loop fusion | flops 1179648 | bytes 1179648 | tf_op jit(solution)/shard_map/concatenate | solution.py:609
  52.5 0.3 collective-permute-done.9.one
  52.8 0.0 collective-permute-done.10.two
  52.8 0.9 %last_keys.1 = bf16[384,768]{1,0:T(8,128)(2,1)} custom-call(bf16[384,256]{1,0:T(8,128)(2,1)S(1)} %get-tuple-element.102.ready, f32[384,512]{1,0:T(8,128)S(1)} %get-tuple-element.103.own, bf16[384,512]{1,0:T(8,128)(2,1)S(1)} %collective-permute-done.9.one, bf16[384,512]{1,0:T(8,128)(2,1)S(1)} %collective-permute-done.10.two), custom_call_target="tpu_custom_call" | custom-call | flops 56623104 | tf_op jit(solution)/shard_map/last_keys/pallas_call | solution.py:504
  53.7 1.4 %collective-permute-done.11.one = bf16[384,256]{1,0:T(8,128)(2,1)S(1)} collective-permute-done((bf16[384,256]{1,0:T(8,128)(2,1)S(1)}, bf16[384,256]{1,0:T(8,128)(2,1)S(1)}, u32[]{:S(2)}, u32[]{:S(2)}) %collective-permute-start.11) | collective-permute-done | bytes 196640 | tf_op jit(solution)/shard_map/ppermute | solution.py:475
  55.1 0.0 collective-permute-done.12.two
  55.1 0.8 %last_queries.1 = bf16[384,768]{1,0:T(8,128)(2,1)} custom-call(bf16[384,512]{1,0:T(8,128)(2,1)S(1)} %get-tuple-element.85.ready, f32[384,256]{1,0:T(8,128)S(1)} %get-tuple-element.107.own, bf16[384,256]{1,0:T(8,128)(2,1)S(1)} %collective-permute-done.11.one, bf16[384,256]{1,0:T(8,128)(2,1)S(1)} %collective-permute-done.12.two), custom_call_target="tpu_custom_call" | custom-call | flops 56623104 | tf_op jit(solution)/shard_map/last_queries/pallas_call | solution.py:504
  (1 shorter events, 0.0 us)
Async XLA Ops:
  0.6 11.1 %copy-start.1 = (s32[8,3]{0,1:T(4,128)S(1)}, s32[8,3]{0,1:T(4,128)}, u32[]{:S(2)}) copy-start(s32[8,3]{0,1:T(4,128)} %param.10) | copy-start | bytes 292
  0.6 11.4 %copy-start = (s32[8,3,4,4]{0,3,2,1:T(4,128)S(1)}, s32[8,3,4,4]{0,3,2,1:T(4,128)}, u32[]{:S(2)}) copy-start(s32[8,3,4,4]{0,3,2,1:T(4,128)} %param.11) | copy-start | bytes 4612
  1.7 15.0 %collective-permute-start.1 = (bf16[2,384,256]{2,1,0:T(8,128)(2,1)S(1)}, bf16[2,384,256]{2,1,0:T(8,128)(2,1)S(1)}, u32[]{:S(2)}, u32[]{:S(2)}) collective-permute-start(bf16[2,384,256]{2,1,0:T(8,128)(2,1)S(1)} %pack_queries.1), channel_id=1, source_target_pairs={{0,4},{4,0},{8,12},{12,8},{1,5},{5,1},{9,13},{13,9},{2,6},{6,2},{1... | collective-permute-start | bytes 1179656 | tf_op jit(solution)/shard_map/ppermute | solution.py:475
  4.8 11.9 %collective-permute-start = (bf16[2,384,256]{2,1,0:T(8,128)(2,1)S(1)}, bf16[2,384,256]{2,1,0:T(8,128)(2,1)S(1)}, u32[]{:S(2)}, u32[]{:S(2)}) collective-permute-start(bf16[2,384,256]{2,1,0:T(8,128)(2,1)S(1)} %pack_queries.1), channel_id=1, source_target_pairs={{4,8},{8,4},{5,9},{9,5},{6,10},{10,6},{7,11},{11,7},{20,24},{24,20... | collective-permute-start | bytes 1179656 | tf_op jit(solution)/shard_map/ppermute | solution.py:476
  6.6 20.1 %collective-permute-start.3 = (bf16[384,512]{1,0:T(8,128)(2,1)S(1)}, bf16[384,512]{1,0:T(8,128)(2,1)S(1)}, u32[]{:S(2)}, u32[]{:S(2)}) collective-permute-start(bf16[384,512]{1,0:T(8,128)(2,1)S(1)} %get-tuple-element.67), channel_id=1, source_target_pairs={{0,4},{4,0},{8,12},{12,8},{1,5},{5,1},{9,13},{13,9},{2,6},{6,2},{1... | collective-permute-start | bytes 1179656 | tf_op jit(solution)/shard_map/ppermute | solution.py:475
  11.1 15.7 %collective-permute-start.2 = (bf16[384,512]{1,0:T(8,128)(2,1)S(1)}, bf16[384,512]{1,0:T(8,128)(2,1)S(1)}, u32[]{:S(2)}, u32[]{:S(2)}) collective-permute-start(bf16[384,512]{1,0:T(8,128)(2,1)S(1)} %get-tuple-element.67), channel_id=1, source_target_pairs={{4,8},{8,4},{5,9},{9,5},{6,10},{10,6},{7,11},{11,7},{20,24},{24,20... | collective-permute-start | bytes 1179656 | tf_op jit(solution)/shard_map/ppermute | solution.py:476
  18.5 9.7 %collective-permute-start.4 = (f32[3,4,192]{2,1,0:T(4,128)S(1)}, f32[3,4,192]{2,1,0:T(4,128)S(1)}, u32[]{:S(2)}, u32[]{:S(2)}) collective-permute-start(f32[3,4,192]{2,1,0:T(4,128)S(1)} %get-tuple-element.71), channel_id=1, source_target_pairs={{0,8},{8,0},{4,12},{12,4},{1,9},{9,1},{5,13},{13,5},{2,10},{10,2},... | collective-permute-start | bytes 27656 | tf_op jit(solution)/shard_map/ppermute | solution.py:484
  24.2 8.6 %collective-permute-start.6 = (bf16[384,512]{1,0:T(8,128)(2,1)S(1)}, bf16[384,512]{1,0:T(8,128)(2,1)S(1)}, u32[]{:S(2)}, u32[]{:S(2)}) collective-permute-start(bf16[384,512]{1,0:T(8,128)(2,1)S(1)} %get-tuple-element.81), channel_id=1, source_target_pairs={{4,8},{8,4},{5,9},{9,5},{6,10},{10,6},{7,11},{11,7},{20,24},{24,20... | collective-permute-start | bytes 1179656 | tf_op jit(solution)/shard_map/ppermute | solution.py:476
  24.9 10.4 %collective-permute-start.5 = (bf16[384,512]{1,0:T(8,128)(2,1)S(1)}, bf16[384,512]{1,0:T(8,128)(2,1)S(1)}, u32[]{:S(2)}, u32[]{:S(2)}) collective-permute-start(bf16[384,512]{1,0:T(8,128)(2,1)S(1)} %get-tuple-element.81), channel_id=1, source_target_pairs={{0,4},{4,0},{8,12},{12,8},{1,5},{5,1},{9,13},{13,9},{2,6},{6,2},{1... | collective-permute-start | bytes 1179656 | tf_op jit(solution)/shard_map/ppermute | solution.py:475
  31.7 12.6 %collective-permute-start.7 = (bf16[408,512]{1,0:T(8,128)(2,1)S(1)}, bf16[408,512]{1,0:T(8,128)(2,1)S(1)}, u32[]{:S(2)}, u32[]{:S(2)}) collective-permute-start(bf16[408,512]{1,0:T(8,128)(2,1)S(1)} %get-tuple-element.91), channel_id=1, source_target_pairs={{0,4},{4,0},{8,12},{12,8},{1,5},{5,1},{9,13},{13,9},{2,6},{6,2},{1... | collective-permute-start | bytes 1253384 | tf_op jit(solution)/shard_map/ppermute | solution.py:475
  32.1 12.3 %collective-permute-start.8 = (bf16[408,512]{1,0:T(8,128)(2,1)S(1)}, bf16[408,512]{1,0:T(8,128)(2,1)S(1)}, u32[]{:S(2)}, u32[]{:S(2)}) collective-permute-start(bf16[408,512]{1,0:T(8,128)(2,1)S(1)} %get-tuple-element.92), channel_id=1, source_target_pairs={{4,8},{8,4},{5,9},{9,5},{6,10},{10,6},{7,11},{11,7},{20,24},{24,20... | collective-permute-start | bytes 1253384 | tf_op jit(solution)/shard_map/ppermute | solution.py:476
  38.7 14.1 %collective-permute-start.9 = (bf16[384,512]{1,0:T(8,128)(2,1)S(1)}, bf16[384,512]{1,0:T(8,128)(2,1)S(1)}, u32[]{:S(2)}, u32[]{:S(2)}) collective-permute-start(bf16[384,512]{1,0:T(8,128)(2,1)S(1)} %get-tuple-element.104), channel_id=1, source_target_pairs={{0,4},{4,0},{8,12},{12,8},{1,5},{5,1},{9,13},{13,9},{2,6},{6,2},{1... | collective-permute-start | bytes 1179656 | tf_op jit(solution)/shard_map/ppermute | solution.py:475
  41.3 11.5 %collective-permute-start.10 = (bf16[384,512]{1,0:T(8,128)(2,1)S(1)}, bf16[384,512]{1,0:T(8,128)(2,1)S(1)}, u32[]{:S(2)}, u32[]{:S(2)}) collective-permute-start(bf16[384,512]{1,0:T(8,128)(2,1)S(1)} %get-tuple-element.105), channel_id=1, source_target_pairs={{4,8},{8,4},{5,9},{9,5},{6,10},{10,6},{7,11},{11,7},{20,24},{24,20... | collective-permute-start | bytes 1179656 | tf_op jit(solution)/shard_map/ppermute | solution.py:476
  45.5 9.5 %collective-permute-start.11 = (bf16[384,256]{1,0:T(8,128)(2,1)S(1)}, bf16[384,256]{1,0:T(8,128)(2,1)S(1)}, u32[]{:S(2)}, u32[]{:S(2)}) collective-permute-start(bf16[384,256]{1,0:T(8,128)(2,1)S(1)} %get-tuple-element.108), channel_id=1, source_target_pairs={{0,4},{4,0},{8,12},{12,8},{1,5},{5,1},{9,13},{13,9},{2,6},{6,2},{1... | collective-permute-start | bytes 589832 | tf_op jit(solution)/shard_map/ppermute | solution.py:475
  49.0 6.1 %collective-permute-start.12 = (bf16[384,256]{1,0:T(8,128)(2,1)S(1)}, bf16[384,256]{1,0:T(8,128)(2,1)S(1)}, u32[]{:S(2)}, u32[]{:S(2)}) collective-permute-start(bf16[384,256]{1,0:T(8,128)(2,1)S(1)} %get-tuple-element.109), channel_id=1, source_target_pairs={{4,8},{8,4},{5,9},{9,5},{6,10},{10,6},{7,11},{11,7},{20,24},{24,20... | collective-permute-start | bytes 589832 | tf_op jit(solution)/shard_map/ppermute | solution.py:476
